TPU v7x, 128 devices: a whole 4x4x4 slice. The times are simulated.
128 devices in a mesh: dp: 32 (over z, x, core), seq: 4 (over y).
Axes of the slice: x: 4, y: 4, z: 4, core: 2. Of those that a mesh axis runs over, the one named last changes fastest.
Arguments:
- queries: bfloat16 [32768, 2560], P(('dp', 'seq')), may hold values from -200 to 200
- keys: bfloat16 [32768, 2560], P(('dp', 'seq')), may hold values from -200 to 200
- values: bfloat16 [32768, 2560], P(('dp', 'seq')), may hold values from -6 to 6
- gain_q: float32 [2560], replicated, may hold values from 0.5 to 1.5
- gain_k: float32 [2560], replicated, may hold values from 0.5 to 1.5
- tile_pairs: int32 [16, 8], replicated, may hold values from 0 to 15, as said below
- tile_lens: int32 [32, 16], P('dp'), may hold values from 40 to 64
- out_grad: bfloat16 [32768, 5120], P(('dp', 'seq')), may hold values from -24 to 24
- w_out: bfloat16 [5120, 2560], P('dp', 'seq'), may hold values from -0.125 to 0.125
Outputs:
- grad_q: bfloat16 [32768, 2560], P(('dp', 'seq'))
- grad_k: bfloat16 [32768, 2560], P(('dp', 'seq'))
- grad_v: bfloat16 [32768, 2560], P(('dp', 'seq'))
- grad_w: float32 [5120, 2560], P('dp', 'seq')
Inputs may be any that keep to these rules, and one draw needn't show every extreme that they name: `tile_pairs`: row a lists 8 different tiles of the window, with tile a first.
All inputs are finite; a program needn't handle non-finite values.
Results may differ from a plain program's by a relative error of at most 0.02.
Values may be sent and summed in bfloat16 or wider, within the bound.
No kernel may reach another device: no remote copies, remote signals or barrier semaphores. Data moves between devices by JAX's collectives and lax.ppermute only.
A program may use at most 128 MiB of HBM per device.

v0:
```python
import math

import jax
import jax.numpy as jnp
from jax import lax
from jax.sharding import PartitionSpec as P

HEAD_DIM = 128


EPS = 1e-06


def multiply(pattern, left, right):
    return jnp.einsum(pattern, left, right, preferred_element_type=jnp.float32)


def normalize(field, gain):
    values_f = field.astype(jnp.float32)
    row_scale = lax.rsqrt(jnp.mean(values_f * values_f, axis=-1, keepdims=True) + EPS)
    return ((values_f * row_scale * gain).astype(jnp.bfloat16), row_scale)


def norm_finish(values_f, row_scale, gated, inner, width):
    return (row_scale * gated - values_f * row_scale**3 * inner / width).astype(jnp.bfloat16)


def tile_attention(query_tiles, key_tiles, value_tiles, grad_tiles, tile_pairs, live_lengths):
    tile_count, tile_rows, head_width = query_tiles.shape
    neighbours = tile_pairs.shape[1]
    factor = 1.0 / math.sqrt(head_width)
    key_near = jnp.take(key_tiles, tile_pairs, axis=0).reshape(
        tile_count, neighbours * tile_rows, head_width
    )
    value_near = jnp.take(value_tiles, tile_pairs, axis=0).reshape(
        tile_count, neighbours * tile_rows, head_width
    )
    near_lengths = jnp.take(live_lengths, tile_pairs, axis=0)
    live = (
        jnp.arange(tile_rows, dtype=jnp.int32)[None, None, :] < near_lengths[:, :, None]
    ).reshape(tile_count, neighbours * tile_rows)
    scores = multiply("aqd,akd->aqk", query_tiles, key_near) * factor
    scores = jnp.where(live[:, None, :], scores, -jnp.inf)
    row_max = jnp.max(scores, axis=-1, keepdims=True)
    weights = jnp.exp(scores - row_max)
    probs = weights / jnp.sum(weights, axis=-1, keepdims=True)
    probs_low = probs.astype(jnp.bfloat16)
    attended = multiply("aqk,akd->aqd", probs_low, value_near).astype(jnp.bfloat16)
    grad_probs = multiply("aqd,akd->aqk", grad_tiles, value_near)
    delta = jnp.sum(probs * grad_probs, axis=-1, keepdims=True)
    grad_scores = (probs * (grad_probs - delta)).astype(jnp.bfloat16)
    grad_query = (multiply("aqk,akd->aqd", grad_scores, key_near) * factor).astype(jnp.bfloat16)
    grad_key_near = multiply("aqk,aqd->akd", grad_scores, query_tiles) * factor
    grad_value_near = multiply("aqk,aqd->akd", probs_low, grad_tiles)
    owners = (
        tile_pairs[:, :, None] == jnp.arange(tile_count, dtype=jnp.int32)[None, None, :]
    ).astype(jnp.float32)
    grad_key = jnp.einsum(
        "anb,antd->btd",
        owners,
        grad_key_near.reshape(tile_count, neighbours, tile_rows, head_width),
        precision=lax.Precision.HIGHEST,
    ).astype(jnp.bfloat16)
    grad_value = jnp.einsum(
        "anb,antd->btd",
        owners,
        grad_value_near.reshape(tile_count, neighbours, tile_rows, head_width),
        precision=lax.Precision.HIGHEST,
    ).astype(jnp.bfloat16)
    return (attended, grad_query, grad_key, grad_value)


def per_device(queries, keys, values, gain_q, gain_k, tile_pairs, tile_lens, out_grad, w_out):
    seq_count = lax.axis_size("seq")
    dp_count = lax.axis_size("dp")
    tok_rows = queries.shape[0]
    width = queries.shape[1]
    local_width = width // seq_count
    clip_rows = tok_rows * seq_count
    tile_count = tile_pairs.shape[0]
    tile_rows = clip_rows // tile_count
    head_count = local_width // HEAD_DIM
    clip_lengths = tile_lens[0]
    query_normed, query_scale = normalize(queries, gain_q)
    key_normed, key_scale = normalize(keys, gain_k)
    query_heads, key_heads, value_heads = (
        lax.all_to_all(query_normed, "seq", split_axis=1, concat_axis=0, tiled=True),
        lax.all_to_all(key_normed, "seq", split_axis=1, concat_axis=0, tiled=True),
        lax.all_to_all(values, "seq", split_axis=1, concat_axis=0, tiled=True),
    )
    cot_all = lax.all_gather(out_grad, "seq", axis=0, tiled=True)
    columns = cot_all
    grad_attended = jnp.dot(
        columns, lax.all_gather(w_out, "dp", axis=0, tiled=True), preferred_element_type=jnp.float32
    ).astype(jnp.bfloat16)

    def split(field):
        return field.reshape(tile_count, tile_rows, head_count, HEAD_DIM).transpose(2, 0, 1, 3)

    def merge(field):
        return field.transpose(1, 2, 0, 3).reshape(clip_rows, local_width)

    def one_head(group):
        return tile_attention(group[0], group[1], group[2], group[3], tile_pairs, clip_lengths)

    attended, grad_qn, grad_kn, grad_vh = lax.map(
        one_head, (split(query_heads), split(key_heads), split(value_heads), split(grad_attended))
    )
    attended = merge(attended)
    grad_qn = merge(grad_qn)
    grad_kn = merge(grad_kn)
    grad_vh = merge(grad_vh)
    columns = cot_all
    grad_w = lax.psum_scatter(
        (
            jnp.einsum("td,te->de", columns, attended, preferred_element_type=jnp.float32)
            / dp_count
        ).astype(jnp.bfloat16),
        "dp",
        scatter_dimension=0,
        tiled=True,
    ).astype(jnp.float32)
    grad_qt, grad_kt, grad_v = (
        lax.all_to_all(grad_qn, "seq", split_axis=0, concat_axis=1, tiled=True),
        lax.all_to_all(grad_kn, "seq", split_axis=0, concat_axis=1, tiled=True),
        lax.all_to_all(grad_vh, "seq", split_axis=0, concat_axis=1, tiled=True),
    )
    query_full = queries.astype(jnp.float32)
    key_full = keys.astype(jnp.float32)
    gated_q = gain_q * grad_qt.astype(jnp.float32)
    gated_k = gain_k * grad_kt.astype(jnp.float32)
    inner_q = jnp.sum(gated_q * query_full, axis=-1, keepdims=True)
    inner_k = jnp.sum(gated_k * key_full, axis=-1, keepdims=True)
    grad_q = norm_finish(query_full, query_scale, gated_q, inner_q, width)
    grad_k = norm_finish(key_full, key_scale, gated_k, inner_k, width)
    return (grad_q, grad_k, grad_v, grad_w)


def solution(mesh):
    return jax.shard_map(
        per_device,
        mesh=mesh,
        in_specs=(
            P(("dp", "seq"), None),
            P(("dp", "seq"), None),
            P(("dp", "seq"), None),
            P(),
            P(),
            P(),
            P("dp", None),
            P(("dp", "seq"), None),
            P("dp", "seq"),
        ),
        out_specs=(
            P(("dp", "seq"), None),
            P(("dp", "seq"), None),
            P(("dp", "seq"), None),
            P("dp", "seq"),
        ),
        check_vma=False,
    )
```

profile of v0, /device:TPU:24, one launch (start us, length us, event | category | flops | bytes accessed | tf_op | source)
XLA Modules:
  0.0 484.3 jit_solution(18076181013758219229)
XLA Ops:
  12.3 4.7 all-to-all-start
  23.4 9.4 %all-to-all-done = bf16[256,4,640]{2,0,1:T(8,128)(2,1)S(1)} async-done(((bf16[256,4,640]{2,0,1:T(8,128)(2,1)}), bf16[256,4,640]{2,0,1:T(8,128)(2,1)S(1)}, u32[]{:S(2)}, u32[]{:S(2)}) %all-to-all-start) | async-done | bytes 1310752 | tf_op jit(solution)/shard_map/all_to_all | solution.py:87
  32.8 5.6 %all-to-all-start.1 = ((bf16[256,4,640]{2,0,1:T(8,128)(2,1)}), bf16[256,4,640]{2,0,1:T(8,128)(2,1)S(1)}, u32[]{:S(2)}, u32[]{:S(2)}) async-start(bf16[256,4,640]{2,0,1:T(8,128)(2,1)} %copy.75), calls=%async_computation.1 | async-start | bytes 2621440 | tf_op jit(solution)/shard_map/all_to_all | solution.py:88
  40.9 12.4 %all-to-all-done.1 = bf16[256,4,640]{2,0,1:T(8,128)(2,1)S(1)} async-done(((bf16[256,4,640]{2,0,1:T(8,128)(2,1)}), bf16[256,4,640]{2,0,1:T(8,128)(2,1)S(1)}, u32[]{:S(2)}, u32[]{:S(2)}) %all-to-all-start.1) | async-done | bytes 1310752 | tf_op jit(solution)/shard_map/all_to_all | solution.py:88
  53.3 6.3 %all-to-all-start.2 = ((bf16[256,4,640]{2,0,1:T(8,128)(2,1)}), bf16[256,4,640]{2,0,1:T(8,128)(2,1)}, u32[]{:S(2)}, u32[]{:S(2)}) async-start(bf16[256,4,640]{2,0,1:T(8,128)(2,1)} %bitcast.186), calls=%async_computation.2 | async-start | bytes 2621440 | tf_op jit(solution)/shard_map/all_to_all | solution.py:89
  67.6 6.1 %all-to-all-done.2 = bf16[256,4,640]{2,0,1:T(8,128)(2,1)} async-done(((bf16[256,4,640]{2,0,1:T(8,128)(2,1)}), bf16[256,4,640]{2,0,1:T(8,128)(2,1)}, u32[]{:S(2)}, u32[]{:S(2)}) %all-to-all-start.2) | async-done | bytes 1310752 | tf_op jit(solution)/shard_map/all_to_all | solution.py:89
  78.4 83.8 %all-gather.3.cloned.1.call-done = bf16[1024,5120]{1,0:T(8,128)(2,1)} async-done(((bf16[256,5120]{1,0:T(8,128)(2,1)}), bf16[1024,5120]{1,0:T(8,128)(2,1)}) %all-gather.3.cloned.1.call-update) | async-done | bytes 10485776 | tf_op jit(solution)/shard_map/all_gather | solution.py:91
  162.2 13.7 %convolution_convert_fusion.1 = bf16[1024,640]{1,0:T(8,128)(2,1)} fusion(bf16[1024,5120]{1,0:T(8,128)(2,1)} %all-gather.3.cloned.1.call-done, bf16[5120,640]{1,0:T(8,128)(2,1)} %all-gather.5.cloned.1.call-done), kind=kOutput, calls=%fused_computation.95 | convolution fusion | flops 6711541760 | bytes 18350080 | tf_op jit(solution)/shard_map/dot_general | solution.py:93
  180.5 182.3 %while.18 = (s32[]{:T(128)}, bf16[5,16,64,128]{3,2,1,0:T(8,128)(2,1)}, bf16[5,16,64,128]{3,2,1,0:T(8,128)(2,1)}, bf16[5,16,64,128]{3,1,2,0:T(8,128)(2,1)}, bf16[...) while((s32[]{:T(128)}, ...), condition=%wide.region_6.8_spmd, body=%wide.region_2.7_spmd.sunk | while | flops 1219638656 | bytes 88276472 | solution.py:106
  186.1 4.0 broadcast_select_fusion.6
  192.6 3.6 fusion.136
  202.7 7.3 %fusion.138 = bf16[5,16,64,128]{3,1,2,0:T(8,128)(2,1)} fusion(bf16[5,16,64,128]{3,1,2,0:T(8,128)(2,1)} %get-tuple-element.341, s32[]{:T(128)S(6)} %copy.142, f32[16,8,64,128]{3,2,1,0:T(8,128)} %bitcast.172, s32[16,8]{0,1:T(8,128)S(1)} %copy.132), kind=kOutput, calls=%fused_computation.26.clone.1 | convolution fusion | flops 201459712 | bytes 4456964 | tf_op jit(solution)/shard_map/while/body/eval_jaxpr/anb,antd->btd/dot_general | solution.py:58
  211.9 5.1 %fusion.140 = bf16[5,16,64,128]{3,1,2,0:T(8,128)(2,1)} fusion(bf16[5,16,64,128]{3,1,2,0:T(8,128)(2,1)} %get-tuple-element.342, s32[]{:T(128)S(6)} %copy.142, f32[16,8,64,128]{3,2,1,0:T(8,128)S(1)} %bitcast.177, s32[16,8]{0,1:T(8,128)S(1)} %copy.132), kind=kOutput, calls=%fused_computation.28.clone.1 | convolution fusion | flops 201459712 | bytes 4456964 | tf_op jit(solution)/shard_map/while/body/eval_jaxpr/anb,antd->btd/dot_general | solution.py:64
  222.5 4.0 broadcast_select_fusion.6
  239.1 7.3 %fusion.138 = bf16[5,16,64,128]{3,1,2,0:T(8,128)(2,1)} fusion(bf16[5,16,64,128]{3,1,2,0:T(8,128)(2,1)} %get-tuple-element.341, s32[]{:T(128)S(6)} %copy.142, f32[16,8,64,128]{3,2,1,0:T(8,128)} %bitcast.172, s32[16,8]{0,1:T(8,128)S(1)} %copy.132), kind=kOutput, calls=%fused_computation.26.clone.1 | convolution fusion | flops 201459712 | bytes 4456964 | tf_op jit(solution)/shard_map/while/body/eval_jaxpr/anb,antd->btd/dot_general | solution.py:58
  248.3 5.1 %fusion.140 = bf16[5,16,64,128]{3,1,2,0:T(8,128)(2,1)} fusion(bf16[5,16,64,128]{3,1,2,0:T(8,128)(2,1)} %get-tuple-element.342, s32[]{:T(128)S(6)} %copy.142, f32[16,8,64,128]{3,2,1,0:T(8,128)S(1)} %bitcast.177, s32[16,8]{0,1:T(8,128)S(1)} %copy.132), kind=kOutput, calls=%fused_computation.28.clone.1 | convolution fusion | flops 201459712 | bytes 4456964 | tf_op jit(solution)/shard_map/while/body/eval_jaxpr/anb,antd->btd/dot_general | solution.py:64
  258.8 4.0 broadcast_select_fusion.6
  275.4 7.2 %fusion.138 = bf16[5,16,64,128]{3,1,2,0:T(8,128)(2,1)} fusion(bf16[5,16,64,128]{3,1,2,0:T(8,128)(2,1)} %get-tuple-element.341, s32[]{:T(128)S(6)} %copy.142, f32[16,8,64,128]{3,2,1,0:T(8,128)} %bitcast.172, s32[16,8]{0,1:T(8,128)S(1)} %copy.132), kind=kOutput, calls=%fused_computation.26.clone.1 | convolution fusion | flops 201459712 | bytes 4456964 | tf_op jit(solution)/shard_map/while/body/eval_jaxpr/anb,antd->btd/dot_general | solution.py:58
  284.6 5.1 %fusion.140 = bf16[5,16,64,128]{3,1,2,0:T(8,128)(2,1)} fusion(bf16[5,16,64,128]{3,1,2,0:T(8,128)(2,1)} %get-tuple-element.342, s32[]{:T(128)S(6)} %copy.142, f32[16,8,64,128]{3,2,1,0:T(8,128)S(1)} %bitcast.177, s32[16,8]{0,1:T(8,128)S(1)} %copy.132), kind=kOutput, calls=%fused_computation.28.clone.1 | convolution fusion | flops 201459712 | bytes 4456964 | tf_op jit(solution)/shard_map/while/body/eval_jaxpr/anb,antd->btd/dot_general | solution.py:64
  295.2 4.0 broadcast_select_fusion.6
  311.8 7.3 %fusion.138 = bf16[5,16,64,128]{3,1,2,0:T(8,128)(2,1)} fusion(bf16[5,16,64,128]{3,1,2,0:T(8,128)(2,1)} %get-tuple-element.341, s32[]{:T(128)S(6)} %copy.142, f32[16,8,64,128]{3,2,1,0:T(8,128)} %bitcast.172, s32[16,8]{0,1:T(8,128)S(1)} %copy.132), kind=kOutput, calls=%fused_computation.26.clone.1 | convolution fusion | flops 201459712 | bytes 4456964 | tf_op jit(solution)/shard_map/while/body/eval_jaxpr/anb,antd->btd/dot_general | solution.py:58
  321.0 5.2 %fusion.140 = bf16[5,16,64,128]{3,1,2,0:T(8,128)(2,1)} fusion(bf16[5,16,64,128]{3,1,2,0:T(8,128)(2,1)} %get-tuple-element.342, s32[]{:T(128)S(6)} %copy.142, f32[16,8,64,128]{3,2,1,0:T(8,128)S(1)} %bitcast.177, s32[16,8]{0,1:T(8,128)S(1)} %copy.132), kind=kOutput, calls=%fused_computation.28.clone.1 | convolution fusion | flops 201459712 | bytes 4456964 | tf_op jit(solution)/shard_map/while/body/eval_jaxpr/anb,antd->btd/dot_general | solution.py:64
  331.6 4.0 broadcast_select_fusion.6
  348.2 7.3 %fusion.138 = bf16[5,16,64,128]{3,1,2,0:T(8,128)(2,1)} fusion(bf16[5,16,64,128]{3,1,2,0:T(8,128)(2,1)} %get-tuple-element.341, s32[]{:T(128)S(6)} %copy.142, f32[16,8,64,128]{3,2,1,0:T(8,128)} %bitcast.172, s32[16,8]{0,1:T(8,128)S(1)} %copy.132), kind=kOutput, calls=%fused_computation.26.clone.1 | convolution fusion | flops 201459712 | bytes 4456964 | tf_op jit(solution)/shard_map/while/body/eval_jaxpr/anb,antd->btd/dot_general | solution.py:58
  357.4 5.2 %fusion.140 = bf16[5,16,64,128]{3,1,2,0:T(8,128)(2,1)} fusion(bf16[5,16,64,128]{3,1,2,0:T(8,128)(2,1)} %get-tuple-element.342, s32[]{:T(128)S(6)} %copy.142, f32[16,8,64,128]{3,2,1,0:T(8,128)S(1)} %bitcast.177, s32[16,8]{0,1:T(8,128)S(1)} %copy.132), kind=kOutput, calls=%fused_computation.28.clone.1 | convolution fusion | flops 201459712 | bytes 4456964 | tf_op jit(solution)/shard_map/while/body/eval_jaxpr/anb,antd->btd/dot_general | solution.py:64
  365.2 11.5 %fusion.68 = bf16[5120,640]{0,1:T(8,128)(2,1)} fusion(bf16[1024,5120]{1,0:T(8,128)(2,1)} %all-gather.3.cloned.1.call-done, bf16[128,8,5,128]{3,2,1,0:T(8,128)(2,1)S(1)} %bitcast.191), kind=kOutput, calls=%fused_computation.66 | convolution fusion | flops 6717440000 | bytes 18350080 | tf_op jit(solution)/shard_map/td,te->de/dot_general | solution.py:116
  376.6 9.5 %copy.97 = bf16[5120,640]{1,0:T(8,128)(2,1)} copy(bf16[5120,640]{0,1:T(8,128)(2,1)} %fusion.68) | data formatting | bytes 13107200
  390.9 5.7 %all-to-all-start.3 = ((bf16[4,256,640]{2,1,0:T(8,128)(2,1)}), bf16[4,256,640]{2,1,0:T(8,128)(2,1)S(1)}, u32[]{:S(2)}, u32[]{:S(2)}) async-start(bf16[4,256,640]{2,1,0:T(8,128)(2,1)} %all_to_all.79), calls=%async_computation.3 | async-start | bytes 2621440 | tf_op jit(solution)/shard_map/all_to_all | solution.py:124
  406.1 6.4 %all-to-all-done.3 = bf16[4,256,640]{2,1,0:T(8,128)(2,1)S(1)} async-done(((bf16[4,256,640]{2,1,0:T(8,128)(2,1)}), bf16[4,256,640]{2,1,0:T(8,128)(2,1)S(1)}, u32[]{:S(2)}, u32[]{:S(2)}) %all-to-all-start.3) | async-done | bytes 1310752 | tf_op jit(solution)/shard_map/all_to_all | solution.py:124
  413.5 5.8 %all-to-all-start.4 = ((bf16[4,256,640]{2,1,0:T(8,128)(2,1)}), bf16[4,256,640]{2,1,0:T(8,128)(2,1)S(1)}, u32[]{:S(2)}, u32[]{:S(2)}) async-start(bf16[4,256,640]{2,1,0:T(8,128)(2,1)} %all_to_all.81), calls=%async_computation.4 | async-start | bytes 2621440 | tf_op jit(solution)/shard_map/all_to_all | solution.py:125
  435.4 5.6 %all-to-all-start.5 = ((bf16[4,256,640]{2,1,0:T(8,128)(2,1)}), bf16[4,256,640]{2,1,0:T(8,128)(2,1)S(1)}, u32[]{:S(2)}, u32[]{:S(2)}) async-start(bf16[4,256,640]{2,1,0:T(8,128)(2,1)} %all_to_all.83), calls=%async_computation.5 | async-start | bytes 2621440 | tf_op jit(solution)/shard_map/all_to_all | solution.py:126
  457.2 18.2 %reduce-scatter.4.cloned.1.call-done = bf16[160,640]{1,0:T(8,128)(2,1)} async-done(((bf16[5120,640]{1,0:T(8,128)(2,1)}), bf16[160,640]{1,0:T(8,128)(2,1)}) %reduce-scatter.4.cloned.1.call-update) | async-done | bytes 204816
  (232 shorter events, 178.8 us)
Async XLA Ops:
  7.2 52.7 %copy-start = (s32[1,16]{1,0:T(1,128)S(1)}, s32[1,16]{1,0:T(1,128)}, u32[]{:S(2)}) copy-start(s32[1,16]{1,0:T(1,128)} %param.19) | copy-start | bytes 196
  7.2 71.2 %all-gather.5.cloned.1.call-start = ((), (), s32[]{:S(2)}) async-start(), calls=%async_computation.8 | async-start | bytes 6758400 | tf_op jit(solution)/shard_map/all_gather | solution.py:94
  7.9 154.3 %all-gather.3.cloned.1.call-start = ((), (), s32[]{:S(2)}) async-start(), calls=%async_computation.7 | async-start | bytes 13107200 | tf_op jit(solution)/shard_map/all_gather | solution.py:91
  12.3 20.5 %all-to-all-start = ((bf16[256,4,640]{2,0,1:T(8,128)(2,1)}), bf16[256,4,640]{2,0,1:T(8,128)(2,1)S(1)}, u32[]{:S(2)}, u32[]{:S(2)}) async-start(bf16[256,4,640]{2,0,1:T(8,128)(2,1)} %copy.73), calls=%async_computation | async-start | bytes 2621440 | tf_op jit(solution)/shard_map/all_to_all | solution.py:87
  18.6 4.9 %copy-start.5 = (bf16[256,2560]{0,1:T(8,128)(2,1)}, bf16[256,2560]{0,1:T(8,128)(2,1)S(1)}, u32[]{:S(2)}) copy-start(bf16[256,2560]{0,1:T(8,128)(2,1)S(1)} %copy.74) | copy-start | bytes 3932164
  19.5 3.9 copy-start.21
  32.8 20.5 %all-to-all-start.1 = ((bf16[256,4,640]{2,0,1:T(8,128)(2,1)}), bf16[256,4,640]{2,0,1:T(8,128)(2,1)S(1)}, u32[]{:S(2)}, u32[]{:S(2)}) async-start(bf16[256,4,640]{2,0,1:T(8,128)(2,1)} %copy.75), calls=%async_computation.1 | async-start | bytes 2621440 | tf_op jit(solution)/shard_map/all_to_all | solution.py:88
  38.4 21.3 %copy-start.20 = (s32[16,8]{0,1:T(8,128)S(1)}, s32[16,8]{0,1:T(8,128)}, u32[]{:S(2)}) copy-start(s32[16,8]{0,1:T(8,128)} %param.18) | copy-start | bytes 1540
  53.3 7.9 %copy-start.11 = (bf16[256,4,640]{2,0,1:T(8,128)(2,1)}, bf16[256,4,640]{2,0,1:T(8,128)(2,1)S(1)}, u32[]{:S(2)}) copy-start(bf16[256,4,640]{2,0,1:T(8,128)(2,1)S(1)} %all-to-all-done.1) | copy-start | bytes 3932164
  53.3 20.5 %all-to-all-start.2 = ((bf16[256,4,640]{2,0,1:T(8,128)(2,1)}), bf16[256,4,640]{2,0,1:T(8,128)(2,1)}, u32[]{:S(2)}, u32[]{:S(2)}) async-start(bf16[256,4,640]{2,0,1:T(8,128)(2,1)} %bitcast.186), calls=%async_computation.2 | async-start | bytes 2621440 | tf_op jit(solution)/shard_map/all_to_all | solution.py:89
  59.6 415.7 %reduce-scatter.4.cloned.1.call-start = ((), (), s32[]{:S(2)}) async-start(), calls=%async_computation.9 | async-start | bytes 6758400
  192.6 3.6 copy-start.2
  192.6 3.6 copy-start.3
  202.7 7.3 %copy-start.4 = (f32[16,64,512]{2,1,0:T(8,128)S(1)}, f32[16,64,512]{2,1,0:T(8,128)}, u32[]{:S(2)}) copy-start(f32[16,64,512]{2,1,0:T(8,128)} %get-tuple-element.322) | copy-start | bytes 6291460 | tf_op jit(solution)/shard_map/while
  229.0 3.6 copy-start.2
  229.0 3.6 copy-start.3
  239.1 7.3 %copy-start.4 = (f32[16,64,512]{2,1,0:T(8,128)S(1)}, f32[16,64,512]{2,1,0:T(8,128)}, u32[]{:S(2)}) copy-start(f32[16,64,512]{2,1,0:T(8,128)} %get-tuple-element.322) | copy-start | bytes 6291460 | tf_op jit(solution)/shard_map/while
  265.4 3.6 copy-start.2
  265.4 3.6 copy-start.3
  275.4 7.3 %copy-start.4 = (f32[16,64,512]{2,1,0:T(8,128)S(1)}, f32[16,64,512]{2,1,0:T(8,128)}, u32[]{:S(2)}) copy-start(f32[16,64,512]{2,1,0:T(8,128)} %get-tuple-element.322) | copy-start | bytes 6291460 | tf_op jit(solution)/shard_map/while
  301.7 3.6 copy-start.2
  301.7 3.6 copy-start.3
  311.8 7.3 %copy-start.4 = (f32[16,64,512]{2,1,0:T(8,128)S(1)}, f32[16,64,512]{2,1,0:T(8,128)}, u32[]{:S(2)}) copy-start(f32[16,64,512]{2,1,0:T(8,128)} %get-tuple-element.322) | copy-start | bytes 6291460 | tf_op jit(solution)/shard_map/while
  338.2 3.6 copy-start.2
  338.2 3.6 copy-start.3
  348.2 7.3 %copy-start.4 = (f32[16,64,512]{2,1,0:T(8,128)S(1)}, f32[16,64,512]{2,1,0:T(8,128)}, u32[]{:S(2)}) copy-start(f32[16,64,512]{2,1,0:T(8,128)} %get-tuple-element.322) | copy-start | bytes 6291460 | tf_op jit(solution)/shard_map/while
  390.9 21.6 %all-to-all-start.3 = ((bf16[4,256,640]{2,1,0:T(8,128)(2,1)}), bf16[4,256,640]{2,1,0:T(8,128)(2,1)S(1)}, u32[]{:S(2)}, u32[]{:S(2)}) async-start(bf16[4,256,640]{2,1,0:T(8,128)(2,1)} %all_to_all.79), calls=%async_computation.3 | async-start | bytes 2621440 | tf_op jit(solution)/shard_map/all_to_all | solution.py:124
  413.5 20.8 %all-to-all-start.4 = ((bf16[4,256,640]{2,1,0:T(8,128)(2,1)}), bf16[4,256,640]{2,1,0:T(8,128)(2,1)S(1)}, u32[]{:S(2)}, u32[]{:S(2)}) async-start(bf16[4,256,640]{2,1,0:T(8,128)(2,1)} %all_to_all.81), calls=%async_computation.4 | async-start | bytes 2621440 | tf_op jit(solution)/shard_map/all_to_all | solution.py:125
  435.4 19.6 %all-to-all-start.5 = ((bf16[4,256,640]{2,1,0:T(8,128)(2,1)}), bf16[4,256,640]{2,1,0:T(8,128)(2,1)S(1)}, u32[]{:S(2)}, u32[]{:S(2)}) async-start(bf16[4,256,640]{2,1,0:T(8,128)(2,1)} %all_to_all.83), calls=%async_computation.5 | async-start | bytes 2621440 | tf_op jit(solution)/shard_map/all_to_all | solution.py:126
  443.9 3.5 copy-start.6
  443.9 3.5 copy-start.19
  454.9 22.4 %copy-start.1 = (s32[1,16]{1,0:T(1,128)S(1)}, s32[1,16]{1,0:T(1,128)}, u32[]{:S(2)}) copy-start(s32[1,16]{1,0:T(1,128)} %param.19) | copy-start | bytes 196
  (16 other events, 34.8 us)
Sparse Core Ops, SparseCore 0:
  10.3 51.7 all-gather.4
  63.8 98.3 all-gather.2
  386.3 89.0 reduce-scatter.3
where the time goes:
time: 494 us; the launch traced here: 484 us
  matrix products  156 us (32%)
  waiting for transfers between devices  140 us (28%)
  local copies, waits for them, and re-layouts  98.9 us (20%)
  other arithmetic  40.3 us (8%)
  starting transfers between devices  33.8 us (7%)
  between operations  14.4 us (3%)
    all_gather x1, waiting for transfers between devices, per_device(): cot_all = lax.all_gather(out_grad, 'seq', axis=0, tiled=True)  83.8 us
    dot_general x25, matrix products, multiply(): return jnp.einsum(pattern, left, right, preferred_element_type=jnp.float32)  57.5 us
    dot_general x5, matrix products, tile_attention(): jnp.einsum('anb,antd->btd', owners, grad_key_near.reshape(tile_count, nei...  36.3 us
    dot_general x5, matrix products, tile_attention(): jnp.einsum('anb,antd->btd', owners, grad_value_near.reshape(tile_count, n...  25.7 us
    unnamed x56, local copies, waits for them, and re-layouts  24.1 us
    select_n x5, other arithmetic, tile_attention(): jnp.take(key_tiles, tile_pairs, axis=0)  20.2 us
    unnamed x4, waiting for transfers between devices  19.6 us
    dot_general x1, matrix products, per_device(): jnp.dot(columns, lax.all_gather(w_out, 'dp', axis=0, tiled=True), preferr...  13.7 us
  transfers between devices with their start and end apart: 9, of which 8 were waited for; matrix products, arithmetic and copies ran while one was open for 12% of the time, Pallas kernels for 0%

commit v1 on v0

v1 whole, which is shorter than its diff:
```python
import functools
import math

import jax
import jax.numpy as jnp
from jax import lax
from jax.experimental import pallas as pl
from jax.experimental.pallas import tpu as pltpu
from jax.sharding import Mesh, PartitionSpec as P

HEAD_DIM = 128


EPS = 1e-06
LOG2E = 1.4426950408889634


def contract(left, right, left_dim, right_dim):
    return lax.dot_general(
        left, right, (((left_dim,), (right_dim,)), ((), ())), preferred_element_type=jnp.float32
    )


def row_scale_of(values_f):
    return lax.rsqrt(jnp.mean(values_f * values_f, axis=-1, keepdims=True) + EPS)


def norm_kernel(x_ref, gain_ref, out_ref):
    values_f = x_ref[...].astype(jnp.float32)
    normed = (values_f * row_scale_of(values_f) * gain_ref[...]).astype(jnp.bfloat16)
    parts, _, width = out_ref.shape
    for part in range(parts):
        out_ref[part] = normed[:, part * width : (part + 1) * width]


def split_kernel(x_ref, out_ref):
    parts, _, width = out_ref.shape
    for part in range(parts):
        out_ref[part] = x_ref[:, part * width : (part + 1) * width]


def to_parts(field, gain, parts, block=64):
    rows, width = field.shape
    row_spec = pl.BlockSpec((block, width), lambda i: (i, 0))
    gain_spec = pl.BlockSpec((1, width), lambda i: (0, 0))
    return pl.pallas_call(
        split_kernel if gain is None else norm_kernel,
        grid=(rows // block,),
        in_specs=[row_spec] if gain is None else [row_spec, gain_spec],
        out_specs=pl.BlockSpec((parts, block, width // parts), lambda i: (0, i, 0)),
        out_shape=jax.ShapeDtypeStruct((parts, rows, width // parts), jnp.bfloat16),
        name="split_rows" if gain is None else "norm_rows",
    )(*((field,) if gain is None else (field, gain.reshape(1, width))))


def norm_back_kernel(x_ref, gain_ref, grad_ref, out_ref):
    parts = grad_ref.shape[0]
    width = x_ref.shape[1]
    values_f = x_ref[...].astype(jnp.float32)
    row_scale = row_scale_of(values_f)
    grad = jnp.concatenate([grad_ref[part] for part in range(parts)], axis=1).astype(jnp.float32)
    gated = gain_ref[...] * grad
    inner = jnp.sum(gated * values_f, axis=-1, keepdims=True)
    out_ref[...] = (
        row_scale * gated - values_f * (row_scale * row_scale * row_scale * inner * (1.0 / width))
    ).astype(jnp.bfloat16)


def join_kernel(parts_ref, out_ref):
    parts, _, width = parts_ref.shape
    for part in range(parts):
        out_ref[:, part * width : (part + 1) * width] = parts_ref[part]


def norm_back(field, gain, grad_parts, block=64):
    rows, width = field.shape
    parts = grad_parts.shape[0]
    row_spec = pl.BlockSpec((block, width), lambda i: (i, 0))
    return pl.pallas_call(
        norm_back_kernel,
        grid=(rows // block,),
        in_specs=[
            row_spec,
            pl.BlockSpec((1, width), lambda i: (0, 0)),
            pl.BlockSpec((parts, block, width // parts), lambda i: (0, i, 0)),
        ],
        out_specs=row_spec,
        out_shape=jax.ShapeDtypeStruct((rows, width), jnp.bfloat16),
        name="norm_back",
    )(field, gain.reshape(1, width), grad_parts)


def join(parts_of, block=64):
    parts, rows, width = parts_of.shape
    return pl.pallas_call(
        join_kernel,
        grid=(rows // block,),
        in_specs=[pl.BlockSpec((parts, block, width), lambda i: (0, i, 0))],
        out_specs=pl.BlockSpec((block, parts * width), lambda i: (i, 0)),
        out_shape=jax.ShapeDtypeStruct((rows, parts * width), jnp.bfloat16),
        name="join_rows",
    )(parts_of)


def attention_kernel(tile_rows, pairs_ref, lens_ref, q_ref, k_ref, v_ref, g_ref,
                     att_ref, gq_ref, gk_ref, gv_ref, gk_acc, gv_acc):
    clip_rows, width = q_ref.shape
    tile_count, neighbours = pairs_ref.shape
    factor = 1.0 / math.sqrt(width)
    rows = 2 * tile_rows
    gk_acc[...] = jnp.zeros_like(gk_acc)
    gv_acc[...] = jnp.zeros_like(gv_acc)
    lane = lax.broadcasted_iota(jnp.int32, (tile_rows, rows), 1)
    slot = lax.broadcasted_iota(jnp.int32, (tile_rows, rows), 0)
    first = lane < tile_rows
    pair_first = (lax.broadcasted_iota(jnp.int32, (rows, 2 * width), 0) < tile_rows) == (
        lax.broadcasted_iota(jnp.int32, (rows, 2 * width), 1) < width)

    def spread(block):
        twice = jnp.concatenate([block, block], axis=1)
        return jnp.where(pair_first, twice, jnp.zeros_like(twice))

    def tile(ref, index):
        return ref[pl.ds(pl.multiple_of(index * tile_rows, tile_rows), tile_rows), :]

    def step(pair, carry):
        row = pl.multiple_of(pair * rows, rows)
        near = [[pairs_ref[2 * pair + half, n] for n in range(neighbours)] for half in range(2)]
        keys = jnp.concatenate(
            [jnp.concatenate([tile(k_ref, near[0][n]), tile(k_ref, near[1][n])], axis=1)
             for n in range(neighbours)], axis=0)
        vals = jnp.concatenate(
            [jnp.concatenate([tile(v_ref, near[0][n]), tile(v_ref, near[1][n])], axis=1)
             for n in range(neighbours)], axis=0)
        queries = spread(q_ref[pl.ds(row, rows), :])
        grads = spread(g_ref[pl.ds(row, rows), :])
        scores = contract(keys, queries, 1, 1)
        live = jnp.concatenate(
            [slot < jnp.where(first, lens_ref[0, near[0][n]], lens_ref[0, near[1][n]])
             for n in range(neighbours)], axis=0)
        scores = jnp.where(live, scores * (factor * LOG2E), -jnp.inf)
        top = jnp.max(scores, axis=0, keepdims=True)
        weights = jnp.exp2(scores - top)
        probs = weights * (1.0 / jnp.sum(weights, axis=0, keepdims=True))
        probs_low = probs.astype(jnp.bfloat16)
        grad_probs = contract(vals, grads, 1, 1)
        delta = jnp.sum(probs * grad_probs, axis=0, keepdims=True)
        grad_scores = (probs * (grad_probs - delta)).astype(jnp.bfloat16)
        attended = contract(probs_low, vals, 0, 0)
        grad_query = contract(grad_scores, keys, 0, 0) * factor
        for half in range(2):
            at = (slice(half * tile_rows, (half + 1) * tile_rows), slice(half * width, (half + 1) * width))
            place = pl.ds(pl.multiple_of(row + half * tile_rows, tile_rows), tile_rows)
            att_ref[place, :] = attended[at].astype(jnp.bfloat16)
            gq_ref[place, :] = grad_query[at].astype(jnp.bfloat16)
        grad_keys = contract(grad_scores, queries, 1, 0)
        grad_vals = contract(probs_low, grads, 1, 0)
        for half in range(2):
            for n in range(neighbours):
                at = (slice(n * tile_rows, (n + 1) * tile_rows), slice(half * width, (half + 1) * width))
                place = pl.ds(pl.multiple_of(near[half][n] * tile_rows, tile_rows), tile_rows)
                gk_acc[place, :] += grad_keys[at]
                gv_acc[place, :] += grad_vals[at]
        return carry

    lax.fori_loop(0, tile_count // 2, step, 0)
    gk_ref[...] = (gk_acc[...] * factor).astype(jnp.bfloat16)
    gv_ref[...] = gv_acc[...].astype(jnp.bfloat16)


def attention(queries, keys, values, grads, tile_pairs, tile_lens):
    clip_rows, local_width = queries.shape
    tile_rows = clip_rows // tile_pairs.shape[0]
    block = pl.BlockSpec((clip_rows, HEAD_DIM), lambda h: (0, h))
    smem = pl.BlockSpec(memory_space=pltpu.SMEM)
    return pl.pallas_call(
        functools.partial(attention_kernel, tile_rows),
        grid=(local_width // HEAD_DIM,),
        in_specs=[smem, smem, block, block, block, block],
        out_specs=[block] * 4,
        out_shape=[jax.ShapeDtypeStruct(queries.shape, jnp.bfloat16)] * 4,
        scratch_shapes=[pltpu.VMEM((clip_rows, HEAD_DIM), jnp.float32)] * 2,
        compiler_params=pltpu.CompilerParams(vmem_limit_bytes=32 << 20),
        name="tile_attention",
    )(tile_pairs, tile_lens, queries, keys, values, grads)


def per_device(queries, keys, values, gain_q, gain_k, tile_pairs, tile_lens, out_grad, w_out):
    seq_count = lax.axis_size("seq")
    dp_count = lax.axis_size("dp")
    tok_rows, width = queries.shape
    local_width = width // seq_count
    clip_rows = tok_rows * seq_count

    def exchange(parts):
        return lax.all_to_all(parts, "seq", split_axis=0, concat_axis=0, tiled=True)

    def to_heads(parts):
        return exchange(parts).reshape(clip_rows, local_width)

    def to_rows(field):
        return exchange(field.reshape(seq_count, tok_rows, local_width))

    query_heads = to_heads(to_parts(queries, gain_q, seq_count))
    key_heads = to_heads(to_parts(keys, gain_k, seq_count))
    value_heads = to_heads(to_parts(values, None, seq_count))
    cot_all = lax.all_gather(out_grad, "seq", axis=0, tiled=True)
    w_all = lax.all_gather(w_out, "dp", axis=0, tiled=True)
    grad_attended = jnp.dot(cot_all, w_all, preferred_element_type=jnp.float32).astype(jnp.bfloat16)
    attended, grad_qn, grad_kn, grad_vh = attention(
        query_heads, key_heads, value_heads, grad_attended, tile_pairs, tile_lens
    )
    grad_w = lax.psum_scatter(
        (
            jnp.einsum("td,te->de", cot_all, attended, preferred_element_type=jnp.float32) / dp_count
        ).astype(jnp.bfloat16),
        "dp",
        scatter_dimension=0,
        tiled=True,
    ).astype(jnp.float32)
    grad_q = norm_back(queries, gain_q, to_rows(grad_qn))
    grad_k = norm_back(keys, gain_k, to_rows(grad_kn))
    grad_v = join(to_rows(grad_vh))
    return (grad_q, grad_k, grad_v, grad_w)


def solution(mesh):
    return jax.shard_map(
        per_device,
        mesh=mesh,
        in_specs=(
            P(("dp", "seq"), None),
            P(("dp", "seq"), None),
            P(("dp", "seq"), None),
            P(),
            P(),
            P(),
            P("dp", None),
            P(("dp", "seq"), None),
            P("dp", "seq"),
        ),
        out_specs=(
            P(("dp", "seq"), None),
            P(("dp", "seq"), None),
            P(("dp", "seq"), None),
            P("dp", "seq"),
        ),
        check_vma=False,
    )
```

time: 494 us -> 340 us (0.69); the launches traced: 484 us -> 338 us
  matrix products: 156 us -> 25.3 us
  local copies, waits for them, and re-layouts: 98.9 us -> 18.5 us
  Pallas kernels: 0 us -> 63 us
  blocking collectives: 0 us -> 41.7 us
  other arithmetic: 40.3 us -> 0 us
  waiting for transfers between devices: 140 us -> 154 us
  starting transfers between devices: 33.8 us -> 22.4 us
    dot_general x37 -> x2, matrix products: 145 us -> 25.3 us  [the longest x1 13.7 us: per_device(): jnp.dot(cot_all, w_all, preferred_element_type=jnp.float32)]
    pallas_call x0 -> x7, Pallas kernels: none -> 63 us  [the longest x1 40.3 us: attention(): pl.pallas_call(functools.partial(attention_kernel, tile_rows), grid=(loca...]
    all_to_all x0 -> x2, blocking collectives: none -> 41.7 us  [exchange(): return lax.all_to_all(parts, 'seq', split_axis=0, concat_axis=0, tiled=True)]
    gather x12 -> x0, local copies, waits for them, and re-layouts: 22.6 us -> none  [the longest x5 10.7 us: tile_attention(): jnp.take(value_tiles, tile_pairs, axis=0)]
    select_n x11 -> x0, other arithmetic: 20.2 us -> none  [the longest x5 20.2 us: tile_attention(): jnp.take(key_tiles, tile_pairs, axis=0)]
    all_gather x1, waiting for transfers between devices: 83.8 us -> 100 us  [per_device(): cot_all = lax.all_gather(out_grad, 'seq', axis=0, tiled=True)]
    all_to_all x7 -> x0, local copies, waits for them, and re-layouts: 14.3 us -> none  [the longest x2 3.09 us: per_device(): lax.all_to_all(grad_vh, 'seq', split_axis=0, concat_axis=1, tiled=True)]
    convert_element_type x11 -> x0, other arithmetic: 13.3 us -> none  [the longest x2 3.49 us: norm_finish(): (row_scale * gated - values_f * row_scale ** 3 * inner / width).astype(jn...]
  transfers between devices with their start and end apart: 9 -> 7, of which waited for: 8 -> 6; matrix products, arithmetic and copies ran while one was open for 12% -> 4% of each run, Pallas kernels for 0% -> 7%
where the time goes in v1:
time: 340 us; the launch traced here: 338 us
  waiting for transfers between devices  154 us (45%)
  Pallas kernels  63 us (19%)
  blocking collectives  41.7 us (12%)
  matrix products  25.3 us (7%)
  starting transfers between devices  22.4 us (7%)
  local copies, waits for them, and re-layouts  18.5 us (5%)
  between operations  13.8 us (4%)
    all_gather x1, waiting for transfers between devices, per_device(): cot_all = lax.all_gather(out_grad, 'seq', axis=0, tiled=True)  100 us
    all_to_all x2, blocking collectives, exchange(): return lax.all_to_all(parts, 'seq', split_axis=0, concat_axis=0, tiled=True)  41.7 us
    pallas_call x1, Pallas kernels, attention(): pl.pallas_call(functools.partial(attention_kernel, tile_rows), grid=(loca...  40.3 us
    all_to_all x4, waiting for transfers between devices, exchange(): return lax.all_to_all(parts, 'seq', split_axis=0, concat_axis=0, tiled=True)  28.6 us
    unnamed x4, waiting for transfers between devices  23.5 us
    all_to_all x4, starting transfers between devices, exchange(): return lax.all_to_all(parts, 'seq', split_axis=0, concat_axis=0, tiled=True)  22.3 us
    unnamed x24, local copies, waits for them, and re-layouts  17.3 us
    dot_general x1, matrix products, per_device(): jnp.dot(cot_all, w_all, preferred_element_type=jnp.float32)  13.7 us
  transfers between devices with their start and end apart: 7, of which 6 were waited for; matrix products, arithmetic and copies ran while one was open for 4% of the time, Pallas kernels for 7%

profile of v1, /device:TPU:24, one launch (start us, length us, event | category | flops | bytes accessed | tf_op | source)
XLA Modules:
  0.0 338.4 jit_solution(14367357194481910096)
XLA Ops:
  7.2 0.7 all-gather.5.cloned.1.call-update
  8.0 0.7 all-gather.3.cloned.1.call-update
  9.3 3.8 %norm_rows.3 = bf16[4,256,640]{2,1,0:T(8,128)(2,1)} custom-call(bf16[256,2560]{1,0:T(8,128)(2,1)} %x_ref.9, f32[1,2560]{1,0:T(1,128)} %reshape.36.gain_ref), custom_call_target="tpu_custom_call" | custom-call | tf_op jit(solution)/shard_map/norm_rows/pallas_call | solution.py:46
  13.0 4.8 %all-to-all-start.1 = ((bf16[4,256,640]{2,1,0:T(8,128)(2,1)}), bf16[4,256,640]{2,1,0:T(8,128)(2,1)S(1)}, u32[]{:S(2)}, u32[]{:S(2)}) async-start(bf16[4,256,640]{2,1,0:T(8,128)(2,1)} %norm_rows.3), calls=%async_computation.1 | async-start | bytes 2621440 | tf_op jit(solution)/shard_map/all_to_all | solution.py:196
  17.8 0.6 reshape.34.gain_ref
  18.5 3.8 %norm_rows.2 = bf16[4,256,640]{2,1,0:T(8,128)(2,1)} custom-call(bf16[256,2560]{1,0:T(8,128)(2,1)} %x_ref.8, f32[1,2560]{1,0:T(1,128)} %reshape.34.gain_ref), custom_call_target="tpu_custom_call" | custom-call | tf_op jit(solution)/shard_map/norm_rows/pallas_call | solution.py:46
  22.2 11.5 %all-to-all-done.1 = bf16[4,256,640]{2,1,0:T(8,128)(2,1)S(1)} async-done(((bf16[4,256,640]{2,1,0:T(8,128)(2,1)}), bf16[4,256,640]{2,1,0:T(8,128)(2,1)S(1)}, u32[]{:S(2)}, u32[]{:S(2)}) %all-to-all-start.1) | async-done | bytes 1310752 | tf_op jit(solution)/shard_map/all_to_all | solution.py:196
  33.7 5.6 %all-to-all-start = ((bf16[4,256,640]{2,1,0:T(8,128)(2,1)}), bf16[4,256,640]{2,1,0:T(8,128)(2,1)S(1)}, u32[]{:S(2)}, u32[]{:S(2)}) async-start(bf16[4,256,640]{2,1,0:T(8,128)(2,1)} %norm_rows.2), calls=%async_computation | async-start | bytes 2621440 | tf_op jit(solution)/shard_map/all_to_all | solution.py:196
  39.3 3.5 %split_rows.1 = bf16[4,256,640]{2,1,0:T(8,128)(2,1)} custom-call(bf16[256,2560]{1,0:T(8,128)(2,1)} %x_ref.7), custom_call_target="tpu_custom_call" | custom-call | tf_op jit(solution)/shard_map/split_rows/pallas_call | solution.py:46
  42.8 11.4 %all-to-all-done = bf16[4,256,640]{2,1,0:T(8,128)(2,1)S(1)} async-done(((bf16[4,256,640]{2,1,0:T(8,128)(2,1)}), bf16[4,256,640]{2,1,0:T(8,128)(2,1)S(1)}, u32[]{:S(2)}, u32[]{:S(2)}) %all-to-all-start) | async-done | bytes 1310752 | tf_op jit(solution)/shard_map/all_to_all | solution.py:196
  54.2 6.3 %all-to-all-start.2 = ((bf16[4,256,640]{2,1,0:T(8,128)(2,1)}), bf16[4,256,640]{2,1,0:T(8,128)(2,1)}, u32[]{:S(2)}, u32[]{:S(2)}) async-start(bf16[4,256,640]{2,1,0:T(8,128)(2,1)} %split_rows.1), calls=%async_computation.2 | async-start | bytes 2621440 | tf_op jit(solution)/shard_map/all_to_all | solution.py:196
  60.5 1.6 all-gather.5.cloned.1.call-done
  62.1 100.1 %all-gather.3.cloned.1.call-done = bf16[1024,5120]{1,0:T(8,128)(2,1)} async-done(((bf16[256,5120]{1,0:T(8,128)(2,1)}), bf16[1024,5120]{1,0:T(8,128)(2,1)}) %all-gather.3.cloned.1.call-update) | async-done | bytes 10485776 | tf_op jit(solution)/shard_map/all_gather | solution.py:207
  162.2 13.7 %convolution_convert_fusion.g_ref = bf16[1024,640]{1,0:T(8,128)(2,1)} fusion(bf16[1024,5120]{1,0:T(8,128)(2,1)} %all-gather.3.cloned.1.call-done, bf16[5120,640]{1,0:T(8,128)(2,1)} %all-gather.5.cloned.1.call-done), kind=kOutput, calls=%fused_computation.2 | convolution fusion | flops 6711541760 | bytes 18350080 | tf_op jit(solution)/shard_map/dot_general | solution.py:209
  175.9 1.3 copy-done.4
  177.2 40.3 %tile_attention.1 = (bf16[1024,640]{1,0:T(8,128)(2,1)S(1)}, bf16[1024,640]{1,0:T(8,128)(2,1)S(1)}, bf16[1024,640]{1,0:T(8,128)(2,1)S(1)}, bf16[1024,640]{1,0:T(8,128)(2,1)}) custom-call(s32[16,8]{1,0:T(8,128)S(1)} %copy.15.pairs_ref, s32[1,16]{1,0:T(1,128)S(1)} %copy-done.5, bf16[1024,640]{1,0:T(8,128)(2,1)S(1)} %bitcast.14, bf16[1024,640]{1,0:T(8,128)(2,1)S(1)} %bitcast.13, ...), custom_call_target="tpu_custom_call" | custom-call | tf_op jit(solution)/shard_map/tile_attention/pallas_call | solution.py:176
  217.5 1.1 copy-done
  218.5 1.1 copy-done.2
  219.6 11.6 %fusion = bf16[5120,640]{0,1:T(8,128)(2,1)} fusion(bf16[1024,640]{1,0:T(8,128)(2,1)S(1)} %get-tuple-element.11, bf16[1024,5120]{1,0:T(8,128)(2,1)} %all-gather.3.cloned.1.call-done), kind=kOutput, calls=%fused_computation.1 | convolution fusion | flops 6717440000 | bytes 18350080 | tf_op jit(solution)/shard_map/td,te->de/dot_general | solution.py:215
  231.2 9.5 %copy.17 = bf16[5120,640]{1,0:T(8,128)(2,1)} copy(bf16[5120,640]{0,1:T(8,128)(2,1)} %fusion) | data formatting | bytes 13107200
  240.6 1.3 copy-done.3
  241.9 21.6 %all_to_all.30.grad_ref = bf16[4,256,640]{2,1,0:T(8,128)(2,1)} all-to-all(bf16[4,256,640]{2,1,0:T(8,128)(2,1)S(1)} %bitcast.16), channel_id=1, replica_groups=mesh['dp'=32,'seq'=4] {'seq'}, dimensions={0} | all-to-all | bytes 2621440 | tf_op jit(solution)/shard_map/all_to_all | solution.py:196
  263.5 20.1 %all_to_all.31.grad_ref = bf16[4,256,640]{2,1,0:T(8,128)(2,1)} all-to-all(bf16[4,256,640]{2,1,0:T(8,128)(2,1)S(1)} %bitcast.15), channel_id=1, replica_groups=mesh['dp'=32,'seq'=4] {'seq'}, dimensions={0} | all-to-all | bytes 2621440 | tf_op jit(solution)/shard_map/all_to_all | solution.py:196
  283.7 5.6 %all-to-all-start.5 = ((bf16[4,256,640]{2,1,0:T(8,128)(2,1)}), bf16[4,256,640]{2,1,0:T(8,128)(2,1)S(1)}, u32[]{:S(2)}, u32[]{:S(2)}) async-start(bf16[4,256,640]{2,1,0:T(8,128)(2,1)} %bitcast.5), calls=%async_computation.5 | async-start | bytes 2621440 | tf_op jit(solution)/shard_map/all_to_all | solution.py:196
  289.2 4.2 %norm_back.3 = bf16[256,2560]{1,0:T(8,128)(2,1)} custom-call(bf16[256,2560]{1,0:T(8,128)(2,1)} %x_ref.9, f32[1,2560]{1,0:T(1,128)} %reshape.36.gain_ref, bf16[4,256,640]{2,1,0:T(8,128)(2,1)} %all_to_all.30.grad_ref), custom_call_target="tpu_custom_call" | custom-call | tf_op jit(solution)/shard_map/norm_back/pallas_call | solution.py:79
  293.4 4.1 %norm_back.2 = bf16[256,2560]{1,0:T(8,128)(2,1)} custom-call(bf16[256,2560]{1,0:T(8,128)(2,1)} %x_ref.8, f32[1,2560]{1,0:T(1,128)} %reshape.34.gain_ref, bf16[4,256,640]{2,1,0:T(8,128)(2,1)} %all_to_all.31.grad_ref), custom_call_target="tpu_custom_call" | custom-call | tf_op jit(solution)/shard_map/norm_back/pallas_call | solution.py:79
  297.5 5.7 %all-to-all-done.5.parts_ref = bf16[4,256,640]{2,1,0:T(8,128)(2,1)S(1)} async-done(((bf16[4,256,640]{2,1,0:T(8,128)(2,1)}), bf16[4,256,640]{2,1,0:T(8,128)(2,1)S(1)}, u32[]{:S(2)}, u32[]{:S(2)}) %all-to-all-start.5) | async-done | bytes 1310752 | tf_op jit(solution)/shard_map/all_to_all | solution.py:196
  303.2 1.1 copy-done.6
  304.3 3.5 %join_rows.1 = bf16[256,2560]{1,0:T(8,128)(2,1)} custom-call(bf16[4,256,640]{2,1,0:T(8,128)(2,1)} %copy-done.6), custom_call_target="tpu_custom_call" | custom-call | tf_op jit(solution)/shard_map/join_rows/pallas_call | solution.py:95
  307.8 22.1 %reduce-scatter.4.cloned.1.call-done = bf16[160,640]{1,0:T(8,128)(2,1)} async-done(((bf16[5120,640]{1,0:T(8,128)(2,1)}), bf16[160,640]{1,0:T(8,128)(2,1)}) %reduce-scatter.4.cloned.1.call-update) | async-done | bytes 204816
  329.9 1.1 copy.18
  331.0 0.9 copy.16
  (22 shorter events, 0.8 us)
Async XLA Ops:
  7.2 54.9 %all-gather.5.cloned.1.call-start = ((), (), s32[]{:S(2)}) async-start(), calls=%async_computation.8 | async-start | bytes 6758400 | tf_op jit(solution)/shard_map/all_gather | solution.py:208
  7.9 0.8 copy-start.7
  7.9 154.2 %all-gather.3.cloned.1.call-start = ((), (), s32[]{:S(2)}) async-start(), calls=%async_computation.7 | async-start | bytes 13107200 | tf_op jit(solution)/shard_map/all_gather | solution.py:207
  13.0 4.8 %copy-start.8 = (f32[2560]{0:T(1024)S(1)}, f32[2560]{0:T(1024)}, u32[]{:S(2)}) copy-start(f32[2560]{0:T(1024)} %param.12) | copy-start | bytes 30724
  13.0 20.7 %all-to-all-start.1 = ((bf16[4,256,640]{2,1,0:T(8,128)(2,1)}), bf16[4,256,640]{2,1,0:T(8,128)(2,1)S(1)}, u32[]{:S(2)}, u32[]{:S(2)}) async-start(bf16[4,256,640]{2,1,0:T(8,128)(2,1)} %norm_rows.3), calls=%async_computation.1 | async-start | bytes 2621440 | tf_op jit(solution)/shard_map/all_to_all | solution.py:196
  22.2 17.1 %copy-start.9 = (s32[16,8]{0,1:T(8,128)S(1)}, s32[16,8]{0,1:T(8,128)}, u32[]{:S(2)}) copy-start(s32[16,8]{0,1:T(8,128)} %param.14) | copy-start | bytes 1540
  33.7 20.5 %all-to-all-start = ((bf16[4,256,640]{2,1,0:T(8,128)(2,1)}), bf16[4,256,640]{2,1,0:T(8,128)(2,1)S(1)}, u32[]{:S(2)}, u32[]{:S(2)}) async-start(bf16[4,256,640]{2,1,0:T(8,128)(2,1)} %norm_rows.2), calls=%async_computation | async-start | bytes 2621440 | tf_op jit(solution)/shard_map/all_to_all | solution.py:196
  54.2 121.7 %all-to-all-start.2 = ((bf16[4,256,640]{2,1,0:T(8,128)(2,1)}), bf16[4,256,640]{2,1,0:T(8,128)(2,1)}, u32[]{:S(2)}, u32[]{:S(2)}) async-start(bf16[4,256,640]{2,1,0:T(8,128)(2,1)} %split_rows.1), calls=%async_computation.2 | async-start | bytes 2621440 | tf_op jit(solution)/shard_map/all_to_all | solution.py:196
  60.5 115.4 %copy-start.5 = (s32[1,16]{1,0:T(1,128)S(1)}, s32[1,16]{1,0:T(1,128)}, u32[]{:S(2)}) copy-start(s32[1,16]{1,0:T(1,128)} %lens_ref.1) | copy-start | bytes 196
  60.5 269.3 %reduce-scatter.4.cloned.1.call-start = ((), (), s32[]{:S(2)}) async-start(), calls=%async_computation.9 | async-start | bytes 6758400
  175.9 1.3 copy-start.4
  217.5 1.1 copy-start
  218.5 1.1 copy-start.2
  240.6 1.3 copy-start.3
  241.9 21.6 %copy-start.1 = (bf16[1024,640]{1,0:T(8,128)(2,1)S(1)}, bf16[1024,640]{1,0:T(8,128)(2,1)}, u32[]{:S(2)}) copy-start(bf16[1024,640]{1,0:T(8,128)(2,1)} %copy-done) | copy-start | bytes 3932164
  283.7 19.6 %all-to-all-start.5 = ((bf16[4,256,640]{2,1,0:T(8,128)(2,1)}), bf16[4,256,640]{2,1,0:T(8,128)(2,1)S(1)}, u32[]{:S(2)}, u32[]{:S(2)}) async-start(bf16[4,256,640]{2,1,0:T(8,128)(2,1)} %bitcast.5), calls=%async_computation.5 | async-start | bytes 2621440 | tf_op jit(solution)/shard_map/all_to_all | solution.py:196
  303.2 1.1 copy-start.6
Sparse Core Ops, SparseCore 0:
  10.2 51.7 all-gather.4
  63.7 98.3 all-gather.2
  240.8 89.0 reduce-scatter.3

commit v2 on v1

v2 whole, which is shorter than its diff:
```python
import functools
import math

import jax
import jax.numpy as jnp
from jax import lax
from jax.experimental import pallas as pl
from jax.experimental.pallas import tpu as pltpu
from jax.sharding import Mesh, PartitionSpec as P

HEAD_DIM = 128


EPS = 1e-06
LOG2E = 1.4426950408889634
MIN_LIVE = 40
SEQ = 4
CORES = 2


def smem():
    return pl.BlockSpec(memory_space=pltpu.SMEM)


def params():
    return pltpu.CompilerParams(vmem_limit_bytes=48 << 20)


def contract(left, right, left_dim, right_dim):
    return lax.dot_general(
        left, right, (((left_dim,), (right_dim,)), ((), ())), preferred_element_type=jnp.float32
    )


def row_scale_of(values_f):
    return lax.rsqrt(jnp.mean(values_f * values_f, axis=-1, keepdims=True) + EPS)


def shard_of(place_ref, round_, width):
    return pl.ds(pl.multiple_of(jnp.bitwise_xor(place_ref[0], round_) * width, 128), width)


def norm_kernel(place_ref, x_ref, gain_ref, *refs):
    outs, normed = refs[:-1], refs[-1]
    values_f = x_ref[...].astype(jnp.float32)
    normed[...] = (values_f * row_scale_of(values_f) * gain_ref[...]).astype(jnp.bfloat16)
    for round_, out in enumerate(outs):
        out[...] = normed[:, shard_of(place_ref, round_, out.shape[1])]


def split_kernel(place_ref, x_ref, *outs):
    for round_, out in enumerate(outs):
        out[...] = x_ref[:, shard_of(place_ref, round_, out.shape[1])]


def to_rounds(place, field, gain, block=64):
    rows, width = field.shape
    row_spec = pl.BlockSpec((block, width), lambda i: (i, 0))
    gain_spec = pl.BlockSpec((1, width), lambda i: (0, 0))
    plain = gain is None
    return pl.pallas_call(
        split_kernel if plain else norm_kernel,
        grid=(rows // block,),
        in_specs=[smem(), row_spec] + ([] if plain else [gain_spec]),
        out_specs=[pl.BlockSpec((block, width // SEQ), lambda i: (i, 0))] * SEQ,
        out_shape=[jax.ShapeDtypeStruct((rows, width // SEQ), jnp.bfloat16)] * SEQ,
        scratch_shapes=[] if plain else [pltpu.VMEM((block, width), jnp.bfloat16)],
        name="split_rows" if plain else "norm_rows",
    )(place, field, *(() if plain else (gain.reshape(1, width),)))


def norm_back_kernel(place_ref, x_ref, gain_ref, *refs):
    parts, out_ref, joined = refs[:-2], refs[-2], refs[-1]
    width = x_ref.shape[1]
    for round_, part in enumerate(parts):
        joined[:, shard_of(place_ref, round_, part.shape[1])] = part[...]
    values_f = x_ref[...].astype(jnp.float32)
    row_scale = row_scale_of(values_f)
    gated = gain_ref[...] * joined[...].astype(jnp.float32)
    inner = jnp.sum(gated * values_f, axis=-1, keepdims=True)
    out_ref[...] = (
        row_scale * gated - values_f * (row_scale * row_scale * row_scale * inner * (1.0 / width))
    ).astype(jnp.bfloat16)


def join_kernel(place_ref, *refs):
    parts, out_ref = refs[:-1], refs[-1]
    for round_, part in enumerate(parts):
        out_ref[:, shard_of(place_ref, round_, part.shape[1])] = part[...]


def from_rounds(place, parts, field=None, gain=None, block=64):
    rows, part_width = parts[0].shape
    width = part_width * SEQ
    row_spec = pl.BlockSpec((block, width), lambda i: (i, 0))
    part_specs = [pl.BlockSpec((block, part_width), lambda i: (i, 0))] * SEQ
    plain = field is None
    return pl.pallas_call(
        join_kernel if plain else norm_back_kernel,
        grid=(rows // block,),
        in_specs=[smem()]
        + ([] if plain else [row_spec, pl.BlockSpec((1, width), lambda i: (0, 0))])
        + part_specs,
        out_specs=row_spec,
        out_shape=jax.ShapeDtypeStruct((rows, width), jnp.bfloat16),
        scratch_shapes=[] if plain else [pltpu.VMEM((block, width), jnp.bfloat16)],
        name="join_rows" if plain else "norm_back",
    )(place, *(() if plain else (field, gain.reshape(1, width))), *parts)


def tile_at(ref, index, rows):
    return ref[pl.ds(pl.multiple_of(index * rows, rows), rows), :]


def gather_pair(ref, near, rows):
    return jnp.concatenate(
        [
            jnp.concatenate([tile_at(ref, one, rows), tile_at(ref, two, rows)], axis=1)
            for one, two in zip(*near)
        ],
        axis=0,
    )


def spread(block, rows):
    twice = jnp.concatenate([block, block], axis=1)
    width = block.shape[1]
    own = (lax.broadcasted_iota(jnp.int32, twice.shape, 0) < rows) == (
        lax.broadcasted_iota(jnp.int32, twice.shape, 1) < width
    )
    return jnp.where(own, twice, jnp.zeros_like(twice))


def near_of(place_ref, pairs_ref, pair):
    flip = place_ref[3]
    return [
        [
            jnp.bitwise_xor(pairs_ref[jnp.bitwise_xor(2 * pair + half, flip), n], flip)
            for n in range(pairs_ref.shape[1])
        ]
        for half in range(2)
    ]


def forward_kernel(place_ref, pairs_ref, lens_ref, *refs):
    q_parts, k_parts, v_parts = refs[:SEQ], refs[SEQ : 2 * SEQ], refs[2 * SEQ : 3 * SEQ]
    att_ref, probs_ref, q_all, k_all, v_all = refs[3 * SEQ :]
    tile_count, neighbours = pairs_ref.shape
    clip_rows, width = q_all.shape
    tile_rows = clip_rows // tile_count
    rows = 2 * tile_rows
    depth = neighbours * tile_rows
    scale = LOG2E / math.sqrt(width)
    for parts, whole in ((q_parts, q_all), (k_parts, k_all), (v_parts, v_all)):
        for at, part in enumerate(parts):
            whole[at * part.shape[0] : (at + 1) * part.shape[0], :] = part[...]
    shape = (tile_rows - MIN_LIVE, rows)
    first = lax.broadcasted_iota(jnp.int32, shape, 1) < tile_rows
    slot = lax.broadcasted_iota(jnp.int32, shape, 0) + MIN_LIVE

    def length(tile):
        return lens_ref[0, jnp.bitwise_xor(tile, place_ref[3])]

    def step(pair, carry):
        row = pl.multiple_of(pair * rows, rows)
        near = near_of(place_ref, pairs_ref, pair)
        keys = gather_pair(k_all, near, tile_rows)
        vals = gather_pair(v_all, near, tile_rows)
        queries = spread(q_all[pl.ds(row, rows), :], tile_rows)
        scores = contract(keys, queries, 1, 1)
        pieces = []
        for n in range(neighbours):
            start = n * tile_rows
            pieces.append(scores[start : start + MIN_LIVE])
            live = slot < jnp.where(first, length(near[0][n]), length(near[1][n]))
            pieces.append(jnp.where(live, scores[start + MIN_LIVE : start + tile_rows], -jnp.inf))
        scores = jnp.concatenate(pieces, axis=0)
        weights = jnp.exp2((scores - jnp.max(scores, axis=0, keepdims=True)) * scale)
        probs = weights * (1.0 / jnp.sum(weights, axis=0, keepdims=True))
        probs_low = probs.astype(jnp.bfloat16)
        probs_ref[0, pl.ds(pl.multiple_of(pair * depth, depth), depth), :] = probs_low
        attended = contract(probs_low, vals, 0, 0)
        for half in range(2):
            part = attended[half * tile_rows : (half + 1) * tile_rows, half * width : (half + 1) * width]
            place = pl.ds(pl.multiple_of(row + half * tile_rows, tile_rows), tile_rows)
            att_ref[place, :] = part.astype(jnp.bfloat16)
        return carry

    lax.fori_loop(0, tile_count // 2, step, 0, unroll=2)


def forward(place, tile_pairs, lens, query_parts, key_parts, value_parts):
    rows, local_width = query_parts[0].shape
    heads = local_width // HEAD_DIM
    clip_rows = rows * SEQ
    pairs = tile_pairs.shape[0] // 2
    depth = tile_pairs.shape[1] * (clip_rows // tile_pairs.shape[0])
    part_spec = pl.BlockSpec((rows, HEAD_DIM), lambda h: (0, h))
    return pl.pallas_call(
        forward_kernel,
        grid=(heads,),
        in_specs=[smem()] * 3 + [part_spec] * (3 * SEQ),
        out_specs=[
            pl.BlockSpec((clip_rows, HEAD_DIM), lambda h: (0, h)),
            pl.BlockSpec((1, pairs * depth, HEAD_DIM), lambda h: (h, 0, 0)),
        ],
        out_shape=[
            jax.ShapeDtypeStruct((clip_rows, local_width), jnp.bfloat16),
            jax.ShapeDtypeStruct((heads, pairs * depth, HEAD_DIM), jnp.bfloat16),
        ],
        scratch_shapes=[pltpu.VMEM((clip_rows, HEAD_DIM), jnp.bfloat16)] * 3,
        compiler_params=params(),
        name="attention_forward",
    )(place, tile_pairs, lens, *query_parts, *key_parts, *value_parts)


def backward_kernel(place_ref, pairs_ref, *refs):
    q_parts, k_parts, v_parts = refs[:SEQ], refs[SEQ : 2 * SEQ], refs[2 * SEQ : 3 * SEQ]
    own_grads, other_grads = refs[3 * SEQ : 4 * SEQ], refs[4 * SEQ : 5 * SEQ]
    probs_ref = refs[5 * SEQ]
    outs = refs[5 * SEQ + 1 : 8 * SEQ + 1]
    q_all, k_all, v_all, g_all, gq_all, gk_acc, gv_acc = refs[8 * SEQ + 1 :]
    tile_count, neighbours = pairs_ref.shape
    clip_rows, width = q_all.shape
    tile_rows = clip_rows // tile_count
    rows = 2 * tile_rows
    depth = neighbours * tile_rows
    factor = 1.0 / math.sqrt(width)
    for parts, whole in ((q_parts, q_all), (k_parts, k_all), (v_parts, v_all)):
        for at, part in enumerate(parts):
            whole[at * part.shape[0] : (at + 1) * part.shape[0], :] = part[...]
    half_rows = own_grads[0].shape[0]
    core = place_ref[1]
    for at in range(SEQ):
        for grads, half in ((own_grads[at], core), (other_grads[at ^ 1], 1 - core)):
            g_all[pl.ds(pl.multiple_of((2 * at + half) * half_rows, half_rows), half_rows), :] = grads[...]
    gk_acc[...] = jnp.zeros_like(gk_acc)
    gv_acc[...] = jnp.zeros_like(gv_acc)

    def step(pair, carry):
        row = pl.multiple_of(pair * rows, rows)
        near = near_of(place_ref, pairs_ref, pair)
        keys = gather_pair(k_all, near, tile_rows)
        vals = gather_pair(v_all, near, tile_rows)
        queries = spread(q_all[pl.ds(row, rows), :], tile_rows)
        grads = spread(g_all[pl.ds(row, rows), :], tile_rows)
        probs_low = probs_ref[0, pl.ds(pl.multiple_of(pair * depth, depth), depth), :]
        probs = probs_low.astype(jnp.float32)
        grad_probs = contract(vals, grads, 1, 1)
        delta = jnp.sum(probs * grad_probs, axis=0, keepdims=True)
        grad_scores = (probs * (grad_probs - delta)).astype(jnp.bfloat16)
        grad_query = contract(grad_scores, keys, 0, 0) * factor
        for half in range(2):
            part = grad_query[half * tile_rows : (half + 1) * tile_rows, half * width : (half + 1) * width]
            place = pl.ds(pl.multiple_of(row + half * tile_rows, tile_rows), tile_rows)
            gq_all[place, :] = part.astype(jnp.bfloat16)
        grad_keys = contract(grad_scores, queries, 1, 0)
        grad_vals = contract(probs_low, grads, 1, 0)
        for half in range(2):
            for n in range(neighbours):
                at = (slice(n * tile_rows, (n + 1) * tile_rows), slice(half * width, (half + 1) * width))
                place = pl.ds(pl.multiple_of(near[half][n] * tile_rows, tile_rows), tile_rows)
                gk_acc[place, :] += grad_keys[at]
                gv_acc[place, :] += grad_vals[at]
        return carry

    lax.fori_loop(0, tile_count // 2, step, 0)
    for at in range(SEQ):
        part = slice(at * outs[0].shape[0], (at + 1) * outs[0].shape[0])
        outs[at][...] = gq_all[part, :]
        outs[SEQ + at][...] = (gk_acc[part, :] * factor).astype(jnp.bfloat16)
        outs[2 * SEQ + at][...] = gv_acc[part, :].astype(jnp.bfloat16)


def backward(place, tile_pairs, query_parts, key_parts, value_parts, own_grads, other_grads, probs):
    rows, local_width = query_parts[0].shape
    heads = local_width // HEAD_DIM
    clip_rows = rows * SEQ
    part_spec = pl.BlockSpec((rows, HEAD_DIM), lambda h: (0, h))
    grad_spec = pl.BlockSpec((own_grads[0].shape[0], HEAD_DIM), lambda h: (0, h))
    bf16_rows = pltpu.VMEM((clip_rows, HEAD_DIM), jnp.bfloat16)
    f32_rows = pltpu.VMEM((clip_rows, HEAD_DIM), jnp.float32)
    outs = pl.pallas_call(
        backward_kernel,
        grid=(heads,),
        in_specs=[smem()] * 2
        + [part_spec] * (3 * SEQ)
        + [grad_spec] * (2 * SEQ)
        + [pl.BlockSpec((1,) + probs.shape[1:], lambda h: (h, 0, 0))],
        out_specs=[part_spec] * (3 * SEQ),
        out_shape=[jax.ShapeDtypeStruct((rows, local_width), jnp.bfloat16)] * (3 * SEQ),
        scratch_shapes=[bf16_rows] * 5 + [f32_rows] * 2,
        compiler_params=params(),
        name="attention_backward",
    )(place, tile_pairs, *query_parts, *key_parts, *value_parts, *own_grads, *other_grads, probs)
    return outs[:SEQ], outs[SEQ : 2 * SEQ], outs[2 * SEQ :]


def weight_grad_kernel(place_ref, mean, att_ref, *refs):
    own, other, out_ref = refs[:SEQ], refs[SEQ : 2 * SEQ], refs[2 * SEQ]
    half_rows = own[0].shape[0]
    core = place_ref[1]
    columns, attended = [], []
    for at in range(SEQ):
        for part, half in ((own[at], core), (other[at ^ 1], 1 - core)):
            columns.append(part[...])
            start = pl.multiple_of((2 * at + half) * half_rows, half_rows)
            attended.append(att_ref[pl.ds(start, half_rows), :])
    total = contract(jnp.concatenate(columns, axis=0), jnp.concatenate(attended, axis=0), 0, 0)
    out_ref[...] = (total * mean).astype(jnp.bfloat16)


def weight_grad(place, attended, own, other, mean, block=640):
    half_rows, features = own[0].shape
    local_width = attended.shape[1]
    return pl.pallas_call(
        lambda place_ref, *refs: weight_grad_kernel(place_ref, mean, *refs),
        grid=(features // block,),
        in_specs=[smem(), pl.BlockSpec(attended.shape, lambda i: (0, 0))]
        + [pl.BlockSpec((half_rows, block), lambda i: (0, i))] * (2 * SEQ),
        out_specs=pl.BlockSpec((block, local_width), lambda i: (i, 0)),
        out_shape=jax.ShapeDtypeStruct((features, local_width), jnp.bfloat16),
        compiler_params=params(),
        name="weight_grad",
    )(place, attended, *own, *other)


def device_of(core, seq):
    return core * SEQ + seq


def outward(round_):
    pairs = []
    for core in range(CORES):
        for token in range(SEQ):
            shard = token ^ round_
            pairs.append((device_of(core, token), device_of(shard % 2, 2 * core + shard // 2)))
    return pairs


def inward(round_):
    return [(target, source) for source, target in outward(round_)]


def send(value, pairs):
    return lax.ppermute(value, ("core", "seq"), pairs)


def swap_cores(value):
    return lax.ppermute(value, "core", [(0, 1), (1, 0)])


def shift(value, axis, by):
    count = lax.axis_size(axis)
    return lax.ppermute(value, axis, [(i, (i + by) % count) for i in range(count)])


def add(*terms):
    total = terms[0].astype(jnp.float32)
    for term in terms[1:]:
        total = total + term.astype(jnp.float32)
    return total.astype(jnp.bfloat16)


def take(value, index, axis=0):
    return lax.dynamic_index_in_dim(value, index, axis, keepdims=False)


def scatter_sum(value, axis, dim=0):
    here = lax.axis_index(axis)
    count = lax.axis_size(axis)
    got = [shift(take(value, (here + by) % count, dim), axis, by) for by in (2, 1, 3)]
    return add(take(value, here, dim), *got)


def to_shard_holders(w_out, core, seq):
    got = []
    for other in range(2):
        pairs = []
        for holder in range(CORES):
            for shard in range(SEQ):
                window = holder ^ other
                pairs.append((device_of(holder, shard), device_of(shard % 2, shard // 2 + 2 * window)))
        got.append(send(w_out, pairs))
    window = seq // 2
    return jnp.where(window == 0, jnp.concatenate(got), jnp.concatenate(got[::-1]))


def to_owners(total, seq):
    half = total.shape[0] // 2
    window = seq // 2
    got = []
    for other in range(2):
        pairs = []
        for core in range(CORES):
            for at in range(SEQ):
                holder = (at // 2) ^ other
                pairs.append((device_of(core, at), device_of(holder, 2 * (at % 2) + core)))
        rows = jnp.where((window ^ other) == 0, total[:half], total[half:])
        got.append(send(rows, pairs))
    return got[0].astype(jnp.float32) + got[1].astype(jnp.float32)


def per_device(queries, keys, values, gain_q, gain_k, tile_pairs, tile_lens, out_grad, w_out):
    core = lax.axis_index("core")
    seq = lax.axis_index("seq")
    count_z = lax.axis_size("z")
    count_x = lax.axis_size("x")
    rows, features = out_grad.shape
    shard = 2 * (seq % 2) + core
    tiles_per_block = tile_pairs.shape[0] // SEQ
    place = jnp.stack([seq, core, shard, shard * tiles_per_block]).astype(jnp.int32)
    lens = jnp.where(seq // 2 == core, tile_lens, swap_cores(tile_lens))

    rounds = range(SEQ)
    key_parts = [send(part, outward(r)) for r, part in enumerate(to_rounds(place, keys, gain_k))]
    query_parts = [send(part, outward(r)) for r, part in enumerate(to_rounds(place, queries, gain_q))]
    value_parts = [send(part, outward(r)) for r, part in enumerate(to_rounds(place, values, None))]

    halves = out_grad.reshape(2, rows // 2, features)
    even = take(halves, seq % 2)
    odd = take(halves, 1 - seq % 2)
    own = [send(odd if r % 2 else even, outward(r)) for r in rounds]
    other = [swap_cores(part) for part in own]

    w_all = lax.all_gather(to_shard_holders(w_out, core, seq), ("z", "x"), axis=0, tiled=True)

    def project(part):
        return jnp.dot(part, w_all, preferred_element_type=jnp.float32).astype(jnp.bfloat16)

    attended, probs = forward(place, tile_pairs, lens, query_parts, key_parts, value_parts)
    own_grads = [project(part) for part in own]
    other_grads = [project(part) for part in other]
    grad_w = weight_grad(place, attended, own, other, 1.0 / (count_z * count_x * CORES))
    grad_qn, grad_kn, grad_vh = backward(
        place, tile_pairs, query_parts, key_parts, value_parts, own_grads, other_grads, probs
    )

    def to_rows(parts):
        return [send(part, inward(r)) for r, part in enumerate(parts)]

    grad_q = from_rounds(place, to_rows(grad_qn), queries, gain_q)
    grad_k = from_rounds(place, to_rows(grad_kn), keys, gain_k)
    grad_v = from_rounds(place, to_rows(grad_vh))

    grad_w = grad_w.reshape(count_z, count_x, 2, -1, grad_w.shape[1])
    one = scatter_sum(scatter_sum(grad_w[:, :, 0], "x", 1), "z")
    two = scatter_sum(scatter_sum(grad_w[:, :, 1], "z"), "x")
    grad_w = to_owners(jnp.concatenate([one, two]), seq)
    return (grad_q, grad_k, grad_v, grad_w)


def solution(mesh):
    dp = mesh.shape["dp"]
    side = math.isqrt(dp // CORES)
    parts = Mesh(mesh.devices.reshape(side, side, CORES, SEQ), ("z", "x", "core", "seq"))
    dp_axes = ("z", "x", "core")
    tokens = P(dp_axes + ("seq",), None)
    return jax.shard_map(
        per_device,
        mesh=parts,
        in_specs=(tokens, tokens, tokens, P(), P(), P(), P(dp_axes, None), tokens, P(dp_axes, "seq")),
        out_specs=(tokens, tokens, tokens, P(dp_axes, "seq")),
        check_vma=False,
    )
```

time: 340 us -> 434 us (1.28)
  starting transfers between devices: 22.4 us -> 107 us
  blocking collectives: 41.7 us -> 0 us
  Pallas kernels: 63 us -> 94.5 us
  local copies, waits for them, and re-layouts: 18.5 us -> 29 us
  other arithmetic: 0 us -> 9.35 us
    ppermute x0 -> x49, waiting for transfers between devices: none -> 153 us  [the longest x32 106 us: send(): return lax.ppermute(value, ('core', 'seq'), pairs)]
    ppermute x0 -> x49, starting transfers between devices: none -> 107 us  [the longest x32 83.5 us: send(): return lax.ppermute(value, ('core', 'seq'), pairs)]
    all_gather x2 -> x1, waiting for transfers between devices: 102 us -> 0.01 us  [per_device(): lax.all_gather(to_shard_holders(w_out, core, seq), ('z', 'x'), axis=0, ti...]
    all_to_all x2 -> x0, blocking collectives: 41.7 us -> none  [exchange(): return lax.all_to_all(parts, 'seq', split_axis=0, concat_axis=0, tiled=True)]
    pallas_call x7 -> x9, Pallas kernels: 63 us -> 94.5 us  [the longest x1 33 us: backward(): pl.pallas_call(backward_kernel, grid=(heads,), in_specs=[smem()] * 2 + [p...]
    all_to_all x4 -> x0, waiting for transfers between devices: 28.6 us -> none  [exchange(): return lax.all_to_all(parts, 'seq', split_axis=0, concat_axis=0, tiled=True)]
    unnamed x4 -> x1, waiting for transfers between devices: 23.5 us -> 0.02 us
    all_to_all x4 -> x0, starting transfers between devices: 22.3 us -> none  [exchange(): return lax.all_to_all(parts, 'seq', split_axis=0, concat_axis=0, tiled=True)]
  transfers between devices with their start and end apart: 7 -> 50, of which waited for: 6 -> 22; matrix products, arithmetic and copies ran while one was open for 4% -> 6% of each run, Pallas kernels for 7% -> 14%
where the time goes in v2:
time: 434 us; the launch traced here: 429 us
  waiting for transfers between devices  153 us (35%)
  starting transfers between devices  107 us (25%)
  Pallas kernels  94.5 us (22%)
  local copies, waits for them, and re-layouts  29 us (7%)
  matrix products  21.1 us (5%)
  between operations  14.6 us (3%)
  other arithmetic  9.35 us (2%)
    ppermute x32, waiting for transfers between devices, send(): return lax.ppermute(value, ('core', 'seq'), pairs)  106 us
    ppermute x32, starting transfers between devices, send(): return lax.ppermute(value, ('core', 'seq'), pairs)  83.5 us
    ppermute x12, waiting for transfers between devices, shift(): lax.ppermute(value, axis, [(i, (i + by) % count) for i in range(count)])  47.7 us
    pallas_call x1, Pallas kernels, backward(): pl.pallas_call(backward_kernel, grid=(heads,), in_specs=[smem()] * 2 + [p...  33 us
    pallas_call x1, Pallas kernels, forward(): pl.pallas_call(forward_kernel, grid=(heads,), in_specs=[smem()] * 3 + [pa...  25.1 us
    ppermute x12, starting transfers between devices, shift(): lax.ppermute(value, axis, [(i, (i + by) % count) for i in range(count)])  21.9 us
    dot_general x8, matrix products, project(): jnp.dot(part, w_all, preferred_element_type=jnp.float32)  21.1 us
    unnamed x73, local copies, waits for them, and re-layouts  13.5 us
  transfers between devices with their start and end apart: 50, of which 22 were waited for; matrix products, arithmetic and copies ran while one was open for 6% of the time, Pallas kernels for 14%

profile of v2, /device:TPU:24, one launch (start us, length us, event | category | flops | bytes accessed | tf_op | source)
XLA Modules:
  0.0 428.5 jit_solution(1924794362919809330)
XLA Ops:
  9.9 4.2 collective-permute-done.14
  18.4 3.7 norm_rows.2
  22.2 5.9 %collective-permute-start = (bf16[256,640]{1,0:T(8,128)(2,1)}, bf16[256,640]{1,0:T(8,128)(2,1)S(1)}, u32[]{:S(2)}, u32[]{:S(2)}) collective-permute-start(bf16[256,640]{1,0:T(8,128)(2,1)} %get-tuple-element.30), channel_id=1, source_target_pairs={{0,0},{1,4},{2,1},{3,5},{4,2},{5,6},{6,3},{7,7},{8,8},{9,12},{10,9... | collective-permute-start | bytes 983048 | tf_op jit(solution)/shard_map/ppermute | solution.py:346
  33.2 3.8 norm_rows.3
  37.0 5.1 %collective-permute-start.4 = (bf16[256,640]{1,0:T(8,128)(2,1)}, bf16[256,640]{1,0:T(8,128)(2,1)S(1)}, u32[]{:S(2)}, u32[]{:S(2)}) collective-permute-start(bf16[256,640]{1,0:T(8,128)(2,1)} %get-tuple-element.34), channel_id=1, source_target_pairs={{0,0},{1,4},{2,1},{3,5},{4,2},{5,6},{6,3},{7,7},{8,8},{9,12},{10,9... | collective-permute-start | bytes 983048 | tf_op jit(solution)/shard_map/ppermute | solution.py:346
  52.7 8.4 %collective-permute-start.5 = (bf16[256,640]{1,0:T(8,128)(2,1)S(1)}, bf16[256,640]{1,0:T(8,128)(2,1)S(1)}, u32[]{:S(2)}, u32[]{:S(2)}) collective-permute-start(bf16[256,640]{1,0:T(8,128)(2,1)S(1)} %copy-done.35), channel_id=1, source_target_pairs={{0,4},{1,0},{2,5},{3,1},{4,6},{5,2},{6,7},{7,3},{8,12},{9,8},{10,1... | collective-permute-start | bytes 983048 | tf_op jit(solution)/shard_map/ppermute | solution.py:346
  61.1 46.7 %collective-permute-done.5.refs_5_ = bf16[256,640]{1,0:T(8,128)(2,1)S(1)} collective-permute-done((bf16[256,640]{1,0:T(8,128)(2,1)S(1)}, bf16[256,640]{1,0:T(8,128)(2,1)S(1)}, u32[]{:S(2)}, u32[]{:S(2)}) %collective-permute-start.5) | collective-permute-done | bytes 327712 | tf_op jit(solution)/shard_map/ppermute | solution.py:346
  109.7 6.6 %collective-permute-done.6.refs_6_ = bf16[256,640]{1,0:T(8,128)(2,1)S(1)} collective-permute-done((bf16[256,640]{1,0:T(8,128)(2,1)S(1)}, bf16[256,640]{1,0:T(8,128)(2,1)S(1)}, u32[]{:S(2)}, u32[]{:S(2)}) %collective-permute-start.6) | collective-permute-done | bytes 327712 | tf_op jit(solution)/shard_map/ppermute | solution.py:346
  117.0 9.6 %collective-permute-start.7 = (bf16[256,640]{1,0:T(8,128)(2,1)}, bf16[256,640]{1,0:T(8,128)(2,1)}, u32[]{:S(2)}, u32[]{:S(2)}) collective-permute-start(bf16[256,640]{1,0:T(8,128)(2,1)} %get-tuple-element.37), channel_id=1, source_target_pairs={{0,5},{1,1},{2,4},{3,0},{4,7},{5,3},{6,6},{7,2},{8,13},{9,9},{10,1... | collective-permute-start | bytes 983048 | tf_op jit(solution)/shard_map/ppermute | solution.py:346
  126.6 3.5 split_rows.1
  135.9 4.2 collective-permute-done.8.refs_8_
  140.8 4.1 collective-permute-start.9
  145.0 5.0 %collective-permute-done.9.refs_9_ = bf16[256,640]{1,0:T(8,128)(2,1)S(1)} collective-permute-done((bf16[256,640]{1,0:T(8,128)(2,1)}, bf16[256,640]{1,0:T(8,128)(2,1)S(1)}, u32[]{:S(2)}, u32[]{:S(2)}) %collective-permute-start.9) | collective-permute-done | bytes 327712 | tf_op jit(solution)/shard_map/ppermute | solution.py:346
  150.9 11.2 %collective-permute-done.10.refs_10_ = bf16[256,640]{1,0:T(8,128)(2,1)S(1)} collective-permute-done((bf16[256,640]{1,0:T(8,128)(2,1)}, bf16[256,640]{1,0:T(8,128)(2,1)S(1)}, u32[]{:S(2)}, u32[]{:S(2)}) %collective-permute-start.10) | collective-permute-done | bytes 327712 | tf_op jit(solution)/shard_map/ppermute | solution.py:346
  164.9 8.3 %collective-permute-done.11.refs_11_ = bf16[256,640]{1,0:T(8,128)(2,1)} collective-permute-done((bf16[256,640]{1,0:T(8,128)(2,1)}, bf16[256,640]{1,0:T(8,128)(2,1)}, u32[]{:S(2)}, u32[]{:S(2)}) %collective-permute-start.11) | collective-permute-done | bytes 327712 | tf_op jit(solution)/shard_map/ppermute | solution.py:346
  179.0 25.1 %attention_forward.1 = (bf16[1024,640]{1,0:T(8,128)(2,1)S(1)}, bf16[5,4096,128]{2,1,0:T(8,128)(2,1)}) custom-call(s32[4]{0:T(128)S(1)} %copy-done.12, s32[16,8]{1,0:T(8,128)S(1)} %copy.14.pairs_ref, s32[1,16]{1,0:T(1,128)S(1)} %broadcast_select_fusion.2.lens_ref, bf16[256,640]{1,0:T(8,128)(2,1)S(1)} %collective-permute-done.refs_0_, ...), custom_call_target="tpu_custom_call" | custom-call | tf_op jit(solution)/shard_map/attention_forward/pallas_call | solution.py:199
  204.1 13.3 %weight_grad.1 = bf16[5120,640]{1,0:T(8,128)(2,1)} custom-call(s32[4]{0:T(128)S(1)} %copy-done.12, bf16[1024,640]{1,0:T(8,128)(2,1)S(1)} %get-tuple-element.55.refs_0_, bf16[128,5120]{1,0:T(8,128)(2,1)S(1)} %collective-permute-done.12.refs_1_, bf16[128,5120]{1,0:T(8,128)(2,1)S(1)} %collective-permute-done.15.refs_2_, ...), custom_call_target="tpu_custom_call" | custom-call | tf_op jit(solution)/shard_map/weight_grad/pallas_call | solution.py:316
  217.4 5.2 %fusion.14 = (bf16[4,4,1,160,640]{4,3,2,1,0:T(8,128)(2,1)}, bf16[4,4,1,160,640]{4,3,2,1,0:T(8,128)(2,1)S(1)}) fusion(bf16[4,4,2,160,640]{4,3,2,1,0:T(8,128)(2,1)} %bitcast.81), kind=kLoop, calls=%fused_computation.44 | loop fusion | bytes 13107200 | tf_op jit(solution)/shard_map/slice | solution.py:447
  225.1 4.0 collective-permute-start.43
  236.9 28.0 %collective-permute-done.43 = bf16[4,160,640]{2,1,0:T(8,128)(2,1)} collective-permute-done((bf16[4,160,640]{2,1,0:T(8,128)(2,1)}, bf16[4,160,640]{2,1,0:T(8,128)(2,1)}, u32[]{:S(2)}, u32[]{:S(2)}) %collective-permute-start.43) | collective-permute-done | bytes 819232 | tf_op jit(solution)/shard_map/ppermute | solution.py:355
  276.6 11.3 %collective-permute-done.35 = bf16[4,160,640]{2,1,0:T(8,128)(2,1)} collective-permute-done((bf16[4,160,640]{2,1,0:T(8,128)(2,1)}, bf16[4,160,640]{2,1,0:T(8,128)(2,1)}, u32[]{:S(2)}, u32[]{:S(2)}) %collective-permute-start.35) | collective-permute-done | bytes 819232 | tf_op jit(solution)/shard_map/ppermute | solution.py:355
  291.3 3.7 collective-permute-start.40
  296.5 3.7 collective-permute-done.40
  300.3 4.3 collective-permute-done.39
  307.0 4.3 convolution_convert_fusion.7.refs_12_
  328.6 33.0 %attention_backward.1 = (bf16[256,640]{1,0:T(8,128)(2,1)S(1)}, bf16[256,640]{1,0:T(8,128)(2,1)S(1)}, bf16[256,640]{1,0:T(8,128)(2,1)S(1)}, bf16[256,640]{1,0:T(8...) custom-call(s32[4]{0:T(128)S(1)} %copy-done.12, ...), custom_call_target="tpu_custom_call" | custom-call | tf_op jit(solution)/shard_map/attention_backward/pallas_call | solution.py:283
  370.2 9.7 %collective-permute-start.26 = (bf16[256,640]{1,0:T(8,128)(2,1)S(1)}, bf16[256,640]{1,0:T(8,128)(2,1)S(1)}, u32[]{:S(2)}, u32[]{:S(2)}) collective-permute-start(bf16[256,640]{1,0:T(8,128)(2,1)S(1)} %get-tuple-element.46), channel_id=1, source_target_pairs={{5,0},{1,1},{4,2},{0,3},{7,4},{3,5},{6,6},{2,7},{13,8},{9,9},{12,1... | collective-permute-start | bytes 983048 | tf_op jit(solution)/shard_map/ppermute | solution.py:346
  385.5 5.2 %collective-permute-start.30 = (bf16[256,640]{1,0:T(8,128)(2,1)S(1)}, bf16[256,640]{1,0:T(8,128)(2,1)}, u32[]{:S(2)}, u32[]{:S(2)}) collective-permute-start(bf16[256,640]{1,0:T(8,128)(2,1)S(1)} %get-tuple-element.50), channel_id=1, source_target_pairs={{5,0},{1,1},{4,2},{0,3},{7,4},{3,5},{6,6},{2,7},{13,8},{9,9},{12,1... | collective-permute-start | bytes 983048 | tf_op jit(solution)/shard_map/ppermute | solution.py:346
  397.3 6.7 %collective-permute-done.29.refs_2_ = bf16[256,640]{1,0:T(8,128)(2,1)S(1)} collective-permute-done((bf16[256,640]{1,0:T(8,128)(2,1)S(1)}, bf16[256,640]{1,0:T(8,128)(2,1)S(1)}, u32[]{:S(2)}, u32[]{:S(2)}) %collective-permute-start.29) | collective-permute-done | bytes 327712 | tf_op jit(solution)/shard_map/ppermute | solution.py:346
  407.5 4.3 %norm_back.2 = bf16[256,2560]{1,0:T(8,128)(2,1)} custom-call(s32[4]{0:T(128)} %pad_add_fusion.place_ref, bf16[256,2560]{1,0:T(8,128)(2,1)} %x_ref.8, f32[1,2560]{1,0:T(1,128)} %reshape.46.gain_ref, bf16[256,640]{1,0:T(8,128)(2,1)} %copy-done.19, bf16[256,640]{1,0:T(8,128)(2,1)} %copy-done.20, bf16[256,640]{1,0:T(8,128)(2,1)} %copy-done.21, ...), custom_call_target="tpu_custom_call" | custom-call | tf_op jit(solution)/shard_map/norm_back/pallas_call | solution.py:98
  411.8 4.3 %norm_back.3 = bf16[256,2560]{1,0:T(8,128)(2,1)} custom-call(s32[4]{0:T(128)} %pad_add_fusion.place_ref, bf16[256,2560]{1,0:T(8,128)(2,1)} %x_ref.9, f32[1,2560]{1,0:T(1,128)} %reshape.47.gain_ref, bf16[256,640]{1,0:T(8,128)(2,1)} %copy-done.23, bf16[256,640]{1,0:T(8,128)(2,1)} %copy-done.24, bf16[256,640]{1,0:T(8,128)(2,1)} %copy-done.25, ...), custom_call_target="tpu_custom_call" | custom-call | tf_op jit(solution)/shard_map/norm_back/pallas_call | solution.py:98
  418.1 3.6 join_rows.1
  (175 shorter events, 114.0 us)
Async XLA Ops:
  7.2 299.8 %all-gather.2.cloned.1.call-start = ((), (), s32[]{:S(2)}) async-start(), calls=%async_computation | async-start | bytes 6963200 | tf_op jit(solution)/shard_map/all_gather | solution.py:426
  22.2 21.7 %collective-permute-start = (bf16[256,640]{1,0:T(8,128)(2,1)}, bf16[256,640]{1,0:T(8,128)(2,1)S(1)}, u32[]{:S(2)}, u32[]{:S(2)}) collective-permute-start(bf16[256,640]{1,0:T(8,128)(2,1)} %get-tuple-element.30), channel_id=1, source_target_pairs={{0,0},{1,4},{2,1},{3,5},{4,2},{5,6},{6,3},{7,7},{8,8},{9,12},{10,9... | collective-permute-start | bytes 983048 | tf_op jit(solution)/shard_map/ppermute | solution.py:346
  28.1 18.8 %collective-permute-start.1 = (bf16[256,640]{1,0:T(8,128)(2,1)}, bf16[256,640]{1,0:T(8,128)(2,1)S(1)}, u32[]{:S(2)}, u32[]{:S(2)}) collective-permute-start(bf16[256,640]{1,0:T(8,128)(2,1)} %get-tuple-element.31), channel_id=1, source_target_pairs={{0,4},{1,0},{2,5},{3,1},{4,6},{5,2},{6,7},{7,3},{8,12},{9,8},{10,1... | collective-permute-start | bytes 983048 | tf_op jit(solution)/shard_map/ppermute | solution.py:346
  29.2 19.7 %collective-permute-start.2 = (bf16[256,640]{1,0:T(8,128)(2,1)}, bf16[256,640]{1,0:T(8,128)(2,1)}, u32[]{:S(2)}, u32[]{:S(2)}) collective-permute-start(bf16[256,640]{1,0:T(8,128)(2,1)} %get-tuple-element.32), channel_id=1, source_target_pairs={{0,1},{1,5},{2,0},{3,4},{4,3},{5,7},{6,2},{7,6},{8,9},{9,13},{10,8... | collective-permute-start | bytes 983048 | tf_op jit(solution)/shard_map/ppermute | solution.py:346
  30.6 19.4 %collective-permute-start.3 = (bf16[256,640]{1,0:T(8,128)(2,1)}, bf16[256,640]{1,0:T(8,128)(2,1)}, u32[]{:S(2)}, u32[]{:S(2)}) collective-permute-start(bf16[256,640]{1,0:T(8,128)(2,1)} %get-tuple-element.33), channel_id=1, source_target_pairs={{0,5},{1,1},{2,4},{3,0},{4,7},{5,3},{6,6},{7,2},{8,13},{9,9},{10,1... | collective-permute-start | bytes 983048 | tf_op jit(solution)/shard_map/ppermute | solution.py:346
  43.9 90.9 %collective-permute-start.12 = (bf16[128,5120]{1,0:T(8,128)(2,1)}, bf16[128,5120]{1,0:T(8,128)(2,1)S(1)}, u32[]{:S(2)}, u32[]{:S(2)}) collective-permute-start(bf16[128,5120]{1,0:T(8,128)(2,1)} %get-tuple-element.68), channel_id=1, source_target_pairs={{0,0},{1,4},{2,1},{3,5},{4,2},{5,6},{6,3},{7,7},{8,8},{9,12},{10,9... | collective-permute-start | bytes 3932168 | tf_op jit(solution)/shard_map/ppermute | solution.py:346
  46.9 87.9 %collective-permute-start.15 = (bf16[128,5120]{1,0:T(8,128)(2,1)}, bf16[128,5120]{1,0:T(8,128)(2,1)S(1)}, u32[]{:S(2)}, u32[]{:S(2)}) collective-permute-start(bf16[128,5120]{1,0:T(8,128)(2,1)} %get-tuple-element.67), channel_id=1, source_target_pairs={{0,4},{1,0},{2,5},{3,1},{4,6},{5,2},{6,7},{7,3},{8,12},{9,8},{10,1... | collective-permute-start | bytes 3932168 | tf_op jit(solution)/shard_map/ppermute | solution.py:346
  48.9 86.4 %collective-permute-start.16 = (bf16[128,5120]{1,0:T(8,128)(2,1)}, bf16[128,5120]{1,0:T(8,128)(2,1)}, u32[]{:S(2)}, u32[]{:S(2)}) collective-permute-start(bf16[128,5120]{1,0:T(8,128)(2,1)} %get-tuple-element.68), channel_id=1, source_target_pairs={{0,1},{1,5},{2,0},{3,4},{4,3},{5,7},{6,2},{7,6},{8,9},{9,13},{10,8... | collective-permute-start | bytes 3932168 | tf_op jit(solution)/shard_map/ppermute | solution.py:346
  50.0 85.4 %collective-permute-start.17 = (bf16[128,5120]{1,0:T(8,128)(2,1)}, bf16[128,5120]{1,0:T(8,128)(2,1)}, u32[]{:S(2)}, u32[]{:S(2)}) collective-permute-start(bf16[128,5120]{1,0:T(8,128)(2,1)} %get-tuple-element.67), channel_id=1, source_target_pairs={{0,5},{1,1},{2,4},{3,0},{4,7},{5,3},{6,6},{7,2},{8,13},{9,9},{10,1... | collective-permute-start | bytes 3932168 | tf_op jit(solution)/shard_map/ppermute | solution.py:346
  52.7 55.2 %collective-permute-start.5 = (bf16[256,640]{1,0:T(8,128)(2,1)S(1)}, bf16[256,640]{1,0:T(8,128)(2,1)S(1)}, u32[]{:S(2)}, u32[]{:S(2)}) collective-permute-start(bf16[256,640]{1,0:T(8,128)(2,1)S(1)} %copy-done.35), channel_id=1, source_target_pairs={{0,4},{1,0},{2,5},{3,1},{4,6},{5,2},{6,7},{7,3},{8,12},{9,8},{10,1... | collective-permute-start | bytes 983048 | tf_op jit(solution)/shard_map/ppermute | solution.py:346
  134.8 69.3 %collective-permute-start.18 = (bf16[128,5120]{1,0:T(8,128)(2,1)S(1)}, bf16[128,5120]{1,0:T(8,128)(2,1)}, u32[]{:S(2)}, u32[]{:S(2)}) collective-permute-start(bf16[128,5120]{1,0:T(8,128)(2,1)S(1)} %collective-permute-done.12.refs_1_), channel_id=1, source_target_pairs={{0,4},{4,0},{1,5},{5,1},{2,6},{6,2},{3,7},{7,3},{8,12},{12,8},{9,1... | collective-permute-start | bytes 3932168 | tf_op jit(solution)/shard_map/ppermute | solution.py:350
  134.9 69.2 %collective-permute-start.19 = (bf16[128,5120]{1,0:T(8,128)(2,1)S(1)}, bf16[128,5120]{1,0:T(8,128)(2,1)}, u32[]{:S(2)}, u32[]{:S(2)}) collective-permute-start(bf16[128,5120]{1,0:T(8,128)(2,1)S(1)} %collective-permute-done.15.refs_2_), channel_id=1, source_target_pairs={{0,4},{4,0},{1,5},{5,1},{2,6},{6,2},{3,7},{7,3},{8,12},{12,8},{9,1... | collective-permute-start | bytes 3932168 | tf_op jit(solution)/shard_map/ppermute | solution.py:350
  135.4 68.7 %collective-permute-start.20 = (bf16[128,5120]{1,0:T(8,128)(2,1)}, bf16[128,5120]{1,0:T(8,128)(2,1)}, u32[]{:S(2)}, u32[]{:S(2)}) collective-permute-start(bf16[128,5120]{1,0:T(8,128)(2,1)} %collective-permute-done.16.refs_3_), channel_id=1, source_target_pairs={{0,4},{4,0},{1,5},{5,1},{2,6},{6,2},{3,7},{7,3},{8,12},{12,8},{9,1... | collective-permute-start | bytes 3932168 | tf_op jit(solution)/shard_map/ppermute | solution.py:350
  135.5 68.6 %collective-permute-start.21 = (bf16[128,5120]{1,0:T(8,128)(2,1)}, bf16[128,5120]{1,0:T(8,128)(2,1)}, u32[]{:S(2)}, u32[]{:S(2)}) collective-permute-start(bf16[128,5120]{1,0:T(8,128)(2,1)} %collective-permute-done.17.refs_4_), channel_id=1, source_target_pairs={{0,4},{4,0},{1,5},{5,1},{2,6},{6,2},{3,7},{7,3},{8,12},{12,8},{9,1... | collective-permute-start | bytes 3932168 | tf_op jit(solution)/shard_map/ppermute | solution.py:350
  225.1 39.8 %collective-permute-start.43 = (bf16[4,160,640]{2,1,0:T(8,128)(2,1)}, bf16[4,160,640]{2,1,0:T(8,128)(2,1)}, u32[]{:S(2)}, u32[]{:S(2)}) collective-permute-start(bf16[4,160,640]{2,1,0:T(8,128)(2,1)} %get-tuple-element.66), channel_id=1, source_target_pairs={{0,96},{32,0},{64,32},{96,64},{1,97},{33,1},{65,33},{97,65},{2,98}... | collective-permute-start | bytes 2457608 | tf_op jit(solution)/shard_map/ppermute | solution.py:355
  229.2 39.1 %collective-permute-start.42 = (bf16[4,160,640]{2,1,0:T(8,128)(2,1)}, bf16[4,160,640]{2,1,0:T(8,128)(2,1)}, u32[]{:S(2)}, u32[]{:S(2)}) collective-permute-start(bf16[4,160,640]{2,1,0:T(8,128)(2,1)} %get-tuple-element.65), channel_id=1, source_target_pairs={{0,32},{32,64},{64,96},{96,0},{1,33},{33,65},{65,97},{97,1},{2,34}... | collective-permute-start | bytes 2457608 | tf_op jit(solution)/shard_map/ppermute | solution.py:355
  229.2 39.1 %collective-permute-start.41 = (bf16[4,160,640]{2,1,0:T(8,128)(2,1)}, bf16[4,160,640]{2,1,0:T(8,128)(2,1)}, u32[]{:S(2)}, u32[]{:S(2)}) collective-permute-start(bf16[4,160,640]{2,1,0:T(8,128)(2,1)} %get-tuple-element.64), channel_id=1, source_target_pairs={{0,64},{32,96},{64,0},{96,32},{1,65},{33,97},{65,1},{97,33},{2,66}... | collective-permute-start | bytes 2457608 | tf_op jit(solution)/shard_map/ppermute | solution.py:355
  234.2 40.2 %collective-permute-start.37 = (bf16[4,160,640]{2,1,0:T(8,128)(2,1)}, bf16[4,160,640]{2,1,0:T(8,128)(2,1)}, u32[]{:S(2)}, u32[]{:S(2)}) collective-permute-start(bf16[4,160,640]{2,1,0:T(8,128)(2,1)} %get-tuple-element.63), channel_id=1, source_target_pairs={{0,24},{8,0},{16,8},{24,16},{1,25},{9,1},{17,9},{25,17},{2,26},{10... | collective-permute-start | bytes 2457608 | tf_op jit(solution)/shard_map/ppermute | solution.py:355
  236.9 39.7 %collective-permute-start.36 = (bf16[4,160,640]{2,1,0:T(8,128)(2,1)}, bf16[4,160,640]{2,1,0:T(8,128)(2,1)}, u32[]{:S(2)}, u32[]{:S(2)}) collective-permute-start(bf16[4,160,640]{2,1,0:T(8,128)(2,1)} %get-tuple-element.62), channel_id=1, source_target_pairs={{0,8},{8,16},{16,24},{24,0},{1,9},{9,17},{17,25},{25,1},{2,10},{10... | collective-permute-start | bytes 2457608 | tf_op jit(solution)/shard_map/ppermute | solution.py:355
  264.9 23.0 %collective-permute-start.35 = (bf16[4,160,640]{2,1,0:T(8,128)(2,1)}, bf16[4,160,640]{2,1,0:T(8,128)(2,1)}, u32[]{:S(2)}, u32[]{:S(2)}) collective-permute-start(bf16[4,160,640]{2,1,0:T(8,128)(2,1)} %get-tuple-element.61), channel_id=1, source_target_pairs={{0,16},{8,24},{16,0},{24,8},{1,17},{9,25},{17,1},{25,9},{2,18},{10... | collective-permute-start | bytes 2457608 | tf_op jit(solution)/shard_map/ppermute | solution.py:355
  271.6 23.5 %collective-permute-start.46 = (bf16[160,640]{1,0:T(8,128)(2,1)S(1)}, bf16[160,640]{1,0:T(8,128)(2,1)}, u32[]{:S(2)}, u32[]{:S(2)}) collective-permute-start(bf16[160,640]{1,0:T(8,128)(2,1)S(1)} %get-tuple-element.73), channel_id=1, source_target_pairs={{0,24},{8,0},{16,8},{24,16},{1,25},{9,1},{17,9},{25,17},{2,26},{10... | collective-permute-start | bytes 614408 | tf_op jit(solution)/shard_map/ppermute | solution.py:355
  274.3 22.2 %collective-permute-start.45 = (bf16[160,640]{1,0:T(8,128)(2,1)}, bf16[160,640]{1,0:T(8,128)(2,1)S(1)}, u32[]{:S(2)}, u32[]{:S(2)}) collective-permute-start(bf16[160,640]{1,0:T(8,128)(2,1)} %get-tuple-element.74), channel_id=1, source_target_pairs={{0,8},{8,16},{16,24},{24,0},{1,9},{9,17},{17,25},{25,1},{2,10},{10... | collective-permute-start | bytes 614408 | tf_op jit(solution)/shard_map/ppermute | solution.py:355
  274.3 22.2 %collective-permute-start.44 = (bf16[160,640]{1,0:T(8,128)(2,1)}, bf16[160,640]{1,0:T(8,128)(2,1)}, u32[]{:S(2)}, u32[]{:S(2)}) collective-permute-start(bf16[160,640]{1,0:T(8,128)(2,1)} %get-tuple-element.72), channel_id=1, source_target_pairs={{0,16},{8,24},{16,0},{24,8},{1,17},{9,25},{17,1},{25,9},{2,18},{10... | collective-permute-start | bytes 614408 | tf_op jit(solution)/shard_map/ppermute | solution.py:355
  361.6 23.3 %collective-permute-start.23 = (bf16[256,640]{1,0:T(8,128)(2,1)S(1)}, bf16[256,640]{1,0:T(8,128)(2,1)S(1)}, u32[]{:S(2)}, u32[]{:S(2)}) collective-permute-start(bf16[256,640]{1,0:T(8,128)(2,1)S(1)} %get-tuple-element.43), channel_id=1, source_target_pairs={{0,0},{4,1},{1,2},{5,3},{2,4},{6,5},{3,6},{7,7},{8,8},{12,9},{9,10... | collective-permute-start | bytes 983048 | tf_op jit(solution)/shard_map/ppermute | solution.py:346
  363.5 21.7 %collective-permute-start.24 = (bf16[256,640]{1,0:T(8,128)(2,1)S(1)}, bf16[256,640]{1,0:T(8,128)(2,1)S(1)}, u32[]{:S(2)}, u32[]{:S(2)}) collective-permute-start(bf16[256,640]{1,0:T(8,128)(2,1)S(1)} %get-tuple-element.44), channel_id=1, source_target_pairs={{4,0},{0,1},{5,2},{1,3},{6,4},{2,5},{7,6},{3,7},{12,8},{8,9},{13,1... | collective-permute-start | bytes 983048 | tf_op jit(solution)/shard_map/ppermute | solution.py:346
  368.8 16.7 %collective-permute-start.25 = (bf16[256,640]{1,0:T(8,128)(2,1)S(1)}, bf16[256,640]{1,0:T(8,128)(2,1)S(1)}, u32[]{:S(2)}, u32[]{:S(2)}) collective-permute-start(bf16[256,640]{1,0:T(8,128)(2,1)S(1)} %get-tuple-element.45), channel_id=1, source_target_pairs={{1,0},{5,1},{0,2},{4,3},{3,4},{7,5},{2,6},{6,7},{9,8},{13,9},{8,10... | collective-permute-start | bytes 983048 | tf_op jit(solution)/shard_map/ppermute | solution.py:346
  370.2 20.5 %collective-permute-start.26 = (bf16[256,640]{1,0:T(8,128)(2,1)S(1)}, bf16[256,640]{1,0:T(8,128)(2,1)S(1)}, u32[]{:S(2)}, u32[]{:S(2)}) collective-permute-start(bf16[256,640]{1,0:T(8,128)(2,1)S(1)} %get-tuple-element.46), channel_id=1, source_target_pairs={{5,0},{1,1},{4,2},{0,3},{7,4},{3,5},{6,6},{2,7},{13,8},{9,9},{12,1... | collective-permute-start | bytes 983048 | tf_op jit(solution)/shard_map/ppermute | solution.py:346
  385.2 18.8 %collective-permute-start.29 = (bf16[256,640]{1,0:T(8,128)(2,1)S(1)}, bf16[256,640]{1,0:T(8,128)(2,1)S(1)}, u32[]{:S(2)}, u32[]{:S(2)}) collective-permute-start(bf16[256,640]{1,0:T(8,128)(2,1)S(1)} %get-tuple-element.49), channel_id=1, source_target_pairs={{1,0},{5,1},{0,2},{4,3},{3,4},{7,5},{2,6},{6,7},{9,8},{13,9},{8,10... | collective-permute-start | bytes 983048 | tf_op jit(solution)/shard_map/ppermute | solution.py:346
  385.5 26.2 %collective-permute-start.30 = (bf16[256,640]{1,0:T(8,128)(2,1)S(1)}, bf16[256,640]{1,0:T(8,128)(2,1)}, u32[]{:S(2)}, u32[]{:S(2)}) collective-permute-start(bf16[256,640]{1,0:T(8,128)(2,1)S(1)} %get-tuple-element.50), channel_id=1, source_target_pairs={{5,0},{1,1},{4,2},{0,3},{7,4},{3,5},{6,6},{2,7},{13,8},{9,9},{12,1... | collective-permute-start | bytes 983048 | tf_op jit(solution)/shard_map/ppermute | solution.py:346
  390.7 25.3 %collective-permute-start.31 = (bf16[256,640]{1,0:T(8,128)(2,1)S(1)}, bf16[256,640]{1,0:T(8,128)(2,1)}, u32[]{:S(2)}, u32[]{:S(2)}) collective-permute-start(bf16[256,640]{1,0:T(8,128)(2,1)S(1)} %get-tuple-element.51), channel_id=1, source_target_pairs={{0,0},{4,1},{1,2},{5,3},{2,4},{6,5},{3,6},{7,7},{8,8},{12,9},{9,10... | collective-permute-start | bytes 983048 | tf_op jit(solution)/shard_map/ppermute | solution.py:346
  395.5 20.6 %collective-permute-start.32 = (bf16[256,640]{1,0:T(8,128)(2,1)S(1)}, bf16[256,640]{1,0:T(8,128)(2,1)S(1)}, u32[]{:S(2)}, u32[]{:S(2)}) collective-permute-start(bf16[256,640]{1,0:T(8,128)(2,1)S(1)} %get-tuple-element.52), channel_id=1, source_target_pairs={{4,0},{0,1},{5,2},{1,3},{6,4},{2,5},{7,6},{3,7},{12,8},{8,9},{13,1... | collective-permute-start | bytes 983048 | tf_op jit(solution)/shard_map/ppermute | solution.py:346
  397.3 19.0 %collective-permute-start.33 = (bf16[256,640]{1,0:T(8,128)(2,1)S(1)}, bf16[256,640]{1,0:T(8,128)(2,1)S(1)}, u32[]{:S(2)}, u32[]{:S(2)}) collective-permute-start(bf16[256,640]{1,0:T(8,128)(2,1)S(1)} %get-tuple-element.53), channel_id=1, source_target_pairs={{1,0},{5,1},{0,2},{4,3},{3,4},{7,5},{2,6},{6,7},{9,8},{13,9},{8,10... | collective-permute-start | bytes 983048 | tf_op jit(solution)/shard_map/ppermute | solution.py:346
  (54 other events, 806.8 us)
Sparse Core Ops, SparseCore 0:
  16.5 67.9 all-gather.1

commit v3 on v2

v3 whole, which is shorter than its diff:
```python
import functools
import math

import jax
import jax.numpy as jnp
from jax import lax
from jax.experimental import pallas as pl
from jax.experimental.pallas import tpu as pltpu
from jax.sharding import Mesh, PartitionSpec as P

HEAD_DIM = 128


EPS = 1e-06
LOG2E = 1.4426950408889634
MIN_LIVE = 40
SEQ = 4
CORES = 2
GROUP = 4


def smem():
    return pl.BlockSpec(memory_space=pltpu.SMEM)


def params():
    return pltpu.CompilerParams(vmem_limit_bytes=48 << 20)


def contract(left, right, left_dim, right_dim):
    return lax.dot_general(
        left, right, (((left_dim,), (right_dim,)), ((), ())), preferred_element_type=jnp.float32
    )


def row_scale_of(values_f):
    return lax.rsqrt(jnp.mean(values_f * values_f, axis=-1, keepdims=True) + EPS)


def shard_of(place_ref, round_, width):
    return pl.ds(pl.multiple_of(jnp.bitwise_xor(place_ref[0], round_) * width, 128), width)


def rounds_kernel(place_ref, q_ref, k_ref, v_ref, gain_q_ref, gain_k_ref, *refs):
    outs, normed = refs[:-1], refs[-1]
    for at, (x_ref, gain_ref) in enumerate(((q_ref, gain_q_ref), (k_ref, gain_k_ref))):
        values_f = x_ref[...].astype(jnp.float32)
        normed[at] = (values_f * row_scale_of(values_f) * gain_ref[...]).astype(jnp.bfloat16)
    for round_, out in enumerate(outs):
        columns = shard_of(place_ref, round_, out.shape[2])
        out[0] = normed[0, :, columns]
        out[1] = normed[1, :, columns]
        out[2] = v_ref[:, columns]


def to_rounds(place, queries, keys, values, gain_q, gain_k, block=64):
    rows, width = queries.shape
    row_spec = pl.BlockSpec((block, width), lambda i: (i, 0))
    gain_spec = pl.BlockSpec((1, width), lambda i: (0, 0))
    return pl.pallas_call(
        rounds_kernel,
        grid=(rows // block,),
        in_specs=[smem()] + [row_spec] * 3 + [gain_spec] * 2,
        out_specs=[pl.BlockSpec((3, block, width // SEQ), lambda i: (0, i, 0))] * SEQ,
        out_shape=[jax.ShapeDtypeStruct((3, rows, width // SEQ), jnp.bfloat16)] * SEQ,
        scratch_shapes=[pltpu.VMEM((2, block, width), jnp.bfloat16)],
        name="norm_rows",
    )(place, queries, keys, values, gain_q.reshape(1, width), gain_k.reshape(1, width))


def finish_kernel(place_ref, q_ref, k_ref, gain_q_ref, gain_k_ref, *refs):
    parts, outs, joined = refs[:SEQ], refs[SEQ:-1], refs[-1]
    width = q_ref.shape[1]
    for round_, part in enumerate(parts):
        columns = shard_of(place_ref, round_, part.shape[2])
        joined[0, :, columns] = part[0]
        joined[1, :, columns] = part[1]
        outs[2][:, columns] = part[2]
    for at, (x_ref, gain_ref) in enumerate(((q_ref, gain_q_ref), (k_ref, gain_k_ref))):
        values_f = x_ref[...].astype(jnp.float32)
        row_scale = row_scale_of(values_f)
        gated = gain_ref[...] * joined[at].astype(jnp.float32)
        inner = jnp.sum(gated * values_f, axis=-1, keepdims=True)
        back = values_f * (row_scale * row_scale * row_scale * inner * (1.0 / width))
        outs[at][...] = (row_scale * gated - back).astype(jnp.bfloat16)


def finish(place, queries, keys, gain_q, gain_k, parts, block=64):
    rows, width = queries.shape
    row_spec = pl.BlockSpec((block, width), lambda i: (i, 0))
    gain_spec = pl.BlockSpec((1, width), lambda i: (0, 0))
    return pl.pallas_call(
        finish_kernel,
        grid=(rows // block,),
        in_specs=[smem()]
        + [row_spec] * 2
        + [gain_spec] * 2
        + [pl.BlockSpec((3, block, width // SEQ), lambda i: (0, i, 0))] * SEQ,
        out_specs=[row_spec] * 3,
        out_shape=[jax.ShapeDtypeStruct((rows, width), jnp.bfloat16)] * 3,
        scratch_shapes=[pltpu.VMEM((2, block, width), jnp.bfloat16)],
        name="norm_back",
    )(place, queries, keys, gain_q.reshape(1, width), gain_k.reshape(1, width), *parts)


def tile_at(ref, index, rows):
    return ref[pl.ds(pl.multiple_of(index * rows, rows), rows), :]


def gather_pair(ref, near, rows):
    return jnp.concatenate(
        [
            jnp.concatenate([tile_at(ref, one, rows), tile_at(ref, two, rows)], axis=1)
            for one, two in zip(*near)
        ],
        axis=0,
    )


def spread(block, rows):
    twice = jnp.concatenate([block, block], axis=1)
    width = block.shape[1]
    own = (lax.broadcasted_iota(jnp.int32, twice.shape, 0) < rows) == (
        lax.broadcasted_iota(jnp.int32, twice.shape, 1) < width
    )
    return jnp.where(own, twice, jnp.zeros_like(twice))


def near_of(place_ref, pairs_ref, pair):
    flip = place_ref[3]
    return [
        [
            jnp.bitwise_xor(pairs_ref[jnp.bitwise_xor(2 * pair + half, flip), n], flip)
            for n in range(pairs_ref.shape[1])
        ]
        for half in range(2)
    ]


def load_parts(parts, whole):
    for at, part in enumerate(parts):
        whole[at * part.shape[0] : (at + 1) * part.shape[0], :] = part[...]


def diagonal(product, half, tile_rows, width):
    return product[half * tile_rows : (half + 1) * tile_rows, half * width : (half + 1) * width]


def forward_kernel(place_ref, pairs_ref, lens_ref, *refs):
    q_parts, k_parts, v_parts = refs[:SEQ], refs[SEQ : 2 * SEQ], refs[2 * SEQ : 3 * SEQ]
    att_ref, probs_ref, q_all, k_all, v_all = refs[3 * SEQ :]
    tile_count, neighbours = pairs_ref.shape
    clip_rows, width = q_all.shape
    tile_rows = clip_rows // tile_count
    rows = 2 * tile_rows
    depth = neighbours * tile_rows
    scale = LOG2E / math.sqrt(width)
    load_parts(q_parts, q_all)
    load_parts(k_parts, k_all)
    load_parts(v_parts, v_all)
    shape = (tile_rows - MIN_LIVE, rows)
    first = lax.broadcasted_iota(jnp.int32, shape, 1) < tile_rows
    slot = lax.broadcasted_iota(jnp.int32, shape, 0) + MIN_LIVE

    def length(tile):
        return lens_ref[0, jnp.bitwise_xor(tile, place_ref[3])]

    def score(pair, near):
        keys = gather_pair(k_all, near, tile_rows)
        queries = spread(q_all[pl.ds(pl.multiple_of(pair * rows, rows), rows), :], tile_rows)
        scores = contract(keys, queries, 1, 1)
        pieces = []
        for n in range(neighbours):
            start = n * tile_rows
            pieces.append(scores[start : start + MIN_LIVE])
            live = slot < jnp.where(first, length(near[0][n]), length(near[1][n]))
            pieces.append(jnp.where(live, scores[start + MIN_LIVE : start + tile_rows], -jnp.inf))
        return jnp.concatenate(pieces, axis=0)

    def soften(scores):
        weights = jnp.exp2((scores - jnp.max(scores, axis=0, keepdims=True)) * scale)
        return (weights * (1.0 / jnp.sum(weights, axis=0, keepdims=True))).astype(jnp.bfloat16)

    def body(group, carry):
        pairs = [group * GROUP + at for at in range(GROUP)]
        nears = [near_of(place_ref, pairs_ref, pair) for pair in pairs]
        probs = [soften(score(pair, near)) for pair, near in zip(pairs, nears)]
        attended = [
            contract(prob, gather_pair(v_all, near, tile_rows), 0, 0) for prob, near in zip(probs, nears)
        ]
        for pair, prob, product in zip(pairs, probs, attended):
            probs_ref[0, pl.ds(pl.multiple_of(pair * depth, depth), depth), :] = prob
            for half in range(2):
                place = pl.ds(pl.multiple_of((2 * pair + half) * tile_rows, tile_rows), tile_rows)
                att_ref[place, :] = diagonal(product, half, tile_rows, width).astype(jnp.bfloat16)
        return carry

    lax.fori_loop(0, tile_count // 2 // GROUP, body, 0)


def pack_specs(rows):
    return [pl.BlockSpec((None, rows, HEAD_DIM), lambda h, which=which: (which, 0, h)) for which in range(3)]


def forward(place, tile_pairs, lens, packs):
    _, rows, local_width = packs[0].shape
    heads = local_width // HEAD_DIM
    clip_rows = rows * SEQ
    pairs = tile_pairs.shape[0] // 2
    depth = tile_pairs.shape[1] * (clip_rows // tile_pairs.shape[0])
    return pl.pallas_call(
        forward_kernel,
        grid=(heads,),
        in_specs=[smem()] * 3 + [spec for spec in pack_specs(rows) for _ in packs],
        out_specs=[
            pl.BlockSpec((clip_rows, HEAD_DIM), lambda h: (0, h)),
            pl.BlockSpec((1, pairs * depth, HEAD_DIM), lambda h: (h, 0, 0)),
        ],
        out_shape=[
            jax.ShapeDtypeStruct((clip_rows, local_width), jnp.bfloat16),
            jax.ShapeDtypeStruct((heads, pairs * depth, HEAD_DIM), jnp.bfloat16),
        ],
        scratch_shapes=[pltpu.VMEM((clip_rows, HEAD_DIM), jnp.bfloat16)] * 3,
        compiler_params=params(),
        name="attention_forward",
    )(place, tile_pairs, lens, *packs, *packs, *packs)


def backward_kernel(place_ref, pairs_ref, *refs):
    q_parts, k_parts, v_parts = refs[:SEQ], refs[SEQ : 2 * SEQ], refs[2 * SEQ : 3 * SEQ]
    own_grads, other_grads = refs[3 * SEQ : 4 * SEQ], refs[4 * SEQ : 5 * SEQ]
    probs_ref = refs[5 * SEQ]
    outs = refs[5 * SEQ + 1 : 6 * SEQ + 1]
    q_all, k_all, v_all, g_all, gq_all, gk_acc, gv_acc = refs[6 * SEQ + 1 :]
    tile_count, neighbours = pairs_ref.shape
    clip_rows, width = q_all.shape
    tile_rows = clip_rows // tile_count
    rows = 2 * tile_rows
    depth = neighbours * tile_rows
    factor = 1.0 / math.sqrt(width)
    load_parts(q_parts, q_all)
    load_parts(k_parts, k_all)
    load_parts(v_parts, v_all)
    half_rows = own_grads[0].shape[0]
    core = place_ref[1]
    for at in range(SEQ):
        for grads, half in ((own_grads[at], core), (other_grads[at ^ 1], 1 - core)):
            g_all[pl.ds(pl.multiple_of((2 * at + half) * half_rows, half_rows), half_rows), :] = grads[...]
    gk_acc[...] = jnp.zeros_like(gk_acc)
    gv_acc[...] = jnp.zeros_like(gv_acc)

    def rows_of(pair):
        return pl.ds(pl.multiple_of(pair * rows, rows), rows)

    def body(group, carry):
        pairs = [group * GROUP + at for at in range(GROUP)]
        nears = [near_of(place_ref, pairs_ref, pair) for pair in pairs]
        probs = [
            probs_ref[0, pl.ds(pl.multiple_of(pair * depth, depth), depth), :] for pair in pairs
        ]
        grads = [spread(g_all[rows_of(pair), :], tile_rows) for pair in pairs]
        grad_scores = []
        for prob, grad, near in zip(probs, grads, nears):
            grad_prob = contract(gather_pair(v_all, near, tile_rows), grad, 1, 1)
            wide = prob.astype(jnp.float32)
            delta = jnp.sum(wide * grad_prob, axis=0, keepdims=True)
            grad_scores.append((wide * (grad_prob - delta)).astype(jnp.bfloat16))
        grad_queries = [
            contract(grad_score, gather_pair(k_all, near, tile_rows), 0, 0) * factor
            for grad_score, near in zip(grad_scores, nears)
        ]
        grad_keys = [
            contract(grad_score, spread(q_all[rows_of(pair), :], tile_rows), 1, 0)
            for grad_score, pair in zip(grad_scores, pairs)
        ]
        grad_vals = [contract(prob, grad, 1, 0) for prob, grad in zip(probs, grads)]
        for pair, near, grad_query, grad_key, grad_val in zip(
            pairs, nears, grad_queries, grad_keys, grad_vals
        ):
            for half in range(2):
                place = pl.ds(pl.multiple_of((2 * pair + half) * tile_rows, tile_rows), tile_rows)
                gq_all[place, :] = diagonal(grad_query, half, tile_rows, width).astype(jnp.bfloat16)
                for n in range(neighbours):
                    at = (slice(n * tile_rows, (n + 1) * tile_rows), slice(half * width, (half + 1) * width))
                    place = pl.ds(pl.multiple_of(near[half][n] * tile_rows, tile_rows), tile_rows)
                    gk_acc[place, :] += grad_key[at]
                    gv_acc[place, :] += grad_val[at]
        return carry

    lax.fori_loop(0, tile_count // 2 // GROUP, body, 0)
    for at, out in enumerate(outs):
        part = slice(at * out.shape[1], (at + 1) * out.shape[1])
        out[0] = gq_all[part, :]
        out[1] = (gk_acc[part, :] * factor).astype(jnp.bfloat16)
        out[2] = gv_acc[part, :].astype(jnp.bfloat16)


def backward(place, tile_pairs, packs, own_grads, other_grads, probs):
    _, rows, local_width = packs[0].shape
    heads = local_width // HEAD_DIM
    clip_rows = rows * SEQ
    grad_spec = pl.BlockSpec((own_grads[0].shape[0], HEAD_DIM), lambda h: (0, h))
    bf16_rows = pltpu.VMEM((clip_rows, HEAD_DIM), jnp.bfloat16)
    f32_rows = pltpu.VMEM((clip_rows, HEAD_DIM), jnp.float32)
    return pl.pallas_call(
        backward_kernel,
        grid=(heads,),
        in_specs=[smem()] * 2
        + [spec for spec in pack_specs(rows) for _ in packs]
        + [grad_spec] * (2 * SEQ)
        + [pl.BlockSpec((1,) + probs.shape[1:], lambda h: (h, 0, 0))],
        out_specs=[pl.BlockSpec((3, rows, HEAD_DIM), lambda h: (0, 0, h))] * SEQ,
        out_shape=[jax.ShapeDtypeStruct((3, rows, local_width), jnp.bfloat16)] * SEQ,
        scratch_shapes=[bf16_rows] * 5 + [f32_rows] * 2,
        compiler_params=params(),
        name="attention_backward",
    )(place, tile_pairs, *packs, *packs, *packs, *own_grads, *other_grads, probs)


def weight_grad_kernel(place_ref, mean, att_ref, *refs):
    own, other, outs = refs[:SEQ], refs[SEQ : 2 * SEQ], refs[2 * SEQ :]
    half_rows = own[0].shape[0]
    core = place_ref[1]
    columns, attended = [], []
    for at in range(SEQ):
        for part, half in ((own[at], core), (other[at ^ 1], 1 - core)):
            columns.append(part[...])
            start = pl.multiple_of((2 * at + half) * half_rows, half_rows)
            attended.append(att_ref[pl.ds(start, half_rows), :])
    total = contract(jnp.concatenate(columns, axis=0), jnp.concatenate(attended, axis=0), 0, 0)
    total = (total * mean).astype(jnp.bfloat16)
    count, piece = outs[0].shape[:2]
    for at in range(count):
        for holder, out in enumerate(outs):
            start = (2 * at + holder) * piece
            out[at] = total[start : start + piece]


def weight_grad(place, attended, own, other, mean, owners, block=640):
    half_rows, features = own[0].shape
    local_width = attended.shape[1]
    piece = features // owners // CORES
    return pl.pallas_call(
        lambda place_ref, *refs: weight_grad_kernel(place_ref, mean, *refs),
        grid=(features // block,),
        in_specs=[smem(), pl.BlockSpec(attended.shape, lambda i: (0, 0))]
        + [pl.BlockSpec((half_rows, block), lambda i: (0, i))] * (2 * SEQ),
        out_specs=[pl.BlockSpec((block // piece // 2, piece, local_width), lambda i: (i, 0, 0))] * CORES,
        out_shape=[jax.ShapeDtypeStruct((owners, piece, local_width), jnp.bfloat16)] * CORES,
        compiler_params=params(),
        name="weight_grad",
    )(place, attended, *own, *other)


def device_of(core, seq):
    return core * SEQ + seq


def outward(round_):
    pairs = []
    for core in range(CORES):
        for token in range(SEQ):
            shard = token ^ round_
            pairs.append((device_of(core, token), device_of(shard % 2, 2 * core + shard // 2)))
    return pairs


def inward(round_):
    return [(target, source) for source, target in outward(round_)]


def send(value, pairs):
    return lax.ppermute(value, ("core", "seq"), pairs)


def swap_cores(value):
    return lax.ppermute(value, "core", [(0, 1), (1, 0)])


def shift(value, axis, by):
    count = lax.axis_size(axis)
    return lax.ppermute(value, axis, [(i, (i + by) % count) for i in range(count)])


def add(*terms):
    total = terms[0].astype(jnp.float32)
    for term in terms[1:]:
        total = total + term.astype(jnp.float32)
    return total.astype(jnp.bfloat16)


def take(value, index, axis=0):
    return lax.dynamic_index_in_dim(value, index, axis, keepdims=False)


def scatter(value, axis, dim=0):
    here = lax.axis_index(axis)
    count = lax.axis_size(axis)
    got = [shift(take(value, (here + by) % count, dim), axis, by) for by in (2, 1, 3)]
    return [take(value, here, dim)] + got


def to_shard_holders(w_out, core, seq):
    got = []
    for other in range(2):
        pairs = []
        for holder in range(CORES):
            for shard in range(SEQ):
                window = holder ^ other
                pairs.append((device_of(holder, shard), device_of(shard % 2, shard // 2 + 2 * window)))
        got.append(send(w_out, pairs))
    window = seq // 2
    return jnp.where(window == 0, jnp.concatenate(got), jnp.concatenate(got[::-1]))


def to_owners(totals, seq):
    window = seq // 2
    got = []
    for other in range(2):
        pairs = []
        for core in range(CORES):
            for at in range(SEQ):
                holder = (at // 2) ^ other
                pairs.append((device_of(core, at), device_of(holder, 2 * (at % 2) + core)))
        got.append(send(jnp.where((window ^ other) == 0, totals[0], totals[1]), pairs))
    return got[0].astype(jnp.float32) + got[1].astype(jnp.float32)


def after(values, *tokens):
    return lax.optimization_barrier((values, tokens))[0]


def per_device(queries, keys, values, gain_q, gain_k, tile_pairs, tile_lens, out_grad, w_out):
    core = lax.axis_index("core")
    seq = lax.axis_index("seq")
    count_z = lax.axis_size("z")
    count_x = lax.axis_size("x")
    rows, features = out_grad.shape
    shard = 2 * (seq % 2) + core
    tiles_per_block = tile_pairs.shape[0] // SEQ
    place = jnp.stack([seq, core, shard, shard * tiles_per_block]).astype(jnp.int32)
    lens = jnp.where(seq // 2 == core, tile_lens, swap_cores(tile_lens))

    def half_rows(rows_in, round_):
        half = seq % 2 if round_ % 2 == 0 else 1 - seq % 2
        return take(rows_in.reshape(2, rows // 2, features), half)

    own = [send(half_rows(out_grad, 0), outward(0))]
    packs = to_rounds(place, queries, keys, values, gain_q, gain_k)
    packs = [send(part, outward(r)) for r, part in enumerate(packs)]
    ready = (packs[0], packs[1], packs[2:])
    own += [send(half_rows(after(out_grad, ready[r - 1]), r), outward(r)) for r in range(1, SEQ)]
    other = [swap_cores(part) for part in own]
    w_all = lax.all_gather(to_shard_holders(w_out, core, seq), ("z", "x"), axis=0, tiled=True)

    def project(part):
        return jnp.dot(part, w_all, preferred_element_type=jnp.float32).astype(jnp.bfloat16)

    attended, probs = forward(place, tile_pairs, lens, packs)
    own_grads = [project(part) for part in own]
    other_grads = [project(part) for part in other]
    attended = after(attended, own_grads[:-1], other_grads[:-1])
    one, two = weight_grad(
        place, attended, own, other, 1.0 / (count_z * count_x * CORES), count_z * count_x
    )
    two = lax.psum_scatter(two, ("z", "x"), scatter_dimension=0, tiled=True)[0]
    one = scatter(one.reshape((count_z, count_x) + one.shape[1:]), "x", 1)
    parts = backward(place, tile_pairs, packs, own_grads, other_grads, after(probs, one[0]))
    token = parts[0]
    parts = [send(part, inward(r)) for r, part in enumerate(parts)]
    one = add(*after(one, token))
    one = add(*scatter(after(one, parts[0], parts[1]), "z"))
    grad_w = to_owners((one, two), seq)
    grad_q, grad_k, grad_v = finish(place, queries, keys, gain_q, gain_k, parts)
    return (grad_q, grad_k, grad_v, grad_w)


def solution(mesh):
    dp = mesh.shape["dp"]
    side = math.isqrt(dp // CORES)
    parts = Mesh(mesh.devices.reshape(side, side, CORES, SEQ), ("z", "x", "core", "seq"))
    dp_axes = ("z", "x", "core")
    tokens = P(dp_axes + ("seq",), None)
    return jax.shard_map(
        per_device,
        mesh=parts,
        in_specs=(tokens, tokens, tokens, P(), P(), P(), P(dp_axes, None), tokens, P(dp_axes, "seq")),
        out_specs=(tokens, tokens, tokens, P(dp_axes, "seq")),
        check_vma=False,
    )
```

time: 434 us -> 286 us (0.66)
  starting transfers between devices: 107 us -> 56.2 us
  waiting for transfers between devices: 153 us -> 113 us
  Pallas kernels: 94.5 us -> 55.9 us
  local copies, waits for them, and re-layouts: 29 us -> 11.6 us
    ppermute x32 -> x16, starting transfers between devices: 83.5 us -> 40.3 us  [send(): return lax.ppermute(value, ('core', 'seq'), pairs)]
    pallas_call x8 -> x4, Pallas kernels: 81.2 us -> 42.5 us  [the longest x1 19.3 us: backward(): pl.pallas_call(backward_kernel, grid=(heads,), in_specs=[smem()] * 2 + [s...]
    ppermute x12 -> x6, waiting for transfers between devices: 47.7 us -> 14.8 us  [shift(): lax.ppermute(value, axis, [(i, (i + by) % count) for i in range(count)])]
    ppermute x32 -> x16, waiting for transfers between devices: 106 us -> 83.9 us  [send(): return lax.ppermute(value, ('core', 'seq'), pairs)]
    unnamed x1 -> x3, waiting for transfers between devices: 0.02 us -> 13.2 us
    unnamed x73 -> x23, local copies, waits for them, and re-layouts: 13.5 us -> 1.57 us
    ppermute x12 -> x6, starting transfers between devices: 21.9 us -> 12.3 us  [shift(): lax.ppermute(value, axis, [(i, (i + by) % count) for i in range(count)])]
    slice x1 -> x0, local copies, waits for them, and re-layouts: 5.21 us -> none  [per_device(): one = scatter_sum(scatter_sum(grad_w[:, :, 0], 'x', 1), 'z')]
  transfers between devices with their start and end apart: 50 -> 29, of which waited for: 22 -> 16; matrix products, arithmetic and copies ran while one was open for 6% -> 14% of each run, Pallas kernels for 14% -> 15%
where the time goes in v3:
time: 286 us; the launch traced here: 281 us
  waiting for transfers between devices  113 us (40%)
  starting transfers between devices  56.2 us (20%)
  Pallas kernels  55.9 us (20%)
  matrix products  24.7 us (9%)
  between operations  14.4 us (5%)
  local copies, waits for them, and re-layouts  11.6 us (4%)
  other arithmetic  5.48 us (2%)
    ppermute x16, waiting for transfers between devices, send(): return lax.ppermute(value, ('core', 'seq'), pairs)  83.9 us
    ppermute x16, starting transfers between devices, send(): return lax.ppermute(value, ('core', 'seq'), pairs)  40.3 us
    dot_general x8, matrix products, project(): jnp.dot(part, w_all, preferred_element_type=jnp.float32)  24.7 us
    pallas_call x1, Pallas kernels, backward(): pl.pallas_call(backward_kernel, grid=(heads,), in_specs=[smem()] * 2 + [s...  19.3 us
    ppermute x6, waiting for transfers between devices, shift(): lax.ppermute(value, axis, [(i, (i + by) % count) for i in range(count)])  14.8 us
    pallas_call x1, Pallas kernels, weight_grad(): pl.pallas_call(lambda place_ref, *refs: weight_grad_kernel(place_ref, mea...  13.4 us
    unnamed x3, waiting for transfers between devices  13.2 us
    ppermute x6, starting transfers between devices, shift(): lax.ppermute(value, axis, [(i, (i + by) % count) for i in range(count)])  12.3 us
  transfers between devices with their start and end apart: 29, of which 16 were waited for; matrix products, arithmetic and copies ran while one was open for 14% of the time, Pallas kernels for 15%

profile of v3, /device:TPU:24, one launch (start us, length us, event | category | flops | bytes accessed | tf_op | source)
XLA Modules:
  0.0 281.2 jit_solution(2492730199219635361)
XLA Ops:
  7.3 2.7 collective-permute-start.5
  10.1 3.9 %collective-permute-done.6 = bf16[160,640]{1,0:T(8,128)(2,1)S(1)} collective-permute-done((bf16[160,640]{1,0:T(8,128)(2,1)}, bf16[160,640]{1,0:T(8,128)(2,1)S(1)}, u32[]{:S(2)}, u32[]{:S(2)}) %collective-permute-start.6) | collective-permute-done | bytes 204832 | tf_op jit(solution)/shard_map/ppermute | solution.py:373
  18.9 5.3 %norm_rows.1 = (bf16[3,256,640]{2,1,0:T(8,128)(2,1)}, bf16[3,256,640]{2,1,0:T(8,128)(2,1)}, bf16[3,256,640]{2,1,0:T(8,128)(2,1)}, bf16[3,256,640]{2,1,0:T(8,128)(2,1)}) custom-call(s32[4]{0:T(128)} %pad_add_fusion.place_ref, bf16[256,2560]{1,0:T(8,128)(2,1)} %q_ref.3, bf16[256,2560]{1,0:T(8,128)(2,1)} %k_ref.3, bf16[256,2560]{1,0:T(8,128)(2,1)} %v_ref.1, ...), custom_call_target="tpu_custom_call" | custom-call | tf_op jit(solution)/shard_map/norm_rows/pallas_call | solution.py:60
  24.2 5.9 %collective-permute-start = (bf16[3,256,640]{2,1,0:T(8,128)(2,1)}, bf16[3,256,640]{2,1,0:T(8,128)(2,1)}, u32[]{:S(2)}, u32[]{:S(2)}) collective-permute-start(bf16[3,256,640]{2,1,0:T(8,128)(2,1)} %get-tuple-element.29), channel_id=1, source_target_pairs={{0,0},{1,4},{2,1},{3,5},{4,2},{5,6},{6,3},{7,7},{8,8},{9,12},{10,9... | collective-permute-start | bytes 2949128 | tf_op jit(solution)/shard_map/ppermute | solution.py:373
  32.6 3.3 %collective-permute-start.3 = (bf16[3,256,640]{2,1,0:T(8,128)(2,1)}, bf16[3,256,640]{2,1,0:T(8,128)(2,1)}, u32[]{:S(2)}, u32[]{:S(2)}) collective-permute-start(bf16[3,256,640]{2,1,0:T(8,128)(2,1)} %get-tuple-element.32), channel_id=1, source_target_pairs={{0,5},{1,1},{2,4},{3,0},{4,7},{5,3},{6,6},{7,2},{8,13},{9,9},{10,1... | collective-permute-start | bytes 2949128 | tf_op jit(solution)/shard_map/ppermute | solution.py:373
  37.1 3.7 %collective-permute-start.4 = (bf16[128,5120]{1,0:T(8,128)(2,1)}, bf16[128,5120]{1,0:T(8,128)(2,1)}, u32[]{:S(2)}, u32[]{:S(2)}) collective-permute-start(bf16[128,5120]{1,0:T(8,128)(2,1)} %dynamic-slice_bitcast_fusion.3), channel_id=1, source_target_pairs={{0,0},{1,4},{2,1},{3,5},{4,2},{5,6},{6,3},{7,7},{8,8},{9,12},{10,9... | collective-permute-start | bytes 3932168 | tf_op jit(solution)/shard_map/ppermute | solution.py:373
  40.9 11.7 %collective-permute-done.refs_0_.refs_4_.refs_8_ = bf16[3,256,640]{2,1,0:T(8,128)(2,1)} collective-permute-done((bf16[3,256,640]{2,1,0:T(8,128)(2,1)}, bf16[3,256,640]{2,1,0:T(8,128)(2,1)}, u32[]{:S(2)}, u32[]{:S(2)}) %collective-permute-start) | collective-permute-done | bytes 983072 | tf_op jit(solution)/shard_map/ppermute | solution.py:373
  53.7 3.1 %collective-permute-start.7 = (bf16[128,5120]{1,0:T(8,128)(2,1)}, bf16[128,5120]{1,0:T(8,128)(2,1)}, u32[]{:S(2)}, u32[]{:S(2)}) collective-permute-start(bf16[128,5120]{1,0:T(8,128)(2,1)} %dynamic-slice_bitcast_fusion.2), channel_id=1, source_target_pairs={{0,4},{1,0},{2,5},{3,1},{4,6},{5,2},{6,7},{7,3},{8,12},{9,8},{10,1... | collective-permute-start | bytes 3932168 | tf_op jit(solution)/shard_map/ppermute | solution.py:373
  56.8 16.7 %collective-permute-done.1.refs_1_.refs_5_.refs_9_ = bf16[3,256,640]{2,1,0:T(8,128)(2,1)} collective-permute-done((bf16[3,256,640]{2,1,0:T(8,128)(2,1)}, bf16[3,256,640]{2,1,0:T(8,128)(2,1)}, u32[]{:S(2)}, u32[]{:S(2)}) %collective-permute-start.1) | collective-permute-done | bytes 983072 | tf_op jit(solution)/shard_map/ppermute | solution.py:373
  74.7 2.6 collective-permute-done.3.refs_3_.refs_7_.refs_11_
  78.5 4.3 %collective-permute-start.9 = (bf16[128,5120]{1,0:T(8,128)(2,1)}, bf16[128,5120]{1,0:T(8,128)(2,1)}, u32[]{:S(2)}, u32[]{:S(2)}) collective-permute-start(bf16[128,5120]{1,0:T(8,128)(2,1)} %dynamic-slice_bitcast_fusion), channel_id=1, source_target_pairs={{0,5},{1,1},{2,4},{3,0},{4,7},{5,3},{6,6},{7,2},{8,13},{9,9},{10,1... | collective-permute-start | bytes 3932168 | tf_op jit(solution)/shard_map/ppermute | solution.py:373
  84.0 11.7 %attention_forward.1 = (bf16[1024,640]{1,0:T(8,128)(2,1)S(1)}, bf16[5,4096,128]{2,1,0:T(8,128)(2,1)}) custom-call(s32[4]{0:T(128)S(1)} %copy-done.2, s32[16,8]{1,0:T(8,128)S(1)} %copy.20.pairs_ref, s32[1,16]{1,0:T(1,128)S(1)} %broadcast_select_fusion.lens_ref, bf16[3,256,640]{2,1,0:T(8,128)(2,1)} %collective-permute-done.refs_0_.refs_4_.refs_8_, ...), custom_call_target="tpu_custom_call" | custom-call | tf_op jit(solution)/shard_map/attention_forward/pallas_call | solution.py:211
  95.7 5.1 %collective-permute-done.4.refs_1_ = bf16[128,5120]{1,0:T(8,128)(2,1)} collective-permute-done((bf16[128,5120]{1,0:T(8,128)(2,1)}, bf16[128,5120]{1,0:T(8,128)(2,1)}, u32[]{:S(2)}, u32[]{:S(2)}) %collective-permute-start.4) | collective-permute-done | bytes 1310752 | tf_op jit(solution)/shard_map/ppermute | solution.py:373
  100.8 28.1 %collective-permute-done.7.refs_2_ = bf16[128,5120]{1,0:T(8,128)(2,1)} collective-permute-done((bf16[128,5120]{1,0:T(8,128)(2,1)}, bf16[128,5120]{1,0:T(8,128)(2,1)}, u32[]{:S(2)}, u32[]{:S(2)}) %collective-permute-start.7) | collective-permute-done | bytes 1310752 | tf_op jit(solution)/shard_map/ppermute | solution.py:373
  129.4 2.9 %collective-permute-done.9.refs_4_ = bf16[128,5120]{1,0:T(8,128)(2,1)} collective-permute-done((bf16[128,5120]{1,0:T(8,128)(2,1)}, bf16[128,5120]{1,0:T(8,128)(2,1)}, u32[]{:S(2)}, u32[]{:S(2)}) %collective-permute-start.9) | collective-permute-done | bytes 1310752 | tf_op jit(solution)/shard_map/ppermute | solution.py:373
  132.3 2.9 %collective-permute-start.13 = (bf16[128,5120]{1,0:T(8,128)(2,1)}, bf16[128,5120]{1,0:T(8,128)(2,1)}, u32[]{:S(2)}, u32[]{:S(2)}) collective-permute-start(bf16[128,5120]{1,0:T(8,128)(2,1)} %collective-permute-done.9.refs_4_), channel_id=1, source_target_pairs={{0,4},{4,0},{1,5},{5,1},{2,6},{6,2},{3,7},{7,3},{8,12},{12,8},{9,1... | collective-permute-start | bytes 3932168 | tf_op jit(solution)/shard_map/ppermute | solution.py:377
  135.2 4.6 %convolution_convert_fusion.7.refs_12_ = bf16[128,640]{1,0:T(8,128)(2,1)S(1)} fusion(bf16[128,5120]{1,0:T(8,128)(2,1)} %collective-permute-done.4.refs_1_, bf16[5120,640]{1,0:T(8,128)(2,1)} %all-gather.2.cloned.1.call-done), kind=kOutput, calls=%fused_computation.12 | convolution fusion | flops 838942720 | bytes 8028160 | tf_op jit(solution)/shard_map/dot_general | solution.py:457
  153.2 13.4 %weight_grad.1 = (bf16[16,160,640]{2,1,0:T(8,128)(2,1)}, bf16[16,160,640]{2,1,0:T(8,128)(2,1)}) custom-call(s32[4]{0:T(128)S(1)} %copy-done.2, bf16[1024,640]{1,0:T(8,128)(2,1)S(1)} %get-tuple-element.38.refs_0_, bf16[128,5120]{1,0:T(8,128)(2,1)} %collective-permute-done.4.refs_1_, bf16[128,5120]{1,0:T(8,128)(2,1)} %collective-permute-done.7.refs_2_, ...), custom_call_target="tpu_custom_call" | custom-call | tf_op jit(solution)/shard_map/weight_grad/pallas_call | solution.py:343
  166.7 3.4 %dynamic-slice_bitcast_fusion.4 = (bf16[4,160,640]{2,1,0:T(8,128)(2,1)}, bf16[4,160,640]{2,1,0:T(8,128)(2,1)}, bf16[4,160,640]{2,1,0:T(8,128)(2,1)}, bf16[4,160,640]{2,1,0:T(8,128)(2,1)S(1)}) fusion(bf16[4,4,160,640]{3,2,1,0:T(8,128)(2,1)} %bitcast.61, s32[]{:T(128)S(6)} %select_n.125, s32[]{:T(128)S(6)} %select_n.123, s32[]{:T(128)S(6)} %select_n.121, ...), kind=kLoop, calls=%fused_computation.13 | loop fusion | bytes 6553616 | tf_op jit(solution)/shard_map/jit(dynamic_index_in_dim)/squeeze | solution.py:393
  170.1 3.0 %collective-permute-start.19 = (bf16[4,160,640]{2,1,0:T(8,128)(2,1)}, bf16[4,160,640]{2,1,0:T(8,128)(2,1)}, u32[]{:S(2)}, u32[]{:S(2)}) collective-permute-start(bf16[4,160,640]{2,1,0:T(8,128)(2,1)} %get-tuple-element.58), channel_id=1, source_target_pairs={{0,16},{8,24},{16,0},{24,8},{1,17},{9,25},{17,1},{25,9},{2,18},{10... | collective-permute-start | bytes 2457608 | tf_op jit(solution)/shard_map/ppermute | solution.py:382
  173.7 2.7 collective-permute-start.21
  176.4 4.6 %convolution_convert_fusion.4.refs_15_ = bf16[128,640]{1,0:T(8,128)(2,1)S(1)} fusion(bf16[128,5120]{1,0:T(8,128)(2,1)} %collective-permute-done.9.refs_4_, bf16[5120,640]{1,0:T(8,128)(2,1)} %all-gather.2.cloned.1.call-done), kind=kOutput, calls=%fused_computation.9 | convolution fusion | flops 838942720 | bytes 8028160 | tf_op jit(solution)/shard_map/dot_general | solution.py:457
  181.1 2.6 convolution_convert_fusion.refs_19_
  183.7 19.3 %attention_backward.1 = (bf16[3,256,640]{2,1,0:T(8,128)(2,1)}, bf16[3,256,640]{2,1,0:T(8,128)(2,1)}, bf16[3,256,640]{2,1,0:T(8,128)(2,1)S(1)}, bf16[3,256,640]{2,1,0:T(8,128)(2,1)S(1)}) custom-call(s32[4]{0:T(128)S(1)} %copy-done.2, s32[16,8]{1,0:T(8,128)S(1)} %copy.20.pairs_ref, bf16[3,256,640]{2,1,0:T(8,128)(2,1)} %collective-permute-done.refs_0_.refs_4_.refs_8_, ...), custom_call_target="tpu_custom_call" | custom-call | tf_op jit(solution)/shard_map/attention_backward/pallas_call | solution.py:305
  205.8 6.1 %collective-permute-start.16 = (bf16[3,256,640]{2,1,0:T(8,128)(2,1)}, bf16[3,256,640]{2,1,0:T(8,128)(2,1)}, u32[]{:S(2)}, u32[]{:S(2)}) collective-permute-start(bf16[3,256,640]{2,1,0:T(8,128)(2,1)} %get-tuple-element.42), channel_id=1, source_target_pairs={{4,0},{0,1},{5,2},{1,3},{6,4},{2,5},{7,6},{3,7},{12,8},{8,9},{13,1... | collective-permute-start | bytes 2949128 | tf_op jit(solution)/shard_map/ppermute | solution.py:373
  213.6 3.5 %collective-permute-done.20 = bf16[4,160,640]{2,1,0:T(8,128)(2,1)} collective-permute-done((bf16[4,160,640]{2,1,0:T(8,128)(2,1)}, bf16[4,160,640]{2,1,0:T(8,128)(2,1)}, u32[]{:S(2)}, u32[]{:S(2)}) %collective-permute-start.20) | collective-permute-done | bytes 819232 | tf_op jit(solution)/shard_map/ppermute | solution.py:382
  221.1 10.0 %collective-permute-done.15.refs_0_ = bf16[3,256,640]{2,1,0:T(8,128)(2,1)} collective-permute-done((bf16[3,256,640]{2,1,0:T(8,128)(2,1)}, bf16[3,256,640]{2,1,0:T(8,128)(2,1)}, u32[]{:S(2)}, u32[]{:S(2)}) %collective-permute-start.15) | collective-permute-done | bytes 983072 | tf_op jit(solution)/shard_map/ppermute | solution.py:373
  232.4 4.0 %collective-permute-start.24 = (bf16[160,640]{1,0:T(8,128)(2,1)S(1)}, bf16[160,640]{1,0:T(8,128)(2,1)S(1)}, u32[]{:S(2)}, u32[]{:S(2)}) collective-permute-start(bf16[160,640]{1,0:T(8,128)(2,1)S(1)} %get-tuple-element.61), channel_id=1, source_target_pairs={{0,96},{32,0},{64,32},{96,64},{1,97},{33,1},{65,33},{97,65},{2,98}... | collective-permute-start | bytes 614408 | tf_op jit(solution)/shard_map/ppermute | solution.py:382
  238.4 2.9 %collective-permute-done.24 = bf16[160,640]{1,0:T(8,128)(2,1)S(1)} collective-permute-done((bf16[160,640]{1,0:T(8,128)(2,1)S(1)}, bf16[160,640]{1,0:T(8,128)(2,1)S(1)}, u32[]{:S(2)}, u32[]{:S(2)}) %collective-permute-start.24) | collective-permute-done | bytes 204832 | tf_op jit(solution)/shard_map/ppermute | solution.py:382
  241.3 8.4 %collective-permute-done.23 = bf16[160,640]{1,0:T(8,128)(2,1)S(1)} collective-permute-done((bf16[160,640]{1,0:T(8,128)(2,1)S(1)}, bf16[160,640]{1,0:T(8,128)(2,1)S(1)}, u32[]{:S(2)}, u32[]{:S(2)}) %collective-permute-start.23) | collective-permute-done | bytes 204832 | tf_op jit(solution)/shard_map/ppermute | solution.py:382
  249.7 13.1 %reduce-scatter.4.cloned.1.call-done = bf16[1,160,640]{2,1,0:T(8,128)(2,1)} async-done(((bf16[16,160,640]{2,1,0:T(8,128)(2,1)}), bf16[1,160,640]{2,1,0:T(8,128)(2,1)}) %reduce-scatter.4.cloned.1.call-update) | async-done | bytes 204816
  267.1 6.2 %norm_back.1 = (bf16[256,2560]{1,0:T(8,128)(2,1)}, bf16[256,2560]{1,0:T(8,128)(2,1)}, bf16[256,2560]{1,0:T(8,128)(2,1)}) custom-call(s32[4]{0:T(128)} %pad_add_fusion.place_ref, bf16[256,2560]{1,0:T(8,128)(2,1)} %q_ref.3, bf16[256,2560]{1,0:T(8,128)(2,1)} %k_ref.3, f32[1,2560]{1,0:T(1,128)} %reshape.33.gain_q_ref, f32[1,2560]{1,0:T(1,128)} %reshape.34.gain_k_ref, ...), custom_call_target="tpu_custom_call" | custom-call | tf_op jit(solution)/shard_map/norm_back/pallas_call | solution.py:92
  (80 shorter events, 44.9 us)
Async XLA Ops:
  7.2 28.8 %copy-start = (bf16[256,5120]{1,0:T(8,128)(2,1)S(1)}, bf16[256,5120]{1,0:T(8,128)(2,1)}, u32[]{:S(2)}) copy-start(bf16[256,5120]{1,0:T(8,128)(2,1)} %param.16) | copy-start | bytes 7864324
  7.2 10.6 %copy-start.6 = (f32[2560]{0:T(1024)S(1)}, f32[2560]{0:T(1024)}, u32[]{:S(2)}) copy-start(f32[2560]{0:T(1024)} %param.13) | copy-start | bytes 30724
  7.2 128.0 %all-gather.2.cloned.1.call-start = ((), (), s32[]{:S(2)}) async-start(), calls=%async_computation.1 | async-start | bytes 6963200 | tf_op jit(solution)/shard_map/all_gather | solution.py:454
  7.2 6.7 %collective-permute-start.6 = (bf16[160,640]{1,0:T(8,128)(2,1)}, bf16[160,640]{1,0:T(8,128)(2,1)S(1)}, u32[]{:S(2)}, u32[]{:S(2)}) collective-permute-start(bf16[160,640]{1,0:T(8,128)(2,1)} %param.17), channel_id=1, source_target_pairs={{0,2},{1,6},{2,3},{3,7},{4,0},{5,4},{6,1},{7,5},{8,10},{9,14},{10,... | collective-permute-start | bytes 614408 | tf_op jit(solution)/shard_map/ppermute | solution.py:373
  7.3 8.1 %collective-permute-start.5 = (bf16[160,640]{1,0:T(8,128)(2,1)}, bf16[160,640]{1,0:T(8,128)(2,1)S(1)}, u32[]{:S(2)}, u32[]{:S(2)}) collective-permute-start(bf16[160,640]{1,0:T(8,128)(2,1)} %param.17), channel_id=1, source_target_pairs={{0,0},{1,4},{2,1},{3,5},{4,2},{5,6},{6,3},{7,7},{8,8},{9,12},{10,9... | collective-permute-start | bytes 614408 | tf_op jit(solution)/shard_map/ppermute | solution.py:373
  16.4 246.4 %reduce-scatter.4.cloned.1.call-start = ((), (), s32[]{:S(2)}) async-start(), calls=%async_computation.2 | async-start | bytes 3481600
  24.2 28.3 %collective-permute-start = (bf16[3,256,640]{2,1,0:T(8,128)(2,1)}, bf16[3,256,640]{2,1,0:T(8,128)(2,1)}, u32[]{:S(2)}, u32[]{:S(2)}) collective-permute-start(bf16[3,256,640]{2,1,0:T(8,128)(2,1)} %get-tuple-element.29), channel_id=1, source_target_pairs={{0,0},{1,4},{2,1},{3,5},{4,2},{5,6},{6,3},{7,7},{8,8},{9,12},{10,9... | collective-permute-start | bytes 2949128 | tf_op jit(solution)/shard_map/ppermute | solution.py:373
  30.1 43.4 %collective-permute-start.1 = (bf16[3,256,640]{2,1,0:T(8,128)(2,1)}, bf16[3,256,640]{2,1,0:T(8,128)(2,1)}, u32[]{:S(2)}, u32[]{:S(2)}) collective-permute-start(bf16[3,256,640]{2,1,0:T(8,128)(2,1)} %get-tuple-element.30), channel_id=1, source_target_pairs={{0,4},{1,0},{2,5},{3,1},{4,6},{5,2},{6,7},{7,3},{8,12},{9,8},{10,1... | collective-permute-start | bytes 2949128 | tf_op jit(solution)/shard_map/ppermute | solution.py:373
  31.3 43.4 %collective-permute-start.2 = (bf16[3,256,640]{2,1,0:T(8,128)(2,1)}, bf16[3,256,640]{2,1,0:T(8,128)(2,1)}, u32[]{:S(2)}, u32[]{:S(2)}) collective-permute-start(bf16[3,256,640]{2,1,0:T(8,128)(2,1)} %get-tuple-element.31), channel_id=1, source_target_pairs={{0,1},{1,5},{2,0},{3,4},{4,3},{5,7},{6,2},{7,6},{8,9},{9,13},{10,8... | collective-permute-start | bytes 2949128 | tf_op jit(solution)/shard_map/ppermute | solution.py:373
  32.6 44.7 %collective-permute-start.3 = (bf16[3,256,640]{2,1,0:T(8,128)(2,1)}, bf16[3,256,640]{2,1,0:T(8,128)(2,1)}, u32[]{:S(2)}, u32[]{:S(2)}) collective-permute-start(bf16[3,256,640]{2,1,0:T(8,128)(2,1)} %get-tuple-element.32), channel_id=1, source_target_pairs={{0,5},{1,1},{2,4},{3,0},{4,7},{5,3},{6,6},{7,2},{8,13},{9,9},{10,1... | collective-permute-start | bytes 2949128 | tf_op jit(solution)/shard_map/ppermute | solution.py:373
  37.1 63.7 %collective-permute-start.4 = (bf16[128,5120]{1,0:T(8,128)(2,1)}, bf16[128,5120]{1,0:T(8,128)(2,1)}, u32[]{:S(2)}, u32[]{:S(2)}) collective-permute-start(bf16[128,5120]{1,0:T(8,128)(2,1)} %dynamic-slice_bitcast_fusion.3), channel_id=1, source_target_pairs={{0,0},{1,4},{2,1},{3,5},{4,2},{5,6},{6,3},{7,7},{8,8},{9,12},{10,9... | collective-permute-start | bytes 3932168 | tf_op jit(solution)/shard_map/ppermute | solution.py:373
  53.7 75.2 %collective-permute-start.7 = (bf16[128,5120]{1,0:T(8,128)(2,1)}, bf16[128,5120]{1,0:T(8,128)(2,1)}, u32[]{:S(2)}, u32[]{:S(2)}) collective-permute-start(bf16[128,5120]{1,0:T(8,128)(2,1)} %dynamic-slice_bitcast_fusion.2), channel_id=1, source_target_pairs={{0,4},{1,0},{2,5},{3,1},{4,6},{5,2},{6,7},{7,3},{8,12},{9,8},{10,1... | collective-permute-start | bytes 3932168 | tf_op jit(solution)/shard_map/ppermute | solution.py:373
  74.7 54.2 %collective-permute-start.8 = (bf16[128,5120]{1,0:T(8,128)(2,1)}, bf16[128,5120]{1,0:T(8,128)(2,1)}, u32[]{:S(2)}, u32[]{:S(2)}) collective-permute-start(bf16[128,5120]{1,0:T(8,128)(2,1)} %dynamic-slice_bitcast_fusion.1), channel_id=1, source_target_pairs={{0,1},{1,5},{2,0},{3,4},{4,3},{5,7},{6,2},{7,6},{8,9},{9,13},{10,8... | collective-permute-start | bytes 3932168 | tf_op jit(solution)/shard_map/ppermute | solution.py:373
  78.5 53.8 %collective-permute-start.9 = (bf16[128,5120]{1,0:T(8,128)(2,1)}, bf16[128,5120]{1,0:T(8,128)(2,1)}, u32[]{:S(2)}, u32[]{:S(2)}) collective-permute-start(bf16[128,5120]{1,0:T(8,128)(2,1)} %dynamic-slice_bitcast_fusion), channel_id=1, source_target_pairs={{0,5},{1,1},{2,4},{3,0},{4,7},{5,3},{6,6},{7,2},{8,13},{9,9},{10,1... | collective-permute-start | bytes 3932168 | tf_op jit(solution)/shard_map/ppermute | solution.py:373
  82.8 1.2 collective-permute-start.14
  100.8 44.7 %collective-permute-start.10 = (bf16[128,5120]{1,0:T(8,128)(2,1)}, bf16[128,5120]{1,0:T(8,128)(2,1)}, u32[]{:S(2)}, u32[]{:S(2)}) collective-permute-start(bf16[128,5120]{1,0:T(8,128)(2,1)} %collective-permute-done.4.refs_1_), channel_id=1, source_target_pairs={{0,4},{4,0},{1,5},{5,1},{2,6},{6,2},{3,7},{7,3},{8,12},{12,8},{9,1... | collective-permute-start | bytes 3932168 | tf_op jit(solution)/shard_map/ppermute | solution.py:377
  128.9 19.2 %collective-permute-start.11 = (bf16[128,5120]{1,0:T(8,128)(2,1)}, bf16[128,5120]{1,0:T(8,128)(2,1)}, u32[]{:S(2)}, u32[]{:S(2)}) collective-permute-start(bf16[128,5120]{1,0:T(8,128)(2,1)} %collective-permute-done.7.refs_2_), channel_id=1, source_target_pairs={{0,4},{4,0},{1,5},{5,1},{2,6},{6,2},{3,7},{7,3},{8,12},{12,8},{9,1... | collective-permute-start | bytes 3932168 | tf_op jit(solution)/shard_map/ppermute | solution.py:377
  128.9 21.7 %collective-permute-start.12 = (bf16[128,5120]{1,0:T(8,128)(2,1)}, bf16[128,5120]{1,0:T(8,128)(2,1)}, u32[]{:S(2)}, u32[]{:S(2)}) collective-permute-start(bf16[128,5120]{1,0:T(8,128)(2,1)} %collective-permute-done.8.refs_3_), channel_id=1, source_target_pairs={{0,4},{4,0},{1,5},{5,1},{2,6},{6,2},{3,7},{7,3},{8,12},{12,8},{9,1... | collective-permute-start | bytes 3932168 | tf_op jit(solution)/shard_map/ppermute | solution.py:377
  132.3 20.9 %collective-permute-start.13 = (bf16[128,5120]{1,0:T(8,128)(2,1)}, bf16[128,5120]{1,0:T(8,128)(2,1)}, u32[]{:S(2)}, u32[]{:S(2)}) collective-permute-start(bf16[128,5120]{1,0:T(8,128)(2,1)} %collective-permute-done.9.refs_4_), channel_id=1, source_target_pairs={{0,4},{4,0},{1,5},{5,1},{2,6},{6,2},{3,7},{7,3},{8,12},{12,8},{9,1... | collective-permute-start | bytes 3932168 | tf_op jit(solution)/shard_map/ppermute | solution.py:377
  170.1 41.8 %collective-permute-start.19 = (bf16[4,160,640]{2,1,0:T(8,128)(2,1)}, bf16[4,160,640]{2,1,0:T(8,128)(2,1)}, u32[]{:S(2)}, u32[]{:S(2)}) collective-permute-start(bf16[4,160,640]{2,1,0:T(8,128)(2,1)} %get-tuple-element.58), channel_id=1, source_target_pairs={{0,16},{8,24},{16,0},{24,8},{1,17},{9,25},{17,1},{25,9},{2,18},{10... | collective-permute-start | bytes 2457608 | tf_op jit(solution)/shard_map/ppermute | solution.py:382
  173.2 43.9 %collective-permute-start.20 = (bf16[4,160,640]{2,1,0:T(8,128)(2,1)}, bf16[4,160,640]{2,1,0:T(8,128)(2,1)}, u32[]{:S(2)}, u32[]{:S(2)}) collective-permute-start(bf16[4,160,640]{2,1,0:T(8,128)(2,1)} %get-tuple-element.57), channel_id=1, source_target_pairs={{0,8},{8,16},{16,24},{24,0},{1,9},{9,17},{17,25},{25,1},{2,10},{10... | collective-permute-start | bytes 2457608 | tf_op jit(solution)/shard_map/ppermute | solution.py:382
  173.7 7.3 %slice-start.1 = ((s8[6553600]{0:T(1024)(128)(4,1)}), s8[2359296]{0:T(1024)(128)(4,1)S(1)}, s32[]{:S(2)}) async-start(s8[6553600]{0:T(1024)(128)(4,1)} %bitcast.59), calls=%async_computation.4 | async-start | bytes 4718592
  173.7 45.3 %collective-permute-start.21 = (bf16[4,160,640]{2,1,0:T(8,128)(2,1)}, bf16[4,160,640]{2,1,0:T(8,128)(2,1)}, u32[]{:S(2)}, u32[]{:S(2)}) collective-permute-start(bf16[4,160,640]{2,1,0:T(8,128)(2,1)} %get-tuple-element.56), channel_id=1, source_target_pairs={{0,24},{8,0},{16,8},{24,16},{1,25},{9,1},{17,9},{25,17},{2,26},{10... | collective-permute-start | bytes 2457608 | tf_op jit(solution)/shard_map/ppermute | solution.py:382
  203.9 27.2 %collective-permute-start.15 = (bf16[3,256,640]{2,1,0:T(8,128)(2,1)}, bf16[3,256,640]{2,1,0:T(8,128)(2,1)}, u32[]{:S(2)}, u32[]{:S(2)}) collective-permute-start(bf16[3,256,640]{2,1,0:T(8,128)(2,1)} %get-tuple-element.41), channel_id=1, source_target_pairs={{0,0},{4,1},{1,2},{5,3},{2,4},{6,5},{3,6},{7,7},{8,8},{12,9},{9,10... | collective-permute-start | bytes 2949128 | tf_op jit(solution)/shard_map/ppermute | solution.py:373
  205.8 26.5 %collective-permute-start.16 = (bf16[3,256,640]{2,1,0:T(8,128)(2,1)}, bf16[3,256,640]{2,1,0:T(8,128)(2,1)}, u32[]{:S(2)}, u32[]{:S(2)}) collective-permute-start(bf16[3,256,640]{2,1,0:T(8,128)(2,1)} %get-tuple-element.42), channel_id=1, source_target_pairs={{4,0},{0,1},{5,2},{1,3},{6,4},{2,5},{7,6},{3,7},{12,8},{8,9},{13,1... | collective-permute-start | bytes 2949128 | tf_op jit(solution)/shard_map/ppermute | solution.py:373
  211.9 55.2 %collective-permute-start.17 = (bf16[3,256,640]{2,1,0:T(8,128)(2,1)}, bf16[3,256,640]{2,1,0:T(8,128)(2,1)}, u32[]{:S(2)}, u32[]{:S(2)}) collective-permute-start(bf16[3,256,640]{2,1,0:T(8,128)(2,1)} %copy-done.3), channel_id=1, source_target_pairs={{1,0},{5,1},{0,2},{4,3},{3,4},{7,5},{2,6},{6,7},{9,8},{13,9},{8,10... | collective-permute-start | bytes 2949128 | tf_op jit(solution)/shard_map/ppermute | solution.py:373
  217.1 50.0 %collective-permute-start.18 = (bf16[3,256,640]{2,1,0:T(8,128)(2,1)S(1)}, bf16[3,256,640]{2,1,0:T(8,128)(2,1)}, u32[]{:S(2)}, u32[]{:S(2)}) collective-permute-start(bf16[3,256,640]{2,1,0:T(8,128)(2,1)S(1)} %get-tuple-element.44), channel_id=1, source_target_pairs={{5,0},{1,1},{4,2},{0,3},{7,4},{3,5},{6,6},{2,7},{13,8},{9,9},{12,1... | collective-permute-start | bytes 2949128 | tf_op jit(solution)/shard_map/ppermute | solution.py:373
  232.4 8.9 %collective-permute-start.24 = (bf16[160,640]{1,0:T(8,128)(2,1)S(1)}, bf16[160,640]{1,0:T(8,128)(2,1)S(1)}, u32[]{:S(2)}, u32[]{:S(2)}) collective-permute-start(bf16[160,640]{1,0:T(8,128)(2,1)S(1)} %get-tuple-element.61), channel_id=1, source_target_pairs={{0,96},{32,0},{64,32},{96,64},{1,97},{33,1},{65,33},{97,65},{2,98}... | collective-permute-start | bytes 614408 | tf_op jit(solution)/shard_map/ppermute | solution.py:382
  236.4 13.2 %collective-permute-start.23 = (bf16[160,640]{1,0:T(8,128)(2,1)S(1)}, bf16[160,640]{1,0:T(8,128)(2,1)S(1)}, u32[]{:S(2)}, u32[]{:S(2)}) collective-permute-start(bf16[160,640]{1,0:T(8,128)(2,1)S(1)} %get-tuple-element.62), channel_id=1, source_target_pairs={{0,32},{32,64},{64,96},{96,0},{1,33},{33,65},{65,97},{97,1},{2,34}... | collective-permute-start | bytes 614408 | tf_op jit(solution)/shard_map/ppermute | solution.py:382
  236.4 13.2 %collective-permute-start.22 = (bf16[160,640]{1,0:T(8,128)(2,1)S(1)}, bf16[160,640]{1,0:T(8,128)(2,1)S(1)}, u32[]{:S(2)}, u32[]{:S(2)}) collective-permute-start(bf16[160,640]{1,0:T(8,128)(2,1)S(1)} %get-tuple-element.60), channel_id=1, source_target_pairs={{0,64},{32,96},{64,0},{96,32},{1,65},{33,97},{65,1},{97,33},{2,66}... | collective-permute-start | bytes 614408 | tf_op jit(solution)/shard_map/ppermute | solution.py:382
  264.0 9.3 %collective-permute-start.26 = (bf16[160,640]{1,0:T(8,128)(2,1)S(1)}, bf16[160,640]{1,0:T(8,128)(2,1)S(1)}, u32[]{:S(2)}, u32[]{:S(2)}) collective-permute-start(bf16[160,640]{1,0:T(8,128)(2,1)S(1)} %bitcast_select_fusion), channel_id=1, source_target_pairs={{0,4},{1,6},{2,0},{3,2},{4,5},{5,7},{6,1},{7,3},{8,12},{9,14},{10,... | collective-permute-start | bytes 614408 | tf_op jit(solution)/shard_map/ppermute | solution.py:373
  264.9 8.6 %collective-permute-start.25 = (bf16[160,640]{1,0:T(8,128)(2,1)S(1)}, bf16[160,640]{1,0:T(8,128)(2,1)S(1)}, u32[]{:S(2)}, u32[]{:S(2)}) collective-permute-start(bf16[160,640]{1,0:T(8,128)(2,1)S(1)} %get-tuple-element.54), channel_id=1, source_target_pairs={{0,0},{1,2},{2,4},{3,6},{4,1},{5,3},{6,5},{7,7},{8,8},{9,10},{10,1... | collective-permute-start | bytes 614408 | tf_op jit(solution)/shard_map/ppermute | solution.py:373
  (8 other events, 39.5 us)
Sparse Core Ops, SparseCore 0:
  16.5 67.9 all-gather.1
  166.8 95.9 reduce-scatter.3

commit v4 on v3

--- a/solution.py
+++ b/solution.py
@@ -317,8 +317,9 @@
     )(place, tile_pairs, *packs, *packs, *packs, *own_grads, *other_grads, probs)
 
 
-def weight_grad_kernel(place_ref, mean, att_ref, *refs):
+def weight_grad_kernel(place_ref, mean, side, att_ref, *refs):
     own, other, outs = refs[:SEQ], refs[SEQ : 2 * SEQ], refs[2 * SEQ :]
+    pieces, second = outs[:-1], outs[-1]
     half_rows = own[0].shape[0]
     core = place_ref[1]
     columns, attended = [], []
@@ -329,24 +330,33 @@
             attended.append(att_ref[pl.ds(start, half_rows), :])
     total = contract(jnp.concatenate(columns, axis=0), jnp.concatenate(attended, axis=0), 0, 0)
     total = (total * mean).astype(jnp.bfloat16)
-    count, piece = outs[0].shape[:2]
+    count, piece = second.shape[:2]
+    step = pl.program_id(0)
     for at in range(count):
-        for holder, out in enumerate(outs):
-            start = (2 * at + holder) * piece
-            out[at] = total[start : start + piece]
-
-
-def weight_grad(place, attended, own, other, mean, owners, block=640):
+        start = 2 * at * piece
+        second[at] = total[start + piece : start + 2 * piece]
+        owner = step * count + at
+        ahead = lax.rem(owner + side - place_ref[4], side)
+        for by, out in enumerate(pieces):
+
+            @pl.when(ahead == by)
+            def _(out=out, start=start, owner=owner):
+                out[owner // side] = total[start : start + piece]
+
+
+def weight_grad(place, attended, own, other, mean, side, block=640):
     half_rows, features = own[0].shape
     local_width = attended.shape[1]
-    piece = features // owners // CORES
+    piece = features // (side * side) // CORES
     return pl.pallas_call(
-        lambda place_ref, *refs: weight_grad_kernel(place_ref, mean, *refs),
+        lambda place_ref, *refs: weight_grad_kernel(place_ref, mean, side, *refs),
         grid=(features // block,),
         in_specs=[smem(), pl.BlockSpec(attended.shape, lambda i: (0, 0))]
         + [pl.BlockSpec((half_rows, block), lambda i: (0, i))] * (2 * SEQ),
-        out_specs=[pl.BlockSpec((block // piece // 2, piece, local_width), lambda i: (i, 0, 0))] * CORES,
-        out_shape=[jax.ShapeDtypeStruct((owners, piece, local_width), jnp.bfloat16)] * CORES,
+        out_specs=[pl.BlockSpec((side, piece, local_width), lambda i: (0, 0, 0))] * side
+        + [pl.BlockSpec((block // piece // 2, piece, local_width), lambda i: (i, 0, 0))],
+        out_shape=[jax.ShapeDtypeStruct((side, piece, local_width), jnp.bfloat16)] * side
+        + [jax.ShapeDtypeStruct((side * side, piece, local_width), jnp.bfloat16)],
         compiler_params=params(),
         name="weight_grad",
     )(place, attended, *own, *other)
@@ -438,7 +448,7 @@
     rows, features = out_grad.shape
     shard = 2 * (seq % 2) + core
     tiles_per_block = tile_pairs.shape[0] // SEQ
-    place = jnp.stack([seq, core, shard, shard * tiles_per_block]).astype(jnp.int32)
+    place = jnp.stack([seq, core, shard, shard * tiles_per_block, lax.axis_index("x")]).astype(jnp.int32)
     lens = jnp.where(seq // 2 == core, tile_lens, swap_cores(tile_lens))
 
     def half_rows(rows_in, round_):
@@ -447,31 +457,35 @@
 
     own = [send(half_rows(out_grad, 0), outward(0))]
     packs = to_rounds(place, queries, keys, values, gain_q, gain_k)
-    packs = [send(part, outward(r)) for r, part in enumerate(packs)]
+    w_out = after(w_out, packs[0])
+    packs = [send(after(part, own[0]) if r == 3 else part, outward(r)) for r, part in enumerate(packs)]
     ready = (packs[0], packs[1], packs[2:])
     own += [send(half_rows(after(out_grad, ready[r - 1]), r), outward(r)) for r in range(1, SEQ)]
-    other = [swap_cores(part) for part in own]
     w_all = lax.all_gather(to_shard_holders(w_out, core, seq), ("z", "x"), axis=0, tiled=True)
 
     def project(part):
         return jnp.dot(part, w_all, preferred_element_type=jnp.float32).astype(jnp.bfloat16)
 
     attended, probs = forward(place, tile_pairs, lens, packs)
-    own_grads = [project(part) for part in own]
+    other = [swap_cores(after(part, attended) if r == 2 else part) for r, part in enumerate(own[:-1])]
+    own_grads = [project(part) for part in own[:-1]]
     other_grads = [project(part) for part in other]
-    attended = after(attended, own_grads[:-1], other_grads[:-1])
-    one, two = weight_grad(
-        place, attended, own, other, 1.0 / (count_z * count_x * CORES), count_z * count_x
-    )
-    two = lax.psum_scatter(two, ("z", "x"), scatter_dimension=0, tiled=True)[0]
-    one = scatter(one.reshape((count_z, count_x) + one.shape[1:]), "x", 1)
-    parts = backward(place, tile_pairs, packs, own_grads, other_grads, after(probs, one[0]))
+    other.append(swap_cores(after(own[-1], own_grads, other_grads[:-1])))
+    attended = after(attended, own_grads, other_grads)
+    own_grads.append(project(own[-1]))
+    other_grads.append(project(other[-1]))
+    *one, two = weight_grad(place, attended, own, other, 1.0 / (count_z * count_x * CORES), count_x)
+    two = lax.psum_scatter(two, "z", scatter_dimension=0, tiled=True)
+    token = one[0]
+    one = [one[0]] + [shift(one[by], "x", by) for by in (2, 1, 3)]
+    parts = backward(place, tile_pairs, packs, own_grads, other_grads, after(probs, token))
     token = parts[0]
-    parts = [send(part, inward(r)) for r, part in enumerate(parts)]
+    parts = {r: send(parts[r], inward(r)) for r in (0, 2, 1, 3)}
     one = add(*after(one, token))
-    one = add(*scatter(after(one, parts[0], parts[1]), "z"))
+    one = add(*scatter(after(one, parts[0], parts[2]), "z"))
+    two = add(*scatter(after(two, parts[0], parts[2]), "x"))
     grad_w = to_owners((one, two), seq)
-    grad_q, grad_k, grad_v = finish(place, queries, keys, gain_q, gain_k, parts)
+    grad_q, grad_k, grad_v = finish(place, queries, keys, gain_q, gain_k, [parts[r] for r in range(SEQ)])
     return (grad_q, grad_k, grad_v, grad_w)
 
 

time: 286 us -> 295 us (1.031)
  starting transfers between devices: 56.2 us -> 75.5 us
  waiting for transfers between devices: 113 us -> 97.4 us
    ppermute x16, starting transfers between devices: 40.3 us -> 59.7 us  [send(): return lax.ppermute(value, ('core', 'seq'), pairs)]
    unnamed x3 -> x2, waiting for transfers between devices: 13.2 us -> 0.03 us
    ppermute x16, waiting for transfers between devices: 83.9 us -> 76 us  [send(): return lax.ppermute(value, ('core', 'seq'), pairs)]
    ppermute x6 -> x9, waiting for transfers between devices: 14.8 us -> 19.7 us  [shift(): lax.ppermute(value, axis, [(i, (i + by) % count) for i in range(count)])]
    ppermute x6 -> x9, starting transfers between devices: 12.3 us -> 14.6 us  [shift(): lax.ppermute(value, axis, [(i, (i + by) % count) for i in range(count)])]
  transfers between devices with their start and end apart: 29 -> 32, of which waited for: 16 -> 17; matrix products, arithmetic and copies ran while one was open for 14% -> 13% of each run, Pallas kernels for 15% -> 13%
where the time goes in v4:
time: 295 us; the launch traced here: 290 us
  waiting for transfers between devices  97.4 us (33%)
  starting transfers between devices  75.5 us (26%)
  Pallas kernels  57 us (19%)
  matrix products  26.4 us (9%)
  between operations  14.4 us (5%)
  local copies, waits for them, and re-layouts  13.5 us (5%)
  other arithmetic  5.96 us (2%)
    ppermute x16, waiting for transfers between devices, send(): return lax.ppermute(value, ('core', 'seq'), pairs)  76 us
    ppermute x16, starting transfers between devices, send(): return lax.ppermute(value, ('core', 'seq'), pairs)  59.7 us
    dot_general x8, matrix products, project(): jnp.dot(part, w_all, preferred_element_type=jnp.float32)  26.4 us
    ppermute x9, waiting for transfers between devices, shift(): lax.ppermute(value, axis, [(i, (i + by) % count) for i in range(count)])  19.7 us
    pallas_call x1, Pallas kernels, backward(): pl.pallas_call(backward_kernel, grid=(heads,), in_specs=[smem()] * 2 + [s...  19.3 us
    ppermute x9, starting transfers between devices, shift(): lax.ppermute(value, axis, [(i, (i + by) % count) for i in range(count)])  14.6 us
    pallas_call x1, Pallas kernels, weight_grad(): pl.pallas_call(lambda place_ref, *refs: weight_grad_kernel(place_ref, mea...  14.4 us
    pallas_call x1, Pallas kernels, forward(): pl.pallas_call(forward_kernel, grid=(heads,), in_specs=[smem()] * 3 + [sp...  11.7 us
  transfers between devices with their start and end apart: 32, of which 17 were waited for; matrix products, arithmetic and copies ran while one was open for 13% of the time, Pallas kernels for 13%

profile of v4, /device:TPU:24, one launch (start us, length us, event | category | flops | bytes accessed | tf_op | source)
XLA Modules:
  0.0 290.2 jit_solution(13517324098959294524)
XLA Ops:
  10.7 5.4 %norm_rows.1 = (bf16[3,256,640]{2,1,0:T(8,128)(2,1)}, bf16[3,256,640]{2,1,0:T(8,128)(2,1)}, bf16[3,256,640]{2,1,0:T(8,128)(2,1)}, bf16[3,256,640]{2,1,0:T(8,128)(2,1)}) custom-call(s32[5]{0:T(128)} %stack.23.place_ref, bf16[256,2560]{1,0:T(8,128)(2,1)} %q_ref.3, bf16[256,2560]{1,0:T(8,128)(2,1)} %k_ref.3, bf16[256,2560]{1,0:T(8,128)(2,1)} %v_ref.1, ...), custom_call_target="tpu_custom_call" | custom-call | tf_op jit(solution)/shard_map/norm_rows/pallas_call | solution.py:60
  16.2 2.6 collective-permute-start.5
  18.8 4.0 %collective-permute-done.6 = bf16[160,640]{1,0:T(8,128)(2,1)S(1)} collective-permute-done((bf16[160,640]{1,0:T(8,128)(2,1)S(1)}, bf16[160,640]{1,0:T(8,128)(2,1)S(1)}, u32[]{:S(2)}, u32[]{:S(2)}) %collective-permute-start.6) | collective-permute-done | bytes 204832 | tf_op jit(solution)/shard_map/ppermute | solution.py:383
  25.1 5.8 %collective-permute-start = (bf16[3,256,640]{2,1,0:T(8,128)(2,1)}, bf16[3,256,640]{2,1,0:T(8,128)(2,1)}, u32[]{:S(2)}, u32[]{:S(2)}) collective-permute-start(bf16[3,256,640]{2,1,0:T(8,128)(2,1)} %get-tuple-element.37), channel_id=1, source_target_pairs={{0,0},{1,4},{2,1},{3,5},{4,2},{5,6},{6,3},{7,7},{8,8},{9,12},{10,9... | collective-permute-start | bytes 2949128 | tf_op jit(solution)/shard_map/ppermute | solution.py:383
  33.3 3.6 %collective-permute-start.3 = (bf16[128,5120]{1,0:T(8,128)(2,1)}, bf16[128,5120]{1,0:T(8,128)(2,1)}, u32[]{:S(2)}, u32[]{:S(2)}) collective-permute-start(bf16[128,5120]{1,0:T(8,128)(2,1)} %dynamic-slice_bitcast_fusion.3), channel_id=1, source_target_pairs={{0,0},{1,4},{2,1},{3,5},{4,2},{5,6},{6,3},{7,7},{8,8},{9,12},{10,9... | collective-permute-start | bytes 3932168 | tf_op jit(solution)/shard_map/ppermute | solution.py:383
  38.3 4.7 %collective-permute-done.refs_0_.refs_4_.refs_8_ = bf16[3,256,640]{2,1,0:T(8,128)(2,1)} collective-permute-done((bf16[3,256,640]{2,1,0:T(8,128)(2,1)}, bf16[3,256,640]{2,1,0:T(8,128)(2,1)}, u32[]{:S(2)}, u32[]{:S(2)}) %collective-permute-start) | collective-permute-done | bytes 983072 | tf_op jit(solution)/shard_map/ppermute | solution.py:383
  43.1 19.0 %collective-permute-done.1.refs_1_.refs_5_.refs_9_ = bf16[3,256,640]{2,1,0:T(8,128)(2,1)} collective-permute-done((bf16[3,256,640]{2,1,0:T(8,128)(2,1)}, bf16[3,256,640]{2,1,0:T(8,128)(2,1)}, u32[]{:S(2)}, u32[]{:S(2)}) %collective-permute-start.1) | collective-permute-done | bytes 983072 | tf_op jit(solution)/shard_map/ppermute | solution.py:383
  63.2 22.3 %collective-permute-done.3.refs_1_ = bf16[128,5120]{1,0:T(8,128)(2,1)} collective-permute-done((bf16[128,5120]{1,0:T(8,128)(2,1)}, bf16[128,5120]{1,0:T(8,128)(2,1)}, u32[]{:S(2)}, u32[]{:S(2)}) %collective-permute-start.3) | collective-permute-done | bytes 1310752 | tf_op jit(solution)/shard_map/ppermute | solution.py:383
  88.6 27.5 %collective-permute-start.7 = (bf16[128,5120]{1,0:T(8,128)(2,1)}, bf16[128,5120]{1,0:T(8,128)(2,1)}, u32[]{:S(2)}, u32[]{:S(2)}) collective-permute-start(bf16[128,5120]{1,0:T(8,128)(2,1)} %dynamic-slice_bitcast_fusion.2), channel_id=1, source_target_pairs={{0,4},{1,0},{2,5},{3,1},{4,6},{5,2},{6,7},{7,3},{8,12},{9,8},{10,1... | collective-permute-start | bytes 3932168 | tf_op jit(solution)/shard_map/ppermute | solution.py:383
  117.5 6.4 %collective-permute-done.4.refs_3_.refs_7_.refs_11_ = bf16[3,256,640]{2,1,0:T(8,128)(2,1)} collective-permute-done((bf16[3,256,640]{2,1,0:T(8,128)(2,1)}, bf16[3,256,640]{2,1,0:T(8,128)(2,1)}, u32[]{:S(2)}, u32[]{:S(2)}) %collective-permute-start.4) | collective-permute-done | bytes 983072 | tf_op jit(solution)/shard_map/ppermute | solution.py:383
  125.1 5.6 %collective-permute-start.9 = (bf16[128,5120]{1,0:T(8,128)(2,1)}, bf16[128,5120]{1,0:T(8,128)(2,1)}, u32[]{:S(2)}, u32[]{:S(2)}) collective-permute-start(bf16[128,5120]{1,0:T(8,128)(2,1)} %dynamic-slice_bitcast_fusion), channel_id=1, source_target_pairs={{0,5},{1,1},{2,4},{3,0},{4,7},{5,3},{6,6},{7,2},{8,13},{9,9},{10,1... | collective-permute-start | bytes 3932168 | tf_op jit(solution)/shard_map/ppermute | solution.py:383
  130.7 11.7 %attention_forward.1 = (bf16[1024,640]{1,0:T(8,128)(2,1)S(1)}, bf16[5,4096,128]{2,1,0:T(8,128)(2,1)}) custom-call(s32[5]{0:T(128)S(1)} %copy-done.2, s32[16,8]{1,0:T(8,128)S(1)} %copy.14.pairs_ref, s32[1,16]{1,0:T(1,128)S(1)} %broadcast_select_fusion.2.lens_ref, bf16[3,256,640]{2,1,0:T(8,128)(2,1)} %collective-permute-done.refs_0_.refs_4_.refs_8_, ...), custom_call_target="tpu_custom_call" | custom-call | tf_op jit(solution)/shard_map/attention_forward/pallas_call | solution.py:211
  143.0 4.6 %convolution_convert_fusion.7.refs_12_ = bf16[128,640]{1,0:T(8,128)(2,1)S(1)} fusion(bf16[128,5120]{1,0:T(8,128)(2,1)} %collective-permute-done.3.refs_1_, bf16[5120,640]{1,0:T(8,128)(2,1)} %all-gather.2.cloned.1.call-done), kind=kOutput, calls=%fused_computation.12 | convolution fusion | flops 838942720 | bytes 8028160 | tf_op jit(solution)/shard_map/dot_general | solution.py:467
  150.7 2.6 convolution_convert_fusion.5.refs_14_
  153.3 2.6 convolution_convert_fusion.3.refs_16_
  155.9 2.6 convolution_convert_fusion.2.refs_17_
  158.8 2.6 convolution_convert_fusion.1.refs_18_
  163.0 14.4 %weight_grad.1 = (bf16[4,160,640]{2,1,0:T(8,128)(2,1)S(1)}, bf16[4,160,640]{2,1,0:T(8,128)(2,1)}, bf16[4,160,640]{2,1,0:T(8,128)(2,1)}, bf16[4,160,640]{2,1,0:T(8,128)(2,1)}, bf16[16,160,640]{2,1,0:T(8,128)(2,1)}) custom-call(s32[5]{0:T(128)S(1)} %copy-done.2, bf16[1024,640]{1,0:T(8,128)(2,1)S(1)} %get-tuple-element.50.refs_0_, ...), custom_call_target="tpu_custom_call" | custom-call | tf_op jit(solution)/shard_map/weight_grad/pallas_call | solution.py:351
  177.5 4.6 %convolution_convert_fusion.4.refs_15_ = bf16[128,640]{1,0:T(8,128)(2,1)S(1)} fusion(bf16[128,5120]{1,0:T(8,128)(2,1)} %collective-permute-done.9.refs_4_, bf16[5120,640]{1,0:T(8,128)(2,1)} %all-gather.2.cloned.1.call-done), kind=kOutput, calls=%fused_computation.9 | convolution fusion | flops 838942720 | bytes 8028160 | tf_op jit(solution)/shard_map/dot_general | solution.py:467
  182.0 3.1 %collective-permute-start.19 = (bf16[4,160,640]{2,1,0:T(8,128)(2,1)}, bf16[4,160,640]{2,1,0:T(8,128)(2,1)}, u32[]{:S(2)}, u32[]{:S(2)}) collective-permute-start(bf16[4,160,640]{2,1,0:T(8,128)(2,1)} %get-tuple-element.60), channel_id=1, source_target_pairs={{0,16},{8,24},{16,0},{24,8},{1,17},{9,25},{17,1},{25,9},{2,18},{10... | collective-permute-start | bytes 2457608 | tf_op jit(solution)/shard_map/ppermute | solution.py:392
  185.7 2.6 collective-permute-start.21
  188.3 4.5 %convolution_convert_fusion.refs_19_ = bf16[128,640]{1,0:T(8,128)(2,1)S(1)} fusion(bf16[128,5120]{1,0:T(8,128)(2,1)S(1)} %copy-done.7, bf16[5120,640]{1,0:T(8,128)(2,1)} %all-gather.2.cloned.1.call-done), kind=kOutput, calls=%fused_computation.5 | convolution fusion | flops 838942720 | bytes 8028160 | tf_op jit(solution)/shard_map/dot_general | solution.py:467
  192.8 19.3 %attention_backward.1 = (bf16[3,256,640]{2,1,0:T(8,128)(2,1)}, bf16[3,256,640]{2,1,0:T(8,128)(2,1)S(1)}, bf16[3,256,640]{2,1,0:T(8,128)(2,1)}, bf16[3,256,640]{2,1,0:T(8,128)(2,1)S(1)}) custom-call(s32[5]{0:T(128)S(1)} %copy-done.2, s32[16,8]{1,0:T(8,128)S(1)} %copy.14.pairs_ref, bf16[3,256,640]{2,1,0:T(8,128)(2,1)} %collective-permute-done.refs_0_.refs_4_.refs_8_, ...), custom_call_target="tpu_custom_call" | custom-call | tf_op jit(solution)/shard_map/attention_backward/pallas_call | solution.py:305
  216.7 5.0 %collective-permute-done.20 = bf16[4,160,640]{2,1,0:T(8,128)(2,1)} collective-permute-done((bf16[4,160,640]{2,1,0:T(8,128)(2,1)}, bf16[4,160,640]{2,1,0:T(8,128)(2,1)}, u32[]{:S(2)}, u32[]{:S(2)}) %collective-permute-start.20) | collective-permute-done | bytes 819232 | tf_op jit(solution)/shard_map/ppermute | solution.py:392
  223.9 8.6 %collective-permute-done.15.refs_0_ = bf16[3,256,640]{2,1,0:T(8,128)(2,1)} collective-permute-done((bf16[3,256,640]{2,1,0:T(8,128)(2,1)}, bf16[3,256,640]{2,1,0:T(8,128)(2,1)}, u32[]{:S(2)}, u32[]{:S(2)}) %collective-permute-start.15) | collective-permute-done | bytes 983072 | tf_op jit(solution)/shard_map/ppermute | solution.py:383
  232.5 8.1 %collective-permute-done.17.refs_2_ = bf16[3,256,640]{2,1,0:T(8,128)(2,1)} collective-permute-done((bf16[3,256,640]{2,1,0:T(8,128)(2,1)}, bf16[3,256,640]{2,1,0:T(8,128)(2,1)}, u32[]{:S(2)}, u32[]{:S(2)}) %collective-permute-start.17) | collective-permute-done | bytes 983072 | tf_op jit(solution)/shard_map/ppermute | solution.py:383
  241.5 3.7 %collective-permute-start.24 = (bf16[160,640]{1,0:T(8,128)(2,1)}, bf16[160,640]{1,0:T(8,128)(2,1)S(1)}, u32[]{:S(2)}, u32[]{:S(2)}) collective-permute-start(bf16[160,640]{1,0:T(8,128)(2,1)} %get-tuple-element.74), channel_id=1, source_target_pairs={{0,96},{32,0},{64,32},{96,64},{1,97},{33,1},{65,33},{97,65},{2,98}... | collective-permute-start | bytes 614408 | tf_op jit(solution)/shard_map/ppermute | solution.py:392
  247.1 3.4 %collective-permute-start.18 = (bf16[3,256,640]{2,1,0:T(8,128)(2,1)S(1)}, bf16[3,256,640]{2,1,0:T(8,128)(2,1)}, u32[]{:S(2)}, u32[]{:S(2)}) collective-permute-start(bf16[3,256,640]{2,1,0:T(8,128)(2,1)S(1)} %get-tuple-element.56), channel_id=1, source_target_pairs={{5,0},{1,1},{4,2},{0,3},{7,4},{3,5},{6,6},{2,7},{13,8},{9,9},{12,1... | collective-permute-start | bytes 2949128 | tf_op jit(solution)/shard_map/ppermute | solution.py:383
  255.1 2.7 collective-permute-done.23
  260.9 8.8 %collective-permute-done.26 = bf16[160,640]{1,0:T(8,128)(2,1)} collective-permute-done((bf16[160,640]{1,0:T(8,128)(2,1)}, bf16[160,640]{1,0:T(8,128)(2,1)}, u32[]{:S(2)}, u32[]{:S(2)}) %collective-permute-start.26) | collective-permute-done | bytes 204832 | tf_op jit(solution)/shard_map/ppermute | solution.py:392
  272.1 2.7 collective-permute-start.28
  276.4 6.2 %norm_back.1 = (bf16[256,2560]{1,0:T(8,128)(2,1)}, bf16[256,2560]{1,0:T(8,128)(2,1)}, bf16[256,2560]{1,0:T(8,128)(2,1)}) custom-call(s32[5]{0:T(128)} %stack.23.place_ref, bf16[256,2560]{1,0:T(8,128)(2,1)} %q_ref.3, bf16[256,2560]{1,0:T(8,128)(2,1)} %k_ref.3, f32[1,2560]{1,0:T(1,128)} %reshape.32.gain_q_ref, f32[1,2560]{1,0:T(1,128)} %reshape.33.gain_k_ref, ...), custom_call_target="tpu_custom_call" | custom-call | tf_op jit(solution)/shard_map/norm_back/pallas_call | solution.py:92
  (85 shorter events, 44.6 us)
Async XLA Ops:
  7.2 135.8 %all-gather.2.cloned.1.call-start = ((), (), s32[]{:S(2)}) async-start(), calls=%async_computation.1 | async-start | bytes 6963200 | tf_op jit(solution)/shard_map/all_gather | solution.py:464
  16.1 6.6 %collective-permute-start.6 = (bf16[160,640]{1,0:T(8,128)(2,1)S(1)}, bf16[160,640]{1,0:T(8,128)(2,1)S(1)}, u32[]{:S(2)}, u32[]{:S(2)}) collective-permute-start(bf16[160,640]{1,0:T(8,128)(2,1)S(1)} %copy-done.10), channel_id=1, source_target_pairs={{0,2},{1,6},{2,3},{3,7},{4,0},{5,4},{6,1},{7,5},{8,10},{9,14},{10,... | collective-permute-start | bytes 614408 | tf_op jit(solution)/shard_map/ppermute | solution.py:383
  16.2 7.9 %collective-permute-start.5 = (bf16[160,640]{1,0:T(8,128)(2,1)S(1)}, bf16[160,640]{1,0:T(8,128)(2,1)S(1)}, u32[]{:S(2)}, u32[]{:S(2)}) collective-permute-start(bf16[160,640]{1,0:T(8,128)(2,1)S(1)} %copy-done.10), channel_id=1, source_target_pairs={{0,0},{1,4},{2,1},{3,5},{4,2},{5,6},{6,3},{7,7},{8,8},{9,12},{10,9... | collective-permute-start | bytes 614408 | tf_op jit(solution)/shard_map/ppermute | solution.py:383
  25.0 225.6 %reduce-scatter.2.cloned.1.call-start = ((), (), s32[]{:S(2)}) async-start(), calls=%async_computation.2 | async-start | bytes 4096000 | tf_op jit(solution)/shard_map/reduce_scatter | solution.py:478
  25.1 18.0 %collective-permute-start = (bf16[3,256,640]{2,1,0:T(8,128)(2,1)}, bf16[3,256,640]{2,1,0:T(8,128)(2,1)}, u32[]{:S(2)}, u32[]{:S(2)}) collective-permute-start(bf16[3,256,640]{2,1,0:T(8,128)(2,1)} %get-tuple-element.37), channel_id=1, source_target_pairs={{0,0},{1,4},{2,1},{3,5},{4,2},{5,6},{6,3},{7,7},{8,8},{9,12},{10,9... | collective-permute-start | bytes 2949128 | tf_op jit(solution)/shard_map/ppermute | solution.py:383
  30.9 31.2 %collective-permute-start.1 = (bf16[3,256,640]{2,1,0:T(8,128)(2,1)}, bf16[3,256,640]{2,1,0:T(8,128)(2,1)}, u32[]{:S(2)}, u32[]{:S(2)}) collective-permute-start(bf16[3,256,640]{2,1,0:T(8,128)(2,1)} %get-tuple-element.38), channel_id=1, source_target_pairs={{0,4},{1,0},{2,5},{3,1},{4,6},{5,2},{6,7},{7,3},{8,12},{9,8},{10,1... | collective-permute-start | bytes 2949128 | tf_op jit(solution)/shard_map/ppermute | solution.py:383
  33.3 52.3 %collective-permute-start.3 = (bf16[128,5120]{1,0:T(8,128)(2,1)}, bf16[128,5120]{1,0:T(8,128)(2,1)}, u32[]{:S(2)}, u32[]{:S(2)}) collective-permute-start(bf16[128,5120]{1,0:T(8,128)(2,1)} %dynamic-slice_bitcast_fusion.3), channel_id=1, source_target_pairs={{0,0},{1,4},{2,1},{3,5},{4,2},{5,6},{6,3},{7,7},{8,8},{9,12},{10,9... | collective-permute-start | bytes 3932168 | tf_op jit(solution)/shard_map/ppermute | solution.py:383
  36.9 80.6 %collective-permute-start.2 = (bf16[3,256,640]{2,1,0:T(8,128)(2,1)}, bf16[3,256,640]{2,1,0:T(8,128)(2,1)}, u32[]{:S(2)}, u32[]{:S(2)}) collective-permute-start(bf16[3,256,640]{2,1,0:T(8,128)(2,1)} %get-tuple-element.39), channel_id=1, source_target_pairs={{0,1},{1,5},{2,0},{3,4},{4,3},{5,7},{6,2},{7,6},{8,9},{9,13},{10,8... | collective-permute-start | bytes 2949128 | tf_op jit(solution)/shard_map/ppermute | solution.py:383
  63.2 79.2 %collective-permute-start.8 = (bf16[128,5120]{1,0:T(8,128)(2,1)}, bf16[128,5120]{1,0:T(8,128)(2,1)}, u32[]{:S(2)}, u32[]{:S(2)}) collective-permute-start(bf16[128,5120]{1,0:T(8,128)(2,1)} %dynamic-slice_bitcast_fusion.1), channel_id=1, source_target_pairs={{0,1},{1,5},{2,0},{3,4},{4,3},{5,7},{6,2},{7,6},{8,9},{9,13},{10,8... | collective-permute-start | bytes 3932168 | tf_op jit(solution)/shard_map/ppermute | solution.py:383
  85.5 38.4 %collective-permute-start.4 = (bf16[3,256,640]{2,1,0:T(8,128)(2,1)}, bf16[3,256,640]{2,1,0:T(8,128)(2,1)}, u32[]{:S(2)}, u32[]{:S(2)}) collective-permute-start(bf16[3,256,640]{2,1,0:T(8,128)(2,1)} %get-tuple-element.41), channel_id=1, source_target_pairs={{0,5},{1,1},{2,4},{3,0},{4,7},{5,3},{6,6},{7,2},{8,13},{9,9},{10,1... | collective-permute-start | bytes 2949128 | tf_op jit(solution)/shard_map/ppermute | solution.py:383
  88.6 53.9 %collective-permute-start.7 = (bf16[128,5120]{1,0:T(8,128)(2,1)}, bf16[128,5120]{1,0:T(8,128)(2,1)}, u32[]{:S(2)}, u32[]{:S(2)}) collective-permute-start(bf16[128,5120]{1,0:T(8,128)(2,1)} %dynamic-slice_bitcast_fusion.2), channel_id=1, source_target_pairs={{0,4},{1,0},{2,5},{3,1},{4,6},{5,2},{6,7},{7,3},{8,12},{9,8},{10,1... | collective-permute-start | bytes 3932168 | tf_op jit(solution)/shard_map/ppermute | solution.py:383
  116.2 1.1 collective-permute-start.12
  117.3 36.0 %collective-permute-start.10 = (bf16[128,5120]{1,0:T(8,128)(2,1)}, bf16[128,5120]{1,0:T(8,128)(2,1)}, u32[]{:S(2)}, u32[]{:S(2)}) collective-permute-start(bf16[128,5120]{1,0:T(8,128)(2,1)} %collective-permute-done.3.refs_1_), channel_id=1, source_target_pairs={{0,4},{4,0},{1,5},{5,1},{2,6},{6,2},{3,7},{7,3},{8,12},{12,8},{9,1... | collective-permute-start | bytes 3932168 | tf_op jit(solution)/shard_map/ppermute | solution.py:387
  125.1 33.4 %collective-permute-start.9 = (bf16[128,5120]{1,0:T(8,128)(2,1)}, bf16[128,5120]{1,0:T(8,128)(2,1)}, u32[]{:S(2)}, u32[]{:S(2)}) collective-permute-start(bf16[128,5120]{1,0:T(8,128)(2,1)} %dynamic-slice_bitcast_fusion), channel_id=1, source_target_pairs={{0,5},{1,1},{2,4},{3,0},{4,7},{5,3},{6,6},{7,2},{8,13},{9,9},{10,1... | collective-permute-start | bytes 3932168 | tf_op jit(solution)/shard_map/ppermute | solution.py:383
  142.4 16.4 %collective-permute-start.13 = (bf16[128,5120]{1,0:T(8,128)(2,1)}, bf16[128,5120]{1,0:T(8,128)(2,1)}, u32[]{:S(2)}, u32[]{:S(2)}) collective-permute-start(bf16[128,5120]{1,0:T(8,128)(2,1)} %collective-permute-done.8.refs_3_), channel_id=1, source_target_pairs={{0,4},{4,0},{1,5},{5,1},{2,6},{6,2},{3,7},{7,3},{8,12},{12,8},{9,1... | collective-permute-start | bytes 3932168 | tf_op jit(solution)/shard_map/ppermute | solution.py:387
  142.5 13.3 %collective-permute-start.11 = (bf16[128,5120]{1,0:T(8,128)(2,1)}, bf16[128,5120]{1,0:T(8,128)(2,1)}, u32[]{:S(2)}, u32[]{:S(2)}) collective-permute-start(bf16[128,5120]{1,0:T(8,128)(2,1)} %collective-permute-done.7.refs_2_), channel_id=1, source_target_pairs={{0,4},{4,0},{1,5},{5,1},{2,6},{6,2},{3,7},{7,3},{8,12},{12,8},{9,1... | collective-permute-start | bytes 3932168 | tf_op jit(solution)/shard_map/ppermute | solution.py:387
  158.4 3.5 %collective-permute-start.14 = (bf16[128,5120]{1,0:T(8,128)(2,1)}, bf16[128,5120]{1,0:T(8,128)(2,1)S(1)}, u32[]{:S(2)}, u32[]{:S(2)}) collective-permute-start(bf16[128,5120]{1,0:T(8,128)(2,1)} %collective-permute-done.9.refs_4_), channel_id=1, source_target_pairs={{0,4},{4,0},{1,5},{5,1},{2,6},{6,2},{3,7},{7,3},{8,12},{12,8},{9,1... | collective-permute-start | bytes 3932168 | tf_op jit(solution)/shard_map/ppermute | solution.py:387
  182.0 34.7 %collective-permute-start.19 = (bf16[4,160,640]{2,1,0:T(8,128)(2,1)}, bf16[4,160,640]{2,1,0:T(8,128)(2,1)}, u32[]{:S(2)}, u32[]{:S(2)}) collective-permute-start(bf16[4,160,640]{2,1,0:T(8,128)(2,1)} %get-tuple-element.60), channel_id=1, source_target_pairs={{0,16},{8,24},{16,0},{24,8},{1,17},{9,25},{17,1},{25,9},{2,18},{10... | collective-permute-start | bytes 2457608 | tf_op jit(solution)/shard_map/ppermute | solution.py:392
  185.1 36.7 %collective-permute-start.20 = (bf16[4,160,640]{2,1,0:T(8,128)(2,1)}, bf16[4,160,640]{2,1,0:T(8,128)(2,1)}, u32[]{:S(2)}, u32[]{:S(2)}) collective-permute-start(bf16[4,160,640]{2,1,0:T(8,128)(2,1)} %get-tuple-element.61), channel_id=1, source_target_pairs={{0,8},{8,16},{16,24},{24,0},{1,9},{9,17},{17,25},{25,1},{2,10},{10... | collective-permute-start | bytes 2457608 | tf_op jit(solution)/shard_map/ppermute | solution.py:392
  185.7 36.2 %collective-permute-start.21 = (bf16[4,160,640]{2,1,0:T(8,128)(2,1)}, bf16[4,160,640]{2,1,0:T(8,128)(2,1)}, u32[]{:S(2)}, u32[]{:S(2)}) collective-permute-start(bf16[4,160,640]{2,1,0:T(8,128)(2,1)} %get-tuple-element.62), channel_id=1, source_target_pairs={{0,24},{8,0},{16,8},{24,16},{1,25},{9,1},{17,9},{25,17},{2,26},{10... | collective-permute-start | bytes 2457608 | tf_op jit(solution)/shard_map/ppermute | solution.py:392
  213.0 19.5 %collective-permute-start.15 = (bf16[3,256,640]{2,1,0:T(8,128)(2,1)}, bf16[3,256,640]{2,1,0:T(8,128)(2,1)}, u32[]{:S(2)}, u32[]{:S(2)}) collective-permute-start(bf16[3,256,640]{2,1,0:T(8,128)(2,1)} %get-tuple-element.53), channel_id=1, source_target_pairs={{0,0},{4,1},{1,2},{5,3},{2,4},{6,5},{3,6},{7,7},{8,8},{12,9},{9,10... | collective-permute-start | bytes 2949128 | tf_op jit(solution)/shard_map/ppermute | solution.py:383
  214.9 25.7 %collective-permute-start.17 = (bf16[3,256,640]{2,1,0:T(8,128)(2,1)}, bf16[3,256,640]{2,1,0:T(8,128)(2,1)}, u32[]{:S(2)}, u32[]{:S(2)}) collective-permute-start(bf16[3,256,640]{2,1,0:T(8,128)(2,1)} %get-tuple-element.55), channel_id=1, source_target_pairs={{1,0},{5,1},{0,2},{4,3},{3,4},{7,5},{2,6},{6,7},{9,8},{13,9},{8,10... | collective-permute-start | bytes 2949128 | tf_op jit(solution)/shard_map/ppermute | solution.py:383
  241.5 13.0 %collective-permute-start.24 = (bf16[160,640]{1,0:T(8,128)(2,1)}, bf16[160,640]{1,0:T(8,128)(2,1)S(1)}, u32[]{:S(2)}, u32[]{:S(2)}) collective-permute-start(bf16[160,640]{1,0:T(8,128)(2,1)} %get-tuple-element.74), channel_id=1, source_target_pairs={{0,96},{32,0},{64,32},{96,64},{1,97},{33,1},{65,33},{97,65},{2,98}... | collective-permute-start | bytes 614408 | tf_op jit(solution)/shard_map/ppermute | solution.py:392
  245.2 12.6 %collective-permute-start.23 = (bf16[160,640]{1,0:T(8,128)(2,1)}, bf16[160,640]{1,0:T(8,128)(2,1)S(1)}, u32[]{:S(2)}, u32[]{:S(2)}) collective-permute-start(bf16[160,640]{1,0:T(8,128)(2,1)} %get-tuple-element.75), channel_id=1, source_target_pairs={{0,32},{32,64},{64,96},{96,0},{1,33},{33,65},{65,97},{97,1},{2,34}... | collective-permute-start | bytes 614408 | tf_op jit(solution)/shard_map/ppermute | solution.py:392
  245.2 12.6 %collective-permute-start.22 = (bf16[160,640]{1,0:T(8,128)(2,1)}, bf16[160,640]{1,0:T(8,128)(2,1)}, u32[]{:S(2)}, u32[]{:S(2)}) collective-permute-start(bf16[160,640]{1,0:T(8,128)(2,1)} %get-tuple-element.73), channel_id=1, source_target_pairs={{0,64},{32,96},{64,0},{96,32},{1,65},{33,97},{65,1},{97,33},{2,66}... | collective-permute-start | bytes 614408 | tf_op jit(solution)/shard_map/ppermute | solution.py:392
  247.1 27.7 %collective-permute-start.16 = (bf16[3,256,640]{2,1,0:T(8,128)(2,1)S(1)}, bf16[3,256,640]{2,1,0:T(8,128)(2,1)}, u32[]{:S(2)}, u32[]{:S(2)}) collective-permute-start(bf16[3,256,640]{2,1,0:T(8,128)(2,1)S(1)} %copy-done.4), channel_id=1, source_target_pairs={{4,0},{0,1},{5,2},{1,3},{6,4},{2,5},{7,6},{3,7},{12,8},{8,9},{13,1... | collective-permute-start | bytes 2949128 | tf_op jit(solution)/shard_map/ppermute | solution.py:383
  247.1 29.2 %collective-permute-start.18 = (bf16[3,256,640]{2,1,0:T(8,128)(2,1)S(1)}, bf16[3,256,640]{2,1,0:T(8,128)(2,1)}, u32[]{:S(2)}, u32[]{:S(2)}) collective-permute-start(bf16[3,256,640]{2,1,0:T(8,128)(2,1)S(1)} %get-tuple-element.56), channel_id=1, source_target_pairs={{5,0},{1,1},{4,2},{0,3},{7,4},{3,5},{6,6},{2,7},{13,8},{9,9},{12,1... | collective-permute-start | bytes 2949128 | tf_op jit(solution)/shard_map/ppermute | solution.py:383
  254.5 6.4 %collective-permute-start.27 = (bf16[160,640]{1,0:T(8,128)(2,1)}, bf16[160,640]{1,0:T(8,128)(2,1)}, u32[]{:S(2)}, u32[]{:S(2)}) collective-permute-start(bf16[160,640]{1,0:T(8,128)(2,1)} %get-tuple-element.77), channel_id=1, source_target_pairs={{0,24},{8,0},{16,8},{24,16},{1,25},{9,1},{17,9},{25,17},{2,26},{10... | collective-permute-start | bytes 614408 | tf_op jit(solution)/shard_map/ppermute | solution.py:392
  257.8 12.0 %collective-permute-start.26 = (bf16[160,640]{1,0:T(8,128)(2,1)}, bf16[160,640]{1,0:T(8,128)(2,1)}, u32[]{:S(2)}, u32[]{:S(2)}) collective-permute-start(bf16[160,640]{1,0:T(8,128)(2,1)} %get-tuple-element.78), channel_id=1, source_target_pairs={{0,8},{8,16},{16,24},{24,0},{1,9},{9,17},{17,25},{25,1},{2,10},{10... | collective-permute-start | bytes 614408 | tf_op jit(solution)/shard_map/ppermute | solution.py:392
  257.8 12.0 %collective-permute-start.25 = (bf16[160,640]{1,0:T(8,128)(2,1)}, bf16[160,640]{1,0:T(8,128)(2,1)}, u32[]{:S(2)}, u32[]{:S(2)}) collective-permute-start(bf16[160,640]{1,0:T(8,128)(2,1)} %get-tuple-element.76), channel_id=1, source_target_pairs={{0,16},{8,24},{16,0},{24,8},{1,17},{9,25},{17,1},{25,9},{2,18},{10... | collective-permute-start | bytes 614408 | tf_op jit(solution)/shard_map/ppermute | solution.py:392
  272.0 10.6 %collective-permute-start.29 = (bf16[160,640]{1,0:T(8,128)(2,1)S(1)}, bf16[160,640]{1,0:T(8,128)(2,1)S(1)}, u32[]{:S(2)}, u32[]{:S(2)}) collective-permute-start(bf16[160,640]{1,0:T(8,128)(2,1)S(1)} %broadcast_select_fusion), channel_id=1, source_target_pairs={{0,4},{1,6},{2,0},{3,2},{4,5},{5,7},{6,1},{7,3},{8,12},{9,14},{10,... | collective-permute-start | bytes 614408 | tf_op jit(solution)/shard_map/ppermute | solution.py:383
  272.1 10.5 %collective-permute-start.28 = (bf16[160,640]{1,0:T(8,128)(2,1)}, bf16[160,640]{1,0:T(8,128)(2,1)S(1)}, u32[]{:S(2)}, u32[]{:S(2)}) collective-permute-start(bf16[160,640]{1,0:T(8,128)(2,1)} %get-tuple-element.70), channel_id=1, source_target_pairs={{0,0},{1,2},{2,4},{3,6},{4,1},{5,3},{6,5},{7,7},{8,8},{9,10},{10,1... | collective-permute-start | bytes 614408 | tf_op jit(solution)/shard_map/ppermute | solution.py:383
  (11 other events, 142.8 us)
Sparse Core Ops, SparseCore 0:
  25.1 67.9 all-gather.1
  177.6 41.8 reduce-scatter.1

commit v5 on v4

--- a/solution.py
+++ b/solution.py
@@ -17,6 +17,7 @@
 SEQ = 4
 CORES = 2
 GROUP = 4
+ORDER = (0, 3, 1, 2)
 
 
 def smem():
@@ -380,7 +381,14 @@
 
 
 def send(value, pairs):
-    return lax.ppermute(value, ("core", "seq"), pairs)
+    others = [pair for pair in pairs if pair[0] != pair[1]]
+    got = lax.ppermute(value, ("core", "seq"), others)
+    mine = [source for source, target in pairs if source == target]
+    if not mine:
+        return got
+    here = device_of(lax.axis_index("core"), lax.axis_index("seq"))
+    keep = functools.reduce(jnp.logical_or, [here == one for one in mine])
+    return jnp.where(keep, value, got)
 
 
 def swap_cores(value):
@@ -410,7 +418,7 @@
     return [take(value, here, dim)] + got
 
 
-def to_shard_holders(w_out, core, seq):
+def to_shard_holders(w_out, seq, token):
     got = []
     for other in range(2):
         pairs = []
@@ -420,6 +428,7 @@
                 pairs.append((device_of(holder, shard), device_of(shard % 2, shard // 2 + 2 * window)))
         got.append(send(w_out, pairs))
     window = seq // 2
+    got = after(got, token)
     return jnp.where(window == 0, jnp.concatenate(got), jnp.concatenate(got[::-1]))
 
 
@@ -455,37 +464,46 @@
         half = seq % 2 if round_ % 2 == 0 else 1 - seq % 2
         return take(rows_in.reshape(2, rows // 2, features), half)
 
-    own = [send(half_rows(out_grad, 0), outward(0))]
-    packs = to_rounds(place, queries, keys, values, gain_q, gain_k)
-    w_out = after(w_out, packs[0])
-    packs = [send(after(part, own[0]) if r == 3 else part, outward(r)) for r, part in enumerate(packs)]
-    ready = (packs[0], packs[1], packs[2:])
-    own += [send(half_rows(after(out_grad, ready[r - 1]), r), outward(r)) for r in range(1, SEQ)]
-    w_all = lax.all_gather(to_shard_holders(w_out, core, seq), ("z", "x"), axis=0, tiled=True)
+    parts = to_rounds(place, queries, keys, values, gain_q, gain_k)
+    w_rows = to_shard_holders(w_out, seq, parts[0])
+    w_all = lax.all_gather(w_rows, ("z", "x"), axis=0, tiled=True)
+    packs = {r: send(parts[r], outward(r)) for r in ORDER}
+    came = [packs[r] for r in ORDER]
+    own = {}
+    for r, token in zip(ORDER, (None, came[0], came[1], came[2:])):
+        own[r] = send(half_rows(out_grad if token is None else after(out_grad, token), r), outward(r))
+    packs = [packs[r] for r in range(SEQ)]
 
     def project(part):
         return jnp.dot(part, w_all, preferred_element_type=jnp.float32).astype(jnp.bfloat16)
 
     attended, probs = forward(place, tile_pairs, lens, packs)
-    other = [swap_cores(after(part, attended) if r == 2 else part) for r, part in enumerate(own[:-1])]
-    own_grads = [project(part) for part in own[:-1]]
-    other_grads = [project(part) for part in other]
-    other.append(swap_cores(after(own[-1], own_grads, other_grads[:-1])))
-    attended = after(attended, own_grads, other_grads)
-    own_grads.append(project(own[-1]))
-    other_grads.append(project(other[-1]))
+    one, two, three, last = ORDER
+    other = {one: swap_cores(own[one]), two: swap_cores(own[two]), three: swap_cores(after(own[three], attended))}
+    own_grads = {r: project(own[r]) for r in ORDER[:-1]}
+    other_grads = {r: project(other[r]) for r in ORDER[:-1]}
+    done = ([own_grads[r] for r in ORDER[:-1]], [other_grads[r] for r in ORDER[:-2]])
+    other[last] = swap_cores(after(own[last], *done))
+    attended = after(attended, *done, other_grads[three])
+    own_grads[last] = project(own[last])
+    other_grads[last] = project(other[last])
+    own, other, own_grads, other_grads = [
+        [table[r] for r in range(SEQ)] for table in (own, other, own_grads, other_grads)
+    ]
     *one, two = weight_grad(place, attended, own, other, 1.0 / (count_z * count_x * CORES), count_x)
     two = lax.psum_scatter(two, "z", scatter_dimension=0, tiled=True)
     token = one[0]
     one = [one[0]] + [shift(one[by], "x", by) for by in (2, 1, 3)]
     parts = backward(place, tile_pairs, packs, own_grads, other_grads, after(probs, token))
-    token = parts[0]
-    parts = {r: send(parts[r], inward(r)) for r in (0, 2, 1, 3)}
-    one = add(*after(one, token))
-    one = add(*scatter(after(one, parts[0], parts[2]), "z"))
-    two = add(*scatter(after(two, parts[0], parts[2]), "x"))
+    parts = {r: send(parts[r], inward(r)) for r in ORDER}
+    one = add(*after(one, parts[ORDER[0]]))
+    one = lax.psum_scatter(one, "z", scatter_dimension=0, tiled=True)[0]
+    two = scatter(after(two, parts[ORDER[0]], parts[ORDER[1]]), "x")
+    two = add(*after(two, parts[ORDER[2]], parts[ORDER[3]]))
     grad_w = to_owners((one, two), seq)
-    grad_q, grad_k, grad_v = finish(place, queries, keys, gain_q, gain_k, [parts[r] for r in range(SEQ)])
+    grad_q, grad_k, grad_v = finish(
+        place, queries, keys, gain_q, gain_k, [parts[r] for r in range(SEQ)]
+    )
     return (grad_q, grad_k, grad_v, grad_w)
 
 

time: 295 us -> 298 us (1.010)
  waiting for transfers between devices: 97.4 us -> 81.6 us
  starting transfers between devices: 75.5 us -> 89.1 us
  other arithmetic: 5.96 us -> 11.6 us
    ppermute x5, starting transfers between devices: 1.15 us -> 27.9 us  [swap_cores(): return lax.ppermute(value, 'core', [(0, 1), (1, 0)])]
    ppermute x16, waiting for transfers between devices: 76 us -> 62.6 us  [send(): got = lax.ppermute(value, ('core', 'seq'), others)]
    ppermute x16, starting transfers between devices: 59.7 us -> 49.7 us  [send(): got = lax.ppermute(value, ('core', 'seq'), others)]
    select_n x0 -> x7, other arithmetic: none -> 7.33 us  [send(): return jnp.where(keep, value, got)]
    unnamed x23 -> x53, local copies, waits for them, and re-layouts: 2.63 us -> 6.69 us
    ppermute x9 -> x6, starting transfers between devices: 14.6 us -> 11.2 us  [shift(): lax.ppermute(value, axis, [(i, (i + by) % count) for i in range(count)])]
    squeeze x6 -> x5, local copies, waits for them, and re-layouts: 7.46 us -> 5.1 us  [take(): return lax.dynamic_index_in_dim(value, index, axis, keepdims=False)]
    ppermute x9 -> x6, waiting for transfers between devices: 19.7 us -> 18.7 us  [shift(): lax.ppermute(value, axis, [(i, (i + by) % count) for i in range(count)])]
  transfers between devices with their start and end apart: 32 -> 30, of which waited for: 17 -> 14; matrix products, arithmetic and copies ran while one was open for 13% -> 15% of each run, Pallas kernels for 13% -> 14%
where the time goes in v5:
time: 298 us; the launch traced here: 293 us
  starting transfers between devices  89.1 us (30%)
  waiting for transfers between devices  81.6 us (27%)
  Pallas kernels  55.9 us (19%)
  matrix products  25.9 us (9%)
  local copies, waits for them, and re-layouts  15.1 us (5%)
  between operations  14.2 us (5%)
  other arithmetic  11.6 us (4%)
    ppermute x16, waiting for transfers between devices, send(): got = lax.ppermute(value, ('core', 'seq'), others)  62.6 us
    ppermute x16, starting transfers between devices, send(): got = lax.ppermute(value, ('core', 'seq'), others)  49.7 us
    ppermute x5, starting transfers between devices, swap_cores(): return lax.ppermute(value, 'core', [(0, 1), (1, 0)])  27.9 us
    dot_general x8, matrix products, project(): jnp.dot(part, w_all, preferred_element_type=jnp.float32)  25.9 us
    pallas_call x1, Pallas kernels, backward(): pl.pallas_call(backward_kernel, grid=(heads,), in_specs=[smem()] * 2 + [s...  19.1 us
    ppermute x6, waiting for transfers between devices, shift(): lax.ppermute(value, axis, [(i, (i + by) % count) for i in range(count)])  18.7 us
    pallas_call x1, Pallas kernels, weight_grad(): pl.pallas_call(lambda place_ref, *refs: weight_grad_kernel(place_ref, mea...  13.4 us
    pallas_call x1, Pallas kernels, forward(): pl.pallas_call(forward_kernel, grid=(heads,), in_specs=[smem()] * 3 + [sp...  11.9 us
  transfers between devices with their start and end apart: 30, of which 14 were waited for; matrix products, arithmetic and copies ran while one was open for 15% of the time, Pallas kernels for 14%

profile of v5, /device:TPU:24, one launch (start us, length us, event | category | flops | bytes accessed | tf_op | source)
XLA Modules:
  0.0 293.4 jit_solution(14460742388308403290)
XLA Ops:
  7.2 2.6 collective-permute-start.5
  13.2 5.4 %norm_rows.1 = (bf16[3,256,640]{2,1,0:T(8,128)(2,1)}, bf16[3,256,640]{2,1,0:T(8,128)(2,1)}, bf16[3,256,640]{2,1,0:T(8,128)(2,1)}, bf16[3,256,640]{2,1,0:T(8,128)(2,1)}) custom-call(s32[5]{0:T(128)} %stack.23.place_ref, bf16[256,2560]{1,0:T(8,128)(2,1)} %q_ref.3, bf16[256,2560]{1,0:T(8,128)(2,1)} %k_ref.3, bf16[256,2560]{1,0:T(8,128)(2,1)} %v_ref.1, ...), custom_call_target="tpu_custom_call" | custom-call | tf_op jit(solution)/shard_map/norm_rows/pallas_call | solution.py:61
  19.6 5.1 %collective-permute-start.3 = (bf16[3,256,640]{2,1,0:T(8,128)(2,1)}, bf16[3,256,640]{2,1,0:T(8,128)(2,1)}, u32[]{:S(2)}, u32[]{:S(2)}) collective-permute-start(bf16[3,256,640]{2,1,0:T(8,128)(2,1)} %get-tuple-element.43), channel_id=1, source_target_pairs={{0,5},{2,4},{3,0},{4,7},{5,3},{7,2},{8,13},{10,12},{11,8},{12,15},... | collective-permute-start | bytes 2949128 | tf_op jit(solution)/shard_map/ppermute | solution.py:385
  24.7 2.4 collective-permute-start
  30.9 2.5 dynamic-slice_bitcast_fusion.3
  35.3 14.3 %collective-permute-done.3 = bf16[3,256,640]{2,1,0:T(8,128)(2,1)} collective-permute-done((bf16[3,256,640]{2,1,0:T(8,128)(2,1)}, bf16[3,256,640]{2,1,0:T(8,128)(2,1)}, u32[]{:S(2)}, u32[]{:S(2)}) %collective-permute-start.3) | collective-permute-done | bytes 983072 | tf_op jit(solution)/shard_map/ppermute | solution.py:385
  53.8 12.7 %collective-permute-done.1.refs_1_.refs_5_.refs_9_ = bf16[3,256,640]{2,1,0:T(8,128)(2,1)S(1)} collective-permute-done((bf16[3,256,640]{2,1,0:T(8,128)(2,1)}, bf16[3,256,640]{2,1,0:T(8,128)(2,1)S(1)}, u32[]{:S(2)}, u32[]{:S(2)}) %collective-permute-start.1) | collective-permute-done | bytes 983072 | tf_op jit(solution)/shard_map/ppermute | solution.py:385
  66.5 2.3 collective-permute-done.2.refs_2_.refs_6_.refs_10_
  68.9 2.4 collective-permute-start.9
  74.8 11.9 %attention_forward.1 = (bf16[1024,640]{1,0:T(8,128)(2,1)S(1)}, bf16[5,4096,128]{2,1,0:T(8,128)(2,1)}) custom-call(s32[5]{0:T(128)S(1)} %copy-done.5, s32[16,8]{1,0:T(8,128)S(1)} %copy.14.pairs_ref, s32[1,16]{1,0:T(1,128)S(1)} %broadcast_select_fusion.7.lens_ref, bf16[3,256,640]{2,1,0:T(8,128)(2,1)S(1)} %broadcast_select_fusion.5.refs_0_.refs_4_.refs_8_, ...), custom_call_target="tpu_custom_call" | custom-call | tf_op jit(solution)/shard_map/attention_forward/pallas_call | solution.py:212
  87.7 27.3 %collective-permute-start.10 = (bf16[128,5120]{1,0:T(8,128)(2,1)S(1)}, bf16[128,5120]{1,0:T(8,128)(2,1)}, u32[]{:S(2)}, u32[]{:S(2)}) collective-permute-start(bf16[128,5120]{1,0:T(8,128)(2,1)S(1)} %broadcast_select_fusion.1.refs_1_), channel_id=1, source_target_pairs={{0,4},{4,0},{1,5},{5,1},{2,6},{6,2},{3,7},{7,3},{8,12},{12,8},{9,1... | collective-permute-start | bytes 3932168 | tf_op jit(solution)/shard_map/ppermute | solution.py:395
  115.0 2.9 collective-permute-done.9
  119.1 4.2 %convolution_convert_fusion.7.refs_12_ = bf16[128,640]{1,0:T(8,128)(2,1)S(1)} fusion(bf16[128,5120]{1,0:T(8,128)(2,1)S(1)} %broadcast_select_fusion.1.refs_1_, bf16[5120,640]{1,0:T(8,128)(2,1)} %all-gather.2.cloned.1.call-done), kind=kOutput, calls=%fused_computation.14 | convolution fusion | flops 838942720 | bytes 8028160 | tf_op jit(solution)/shard_map/dot_general | solution.py:478
  123.8 2.6 convolution_convert_fusion.6.refs_13_
  126.4 2.6 convolution_convert_fusion.4.refs_15_
  129.0 2.6 convolution_convert_fusion.3.refs_16_
  131.7 2.6 convolution_convert_fusion.1.refs_19_
  134.9 2.6 convolution_convert_fusion.2.refs_17_
  138.8 13.4 %weight_grad.1 = (bf16[4,160,640]{2,1,0:T(8,128)(2,1)S(1)}, bf16[4,160,640]{2,1,0:T(8,128)(2,1)S(1)}, bf16[4,160,640]{2,1,0:T(8,128)(2,1)S(1)}, bf16[4,160,640]{2,1,0:T(8,128)(2,1)S(1)}, bf16[16,160,640]{2,1,0:T(8,128)(2,1)}) custom-call(s32[5]{0:T(128)S(1)} %copy-done.5, bf16[1024,640]{1,0:T(8,128)(2,1)S(1)} %copy-done.4, ...), custom_call_target="tpu_custom_call" | custom-call | tf_op jit(solution)/shard_map/weight_grad/pallas_call | solution.py:352
  155.3 4.6 %convolution_convert_fusion.5.refs_14_ = bf16[128,640]{1,0:T(8,128)(2,1)S(1)} fusion(bf16[128,5120]{1,0:T(8,128)(2,1)} %collective-permute-done.8.refs_3_, bf16[5120,640]{1,0:T(8,128)(2,1)} %all-gather.2.cloned.1.call-done), kind=kOutput, calls=%fused_computation.12 | convolution fusion | flops 838942720 | bytes 8028160 | tf_op jit(solution)/shard_map/dot_general | solution.py:478
  159.8 4.1 %convolution_convert_fusion.refs_18_ = bf16[128,640]{1,0:T(8,128)(2,1)S(1)} fusion(bf16[128,5120]{1,0:T(8,128)(2,1)S(1)} %copy-done.18, bf16[5120,640]{1,0:T(8,128)(2,1)} %all-gather.2.cloned.1.call-done), kind=kOutput, calls=%fused_computation.7 | convolution fusion | flops 838942720 | bytes 8028160 | tf_op jit(solution)/shard_map/dot_general | solution.py:478
  164.0 19.1 %attention_backward.1 = (bf16[3,256,640]{2,1,0:T(8,128)(2,1)S(1)}, bf16[3,256,640]{2,1,0:T(8,128)(2,1)S(1)}, bf16[3,256,640]{2,1,0:T(8,128)(2,1)S(1)}, bf16[3,256,640]{2,1,0:T(8,128)(2,1)S(1)}) custom-call(s32[5]{0:T(128)S(1)} %copy-done.5, s32[16,8]{1,0:T(8,128)S(1)} %copy.14.pairs_ref, bf16[3,256,640]{2,1,0:T(8,128)(2,1)} %copy-done.1, ...), custom_call_target="tpu_custom_call" | custom-call | tf_op jit(solution)/shard_map/attention_backward/pallas_call | solution.py:306
  183.1 10.9 %collective-permute-start.15 = (bf16[3,256,640]{2,1,0:T(8,128)(2,1)S(1)}, bf16[3,256,640]{2,1,0:T(8,128)(2,1)S(1)}, u32[]{:S(2)}, u32[]{:S(2)}) collective-permute-start(bf16[3,256,640]{2,1,0:T(8,128)(2,1)S(1)} %get-tuple-element.56), channel_id=1, source_target_pairs={{4,1},{1,2},{5,3},{2,4},{6,5},{3,6},{12,9},{9,10},{13,11},{10,12},... | collective-permute-start | bytes 2949128 | tf_op jit(solution)/shard_map/ppermute | solution.py:385
  194.0 3.1 %collective-permute-start.19 = (bf16[4,160,640]{2,1,0:T(8,128)(2,1)S(1)}, bf16[4,160,640]{2,1,0:T(8,128)(2,1)S(1)}, u32[]{:S(2)}, u32[]{:S(2)}) collective-permute-start(bf16[4,160,640]{2,1,0:T(8,128)(2,1)S(1)} %copy-done.14), channel_id=1, source_target_pairs={{0,16},{8,24},{16,0},{24,8},{1,17},{9,25},{17,1},{25,9},{2,18},{10... | collective-permute-start | bytes 2457608 | tf_op jit(solution)/shard_map/ppermute | solution.py:400
  197.7 2.6 collective-permute-start.21
  200.3 8.3 %collective-permute-done.15 = bf16[3,256,640]{2,1,0:T(8,128)(2,1)S(1)} collective-permute-done((bf16[3,256,640]{2,1,0:T(8,128)(2,1)S(1)}, bf16[3,256,640]{2,1,0:T(8,128)(2,1)S(1)}, u32[]{:S(2)}, u32[]{:S(2)}) %collective-permute-start.15) | collective-permute-done | bytes 983072 | tf_op jit(solution)/shard_map/ppermute | solution.py:385
  209.8 5.1 %collective-permute-done.19 = bf16[4,160,640]{2,1,0:T(8,128)(2,1)S(1)} collective-permute-done((bf16[4,160,640]{2,1,0:T(8,128)(2,1)S(1)}, bf16[4,160,640]{2,1,0:T(8,128)(2,1)S(1)}, u32[]{:S(2)}, u32[]{:S(2)}) %collective-permute-start.19) | collective-permute-done | bytes 819232 | tf_op jit(solution)/shard_map/ppermute | solution.py:400
  214.9 8.6 %collective-permute-done.20 = bf16[4,160,640]{2,1,0:T(8,128)(2,1)S(1)} collective-permute-done((bf16[4,160,640]{2,1,0:T(8,128)(2,1)S(1)}, bf16[4,160,640]{2,1,0:T(8,128)(2,1)S(1)}, u32[]{:S(2)}, u32[]{:S(2)}) %collective-permute-start.20) | collective-permute-done | bytes 819232 | tf_op jit(solution)/shard_map/ppermute | solution.py:400
  225.1 14.4 %collective-permute-start.18 = (bf16[3,256,640]{2,1,0:T(8,128)(2,1)S(1)}, bf16[3,256,640]{2,1,0:T(8,128)(2,1)}, u32[]{:S(2)}, u32[]{:S(2)}) collective-permute-start(bf16[3,256,640]{2,1,0:T(8,128)(2,1)S(1)} %get-tuple-element.59), channel_id=1, source_target_pairs={{5,0},{4,2},{0,3},{7,4},{3,5},{2,7},{13,8},{12,10},{8,11},{15,12},... | collective-permute-start | bytes 2949128 | tf_op jit(solution)/shard_map/ppermute | solution.py:385
  240.3 21.5 %collective-permute-done.18 = bf16[3,256,640]{2,1,0:T(8,128)(2,1)} collective-permute-done((bf16[3,256,640]{2,1,0:T(8,128)(2,1)S(1)}, bf16[3,256,640]{2,1,0:T(8,128)(2,1)}, u32[]{:S(2)}, u32[]{:S(2)}) %collective-permute-start.18) | collective-permute-done | bytes 983072 | tf_op jit(solution)/shard_map/ppermute | solution.py:385
  270.2 2.5 collective-permute-done.22
  279.4 6.1 %norm_back.1 = (bf16[256,2560]{1,0:T(8,128)(2,1)}, bf16[256,2560]{1,0:T(8,128)(2,1)}, bf16[256,2560]{1,0:T(8,128)(2,1)}) custom-call(s32[5]{0:T(128)} %stack.23.place_ref, bf16[256,2560]{1,0:T(8,128)(2,1)} %q_ref.3, bf16[256,2560]{1,0:T(8,128)(2,1)} %k_ref.3, f32[1,2560]{1,0:T(1,128)} %reshape.28.gain_q_ref, f32[1,2560]{1,0:T(1,128)} %reshape.29.gain_k_ref, ...), custom_call_target="tpu_custom_call" | custom-call | tf_op jit(solution)/shard_map/norm_back/pallas_call | solution.py:93
  (118 shorter events, 45.9 us)
Async XLA Ops:
  7.2 111.9 %all-gather.2.cloned.1.call-start = ((), (), s32[]{:S(2)}) async-start(), calls=%async_computation.2 | async-start | bytes 6963200 | tf_op jit(solution)/shard_map/all_gather | solution.py:469
  7.2 11.4 %collective-permute-start.5 = (bf16[160,640]{1,0:T(8,128)(2,1)}, bf16[160,640]{1,0:T(8,128)(2,1)S(1)}, u32[]{:S(2)}, u32[]{:S(2)}) collective-permute-start(bf16[160,640]{1,0:T(8,128)(2,1)} %param.17), channel_id=1, source_target_pairs={{1,4},{2,1},{3,5},{4,2},{5,6},{6,3},{9,12},{10,9},{11,13},{12,10},... | collective-permute-start | bytes 614408 | tf_op jit(solution)/shard_map/ppermute | solution.py:385
  9.8 8.9 %collective-permute-start.6 = (bf16[160,640]{1,0:T(8,128)(2,1)}, bf16[160,640]{1,0:T(8,128)(2,1)S(1)}, u32[]{:S(2)}, u32[]{:S(2)}) collective-permute-start(bf16[160,640]{1,0:T(8,128)(2,1)} %param.17), channel_id=1, source_target_pairs={{0,2},{1,6},{2,3},{3,7},{4,0},{5,4},{6,1},{7,5},{8,10},{9,14},{10,... | collective-permute-start | bytes 614408 | tf_op jit(solution)/shard_map/ppermute | solution.py:385
  19.6 244.4 %reduce-scatter.5.cloned.1.call-start = ((), (), s32[]{:S(2)}) async-start(), calls=%async_computation.4 | async-start | bytes 4096000 | tf_op jit(solution)/shard_map/reduce_scatter | solution.py:494
  19.6 30.0 %collective-permute-start.3 = (bf16[3,256,640]{2,1,0:T(8,128)(2,1)}, bf16[3,256,640]{2,1,0:T(8,128)(2,1)}, u32[]{:S(2)}, u32[]{:S(2)}) collective-permute-start(bf16[3,256,640]{2,1,0:T(8,128)(2,1)} %get-tuple-element.43), channel_id=1, source_target_pairs={{0,5},{2,4},{3,0},{4,7},{5,3},{7,2},{8,13},{10,12},{11,8},{12,15},... | collective-permute-start | bytes 2949128 | tf_op jit(solution)/shard_map/ppermute | solution.py:385
  24.7 26.4 %collective-permute-start = (bf16[3,256,640]{2,1,0:T(8,128)(2,1)S(1)}, bf16[3,256,640]{2,1,0:T(8,128)(2,1)}, u32[]{:S(2)}, u32[]{:S(2)}) collective-permute-start(bf16[3,256,640]{2,1,0:T(8,128)(2,1)S(1)} %copy-done.20), channel_id=1, source_target_pairs={{1,4},{2,1},{3,5},{4,2},{5,6},{6,3},{9,12},{10,9},{11,13},{12,10},... | collective-permute-start | bytes 2949128 | tf_op jit(solution)/shard_map/ppermute | solution.py:385
  27.1 39.4 %collective-permute-start.1 = (bf16[3,256,640]{2,1,0:T(8,128)(2,1)}, bf16[3,256,640]{2,1,0:T(8,128)(2,1)S(1)}, u32[]{:S(2)}, u32[]{:S(2)}) collective-permute-start(bf16[3,256,640]{2,1,0:T(8,128)(2,1)} %get-tuple-element.41), channel_id=1, source_target_pairs={{0,4},{1,0},{2,5},{3,1},{4,6},{5,2},{6,7},{7,3},{8,12},{9,8},{10,1... | collective-permute-start | bytes 2949128 | tf_op jit(solution)/shard_map/ppermute | solution.py:385
  29.0 39.9 %collective-permute-start.2 = (bf16[3,256,640]{2,1,0:T(8,128)(2,1)}, bf16[3,256,640]{2,1,0:T(8,128)(2,1)}, u32[]{:S(2)}, u32[]{:S(2)}) collective-permute-start(bf16[3,256,640]{2,1,0:T(8,128)(2,1)} %get-tuple-element.42), channel_id=1, source_target_pairs={{0,1},{1,5},{2,0},{3,4},{4,3},{5,7},{6,2},{7,6},{8,9},{9,13},{10,8... | collective-permute-start | bytes 2949128 | tf_op jit(solution)/shard_map/ppermute | solution.py:385
  30.9 2.5 collective-permute-start.11
  33.4 53.2 %collective-permute-start.4 = (bf16[128,5120]{1,0:T(8,128)(2,1)}, bf16[128,5120]{1,0:T(8,128)(2,1)S(1)}, u32[]{:S(2)}, u32[]{:S(2)}) collective-permute-start(bf16[128,5120]{1,0:T(8,128)(2,1)} %dynamic-slice_bitcast_fusion.3), channel_id=1, source_target_pairs={{1,4},{2,1},{3,5},{4,2},{5,6},{6,3},{9,12},{10,9},{11,13},{12,10},... | collective-permute-start | bytes 3932168 | tf_op jit(solution)/shard_map/ppermute | solution.py:385
  51.0 63.9 %collective-permute-start.7 = (bf16[128,5120]{1,0:T(8,128)(2,1)S(1)}, bf16[128,5120]{1,0:T(8,128)(2,1)}, u32[]{:S(2)}, u32[]{:S(2)}) collective-permute-start(bf16[128,5120]{1,0:T(8,128)(2,1)S(1)} %dynamic-slice_bitcast_fusion.2), channel_id=1, source_target_pairs={{0,4},{1,0},{2,5},{3,1},{4,6},{5,2},{6,7},{7,3},{8,12},{9,8},{10,1... | collective-permute-start | bytes 3932168 | tf_op jit(solution)/shard_map/ppermute | solution.py:385
  68.9 48.9 %collective-permute-start.9 = (bf16[128,5120]{1,0:T(8,128)(2,1)S(1)}, bf16[128,5120]{1,0:T(8,128)(2,1)S(1)}, u32[]{:S(2)}, u32[]{:S(2)}) collective-permute-start(bf16[128,5120]{1,0:T(8,128)(2,1)S(1)} %dynamic-slice_bitcast_fusion), channel_id=1, source_target_pairs={{0,5},{2,4},{3,0},{4,7},{5,3},{7,2},{8,13},{10,12},{11,8},{12,15},... | collective-permute-start | bytes 3932168 | tf_op jit(solution)/shard_map/ppermute | solution.py:385
  72.5 61.8 %collective-permute-start.8 = (bf16[128,5120]{1,0:T(8,128)(2,1)}, bf16[128,5120]{1,0:T(8,128)(2,1)}, u32[]{:S(2)}, u32[]{:S(2)}) collective-permute-start(bf16[128,5120]{1,0:T(8,128)(2,1)} %dynamic-slice_bitcast_fusion.1), channel_id=1, source_target_pairs={{0,1},{1,5},{2,0},{3,4},{4,3},{5,7},{6,2},{7,6},{8,9},{9,13},{10,8... | collective-permute-start | bytes 3932168 | tf_op jit(solution)/shard_map/ppermute | solution.py:385
  87.7 41.3 %collective-permute-start.10 = (bf16[128,5120]{1,0:T(8,128)(2,1)S(1)}, bf16[128,5120]{1,0:T(8,128)(2,1)}, u32[]{:S(2)}, u32[]{:S(2)}) collective-permute-start(bf16[128,5120]{1,0:T(8,128)(2,1)S(1)} %broadcast_select_fusion.1.refs_1_), channel_id=1, source_target_pairs={{0,4},{4,0},{1,5},{5,1},{2,6},{6,2},{3,7},{7,3},{8,12},{12,8},{9,1... | collective-permute-start | bytes 3932168 | tf_op jit(solution)/shard_map/ppermute | solution.py:395
  115.0 19.9 %collective-permute-start.12 = (bf16[128,5120]{1,0:T(8,128)(2,1)}, bf16[128,5120]{1,0:T(8,128)(2,1)}, u32[]{:S(2)}, u32[]{:S(2)}) collective-permute-start(bf16[128,5120]{1,0:T(8,128)(2,1)} %collective-permute-done.7.refs_2_), channel_id=1, source_target_pairs={{0,4},{4,0},{1,5},{5,1},{2,6},{6,2},{3,7},{7,3},{8,12},{12,8},{9,1... | collective-permute-start | bytes 3932168 | tf_op jit(solution)/shard_map/ppermute | solution.py:395
  119.1 12.6 %collective-permute-start.13 = (bf16[128,5120]{1,0:T(8,128)(2,1)}, bf16[128,5120]{1,0:T(8,128)(2,1)}, u32[]{:S(2)}, u32[]{:S(2)}) collective-permute-start(bf16[128,5120]{1,0:T(8,128)(2,1)} %broadcast_select_fusion.refs_4_), channel_id=1, source_target_pairs={{0,4},{4,0},{1,5},{5,1},{2,6},{6,2},{3,7},{7,3},{8,12},{12,8},{9,1... | collective-permute-start | bytes 3932168 | tf_op jit(solution)/shard_map/ppermute | solution.py:395
  134.3 3.4 %collective-permute-start.14 = (bf16[128,5120]{1,0:T(8,128)(2,1)}, bf16[128,5120]{1,0:T(8,128)(2,1)S(1)}, u32[]{:S(2)}, u32[]{:S(2)}) collective-permute-start(bf16[128,5120]{1,0:T(8,128)(2,1)} %collective-permute-done.8.refs_3_), channel_id=1, source_target_pairs={{0,4},{4,0},{1,5},{5,1},{2,6},{6,2},{3,7},{7,3},{8,12},{12,8},{9,1... | collective-permute-start | bytes 3932168 | tf_op jit(solution)/shard_map/ppermute | solution.py:395
  155.0 120.0 %reduce-scatter.3.cloned.1.call-start = ((), (), s32[]{:S(2)}) async-start(), calls=%async_computation.3 | async-start | bytes 1024000 | tf_op jit(solution)/shard_map/reduce_scatter | solution.py:500
  163.9 33.2 %copy-start.12 = (bf16[4,160,640]{2,1,0:T(8,128)(2,1)S(1)}, bf16[4,160,640]{2,1,0:T(8,128)(2,1)}, u32[]{:S(2)}) copy-start(bf16[4,160,640]{2,1,0:T(8,128)(2,1)} %copy-done.11) | copy-start | bytes 2457604
  164.0 33.8 %copy-start.10 = (bf16[4,160,640]{2,1,0:T(8,128)(2,1)S(1)}, bf16[4,160,640]{2,1,0:T(8,128)(2,1)}, u32[]{:S(2)}) copy-start(bf16[4,160,640]{2,1,0:T(8,128)(2,1)} %copy-done.9) | copy-start | bytes 2457604
  183.1 25.6 %collective-permute-start.15 = (bf16[3,256,640]{2,1,0:T(8,128)(2,1)S(1)}, bf16[3,256,640]{2,1,0:T(8,128)(2,1)S(1)}, u32[]{:S(2)}, u32[]{:S(2)}) collective-permute-start(bf16[3,256,640]{2,1,0:T(8,128)(2,1)S(1)} %get-tuple-element.56), channel_id=1, source_target_pairs={{4,1},{1,2},{5,3},{2,4},{6,5},{3,6},{12,9},{9,10},{13,11},{10,12},... | collective-permute-start | bytes 2949128 | tf_op jit(solution)/shard_map/ppermute | solution.py:385
  194.0 20.9 %collective-permute-start.19 = (bf16[4,160,640]{2,1,0:T(8,128)(2,1)S(1)}, bf16[4,160,640]{2,1,0:T(8,128)(2,1)S(1)}, u32[]{:S(2)}, u32[]{:S(2)}) collective-permute-start(bf16[4,160,640]{2,1,0:T(8,128)(2,1)S(1)} %copy-done.14), channel_id=1, source_target_pairs={{0,16},{8,24},{16,0},{24,8},{1,17},{9,25},{17,1},{25,9},{2,18},{10... | collective-permute-start | bytes 2457608 | tf_op jit(solution)/shard_map/ppermute | solution.py:400
  197.1 26.4 %collective-permute-start.20 = (bf16[4,160,640]{2,1,0:T(8,128)(2,1)S(1)}, bf16[4,160,640]{2,1,0:T(8,128)(2,1)S(1)}, u32[]{:S(2)}, u32[]{:S(2)}) collective-permute-start(bf16[4,160,640]{2,1,0:T(8,128)(2,1)S(1)} %copy-done.12), channel_id=1, source_target_pairs={{0,8},{8,16},{16,24},{24,0},{1,9},{9,17},{17,25},{25,1},{2,10},{10... | collective-permute-start | bytes 2457608 | tf_op jit(solution)/shard_map/ppermute | solution.py:400
  197.7 26.0 %collective-permute-start.21 = (bf16[4,160,640]{2,1,0:T(8,128)(2,1)S(1)}, bf16[4,160,640]{2,1,0:T(8,128)(2,1)S(1)}, u32[]{:S(2)}, u32[]{:S(2)}) collective-permute-start(bf16[4,160,640]{2,1,0:T(8,128)(2,1)S(1)} %copy-done.10), channel_id=1, source_target_pairs={{0,24},{8,0},{16,8},{24,16},{1,25},{9,1},{17,9},{25,17},{2,26},{10... | collective-permute-start | bytes 2457608 | tf_op jit(solution)/shard_map/ppermute | solution.py:400
  225.1 36.7 %collective-permute-start.18 = (bf16[3,256,640]{2,1,0:T(8,128)(2,1)S(1)}, bf16[3,256,640]{2,1,0:T(8,128)(2,1)}, u32[]{:S(2)}, u32[]{:S(2)}) collective-permute-start(bf16[3,256,640]{2,1,0:T(8,128)(2,1)S(1)} %get-tuple-element.59), channel_id=1, source_target_pairs={{5,0},{4,2},{0,3},{7,4},{3,5},{2,7},{13,8},{12,10},{8,11},{15,12},... | collective-permute-start | bytes 2949128 | tf_op jit(solution)/shard_map/ppermute | solution.py:385
  239.5 30.7 %collective-permute-start.16 = (bf16[3,256,640]{2,1,0:T(8,128)(2,1)}, bf16[3,256,640]{2,1,0:T(8,128)(2,1)S(1)}, u32[]{:S(2)}, u32[]{:S(2)}) collective-permute-start(bf16[3,256,640]{2,1,0:T(8,128)(2,1)} %copy-done.8), channel_id=1, source_target_pairs={{4,0},{0,1},{5,2},{1,3},{6,4},{2,5},{7,6},{3,7},{12,8},{8,9},{13,1... | collective-permute-start | bytes 2949128 | tf_op jit(solution)/shard_map/ppermute | solution.py:385
  239.6 30.6 %collective-permute-start.17 = (bf16[3,256,640]{2,1,0:T(8,128)(2,1)S(1)}, bf16[3,256,640]{2,1,0:T(8,128)(2,1)}, u32[]{:S(2)}, u32[]{:S(2)}) collective-permute-start(bf16[3,256,640]{2,1,0:T(8,128)(2,1)S(1)} %copy-done.7), channel_id=1, source_target_pairs={{1,0},{5,1},{0,2},{4,3},{3,4},{7,5},{2,6},{6,7},{9,8},{13,9},{8,10... | collective-permute-start | bytes 2949128 | tf_op jit(solution)/shard_map/ppermute | solution.py:385
  265.3 7.4 %collective-permute-start.22 = (bf16[160,640]{1,0:T(8,128)(2,1)S(1)}, bf16[160,640]{1,0:T(8,128)(2,1)S(1)}, u32[]{:S(2)}, u32[]{:S(2)}) collective-permute-start(bf16[160,640]{1,0:T(8,128)(2,1)S(1)} %get-tuple-element.80), channel_id=1, source_target_pairs={{0,16},{8,24},{16,0},{24,8},{1,17},{9,25},{17,1},{25,9},{2,18},{10... | collective-permute-start | bytes 614408 | tf_op jit(solution)/shard_map/ppermute | solution.py:400
  267.0 7.9 %collective-permute-start.23 = (bf16[160,640]{1,0:T(8,128)(2,1)S(1)}, bf16[160,640]{1,0:T(8,128)(2,1)S(1)}, u32[]{:S(2)}, u32[]{:S(2)}) collective-permute-start(bf16[160,640]{1,0:T(8,128)(2,1)S(1)} %get-tuple-element.79), channel_id=1, source_target_pairs={{0,8},{8,16},{16,24},{24,0},{1,9},{9,17},{17,25},{25,1},{2,10},{10... | collective-permute-start | bytes 614408 | tf_op jit(solution)/shard_map/ppermute | solution.py:400
  269.0 6.0 %collective-permute-start.24 = (bf16[160,640]{1,0:T(8,128)(2,1)S(1)}, bf16[160,640]{1,0:T(8,128)(2,1)}, u32[]{:S(2)}, u32[]{:S(2)}) collective-permute-start(bf16[160,640]{1,0:T(8,128)(2,1)S(1)} %get-tuple-element.78), channel_id=1, source_target_pairs={{0,24},{8,0},{16,8},{24,16},{1,25},{9,1},{17,9},{25,17},{2,26},{10... | collective-permute-start | bytes 614408 | tf_op jit(solution)/shard_map/ppermute | solution.py:400
  276.3 9.2 %collective-permute-start.26 = (bf16[160,640]{1,0:T(8,128)(2,1)S(1)}, bf16[160,640]{1,0:T(8,128)(2,1)S(1)}, u32[]{:S(2)}, u32[]{:S(2)}) collective-permute-start(bf16[160,640]{1,0:T(8,128)(2,1)S(1)} %bitcast_select_fusion), channel_id=1, source_target_pairs={{0,4},{1,6},{2,0},{3,2},{4,5},{5,7},{6,1},{7,3},{8,12},{9,14},{10,... | collective-permute-start | bytes 614408 | tf_op jit(solution)/shard_map/ppermute | solution.py:385
  277.5 8.6 %collective-permute-start.25 = (bf16[160,640]{1,0:T(8,128)(2,1)S(1)}, bf16[160,640]{1,0:T(8,128)(2,1)S(1)}, u32[]{:S(2)}, u32[]{:S(2)}) collective-permute-start(bf16[160,640]{1,0:T(8,128)(2,1)S(1)} %get-tuple-element.76), channel_id=1, source_target_pairs={{1,2},{2,4},{3,6},{4,1},{5,3},{6,5},{9,10},{10,12},{11,14},{12,9},... | collective-permute-start | bytes 614408 | tf_op jit(solution)/shard_map/ppermute | solution.py:385
  (24 other events, 251.9 us)
Sparse Core Ops, SparseCore 0:
  19.7 66.0 all-gather.1
  155.1 50.4 reduce-scatter.4
  225.2 35.1 reduce-scatter.2

commit v6 on v5

--- a/solution.py
+++ b/solution.py
@@ -46,7 +46,7 @@
     outs, normed = refs[:-1], refs[-1]
     for at, (x_ref, gain_ref) in enumerate(((q_ref, gain_q_ref), (k_ref, gain_k_ref))):
         values_f = x_ref[...].astype(jnp.float32)
-        normed[at] = (values_f * row_scale_of(values_f) * gain_ref[...]).astype(jnp.bfloat16)
+        normed[at] = (values_f * row_scale_of(values_f) * gain_ref[...][None, :]).astype(jnp.bfloat16)
     for round_, out in enumerate(outs):
         columns = shard_of(place_ref, round_, out.shape[2])
         out[0] = normed[0, :, columns]
@@ -57,7 +57,7 @@
 def to_rounds(place, queries, keys, values, gain_q, gain_k, block=64):
     rows, width = queries.shape
     row_spec = pl.BlockSpec((block, width), lambda i: (i, 0))
-    gain_spec = pl.BlockSpec((1, width), lambda i: (0, 0))
+    gain_spec = pl.BlockSpec((width,), lambda i: (0,))
     return pl.pallas_call(
         rounds_kernel,
         grid=(rows // block,),
@@ -66,7 +66,7 @@
         out_shape=[jax.ShapeDtypeStruct((3, rows, width // SEQ), jnp.bfloat16)] * SEQ,
         scratch_shapes=[pltpu.VMEM((2, block, width), jnp.bfloat16)],
         name="norm_rows",
-    )(place, queries, keys, values, gain_q.reshape(1, width), gain_k.reshape(1, width))
+    )(place, queries, keys, values, gain_q, gain_k)
 
 
 def finish_kernel(place_ref, q_ref, k_ref, gain_q_ref, gain_k_ref, *refs):
@@ -80,7 +80,7 @@
     for at, (x_ref, gain_ref) in enumerate(((q_ref, gain_q_ref), (k_ref, gain_k_ref))):
         values_f = x_ref[...].astype(jnp.float32)
         row_scale = row_scale_of(values_f)
-        gated = gain_ref[...] * joined[at].astype(jnp.float32)
+        gated = gain_ref[...][None, :] * joined[at].astype(jnp.float32)
         inner = jnp.sum(gated * values_f, axis=-1, keepdims=True)
         back = values_f * (row_scale * row_scale * row_scale * inner * (1.0 / width))
         outs[at][...] = (row_scale * gated - back).astype(jnp.bfloat16)
@@ -89,7 +89,7 @@
 def finish(place, queries, keys, gain_q, gain_k, parts, block=64):
     rows, width = queries.shape
     row_spec = pl.BlockSpec((block, width), lambda i: (i, 0))
-    gain_spec = pl.BlockSpec((1, width), lambda i: (0, 0))
+    gain_spec = pl.BlockSpec((width,), lambda i: (0,))
     return pl.pallas_call(
         finish_kernel,
         grid=(rows // block,),
@@ -101,7 +101,7 @@
         out_shape=[jax.ShapeDtypeStruct((rows, width), jnp.bfloat16)] * 3,
         scratch_shapes=[pltpu.VMEM((2, block, width), jnp.bfloat16)],
         name="norm_back",
-    )(place, queries, keys, gain_q.reshape(1, width), gain_k.reshape(1, width), *parts)
+    )(place, queries, keys, gain_q, gain_k, *parts)
 
 
 def tile_at(ref, index, rows):
@@ -470,8 +470,8 @@
     packs = {r: send(parts[r], outward(r)) for r in ORDER}
     came = [packs[r] for r in ORDER]
     own = {}
-    for r, token in zip(ORDER, (None, came[0], came[1], came[2:])):
-        own[r] = send(half_rows(out_grad if token is None else after(out_grad, token), r), outward(r))
+    for r, token in zip(ORDER, came):
+        own[r] = send(half_rows(after(out_grad, token), r), outward(r))
     packs = [packs[r] for r in range(SEQ)]
 
     def project(part):
@@ -479,14 +479,16 @@
 
     attended, probs = forward(place, tile_pairs, lens, packs)
     one, two, three, last = ORDER
-    other = {one: swap_cores(own[one]), two: swap_cores(own[two]), three: swap_cores(after(own[three], attended))}
-    own_grads = {r: project(own[r]) for r in ORDER[:-1]}
-    other_grads = {r: project(other[r]) for r in ORDER[:-1]}
+    other = {one: swap_cores(own[one]), two: swap_cores(after(own[two], attended))}
+    own_grads = {one: project(own[one]), two: project(own[two])}
+    other_grads = {one: project(other[one]), two: project(other[two])}
+    other[three] = swap_cores(after(own[three], own_grads[one], other_grads[one]))
+    own_grads[three], other_grads[three] = project(own[three]), project(other[three])
     done = ([own_grads[r] for r in ORDER[:-1]], [other_grads[r] for r in ORDER[:-2]])
     other[last] = swap_cores(after(own[last], *done))
-    attended = after(attended, *done, other_grads[three])
     own_grads[last] = project(own[last])
     other_grads[last] = project(other[last])
+    attended = after(attended, own_grads, other_grads)
     own, other, own_grads, other_grads = [
         [table[r] for r in range(SEQ)] for table in (own, other, own_grads, other_grads)
     ]
@@ -495,9 +497,9 @@
     token = one[0]
     one = [one[0]] + [shift(one[by], "x", by) for by in (2, 1, 3)]
     parts = backward(place, tile_pairs, packs, own_grads, other_grads, after(probs, token))
+    one = add(*after(one, parts[0]))
+    one = lax.psum_scatter(one, "z", scatter_dimension=0, tiled=True)[0]
     parts = {r: send(parts[r], inward(r)) for r in ORDER}
-    one = add(*after(one, parts[ORDER[0]]))
-    one = lax.psum_scatter(one, "z", scatter_dimension=0, tiled=True)[0]
     two = scatter(after(two, parts[ORDER[0]], parts[ORDER[1]]), "x")
     two = add(*after(two, parts[ORDER[2]], parts[ORDER[3]]))
     grad_w = to_owners((one, two), seq)

time: 298 us -> 272 us (0.913)
  starting transfers between devices: 89.1 us -> 75 us
  waiting for transfers between devices: 81.6 us -> 75.8 us
  matrix products: 25.9 us -> 21.2 us
  local copies, waits for them, and re-layouts: 15.1 us -> 11.6 us
    ppermute x16, starting transfers between devices: 49.7 us -> 37.5 us  [send(): got = lax.ppermute(value, ('core', 'seq'), others)]
    ppermute x6, waiting for transfers between devices: 18.7 us -> 10.8 us  [shift(): lax.ppermute(value, axis, [(i, (i + by) % count) for i in range(count)])]
    dot_general x8, matrix products: 25.9 us -> 21.2 us  [project(): jnp.dot(part, w_all, preferred_element_type=jnp.float32)]
    unnamed x53 -> x49, local copies, waits for them, and re-layouts: 6.69 us -> 7.2 us
  transfers between devices with their start and end apart: 30 -> 30, of which waited for: 14 -> 14; matrix products, arithmetic and copies ran while one was open for 15% -> 12% of each run, Pallas kernels for 14% -> 16%
where the time goes in v6:
time: 272 us; the launch traced here: 267 us
  waiting for transfers between devices  75.8 us (28%)
  starting transfers between devices  75 us (28%)
  Pallas kernels  57.1 us (21%)
  matrix products  21.2 us (8%)
  between operations  14.2 us (5%)
  other arithmetic  11.7 us (4%)
  local copies, waits for them, and re-layouts  11.6 us (4%)
    ppermute x16, waiting for transfers between devices, send(): got = lax.ppermute(value, ('core', 'seq'), others)  64.2 us
    ppermute x16, starting transfers between devices, send(): got = lax.ppermute(value, ('core', 'seq'), others)  37.5 us
    ppermute x5, starting transfers between devices, swap_cores(): return lax.ppermute(value, 'core', [(0, 1), (1, 0)])  25.6 us
    dot_general x8, matrix products, project(): jnp.dot(part, w_all, preferred_element_type=jnp.float32)  21.2 us
    pallas_call x1, Pallas kernels, backward(): pl.pallas_call(backward_kernel, grid=(heads,), in_specs=[smem()] * 2 + [s...  19.5 us
    pallas_call x1, Pallas kernels, weight_grad(): pl.pallas_call(lambda place_ref, *refs: weight_grad_kernel(place_ref, mea...  14.2 us
    pallas_call x1, Pallas kernels, forward(): pl.pallas_call(forward_kernel, grid=(heads,), in_specs=[smem()] * 3 + [sp...  11.9 us
    ppermute x6, starting transfers between devices, shift(): lax.ppermute(value, axis, [(i, (i + by) % count) for i in range(count)])  11.8 us
  transfers between devices with their start and end apart: 30, of which 14 were waited for; matrix products, arithmetic and copies ran while one was open for 12% of the time, Pallas kernels for 16%

profile of v6, /device:TPU:24, one launch (start us, length us, event | category | flops | bytes accessed | tf_op | source)
XLA Modules:
  0.0 266.6 jit_solution(3930496081523193401)
XLA Ops:
  7.2 2.6 collective-permute-start.5
  10.5 5.4 %norm_rows.1 = (bf16[3,256,640]{2,1,0:T(8,128)(2,1)}, bf16[3,256,640]{2,1,0:T(8,128)(2,1)}, bf16[3,256,640]{2,1,0:T(8,128)(2,1)}, bf16[3,256,640]{2,1,0:T(8,128)(2,1)}) custom-call(s32[5]{0:T(128)} %stack.23.place_ref, bf16[256,2560]{1,0:T(8,128)(2,1)} %q_ref.3, bf16[256,2560]{1,0:T(8,128)(2,1)} %k_ref.3, bf16[256,2560]{1,0:T(8,128)(2,1)} %v_ref.1, ...), custom_call_target="tpu_custom_call" | custom-call | tf_op jit(solution)/shard_map/norm_rows/pallas_call | solution.py:61
  17.6 4.8 %collective-permute-start = (bf16[3,256,640]{2,1,0:T(8,128)(2,1)}, bf16[3,256,640]{2,1,0:T(8,128)(2,1)}, u32[]{:S(2)}, u32[]{:S(2)}) collective-permute-start(bf16[3,256,640]{2,1,0:T(8,128)(2,1)} %get-tuple-element.42), channel_id=1, source_target_pairs={{1,4},{2,1},{3,5},{4,2},{5,6},{6,3},{9,12},{10,9},{11,13},{12,10},... | collective-permute-start | bytes 2949128 | tf_op jit(solution)/shard_map/ppermute | solution.py:385
  22.4 3.4 %collective-permute-start.1 = (bf16[3,256,640]{2,1,0:T(8,128)(2,1)}, bf16[3,256,640]{2,1,0:T(8,128)(2,1)S(1)}, u32[]{:S(2)}, u32[]{:S(2)}) collective-permute-start(bf16[3,256,640]{2,1,0:T(8,128)(2,1)} %get-tuple-element.43), channel_id=1, source_target_pairs={{0,4},{1,0},{2,5},{3,1},{4,6},{5,2},{6,7},{7,3},{8,12},{9,8},{10,1... | collective-permute-start | bytes 2949128 | tf_op jit(solution)/shard_map/ppermute | solution.py:385
  26.0 2.4 collective-permute-start.3
  29.8 14.4 %collective-permute-done = bf16[3,256,640]{2,1,0:T(8,128)(2,1)} collective-permute-done((bf16[3,256,640]{2,1,0:T(8,128)(2,1)}, bf16[3,256,640]{2,1,0:T(8,128)(2,1)}, u32[]{:S(2)}, u32[]{:S(2)}) %collective-permute-start) | collective-permute-done | bytes 983072 | tf_op jit(solution)/shard_map/ppermute | solution.py:385
  45.6 5.6 %collective-permute-start.4 = (bf16[128,5120]{1,0:T(8,128)(2,1)S(1)}, bf16[128,5120]{1,0:T(8,128)(2,1)S(1)}, u32[]{:S(2)}, u32[]{:S(2)}) collective-permute-start(bf16[128,5120]{1,0:T(8,128)(2,1)S(1)} %dynamic-slice_bitcast_fusion.3), channel_id=1, source_target_pairs={{1,4},{2,1},{3,5},{4,2},{5,6},{6,3},{9,12},{10,9},{11,13},{12,10},... | collective-permute-start | bytes 3932168 | tf_op jit(solution)/shard_map/ppermute | solution.py:385
  51.2 14.0 %collective-permute-done.1.refs_1_.refs_5_.refs_9_ = bf16[3,256,640]{2,1,0:T(8,128)(2,1)S(1)} collective-permute-done((bf16[3,256,640]{2,1,0:T(8,128)(2,1)}, bf16[3,256,640]{2,1,0:T(8,128)(2,1)S(1)}, u32[]{:S(2)}, u32[]{:S(2)}) %collective-permute-start.1) | collective-permute-done | bytes 983072 | tf_op jit(solution)/shard_map/ppermute | solution.py:385
  66.4 3.9 %collective-permute-start.7 = (bf16[128,5120]{1,0:T(8,128)(2,1)}, bf16[128,5120]{1,0:T(8,128)(2,1)}, u32[]{:S(2)}, u32[]{:S(2)}) collective-permute-start(bf16[128,5120]{1,0:T(8,128)(2,1)} %dynamic-slice_bitcast_fusion.2), channel_id=1, source_target_pairs={{0,4},{1,0},{2,5},{3,1},{4,6},{5,2},{6,7},{7,3},{8,12},{9,8},{10,1... | collective-permute-start | bytes 3932168 | tf_op jit(solution)/shard_map/ppermute | solution.py:385
  72.8 3.5 %collective-permute-start.9 = (bf16[128,5120]{1,0:T(8,128)(2,1)S(1)}, bf16[128,5120]{1,0:T(8,128)(2,1)S(1)}, u32[]{:S(2)}, u32[]{:S(2)}) collective-permute-start(bf16[128,5120]{1,0:T(8,128)(2,1)S(1)} %dynamic-slice_bitcast_fusion), channel_id=1, source_target_pairs={{0,5},{2,4},{3,0},{4,7},{5,3},{7,2},{8,13},{10,12},{11,8},{12,15},... | collective-permute-start | bytes 3932168 | tf_op jit(solution)/shard_map/ppermute | solution.py:385
  79.1 11.9 %attention_forward.1 = (bf16[1024,640]{1,0:T(8,128)(2,1)S(1)}, bf16[5,4096,128]{2,1,0:T(8,128)(2,1)}) custom-call(s32[5]{0:T(128)S(1)} %copy-done.9, s32[16,8]{1,0:T(8,128)S(1)} %copy.14.pairs_ref, s32[1,16]{1,0:T(1,128)S(1)} %broadcast_select_fusion.7.lens_ref, bf16[3,256,640]{2,1,0:T(8,128)(2,1)S(1)} %broadcast_select_fusion.5.refs_0_.refs_4_.refs_8_, ...), custom_call_target="tpu_custom_call" | custom-call | tf_op jit(solution)/shard_map/attention_forward/pallas_call | solution.py:212
  92.0 24.6 %collective-permute-start.10 = (bf16[128,5120]{1,0:T(8,128)(2,1)S(1)}, bf16[128,5120]{1,0:T(8,128)(2,1)}, u32[]{:S(2)}, u32[]{:S(2)}) collective-permute-start(bf16[128,5120]{1,0:T(8,128)(2,1)S(1)} %broadcast_select_fusion.1.refs_1_), channel_id=1, source_target_pairs={{0,4},{4,0},{1,5},{5,1},{2,6},{6,2},{3,7},{7,3},{8,12},{12,8},{9,1... | collective-permute-start | bytes 3932168 | tf_op jit(solution)/shard_map/ppermute | solution.py:395
  116.6 1.9 collective-permute-done.9
  118.8 4.4 %convolution_convert_fusion.7.refs_12_ = bf16[128,640]{1,0:T(8,128)(2,1)S(1)} fusion(bf16[128,5120]{1,0:T(8,128)(2,1)S(1)} %broadcast_select_fusion.1.refs_1_, bf16[5120,640]{1,0:T(8,128)(2,1)} %all-gather.2.cloned.1.call-done), kind=kOutput, calls=%fused_computation.14 | convolution fusion | flops 838942720 | bytes 8028160 | tf_op jit(solution)/shard_map/dot_general | solution.py:478
  123.9 2.6 convolution_convert_fusion.3.refs_16_
  126.9 2.6 convolution_convert_fusion.6.refs_13_
  130.8 3.3 %convolution_convert_fusion.1.refs_19_ = bf16[128,640]{1,0:T(8,128)(2,1)} fusion(bf16[128,5120]{1,0:T(8,128)(2,1)} %collective-permute-done.13.refs_8_, bf16[5120,640]{1,0:T(8,128)(2,1)S(1)} %copy-done.12), kind=kOutput, calls=%fused_computation.8 | convolution fusion | flops 838942720 | bytes 8028160 | tf_op jit(solution)/shard_map/dot_general | solution.py:478
  135.4 3.3 %convolution_convert_fusion.5.refs_14_ = bf16[128,640]{1,0:T(8,128)(2,1)} fusion(bf16[128,5120]{1,0:T(8,128)(2,1)} %collective-permute-done.8.refs_3_, bf16[5120,640]{1,0:T(8,128)(2,1)S(1)} %copy-done.12), kind=kOutput, calls=%fused_computation.12 | convolution fusion | flops 838942720 | bytes 8028160 | tf_op jit(solution)/shard_map/dot_general | solution.py:478
  142.5 14.2 %weight_grad.1 = (bf16[4,160,640]{2,1,0:T(8,128)(2,1)S(1)}, bf16[4,160,640]{2,1,0:T(8,128)(2,1)}, bf16[4,160,640]{2,1,0:T(8,128)(2,1)}, bf16[4,160,640]{2,1,0:T(8,128)(2,1)}, bf16[16,160,640]{2,1,0:T(8,128)(2,1)}) custom-call(s32[5]{0:T(128)S(1)} %copy-done.9, bf16[1024,640]{1,0:T(8,128)(2,1)S(1)} %copy-done.4, ...), custom_call_target="tpu_custom_call" | custom-call | tf_op jit(solution)/shard_map/weight_grad/pallas_call | solution.py:352
  156.8 3.1 %collective-permute-start.19 = (bf16[4,160,640]{2,1,0:T(8,128)(2,1)}, bf16[4,160,640]{2,1,0:T(8,128)(2,1)S(1)}, u32[]{:S(2)}, u32[]{:S(2)}) collective-permute-start(bf16[4,160,640]{2,1,0:T(8,128)(2,1)} %get-tuple-element.67), channel_id=1, source_target_pairs={{0,16},{8,24},{16,0},{24,8},{1,17},{9,25},{17,1},{25,9},{2,18},{10... | collective-permute-start | bytes 2457608 | tf_op jit(solution)/shard_map/ppermute | solution.py:400
  160.5 2.6 collective-permute-start.21
  166.8 19.5 %attention_backward.1 = (bf16[3,256,640]{2,1,0:T(8,128)(2,1)S(1)}, bf16[3,256,640]{2,1,0:T(8,128)(2,1)S(1)}, bf16[3,256,640]{2,1,0:T(8,128)(2,1)S(1)}, bf16[3,256,640]{2,1,0:T(8,128)(2,1)S(1)}) custom-call(s32[5]{0:T(128)S(1)} %copy-done.9, s32[16,8]{1,0:T(8,128)S(1)} %copy.14.pairs_ref, bf16[3,256,640]{2,1,0:T(8,128)(2,1)} %copy-done, ...), custom_call_target="tpu_custom_call" | custom-call | tf_op jit(solution)/shard_map/attention_backward/pallas_call | solution.py:306
  190.1 6.7 %collective-permute-done.20 = bf16[4,160,640]{2,1,0:T(8,128)(2,1)S(1)} collective-permute-done((bf16[4,160,640]{2,1,0:T(8,128)(2,1)}, bf16[4,160,640]{2,1,0:T(8,128)(2,1)S(1)}, u32[]{:S(2)}, u32[]{:S(2)}) %collective-permute-start.20) | collective-permute-done | bytes 819232 | tf_op jit(solution)/shard_map/ppermute | solution.py:400
  198.3 2.1 collective-permute-start.18
  201.3 2.5 collective-permute-start.17
  205.2 2.3 broadcast_select_fusion.4.refs_0_
  207.5 28.7 %collective-permute-done.18 = bf16[3,256,640]{2,1,0:T(8,128)(2,1)} collective-permute-done((bf16[3,256,640]{2,1,0:T(8,128)(2,1)S(1)}, bf16[3,256,640]{2,1,0:T(8,128)(2,1)}, u32[]{:S(2)}, u32[]{:S(2)}) %collective-permute-start.18) | collective-permute-done | bytes 983072 | tf_op jit(solution)/shard_map/ppermute | solution.py:385
  236.2 2.3 broadcast_select_fusion.2.refs_3_
  239.8 2.3 collective-permute-start.22
  242.9 2.4 collective-permute-start.24
  247.2 2.2 collective-permute-done.23
  252.6 6.1 %norm_back.1 = (bf16[256,2560]{1,0:T(8,128)(2,1)}, bf16[256,2560]{1,0:T(8,128)(2,1)}, bf16[256,2560]{1,0:T(8,128)(2,1)}) custom-call(s32[5]{0:T(128)} %stack.23.place_ref, bf16[256,2560]{1,0:T(8,128)(2,1)} %q_ref.3, bf16[256,2560]{1,0:T(8,128)(2,1)} %k_ref.3, f32[2560]{0:T(1024)} %gain_q_ref.3, f32[2560]{0:T(1024)} %gain_k_ref.3, ...), custom_call_target="tpu_custom_call" | custom-call | tf_op jit(solution)/shard_map/norm_back/pallas_call | solution.py:93
  (112 shorter events, 41.0 us)
Async XLA Ops:
  7.2 111.6 %all-gather.2.cloned.1.call-start = ((), (), s32[]{:S(2)}) async-start(), calls=%async_computation.2 | async-start | bytes 6963200 | tf_op jit(solution)/shard_map/all_gather | solution.py:469
  7.2 8.7 %collective-permute-start.5 = (bf16[160,640]{1,0:T(8,128)(2,1)}, bf16[160,640]{1,0:T(8,128)(2,1)S(1)}, u32[]{:S(2)}, u32[]{:S(2)}) collective-permute-start(bf16[160,640]{1,0:T(8,128)(2,1)} %param.17), channel_id=1, source_target_pairs={{1,4},{2,1},{3,5},{4,2},{5,6},{6,3},{9,12},{10,9},{11,13},{12,10},... | collective-permute-start | bytes 614408 | tf_op jit(solution)/shard_map/ppermute | solution.py:385
  9.8 6.9 %collective-permute-start.6 = (bf16[160,640]{1,0:T(8,128)(2,1)}, bf16[160,640]{1,0:T(8,128)(2,1)S(1)}, u32[]{:S(2)}, u32[]{:S(2)}) collective-permute-start(bf16[160,640]{1,0:T(8,128)(2,1)} %param.17), channel_id=1, source_target_pairs={{0,2},{1,6},{2,3},{3,7},{4,0},{5,4},{6,1},{7,5},{8,10},{9,14},{10,... | collective-permute-start | bytes 614408 | tf_op jit(solution)/shard_map/ppermute | solution.py:385
  17.6 220.9 %reduce-scatter.5.cloned.1.call-start = ((), (), s32[]{:S(2)}) async-start(), calls=%async_computation.4 | async-start | bytes 4096000 | tf_op jit(solution)/shard_map/reduce_scatter | solution.py:496
  17.6 26.5 %collective-permute-start = (bf16[3,256,640]{2,1,0:T(8,128)(2,1)}, bf16[3,256,640]{2,1,0:T(8,128)(2,1)}, u32[]{:S(2)}, u32[]{:S(2)}) collective-permute-start(bf16[3,256,640]{2,1,0:T(8,128)(2,1)} %get-tuple-element.42), channel_id=1, source_target_pairs={{1,4},{2,1},{3,5},{4,2},{5,6},{6,3},{9,12},{10,9},{11,13},{12,10},... | collective-permute-start | bytes 2949128 | tf_op jit(solution)/shard_map/ppermute | solution.py:385
  22.4 42.8 %collective-permute-start.1 = (bf16[3,256,640]{2,1,0:T(8,128)(2,1)}, bf16[3,256,640]{2,1,0:T(8,128)(2,1)S(1)}, u32[]{:S(2)}, u32[]{:S(2)}) collective-permute-start(bf16[3,256,640]{2,1,0:T(8,128)(2,1)} %get-tuple-element.43), channel_id=1, source_target_pairs={{0,4},{1,0},{2,5},{3,1},{4,6},{5,2},{6,7},{7,3},{8,12},{9,8},{10,1... | collective-permute-start | bytes 2949128 | tf_op jit(solution)/shard_map/ppermute | solution.py:385
  25.8 46.9 %collective-permute-start.2 = (bf16[3,256,640]{2,1,0:T(8,128)(2,1)}, bf16[3,256,640]{2,1,0:T(8,128)(2,1)}, u32[]{:S(2)}, u32[]{:S(2)}) collective-permute-start(bf16[3,256,640]{2,1,0:T(8,128)(2,1)} %get-tuple-element.44), channel_id=1, source_target_pairs={{0,1},{1,5},{2,0},{3,4},{4,3},{5,7},{6,2},{7,6},{8,9},{9,13},{10,8... | collective-permute-start | bytes 2949128 | tf_op jit(solution)/shard_map/ppermute | solution.py:385
  26.0 45.3 %collective-permute-start.3 = (bf16[3,256,640]{2,1,0:T(8,128)(2,1)S(1)}, bf16[3,256,640]{2,1,0:T(8,128)(2,1)}, u32[]{:S(2)}, u32[]{:S(2)}) collective-permute-start(bf16[3,256,640]{2,1,0:T(8,128)(2,1)S(1)} %copy-done.18), channel_id=1, source_target_pairs={{0,5},{2,4},{3,0},{4,7},{5,3},{7,2},{8,13},{10,12},{11,8},{12,15},... | collective-permute-start | bytes 2949128 | tf_op jit(solution)/shard_map/ppermute | solution.py:385
  28.4 1.4 collective-permute-start.12
  29.8 15.8 %copy-start.13 = (bf16[256,5120]{1,0:T(8,128)(2,1)S(1)}, bf16[256,5120]{1,0:T(8,128)(2,1)}, u32[]{:S(2)}) copy-start(bf16[256,5120]{1,0:T(8,128)(2,1)} %param.16) | copy-start | bytes 7864324
  45.5 33.6 %copy-start = (bf16[3,256,640]{2,1,0:T(8,128)(2,1)}, bf16[3,256,640]{2,1,0:T(8,128)(2,1)S(1)}, u32[]{:S(2)}) copy-start(bf16[3,256,640]{2,1,0:T(8,128)(2,1)S(1)} %broadcast_select_fusion.5.refs_0_.refs_4_.refs_8_) | copy-start | bytes 2949124
  45.6 45.4 %collective-permute-start.4 = (bf16[128,5120]{1,0:T(8,128)(2,1)S(1)}, bf16[128,5120]{1,0:T(8,128)(2,1)S(1)}, u32[]{:S(2)}, u32[]{:S(2)}) collective-permute-start(bf16[128,5120]{1,0:T(8,128)(2,1)S(1)} %dynamic-slice_bitcast_fusion.3), channel_id=1, source_target_pairs={{1,4},{2,1},{3,5},{4,2},{5,6},{6,3},{9,12},{10,9},{11,13},{12,10},... | collective-permute-start | bytes 3932168 | tf_op jit(solution)/shard_map/ppermute | solution.py:385
  66.4 60.1 %collective-permute-start.7 = (bf16[128,5120]{1,0:T(8,128)(2,1)}, bf16[128,5120]{1,0:T(8,128)(2,1)}, u32[]{:S(2)}, u32[]{:S(2)}) collective-permute-start(bf16[128,5120]{1,0:T(8,128)(2,1)} %dynamic-slice_bitcast_fusion.2), channel_id=1, source_target_pairs={{0,4},{1,0},{2,5},{3,1},{4,6},{5,2},{6,7},{7,3},{8,12},{9,8},{10,1... | collective-permute-start | bytes 3932168 | tf_op jit(solution)/shard_map/ppermute | solution.py:385
  72.8 45.7 %collective-permute-start.9 = (bf16[128,5120]{1,0:T(8,128)(2,1)S(1)}, bf16[128,5120]{1,0:T(8,128)(2,1)S(1)}, u32[]{:S(2)}, u32[]{:S(2)}) collective-permute-start(bf16[128,5120]{1,0:T(8,128)(2,1)S(1)} %dynamic-slice_bitcast_fusion), channel_id=1, source_target_pairs={{0,5},{2,4},{3,0},{4,7},{5,3},{7,2},{8,13},{10,12},{11,8},{12,15},... | collective-permute-start | bytes 3932168 | tf_op jit(solution)/shard_map/ppermute | solution.py:385
  77.5 58.0 %collective-permute-start.8 = (bf16[128,5120]{1,0:T(8,128)(2,1)}, bf16[128,5120]{1,0:T(8,128)(2,1)}, u32[]{:S(2)}, u32[]{:S(2)}) collective-permute-start(bf16[128,5120]{1,0:T(8,128)(2,1)} %dynamic-slice_bitcast_fusion.1), channel_id=1, source_target_pairs={{0,1},{1,5},{2,0},{3,4},{4,3},{5,7},{6,2},{7,6},{8,9},{9,13},{10,8... | collective-permute-start | bytes 3932168 | tf_op jit(solution)/shard_map/ppermute | solution.py:385
  92.0 31.2 %collective-permute-start.10 = (bf16[128,5120]{1,0:T(8,128)(2,1)S(1)}, bf16[128,5120]{1,0:T(8,128)(2,1)}, u32[]{:S(2)}, u32[]{:S(2)}) collective-permute-start(bf16[128,5120]{1,0:T(8,128)(2,1)S(1)} %broadcast_select_fusion.1.refs_1_), channel_id=1, source_target_pairs={{0,4},{4,0},{1,5},{5,1},{2,6},{6,2},{3,7},{7,3},{8,12},{12,8},{9,1... | collective-permute-start | bytes 3932168 | tf_op jit(solution)/shard_map/ppermute | solution.py:395
  118.7 12.1 %collective-permute-start.13 = (bf16[128,5120]{1,0:T(8,128)(2,1)S(1)}, bf16[128,5120]{1,0:T(8,128)(2,1)}, u32[]{:S(2)}, u32[]{:S(2)}) collective-permute-start(bf16[128,5120]{1,0:T(8,128)(2,1)S(1)} %broadcast_select_fusion.refs_4_), channel_id=1, source_target_pairs={{0,4},{4,0},{1,5},{5,1},{2,6},{6,2},{3,7},{7,3},{8,12},{12,8},{9,1... | collective-permute-start | bytes 3932168 | tf_op jit(solution)/shard_map/ppermute | solution.py:395
  126.5 12.2 %collective-permute-start.11 = (bf16[128,5120]{1,0:T(8,128)(2,1)}, bf16[128,5120]{1,0:T(8,128)(2,1)S(1)}, u32[]{:S(2)}, u32[]{:S(2)}) collective-permute-start(bf16[128,5120]{1,0:T(8,128)(2,1)} %collective-permute-done.7.refs_2_), channel_id=1, source_target_pairs={{0,4},{4,0},{1,5},{5,1},{2,6},{6,2},{3,7},{7,3},{8,12},{12,8},{9,1... | collective-permute-start | bytes 3932168 | tf_op jit(solution)/shard_map/ppermute | solution.py:395
  135.4 5.2 %collective-permute-start.14 = (bf16[128,5120]{1,0:T(8,128)(2,1)}, bf16[128,5120]{1,0:T(8,128)(2,1)S(1)}, u32[]{:S(2)}, u32[]{:S(2)}) collective-permute-start(bf16[128,5120]{1,0:T(8,128)(2,1)} %collective-permute-done.8.refs_3_), channel_id=1, source_target_pairs={{0,4},{4,0},{1,5},{5,1},{2,6},{6,2},{3,7},{7,3},{8,12},{12,8},{9,1... | collective-permute-start | bytes 3932168 | tf_op jit(solution)/shard_map/ppermute | solution.py:395
  156.8 92.6 %reduce-scatter.3.cloned.1.call-start = ((), (), s32[]{:S(2)}) async-start(), calls=%async_computation.3 | async-start | bytes 1024000 | tf_op jit(solution)/shard_map/reduce_scatter | solution.py:501
  156.8 33.3 %collective-permute-start.19 = (bf16[4,160,640]{2,1,0:T(8,128)(2,1)}, bf16[4,160,640]{2,1,0:T(8,128)(2,1)S(1)}, u32[]{:S(2)}, u32[]{:S(2)}) collective-permute-start(bf16[4,160,640]{2,1,0:T(8,128)(2,1)} %get-tuple-element.67), channel_id=1, source_target_pairs={{0,16},{8,24},{16,0},{24,8},{1,17},{9,25},{17,1},{25,9},{2,18},{10... | collective-permute-start | bytes 2457608 | tf_op jit(solution)/shard_map/ppermute | solution.py:400
  159.9 36.9 %collective-permute-start.20 = (bf16[4,160,640]{2,1,0:T(8,128)(2,1)}, bf16[4,160,640]{2,1,0:T(8,128)(2,1)S(1)}, u32[]{:S(2)}, u32[]{:S(2)}) collective-permute-start(bf16[4,160,640]{2,1,0:T(8,128)(2,1)} %get-tuple-element.68), channel_id=1, source_target_pairs={{0,8},{8,16},{16,24},{24,0},{1,9},{9,17},{17,25},{25,1},{2,10},{10... | collective-permute-start | bytes 2457608 | tf_op jit(solution)/shard_map/ppermute | solution.py:400
  160.5 36.4 %collective-permute-start.21 = (bf16[4,160,640]{2,1,0:T(8,128)(2,1)}, bf16[4,160,640]{2,1,0:T(8,128)(2,1)S(1)}, u32[]{:S(2)}, u32[]{:S(2)}) collective-permute-start(bf16[4,160,640]{2,1,0:T(8,128)(2,1)} %get-tuple-element.69), channel_id=1, source_target_pairs={{0,24},{8,0},{16,8},{24,16},{1,25},{9,1},{17,9},{25,17},{2,26},{10... | collective-permute-start | bytes 2457608 | tf_op jit(solution)/shard_map/ppermute | solution.py:400
  188.2 17.0 %collective-permute-start.15 = (bf16[3,256,640]{2,1,0:T(8,128)(2,1)S(1)}, bf16[3,256,640]{2,1,0:T(8,128)(2,1)}, u32[]{:S(2)}, u32[]{:S(2)}) collective-permute-start(bf16[3,256,640]{2,1,0:T(8,128)(2,1)S(1)} %get-tuple-element.60), channel_id=1, source_target_pairs={{4,1},{1,2},{5,3},{2,4},{6,5},{3,6},{12,9},{9,10},{13,11},{10,12},... | collective-permute-start | bytes 2949128 | tf_op jit(solution)/shard_map/ppermute | solution.py:385
  198.3 37.9 %collective-permute-start.18 = (bf16[3,256,640]{2,1,0:T(8,128)(2,1)S(1)}, bf16[3,256,640]{2,1,0:T(8,128)(2,1)}, u32[]{:S(2)}, u32[]{:S(2)}) collective-permute-start(bf16[3,256,640]{2,1,0:T(8,128)(2,1)S(1)} %get-tuple-element.63), channel_id=1, source_target_pairs={{5,0},{4,2},{0,3},{7,4},{3,5},{2,7},{13,8},{12,10},{8,11},{15,12},... | collective-permute-start | bytes 2949128 | tf_op jit(solution)/shard_map/ppermute | solution.py:385
  200.4 45.0 %collective-permute-start.16 = (bf16[3,256,640]{2,1,0:T(8,128)(2,1)}, bf16[3,256,640]{2,1,0:T(8,128)(2,1)S(1)}, u32[]{:S(2)}, u32[]{:S(2)}) collective-permute-start(bf16[3,256,640]{2,1,0:T(8,128)(2,1)} %copy-done.11), channel_id=1, source_target_pairs={{4,0},{0,1},{5,2},{1,3},{6,4},{2,5},{7,6},{3,7},{12,8},{8,9},{13,1... | collective-permute-start | bytes 2949128 | tf_op jit(solution)/shard_map/ppermute | solution.py:385
  201.3 44.0 %collective-permute-start.17 = (bf16[3,256,640]{2,1,0:T(8,128)(2,1)}, bf16[3,256,640]{2,1,0:T(8,128)(2,1)}, u32[]{:S(2)}, u32[]{:S(2)}) collective-permute-start(bf16[3,256,640]{2,1,0:T(8,128)(2,1)} %copy-done.10), channel_id=1, source_target_pairs={{1,0},{5,1},{0,2},{4,3},{3,4},{7,5},{2,6},{6,7},{9,8},{13,9},{8,10... | collective-permute-start | bytes 2949128 | tf_op jit(solution)/shard_map/ppermute | solution.py:385
  239.8 7.4 %collective-permute-start.22 = (bf16[160,640]{1,0:T(8,128)(2,1)S(1)}, bf16[160,640]{1,0:T(8,128)(2,1)S(1)}, u32[]{:S(2)}, u32[]{:S(2)}) collective-permute-start(bf16[160,640]{1,0:T(8,128)(2,1)S(1)} %get-tuple-element.84), channel_id=1, source_target_pairs={{0,16},{8,24},{16,0},{24,8},{1,17},{9,25},{17,1},{25,9},{2,18},{10... | collective-permute-start | bytes 614408 | tf_op jit(solution)/shard_map/ppermute | solution.py:400
  242.1 7.3 %collective-permute-start.23 = (bf16[160,640]{1,0:T(8,128)(2,1)S(1)}, bf16[160,640]{1,0:T(8,128)(2,1)S(1)}, u32[]{:S(2)}, u32[]{:S(2)}) collective-permute-start(bf16[160,640]{1,0:T(8,128)(2,1)S(1)} %get-tuple-element.83), channel_id=1, source_target_pairs={{0,8},{8,16},{16,24},{24,0},{1,9},{9,17},{17,25},{25,1},{2,10},{10... | collective-permute-start | bytes 614408 | tf_op jit(solution)/shard_map/ppermute | solution.py:400
  242.9 6.4 %collective-permute-start.24 = (bf16[160,640]{1,0:T(8,128)(2,1)S(1)}, bf16[160,640]{1,0:T(8,128)(2,1)S(1)}, u32[]{:S(2)}, u32[]{:S(2)}) collective-permute-start(bf16[160,640]{1,0:T(8,128)(2,1)S(1)} %get-tuple-element.82), channel_id=1, source_target_pairs={{0,24},{8,0},{16,8},{24,16},{1,25},{9,1},{17,9},{25,17},{2,26},{10... | collective-permute-start | bytes 614408 | tf_op jit(solution)/shard_map/ppermute | solution.py:400
  250.6 8.1 %collective-permute-start.26 = (bf16[160,640]{1,0:T(8,128)(2,1)S(1)}, bf16[160,640]{1,0:T(8,128)(2,1)S(1)}, u32[]{:S(2)}, u32[]{:S(2)}) collective-permute-start(bf16[160,640]{1,0:T(8,128)(2,1)S(1)} %bitcast_select_fusion), channel_id=1, source_target_pairs={{0,4},{1,6},{2,0},{3,2},{4,5},{5,7},{6,1},{7,3},{8,12},{9,14},{10,... | collective-permute-start | bytes 614408 | tf_op jit(solution)/shard_map/ppermute | solution.py:385
  250.6 8.6 %collective-permute-start.25 = (bf16[160,640]{1,0:T(8,128)(2,1)S(1)}, bf16[160,640]{1,0:T(8,128)(2,1)S(1)}, u32[]{:S(2)}, u32[]{:S(2)}) collective-permute-start(bf16[160,640]{1,0:T(8,128)(2,1)S(1)} %get-tuple-element.80), channel_id=1, source_target_pairs={{1,2},{2,4},{3,6},{4,1},{5,3},{6,5},{9,10},{10,12},{11,14},{12,9},... | collective-permute-start | bytes 614408 | tf_op jit(solution)/shard_map/ppermute | solution.py:385
  (22 other events, 106.9 us)
Sparse Core Ops, SparseCore 0:
  17.7 68.0 all-gather.1
  156.9 41.6 reduce-scatter.4
  201.6 22.3 reduce-scatter.2

commit v7 on v6

--- a/solution.py
+++ b/solution.py
@@ -470,8 +470,8 @@
     packs = {r: send(parts[r], outward(r)) for r in ORDER}
     came = [packs[r] for r in ORDER]
     own = {}
-    for r, token in zip(ORDER, came):
-        own[r] = send(half_rows(after(out_grad, token), r), outward(r))
+    for r in ORDER:
+        own[r] = send(half_rows(after(out_grad, came), r), outward(r))
     packs = [packs[r] for r in range(SEQ)]
 
     def project(part):
@@ -498,10 +498,9 @@
     one = [one[0]] + [shift(one[by], "x", by) for by in (2, 1, 3)]
     parts = backward(place, tile_pairs, packs, own_grads, other_grads, after(probs, token))
     one = add(*after(one, parts[0]))
-    one = lax.psum_scatter(one, "z", scatter_dimension=0, tiled=True)[0]
-    parts = {r: send(parts[r], inward(r)) for r in ORDER}
-    two = scatter(after(two, parts[ORDER[0]], parts[ORDER[1]]), "x")
-    two = add(*after(two, parts[ORDER[2]], parts[ORDER[3]]))
+    two = lax.optimization_barrier(add(*scatter(after(two, one), "x")))
+    one = lax.optimization_barrier(add(*scatter(one, "z")))
+    parts = {r: send(parts[r] if r in ORDER[:2] else after(parts[r], two), inward(r)) for r in ORDER}
     grad_w = to_owners((one, two), seq)
     grad_q, grad_k, grad_v = finish(
         place, queries, keys, gain_q, gain_k, [parts[r] for r in range(SEQ)]

time: 272 us -> 271 us (level); the launches traced: 267 us -> 269 us
  starting transfers between devices: 75 us -> 49.8 us
  waiting for transfers between devices: 75.8 us -> 99.2 us
  other arithmetic: 11.7 us -> 14.7 us
    ppermute x5, starting transfers between devices: 25.6 us -> 3.03 us  [swap_cores(): return lax.ppermute(value, 'core', [(0, 1), (1, 0)])]
    ppermute x16, waiting for transfers between devices: 64.2 us -> 83.3 us  [send(): got = lax.ppermute(value, ('core', 'seq'), others)]
    ppermute x16, starting transfers between devices: 37.5 us -> 31.9 us  [send(): got = lax.ppermute(value, ('core', 'seq'), others)]
    ppermute x6 -> x9, waiting for transfers between devices: 10.8 us -> 15.8 us  [shift(): lax.ppermute(value, axis, [(i, (i + by) % count) for i in range(count)])]
    ppermute x6 -> x9, starting transfers between devices: 11.8 us -> 14.8 us  [shift(): lax.ppermute(value, axis, [(i, (i + by) % count) for i in range(count)])]
    convert_element_type x1 -> x3, other arithmetic: 1.31 us -> 4.14 us  [add(): return total.astype(jnp.bfloat16)]
    unnamed x49 -> x57, local copies, waits for them, and re-layouts: 7.2 us -> 8.16 us
  transfers between devices with their start and end apart: 30 -> 32, of which waited for: 14 -> 17; matrix products, arithmetic and copies ran while one was open for 12% -> 14% of each run, Pallas kernels for 16% -> 14%
where the time goes in v7:
time: 271 us; the launch traced here: 269 us
  waiting for transfers between devices  99.2 us (37%)
  Pallas kernels  56.7 us (21%)
  starting transfers between devices  49.8 us (18%)
  matrix products  21.2 us (8%)
  other arithmetic  14.7 us (5%)
  between operations  14.6 us (5%)
  local copies, waits for them, and re-layouts  12.4 us (5%)
    ppermute x16, waiting for transfers between devices, send(): got = lax.ppermute(value, ('core', 'seq'), others)  83.3 us
    ppermute x16, starting transfers between devices, send(): got = lax.ppermute(value, ('core', 'seq'), others)  31.9 us
    dot_general x8, matrix products, project(): jnp.dot(part, w_all, preferred_element_type=jnp.float32)  21.2 us
    pallas_call x1, Pallas kernels, backward(): pl.pallas_call(backward_kernel, grid=(heads,), in_specs=[smem()] * 2 + [s...  19.1 us
    ppermute x9, waiting for transfers between devices, shift(): lax.ppermute(value, axis, [(i, (i + by) % count) for i in range(count)])  15.8 us
    ppermute x9, starting transfers between devices, shift(): lax.ppermute(value, axis, [(i, (i + by) % count) for i in range(count)])  14.8 us
    pallas_call x1, Pallas kernels, weight_grad(): pl.pallas_call(lambda place_ref, *refs: weight_grad_kernel(place_ref, mea...  14.3 us
    pallas_call x1, Pallas kernels, forward(): pl.pallas_call(forward_kernel, grid=(heads,), in_specs=[smem()] * 3 + [sp...  11.8 us
  transfers between devices with their start and end apart: 32, of which 17 were waited for; matrix products, arithmetic and copies ran while one was open for 14% of the time, Pallas kernels for 14%

profile of v7, /device:TPU:24, one launch (start us, length us, event | category | flops | bytes accessed | tf_op | source)
XLA Modules:
  0.0 268.5 jit_solution(8177476828894792462)
XLA Ops:
  10.6 5.4 %norm_rows.1 = (bf16[3,256,640]{2,1,0:T(8,128)(2,1)}, bf16[3,256,640]{2,1,0:T(8,128)(2,1)}, bf16[3,256,640]{2,1,0:T(8,128)(2,1)}, bf16[3,256,640]{2,1,0:T(8,128)(2,1)}) custom-call(s32[5]{0:T(128)} %stack.23.place_ref, bf16[256,2560]{1,0:T(8,128)(2,1)} %q_ref.3, bf16[256,2560]{1,0:T(8,128)(2,1)} %k_ref.3, bf16[256,2560]{1,0:T(8,128)(2,1)} %v_ref.1, ...), custom_call_target="tpu_custom_call" | custom-call | tf_op jit(solution)/shard_map/norm_rows/pallas_call | solution.py:61
  17.6 4.8 %collective-permute-start = (bf16[3,256,640]{2,1,0:T(8,128)(2,1)}, bf16[3,256,640]{2,1,0:T(8,128)(2,1)}, u32[]{:S(2)}, u32[]{:S(2)}) collective-permute-start(bf16[3,256,640]{2,1,0:T(8,128)(2,1)} %get-tuple-element.37), channel_id=1, source_target_pairs={{1,4},{2,1},{3,5},{4,2},{5,6},{6,3},{9,12},{10,9},{11,13},{12,10},... | collective-permute-start | bytes 2949128 | tf_op jit(solution)/shard_map/ppermute | solution.py:385
  24.4 3.0 %collective-permute-start.1 = (bf16[3,256,640]{2,1,0:T(8,128)(2,1)}, bf16[3,256,640]{2,1,0:T(8,128)(2,1)S(1)}, u32[]{:S(2)}, u32[]{:S(2)}) collective-permute-start(bf16[3,256,640]{2,1,0:T(8,128)(2,1)} %get-tuple-element.38), channel_id=1, source_target_pairs={{0,4},{1,0},{2,5},{3,1},{4,6},{5,2},{6,7},{7,3},{8,12},{9,8},{10,1... | collective-permute-start | bytes 2949128 | tf_op jit(solution)/shard_map/ppermute | solution.py:385
  27.6 13.7 %collective-permute-done = bf16[3,256,640]{2,1,0:T(8,128)(2,1)} collective-permute-done((bf16[3,256,640]{2,1,0:T(8,128)(2,1)}, bf16[3,256,640]{2,1,0:T(8,128)(2,1)}, u32[]{:S(2)}, u32[]{:S(2)}) %collective-permute-start) | collective-permute-done | bytes 983072 | tf_op jit(solution)/shard_map/ppermute | solution.py:385
  42.6 7.5 %collective-permute-done.3 = bf16[3,256,640]{2,1,0:T(8,128)(2,1)} collective-permute-done((bf16[3,256,640]{2,1,0:T(8,128)(2,1)S(1)}, bf16[3,256,640]{2,1,0:T(8,128)(2,1)}, u32[]{:S(2)}, u32[]{:S(2)}) %collective-permute-start.3) | collective-permute-done | bytes 983072 | tf_op jit(solution)/shard_map/ppermute | solution.py:385
  51.4 10.2 %collective-permute-done.1.refs_1_.refs_5_.refs_9_ = bf16[3,256,640]{2,1,0:T(8,128)(2,1)S(1)} collective-permute-done((bf16[3,256,640]{2,1,0:T(8,128)(2,1)}, bf16[3,256,640]{2,1,0:T(8,128)(2,1)S(1)}, u32[]{:S(2)}, u32[]{:S(2)}) %collective-permute-start.1) | collective-permute-done | bytes 983072 | tf_op jit(solution)/shard_map/ppermute | solution.py:385
  61.6 9.3 %collective-permute-done.2.refs_2_.refs_6_.refs_10_ = bf16[3,256,640]{2,1,0:T(8,128)(2,1)} collective-permute-done((bf16[3,256,640]{2,1,0:T(8,128)(2,1)}, bf16[3,256,640]{2,1,0:T(8,128)(2,1)}, u32[]{:S(2)}, u32[]{:S(2)}) %collective-permute-start.2) | collective-permute-done | bytes 983072 | tf_op jit(solution)/shard_map/ppermute | solution.py:385
  74.7 2.7 %collective-permute-start.9 = (bf16[128,5120]{1,0:T(8,128)(2,1)}, bf16[128,5120]{1,0:T(8,128)(2,1)S(1)}, u32[]{:S(2)}, u32[]{:S(2)}) collective-permute-start(bf16[128,5120]{1,0:T(8,128)(2,1)} %get-tuple-element.70), channel_id=1, source_target_pairs={{0,5},{2,4},{3,0},{4,7},{5,3},{7,2},{8,13},{10,12},{11,8},{12,15},... | collective-permute-start | bytes 3932168 | tf_op jit(solution)/shard_map/ppermute | solution.py:385
  79.8 11.8 %attention_forward.1 = (bf16[1024,640]{1,0:T(8,128)(2,1)S(1)}, bf16[5,4096,128]{2,1,0:T(8,128)(2,1)}) custom-call(s32[5]{0:T(128)S(1)} %copy-done.9, s32[16,8]{1,0:T(8,128)S(1)} %copy.14.pairs_ref, s32[1,16]{1,0:T(1,128)S(1)} %broadcast_select_fusion.9.lens_ref, bf16[3,256,640]{2,1,0:T(8,128)(2,1)S(1)} %broadcast_select_fusion.5.refs_0_.refs_4_.refs_8_, ...), custom_call_target="tpu_custom_call" | custom-call | tf_op jit(solution)/shard_map/attention_forward/pallas_call | solution.py:212
  91.7 11.3 %collective-permute-done.4 = bf16[128,5120]{1,0:T(8,128)(2,1)} collective-permute-done((bf16[128,5120]{1,0:T(8,128)(2,1)}, bf16[128,5120]{1,0:T(8,128)(2,1)}, u32[]{:S(2)}, u32[]{:S(2)}) %collective-permute-start.4) | collective-permute-done | bytes 1310752 | tf_op jit(solution)/shard_map/ppermute | solution.py:385
  104.6 4.9 %collective-permute-done.9 = bf16[128,5120]{1,0:T(8,128)(2,1)S(1)} collective-permute-done((bf16[128,5120]{1,0:T(8,128)(2,1)}, bf16[128,5120]{1,0:T(8,128)(2,1)S(1)}, u32[]{:S(2)}, u32[]{:S(2)}) %collective-permute-start.9) | collective-permute-done | bytes 1310752 | tf_op jit(solution)/shard_map/ppermute | solution.py:385
  109.7 4.4 %convolution_convert_fusion.7.refs_12_ = bf16[128,640]{1,0:T(8,128)(2,1)S(1)} fusion(bf16[128,5120]{1,0:T(8,128)(2,1)S(1)} %broadcast_select_fusion.1.refs_1_, bf16[5120,640]{1,0:T(8,128)(2,1)} %all-gather.2.cloned.1.call-done), kind=kOutput, calls=%fused_computation.12 | convolution fusion | flops 838942720 | bytes 8028160 | tf_op jit(solution)/shard_map/dot_general | solution.py:478
  117.4 11.0 %collective-permute-done.7.refs_2_ = bf16[128,5120]{1,0:T(8,128)(2,1)} collective-permute-done((bf16[128,5120]{1,0:T(8,128)(2,1)}, bf16[128,5120]{1,0:T(8,128)(2,1)}, u32[]{:S(2)}, u32[]{:S(2)}) %collective-permute-start.7) | collective-permute-done | bytes 1310752 | tf_op jit(solution)/shard_map/ppermute | solution.py:385
  128.4 2.8 %collective-permute-start.11 = (bf16[128,5120]{1,0:T(8,128)(2,1)}, bf16[128,5120]{1,0:T(8,128)(2,1)S(1)}, u32[]{:S(2)}, u32[]{:S(2)}) collective-permute-start(bf16[128,5120]{1,0:T(8,128)(2,1)} %collective-permute-done.7.refs_2_), channel_id=1, source_target_pairs={{0,4},{4,0},{1,5},{5,1},{2,6},{6,2},{3,7},{7,3},{8,12},{12,8},{9,1... | collective-permute-start | bytes 3932168 | tf_op jit(solution)/shard_map/ppermute | solution.py:395
  131.2 2.6 convolution_convert_fusion.6.refs_13_
  135.1 3.3 %convolution_convert_fusion.1.refs_19_ = bf16[128,640]{1,0:T(8,128)(2,1)} fusion(bf16[128,5120]{1,0:T(8,128)(2,1)} %collective-permute-done.13.refs_8_, bf16[5120,640]{1,0:T(8,128)(2,1)S(1)} %copy-done.14), kind=kOutput, calls=%fused_computation.6 | convolution fusion | flops 838942720 | bytes 8028160 | tf_op jit(solution)/shard_map/dot_general | solution.py:478
  138.4 3.3 %convolution_convert_fusion.5.refs_14_ = bf16[128,640]{1,0:T(8,128)(2,1)} fusion(bf16[128,5120]{1,0:T(8,128)(2,1)} %collective-permute-done.8.refs_3_, bf16[5120,640]{1,0:T(8,128)(2,1)S(1)} %copy-done.14), kind=kOutput, calls=%fused_computation.10 | convolution fusion | flops 838942720 | bytes 8028160 | tf_op jit(solution)/shard_map/dot_general | solution.py:478
  145.4 14.3 %weight_grad.1 = (bf16[4,160,640]{2,1,0:T(8,128)(2,1)S(1)}, bf16[4,160,640]{2,1,0:T(8,128)(2,1)}, bf16[4,160,640]{2,1,0:T(8,128)(2,1)}, bf16[4,160,640]{2,1,0:T(8,128)(2,1)}, bf16[16,160,640]{2,1,0:T(8,128)(2,1)}) custom-call(s32[5]{0:T(128)S(1)} %copy-done.9, bf16[1024,640]{1,0:T(8,128)(2,1)S(1)} %copy-done.4, ...), custom_call_target="tpu_custom_call" | custom-call | tf_op jit(solution)/shard_map/weight_grad/pallas_call | solution.py:352
  159.7 3.1 %collective-permute-start.16 = (bf16[4,160,640]{2,1,0:T(8,128)(2,1)}, bf16[4,160,640]{2,1,0:T(8,128)(2,1)}, u32[]{:S(2)}, u32[]{:S(2)}) collective-permute-start(bf16[4,160,640]{2,1,0:T(8,128)(2,1)} %get-tuple-element.55), channel_id=1, source_target_pairs={{0,16},{8,24},{16,0},{24,8},{1,17},{9,25},{17,1},{25,9},{2,18},{10... | collective-permute-start | bytes 2457608 | tf_op jit(solution)/shard_map/ppermute | solution.py:400
  163.5 2.6 collective-permute-start.18
  169.7 19.1 %attention_backward.1 = (bf16[3,256,640]{2,1,0:T(8,128)(2,1)S(1)}, bf16[3,256,640]{2,1,0:T(8,128)(2,1)S(1)}, bf16[3,256,640]{2,1,0:T(8,128)(2,1)S(1)}, bf16[3,256,640]{2,1,0:T(8,128)(2,1)S(1)}) custom-call(s32[5]{0:T(128)S(1)} %copy-done.9, s32[16,8]{1,0:T(8,128)S(1)} %copy.14.pairs_ref, bf16[3,256,640]{2,1,0:T(8,128)(2,1)} %copy-done, ...), custom_call_target="tpu_custom_call" | custom-call | tf_op jit(solution)/shard_map/attention_backward/pallas_call | solution.py:306
  192.8 5.4 %collective-permute-start.24 = (bf16[3,256,640]{2,1,0:T(8,128)(2,1)S(1)}, bf16[3,256,640]{2,1,0:T(8,128)(2,1)}, u32[]{:S(2)}, u32[]{:S(2)}) collective-permute-start(bf16[3,256,640]{2,1,0:T(8,128)(2,1)S(1)} %get-tuple-element.66), channel_id=1, source_target_pairs={{5,0},{4,2},{0,3},{7,4},{3,5},{2,7},{13,8},{12,10},{8,11},{15,12},... | collective-permute-start | bytes 2949128 | tf_op jit(solution)/shard_map/ppermute | solution.py:385
  203.7 4.0 %collective-permute-start.27 = (bf16[160,640]{1,0:T(8,128)(2,1)S(1)}, bf16[160,640]{1,0:T(8,128)(2,1)S(1)}, u32[]{:S(2)}, u32[]{:S(2)}) collective-permute-start(bf16[160,640]{1,0:T(8,128)(2,1)S(1)} %get-tuple-element.73), channel_id=1, source_target_pairs={{0,96},{32,0},{64,32},{96,64},{1,97},{33,1},{65,33},{97,65},{2,98}... | collective-permute-start | bytes 614408 | tf_op jit(solution)/shard_map/ppermute | solution.py:400
  208.9 2.7 %collective-permute-start.21 = (bf16[160,640]{1,0:T(8,128)(2,1)S(1)}, bf16[160,640]{1,0:T(8,128)(2,1)S(1)}, u32[]{:S(2)}, u32[]{:S(2)}) collective-permute-start(bf16[160,640]{1,0:T(8,128)(2,1)S(1)} %get-tuple-element.76), channel_id=1, source_target_pairs={{0,24},{8,0},{16,8},{24,16},{1,25},{9,1},{17,9},{25,17},{2,26},{10... | collective-permute-start | bytes 614408 | tf_op jit(solution)/shard_map/ppermute | solution.py:400
  215.4 4.8 %collective-permute-done.21 = bf16[160,640]{1,0:T(8,128)(2,1)S(1)} collective-permute-done((bf16[160,640]{1,0:T(8,128)(2,1)S(1)}, bf16[160,640]{1,0:T(8,128)(2,1)S(1)}, u32[]{:S(2)}, u32[]{:S(2)}) %collective-permute-start.21) | collective-permute-done | bytes 204832 | tf_op jit(solution)/shard_map/ppermute | solution.py:400
  220.2 3.4 %collective-permute-done.20 = bf16[160,640]{1,0:T(8,128)(2,1)S(1)} collective-permute-done((bf16[160,640]{1,0:T(8,128)(2,1)S(1)}, bf16[160,640]{1,0:T(8,128)(2,1)S(1)}, u32[]{:S(2)}, u32[]{:S(2)}) %collective-permute-start.20) | collective-permute-done | bytes 204832 | tf_op jit(solution)/shard_map/ppermute | solution.py:400
  225.1 2.9 %collective-permute-done.26 = bf16[160,640]{1,0:T(8,128)(2,1)S(1)} collective-permute-done((bf16[160,640]{1,0:T(8,128)(2,1)}, bf16[160,640]{1,0:T(8,128)(2,1)S(1)}, u32[]{:S(2)}, u32[]{:S(2)}) %collective-permute-start.26) | collective-permute-done | bytes 204832 | tf_op jit(solution)/shard_map/ppermute | solution.py:400
  228.0 2.9 %collective-permute-done.25 = bf16[160,640]{1,0:T(8,128)(2,1)S(1)} collective-permute-done((bf16[160,640]{1,0:T(8,128)(2,1)S(1)}, bf16[160,640]{1,0:T(8,128)(2,1)S(1)}, u32[]{:S(2)}, u32[]{:S(2)}) %collective-permute-start.25) | collective-permute-done | bytes 204832 | tf_op jit(solution)/shard_map/ppermute | solution.py:400
  232.7 4.1 %collective-permute-start.28 = (bf16[160,640]{1,0:T(8,128)(2,1)S(1)}, bf16[160,640]{1,0:T(8,128)(2,1)S(1)}, u32[]{:S(2)}, u32[]{:S(2)}) collective-permute-start(bf16[160,640]{1,0:T(8,128)(2,1)S(1)} %get-tuple-element.78), channel_id=1, source_target_pairs={{1,2},{2,4},{3,6},{4,1},{5,3},{6,5},{9,10},{10,12},{11,14},{12,9},... | collective-permute-start | bytes 614408 | tf_op jit(solution)/shard_map/ppermute | solution.py:385
  239.1 4.5 %collective-permute-done.28 = bf16[160,640]{1,0:T(8,128)(2,1)S(1)} collective-permute-done((bf16[160,640]{1,0:T(8,128)(2,1)S(1)}, bf16[160,640]{1,0:T(8,128)(2,1)S(1)}, u32[]{:S(2)}, u32[]{:S(2)}) %collective-permute-start.28) | collective-permute-done | bytes 204832 | tf_op jit(solution)/shard_map/ppermute | solution.py:385
  245.0 9.7 %collective-permute-done.23.refs_2_ = bf16[3,256,640]{2,1,0:T(8,128)(2,1)S(1)} collective-permute-done((bf16[3,256,640]{2,1,0:T(8,128)(2,1)S(1)}, bf16[3,256,640]{2,1,0:T(8,128)(2,1)S(1)}, u32[]{:S(2)}, u32[]{:S(2)}) %collective-permute-start.23) | collective-permute-done | bytes 983072 | tf_op jit(solution)/shard_map/ppermute | solution.py:385
  255.6 6.1 %norm_back.1 = (bf16[256,2560]{1,0:T(8,128)(2,1)}, bf16[256,2560]{1,0:T(8,128)(2,1)}, bf16[256,2560]{1,0:T(8,128)(2,1)}) custom-call(s32[5]{0:T(128)} %stack.23.place_ref, bf16[256,2560]{1,0:T(8,128)(2,1)} %q_ref.3, bf16[256,2560]{1,0:T(8,128)(2,1)} %k_ref.3, f32[2560]{0:T(1024)} %gain_q_ref.3, f32[2560]{0:T(1024)} %gain_k_ref.3, ...), custom_call_target="tpu_custom_call" | custom-call | tf_op jit(solution)/shard_map/norm_back/pallas_call | solution.py:93
  (122 shorter events, 52.4 us)
Async XLA Ops:
  7.2 102.5 %all-gather.2.cloned.1.call-start = ((), (), s32[]{:S(2)}) async-start(), calls=%async_computation.1 | async-start | bytes 6963200 | tf_op jit(solution)/shard_map/all_gather | solution.py:469
  7.2 8.7 %collective-permute-start.5 = (bf16[160,640]{1,0:T(8,128)(2,1)}, bf16[160,640]{1,0:T(8,128)(2,1)S(1)}, u32[]{:S(2)}, u32[]{:S(2)}) collective-permute-start(bf16[160,640]{1,0:T(8,128)(2,1)} %param.17), channel_id=1, source_target_pairs={{1,4},{2,1},{3,5},{4,2},{5,6},{6,3},{9,12},{10,9},{11,13},{12,10},... | collective-permute-start | bytes 614408 | tf_op jit(solution)/shard_map/ppermute | solution.py:385
  9.8 6.9 %collective-permute-start.6 = (bf16[160,640]{1,0:T(8,128)(2,1)}, bf16[160,640]{1,0:T(8,128)(2,1)S(1)}, u32[]{:S(2)}, u32[]{:S(2)}) collective-permute-start(bf16[160,640]{1,0:T(8,128)(2,1)} %param.17), channel_id=1, source_target_pairs={{0,2},{1,6},{2,3},{3,7},{4,0},{5,4},{6,1},{7,5},{8,10},{9,14},{10,... | collective-permute-start | bytes 614408 | tf_op jit(solution)/shard_map/ppermute | solution.py:385
  17.6 190.1 %reduce-scatter.2.cloned.1.call-start = ((), (), s32[]{:S(2)}) async-start(), calls=%async_computation.2 | async-start | bytes 4096000 | tf_op jit(solution)/shard_map/reduce_scatter | solution.py:496
  17.6 23.7 %collective-permute-start = (bf16[3,256,640]{2,1,0:T(8,128)(2,1)}, bf16[3,256,640]{2,1,0:T(8,128)(2,1)}, u32[]{:S(2)}, u32[]{:S(2)}) collective-permute-start(bf16[3,256,640]{2,1,0:T(8,128)(2,1)} %get-tuple-element.37), channel_id=1, source_target_pairs={{1,4},{2,1},{3,5},{4,2},{5,6},{6,3},{9,12},{10,9},{11,13},{12,10},... | collective-permute-start | bytes 2949128 | tf_op jit(solution)/shard_map/ppermute | solution.py:385
  22.5 27.6 %collective-permute-start.3 = (bf16[3,256,640]{2,1,0:T(8,128)(2,1)S(1)}, bf16[3,256,640]{2,1,0:T(8,128)(2,1)}, u32[]{:S(2)}, u32[]{:S(2)}) collective-permute-start(bf16[3,256,640]{2,1,0:T(8,128)(2,1)S(1)} %copy-done.22), channel_id=1, source_target_pairs={{0,5},{2,4},{3,0},{4,7},{5,3},{7,2},{8,13},{10,12},{11,8},{12,15},... | collective-permute-start | bytes 2949128 | tf_op jit(solution)/shard_map/ppermute | solution.py:385
  24.4 37.2 %collective-permute-start.1 = (bf16[3,256,640]{2,1,0:T(8,128)(2,1)}, bf16[3,256,640]{2,1,0:T(8,128)(2,1)S(1)}, u32[]{:S(2)}, u32[]{:S(2)}) collective-permute-start(bf16[3,256,640]{2,1,0:T(8,128)(2,1)} %get-tuple-element.38), channel_id=1, source_target_pairs={{0,4},{1,0},{2,5},{3,1},{4,6},{5,2},{6,7},{7,3},{8,12},{9,8},{10,1... | collective-permute-start | bytes 2949128 | tf_op jit(solution)/shard_map/ppermute | solution.py:385
  27.4 43.5 %collective-permute-start.2 = (bf16[3,256,640]{2,1,0:T(8,128)(2,1)}, bf16[3,256,640]{2,1,0:T(8,128)(2,1)}, u32[]{:S(2)}, u32[]{:S(2)}) collective-permute-start(bf16[3,256,640]{2,1,0:T(8,128)(2,1)} %get-tuple-element.39), channel_id=1, source_target_pairs={{0,1},{1,5},{2,0},{3,4},{4,3},{5,7},{6,2},{7,6},{8,9},{9,13},{10,8... | collective-permute-start | bytes 2949128 | tf_op jit(solution)/shard_map/ppermute | solution.py:385
  72.6 30.4 %collective-permute-start.4 = (bf16[128,5120]{1,0:T(8,128)(2,1)}, bf16[128,5120]{1,0:T(8,128)(2,1)}, u32[]{:S(2)}, u32[]{:S(2)}) collective-permute-start(bf16[128,5120]{1,0:T(8,128)(2,1)} %get-tuple-element.71), channel_id=1, source_target_pairs={{1,4},{2,1},{3,5},{4,2},{5,6},{6,3},{9,12},{10,9},{11,13},{12,10},... | collective-permute-start | bytes 3932168 | tf_op jit(solution)/shard_map/ppermute | solution.py:385
  74.5 2.9 %collective-permute-start.12 = (s32[1,16]{1,0:T(1,128)S(1)}, s32[1,16]{1,0:T(1,128)S(1)}, u32[]{:S(2)}, u32[]{:S(2)}) collective-permute-start(s32[1,16]{1,0:T(1,128)S(1)} %copy-done.27), channel_id=1, source_target_pairs={{0,4},{4,0},{1,5},{5,1},{2,6},{6,2},{3,7},{7,3},{8,12},{12,8},{9,1... | collective-permute-start | bytes 200 | tf_op jit(solution)/shard_map/ppermute | solution.py:395
  74.7 34.7 %collective-permute-start.9 = (bf16[128,5120]{1,0:T(8,128)(2,1)}, bf16[128,5120]{1,0:T(8,128)(2,1)S(1)}, u32[]{:S(2)}, u32[]{:S(2)}) collective-permute-start(bf16[128,5120]{1,0:T(8,128)(2,1)} %get-tuple-element.70), channel_id=1, source_target_pairs={{0,5},{2,4},{3,0},{4,7},{5,3},{7,2},{8,13},{10,12},{11,8},{12,15},... | collective-permute-start | bytes 3932168 | tf_op jit(solution)/shard_map/ppermute | solution.py:385
  77.4 51.0 %collective-permute-start.7 = (bf16[128,5120]{1,0:T(8,128)(2,1)}, bf16[128,5120]{1,0:T(8,128)(2,1)}, u32[]{:S(2)}, u32[]{:S(2)}) collective-permute-start(bf16[128,5120]{1,0:T(8,128)(2,1)} %get-tuple-element.70), channel_id=1, source_target_pairs={{0,4},{1,0},{2,5},{3,1},{4,6},{5,2},{6,7},{7,3},{8,12},{9,8},{10,1... | collective-permute-start | bytes 3932168 | tf_op jit(solution)/shard_map/ppermute | solution.py:385
  77.5 60.8 %collective-permute-start.8 = (bf16[128,5120]{1,0:T(8,128)(2,1)}, bf16[128,5120]{1,0:T(8,128)(2,1)}, u32[]{:S(2)}, u32[]{:S(2)}) collective-permute-start(bf16[128,5120]{1,0:T(8,128)(2,1)} %get-tuple-element.71), channel_id=1, source_target_pairs={{0,1},{1,5},{2,0},{3,4},{4,3},{5,7},{6,2},{7,6},{8,9},{9,13},{10,8... | collective-permute-start | bytes 3932168 | tf_op jit(solution)/shard_map/ppermute | solution.py:385
  104.5 9.7 %collective-permute-start.10 = (bf16[128,5120]{1,0:T(8,128)(2,1)S(1)}, bf16[128,5120]{1,0:T(8,128)(2,1)}, u32[]{:S(2)}, u32[]{:S(2)}) collective-permute-start(bf16[128,5120]{1,0:T(8,128)(2,1)S(1)} %broadcast_select_fusion.1.refs_1_), channel_id=1, source_target_pairs={{0,4},{4,0},{1,5},{5,1},{2,6},{6,2},{3,7},{7,3},{8,12},{12,8},{9,1... | collective-permute-start | bytes 3932168 | tf_op jit(solution)/shard_map/ppermute | solution.py:395
  109.6 25.5 %collective-permute-start.13 = (bf16[128,5120]{1,0:T(8,128)(2,1)S(1)}, bf16[128,5120]{1,0:T(8,128)(2,1)}, u32[]{:S(2)}, u32[]{:S(2)}) collective-permute-start(bf16[128,5120]{1,0:T(8,128)(2,1)S(1)} %broadcast_select_fusion.refs_4_), channel_id=1, source_target_pairs={{0,4},{4,0},{1,5},{5,1},{2,6},{6,2},{3,7},{7,3},{8,12},{12,8},{9,1... | collective-permute-start | bytes 3932168 | tf_op jit(solution)/shard_map/ppermute | solution.py:395
  128.4 13.2 %collective-permute-start.11 = (bf16[128,5120]{1,0:T(8,128)(2,1)}, bf16[128,5120]{1,0:T(8,128)(2,1)S(1)}, u32[]{:S(2)}, u32[]{:S(2)}) collective-permute-start(bf16[128,5120]{1,0:T(8,128)(2,1)} %collective-permute-done.7.refs_2_), channel_id=1, source_target_pairs={{0,4},{4,0},{1,5},{5,1},{2,6},{6,2},{3,7},{7,3},{8,12},{12,8},{9,1... | collective-permute-start | bytes 3932168 | tf_op jit(solution)/shard_map/ppermute | solution.py:395
  138.4 5.2 %collective-permute-start.14 = (bf16[128,5120]{1,0:T(8,128)(2,1)}, bf16[128,5120]{1,0:T(8,128)(2,1)S(1)}, u32[]{:S(2)}, u32[]{:S(2)}) collective-permute-start(bf16[128,5120]{1,0:T(8,128)(2,1)} %collective-permute-done.8.refs_3_), channel_id=1, source_target_pairs={{0,4},{4,0},{1,5},{5,1},{2,6},{6,2},{3,7},{7,3},{8,12},{12,8},{9,1... | collective-permute-start | bytes 3932168 | tf_op jit(solution)/shard_map/ppermute | solution.py:395
  159.7 38.4 %collective-permute-start.16 = (bf16[4,160,640]{2,1,0:T(8,128)(2,1)}, bf16[4,160,640]{2,1,0:T(8,128)(2,1)}, u32[]{:S(2)}, u32[]{:S(2)}) collective-permute-start(bf16[4,160,640]{2,1,0:T(8,128)(2,1)} %get-tuple-element.55), channel_id=1, source_target_pairs={{0,16},{8,24},{16,0},{24,8},{1,17},{9,25},{17,1},{25,9},{2,18},{10... | collective-permute-start | bytes 2457608 | tf_op jit(solution)/shard_map/ppermute | solution.py:400
  162.8 37.0 %collective-permute-start.17 = (bf16[4,160,640]{2,1,0:T(8,128)(2,1)}, bf16[4,160,640]{2,1,0:T(8,128)(2,1)}, u32[]{:S(2)}, u32[]{:S(2)}) collective-permute-start(bf16[4,160,640]{2,1,0:T(8,128)(2,1)} %get-tuple-element.56), channel_id=1, source_target_pairs={{0,8},{8,16},{16,24},{24,0},{1,9},{9,17},{17,25},{25,1},{2,10},{10... | collective-permute-start | bytes 2457608 | tf_op jit(solution)/shard_map/ppermute | solution.py:400
  163.5 36.5 %collective-permute-start.18 = (bf16[4,160,640]{2,1,0:T(8,128)(2,1)}, bf16[4,160,640]{2,1,0:T(8,128)(2,1)}, u32[]{:S(2)}, u32[]{:S(2)}) collective-permute-start(bf16[4,160,640]{2,1,0:T(8,128)(2,1)} %get-tuple-element.57), channel_id=1, source_target_pairs={{0,24},{8,0},{16,8},{24,16},{1,25},{9,1},{17,9},{25,17},{2,26},{10... | collective-permute-start | bytes 2457608 | tf_op jit(solution)/shard_map/ppermute | solution.py:400
  190.8 20.8 %collective-permute-start.15 = (bf16[3,256,640]{2,1,0:T(8,128)(2,1)S(1)}, bf16[3,256,640]{2,1,0:T(8,128)(2,1)}, u32[]{:S(2)}, u32[]{:S(2)}) collective-permute-start(bf16[3,256,640]{2,1,0:T(8,128)(2,1)S(1)} %get-tuple-element.52), channel_id=1, source_target_pairs={{4,1},{1,2},{5,3},{2,4},{6,5},{3,6},{12,9},{9,10},{13,11},{10,12},... | collective-permute-start | bytes 2949128 | tf_op jit(solution)/shard_map/ppermute | solution.py:385
  192.8 44.0 %collective-permute-start.24 = (bf16[3,256,640]{2,1,0:T(8,128)(2,1)S(1)}, bf16[3,256,640]{2,1,0:T(8,128)(2,1)}, u32[]{:S(2)}, u32[]{:S(2)}) collective-permute-start(bf16[3,256,640]{2,1,0:T(8,128)(2,1)S(1)} %get-tuple-element.66), channel_id=1, source_target_pairs={{5,0},{4,2},{0,3},{7,4},{3,5},{2,7},{13,8},{12,10},{8,11},{15,12},... | collective-permute-start | bytes 2949128 | tf_op jit(solution)/shard_map/ppermute | solution.py:385
  203.7 21.3 %collective-permute-start.27 = (bf16[160,640]{1,0:T(8,128)(2,1)S(1)}, bf16[160,640]{1,0:T(8,128)(2,1)S(1)}, u32[]{:S(2)}, u32[]{:S(2)}) collective-permute-start(bf16[160,640]{1,0:T(8,128)(2,1)S(1)} %get-tuple-element.73), channel_id=1, source_target_pairs={{0,96},{32,0},{64,32},{96,64},{1,97},{33,1},{65,33},{97,65},{2,98}... | collective-permute-start | bytes 614408 | tf_op jit(solution)/shard_map/ppermute | solution.py:400
  208.9 11.4 %collective-permute-start.21 = (bf16[160,640]{1,0:T(8,128)(2,1)S(1)}, bf16[160,640]{1,0:T(8,128)(2,1)S(1)}, u32[]{:S(2)}, u32[]{:S(2)}) collective-permute-start(bf16[160,640]{1,0:T(8,128)(2,1)S(1)} %get-tuple-element.76), channel_id=1, source_target_pairs={{0,24},{8,0},{16,8},{24,16},{1,25},{9,1},{17,9},{25,17},{2,26},{10... | collective-permute-start | bytes 614408 | tf_op jit(solution)/shard_map/ppermute | solution.py:400
  211.6 12.0 %collective-permute-start.20 = (bf16[160,640]{1,0:T(8,128)(2,1)S(1)}, bf16[160,640]{1,0:T(8,128)(2,1)S(1)}, u32[]{:S(2)}, u32[]{:S(2)}) collective-permute-start(bf16[160,640]{1,0:T(8,128)(2,1)S(1)} %get-tuple-element.77), channel_id=1, source_target_pairs={{0,8},{8,16},{16,24},{24,0},{1,9},{9,17},{17,25},{25,1},{2,10},{10... | collective-permute-start | bytes 614408 | tf_op jit(solution)/shard_map/ppermute | solution.py:400
  211.6 12.2 %collective-permute-start.19 = (bf16[160,640]{1,0:T(8,128)(2,1)S(1)}, bf16[160,640]{1,0:T(8,128)(2,1)S(1)}, u32[]{:S(2)}, u32[]{:S(2)}) collective-permute-start(bf16[160,640]{1,0:T(8,128)(2,1)S(1)} %get-tuple-element.75), channel_id=1, source_target_pairs={{0,16},{8,24},{16,0},{24,8},{1,17},{9,25},{17,1},{25,9},{2,18},{10... | collective-permute-start | bytes 614408 | tf_op jit(solution)/shard_map/ppermute | solution.py:400
  220.2 7.8 %collective-permute-start.26 = (bf16[160,640]{1,0:T(8,128)(2,1)}, bf16[160,640]{1,0:T(8,128)(2,1)S(1)}, u32[]{:S(2)}, u32[]{:S(2)}) collective-permute-start(bf16[160,640]{1,0:T(8,128)(2,1)} %get-tuple-element.74), channel_id=1, source_target_pairs={{0,32},{32,64},{64,96},{96,0},{1,33},{33,65},{65,97},{97,1},{2,34}... | collective-permute-start | bytes 614408 | tf_op jit(solution)/shard_map/ppermute | solution.py:400
  223.6 7.3 %collective-permute-start.25 = (bf16[160,640]{1,0:T(8,128)(2,1)S(1)}, bf16[160,640]{1,0:T(8,128)(2,1)S(1)}, u32[]{:S(2)}, u32[]{:S(2)}) collective-permute-start(bf16[160,640]{1,0:T(8,128)(2,1)S(1)} %get-tuple-element.72), channel_id=1, source_target_pairs={{0,64},{32,96},{64,0},{96,32},{1,65},{33,97},{65,1},{97,33},{2,66}... | collective-permute-start | bytes 614408 | tf_op jit(solution)/shard_map/ppermute | solution.py:400
  224.8 20.2 %collective-permute-start.22 = (bf16[3,256,640]{2,1,0:T(8,128)(2,1)S(1)}, bf16[3,256,640]{2,1,0:T(8,128)(2,1)S(1)}, u32[]{:S(2)}, u32[]{:S(2)}) collective-permute-start(bf16[3,256,640]{2,1,0:T(8,128)(2,1)S(1)} %copy-done.13), channel_id=1, source_target_pairs={{4,0},{0,1},{5,2},{1,3},{6,4},{2,5},{7,6},{3,7},{12,8},{8,9},{13,1... | collective-permute-start | bytes 2949128 | tf_op jit(solution)/shard_map/ppermute | solution.py:385
  224.9 29.7 %collective-permute-start.23 = (bf16[3,256,640]{2,1,0:T(8,128)(2,1)S(1)}, bf16[3,256,640]{2,1,0:T(8,128)(2,1)S(1)}, u32[]{:S(2)}, u32[]{:S(2)}) collective-permute-start(bf16[3,256,640]{2,1,0:T(8,128)(2,1)S(1)} %copy-done.11), channel_id=1, source_target_pairs={{1,0},{5,1},{0,2},{4,3},{3,4},{7,5},{2,6},{6,7},{9,8},{13,9},{8,10... | collective-permute-start | bytes 2949128 | tf_op jit(solution)/shard_map/ppermute | solution.py:385
  232.0 7.1 %collective-permute-start.29 = (bf16[160,640]{1,0:T(8,128)(2,1)S(1)}, bf16[160,640]{1,0:T(8,128)(2,1)S(1)}, u32[]{:S(2)}, u32[]{:S(2)}) collective-permute-start(bf16[160,640]{1,0:T(8,128)(2,1)S(1)} %get-tuple-element.79), channel_id=1, source_target_pairs={{0,4},{1,6},{2,0},{3,2},{4,5},{5,7},{6,1},{7,3},{8,12},{9,14},{10,... | collective-permute-start | bytes 614408 | tf_op jit(solution)/shard_map/ppermute | solution.py:385
  232.7 10.9 %collective-permute-start.28 = (bf16[160,640]{1,0:T(8,128)(2,1)S(1)}, bf16[160,640]{1,0:T(8,128)(2,1)S(1)}, u32[]{:S(2)}, u32[]{:S(2)}) collective-permute-start(bf16[160,640]{1,0:T(8,128)(2,1)S(1)} %get-tuple-element.78), channel_id=1, source_target_pairs={{1,2},{2,4},{3,6},{4,1},{5,3},{6,5},{9,10},{10,12},{11,14},{12,9},... | collective-permute-start | bytes 614408 | tf_op jit(solution)/shard_map/ppermute | solution.py:385
  (28 other events, 272.0 us)
Sparse Core Ops, SparseCore 0:
  17.7 68.0 all-gather.1
  159.9 42.0 reduce-scatter.1

commit v8 on v7

--- a/solution.py
+++ b/solution.py
@@ -229,10 +229,9 @@
 
 def backward_kernel(place_ref, pairs_ref, *refs):
     q_parts, k_parts, v_parts = refs[:SEQ], refs[SEQ : 2 * SEQ], refs[2 * SEQ : 3 * SEQ]
-    own_grads, other_grads = refs[3 * SEQ : 4 * SEQ], refs[4 * SEQ : 5 * SEQ]
-    probs_ref = refs[5 * SEQ]
-    outs = refs[5 * SEQ + 1 : 6 * SEQ + 1]
-    q_all, k_all, v_all, g_all, gq_all, gk_acc, gv_acc = refs[6 * SEQ + 1 :]
+    g_all, probs_ref = refs[3 * SEQ : 3 * SEQ + 2]
+    outs = refs[3 * SEQ + 2 : 4 * SEQ + 2]
+    q_all, k_all, v_all, gq_all, gk_acc, gv_acc = refs[4 * SEQ + 2 :]
     tile_count, neighbours = pairs_ref.shape
     clip_rows, width = q_all.shape
     tile_rows = clip_rows // tile_count
@@ -242,11 +241,6 @@
     load_parts(q_parts, q_all)
     load_parts(k_parts, k_all)
     load_parts(v_parts, v_all)
-    half_rows = own_grads[0].shape[0]
-    core = place_ref[1]
-    for at in range(SEQ):
-        for grads, half in ((own_grads[at], core), (other_grads[at ^ 1], 1 - core)):
-            g_all[pl.ds(pl.multiple_of((2 * at + half) * half_rows, half_rows), half_rows), :] = grads[...]
     gk_acc[...] = jnp.zeros_like(gk_acc)
     gv_acc[...] = jnp.zeros_like(gv_acc)
 
@@ -296,11 +290,10 @@
         out[2] = gv_acc[part, :].astype(jnp.bfloat16)
 
 
-def backward(place, tile_pairs, packs, own_grads, other_grads, probs):
+def backward(place, tile_pairs, packs, grads, probs):
     _, rows, local_width = packs[0].shape
     heads = local_width // HEAD_DIM
     clip_rows = rows * SEQ
-    grad_spec = pl.BlockSpec((own_grads[0].shape[0], HEAD_DIM), lambda h: (0, h))
     bf16_rows = pltpu.VMEM((clip_rows, HEAD_DIM), jnp.bfloat16)
     f32_rows = pltpu.VMEM((clip_rows, HEAD_DIM), jnp.float32)
     return pl.pallas_call(
@@ -308,31 +301,41 @@
         grid=(heads,),
         in_specs=[smem()] * 2
         + [spec for spec in pack_specs(rows) for _ in packs]
-        + [grad_spec] * (2 * SEQ)
+        + [pl.BlockSpec((clip_rows, HEAD_DIM), lambda h: (0, h))]
         + [pl.BlockSpec((1,) + probs.shape[1:], lambda h: (h, 0, 0))],
         out_specs=[pl.BlockSpec((3, rows, HEAD_DIM), lambda h: (0, 0, h))] * SEQ,
         out_shape=[jax.ShapeDtypeStruct((3, rows, local_width), jnp.bfloat16)] * SEQ,
-        scratch_shapes=[bf16_rows] * 5 + [f32_rows] * 2,
+        scratch_shapes=[bf16_rows] * 4 + [f32_rows] * 2,
         compiler_params=params(),
         name="attention_backward",
-    )(place, tile_pairs, *packs, *packs, *packs, *own_grads, *other_grads, probs)
-
-
-def weight_grad_kernel(place_ref, mean, side, att_ref, *refs):
-    own, other, outs = refs[:SEQ], refs[SEQ : 2 * SEQ], refs[2 * SEQ :]
-    pieces, second = outs[:-1], outs[-1]
+    )(place, tile_pairs, *packs, *packs, *packs, grads, probs)
+
+
+def project_kernel(place_ref, mean, side, att_ref, w_ref, *refs):
+    own, other = refs[:SEQ], refs[SEQ : 2 * SEQ]
+    pieces, second, grad_ref, grad_acc = refs[2 * SEQ : -3], refs[-3], refs[-2], refs[-1]
     half_rows = own[0].shape[0]
     core = place_ref[1]
-    columns, attended = [], []
+    columns, starts = [], []
     for at in range(SEQ):
         for part, half in ((own[at], core), (other[at ^ 1], 1 - core)):
             columns.append(part[...])
-            start = pl.multiple_of((2 * at + half) * half_rows, half_rows)
-            attended.append(att_ref[pl.ds(start, half_rows), :])
-    total = contract(jnp.concatenate(columns, axis=0), jnp.concatenate(attended, axis=0), 0, 0)
-    total = (total * mean).astype(jnp.bfloat16)
+            starts.append(pl.multiple_of((2 * at + half) * half_rows, half_rows))
+    columns = jnp.concatenate(columns, axis=0)
+    attended = jnp.concatenate([att_ref[pl.ds(start, half_rows), :] for start in starts], axis=0)
+    step = pl.program_id(0)
+    product = contract(columns, w_ref[...], 1, 0)
+
+    @pl.when(step == 0)
+    def _():
+        grad_acc[...] = product
+
+    @pl.when(step > 0)
+    def _():
+        grad_acc[...] += product
+
+    total = (contract(columns, attended, 0, 0) * mean).astype(jnp.bfloat16)
     count, piece = second.shape[:2]
-    step = pl.program_id(0)
     for at in range(count):
         start = 2 * at * piece
         second[at] = total[start + piece : start + 2 * piece]
@@ -344,23 +347,34 @@
             def _(out=out, start=start, owner=owner):
                 out[owner // side] = total[start : start + piece]
 
-
-def weight_grad(place, attended, own, other, mean, side, block=640):
+    @pl.when(step == pl.num_programs(0) - 1)
+    def _():
+        for at, start in enumerate(starts):
+            part = grad_acc[at * half_rows : (at + 1) * half_rows, :]
+            grad_ref[pl.ds(start, half_rows), :] = part.astype(jnp.bfloat16)
+
+
+def project(place, attended, w_all, own, other, mean, side, block=640):
     half_rows, features = own[0].shape
-    local_width = attended.shape[1]
+    clip_rows, local_width = attended.shape
     piece = features // (side * side) // CORES
+    whole = pl.BlockSpec((clip_rows, local_width), lambda i: (0, 0))
     return pl.pallas_call(
-        lambda place_ref, *refs: weight_grad_kernel(place_ref, mean, side, *refs),
+        lambda place_ref, *refs: project_kernel(place_ref, mean, side, *refs),
         grid=(features // block,),
-        in_specs=[smem(), pl.BlockSpec(attended.shape, lambda i: (0, 0))]
+        in_specs=[smem(), whole, pl.BlockSpec((block, local_width), lambda i: (i, 0))]
         + [pl.BlockSpec((half_rows, block), lambda i: (0, i))] * (2 * SEQ),
         out_specs=[pl.BlockSpec((side, piece, local_width), lambda i: (0, 0, 0))] * side
-        + [pl.BlockSpec((block // piece // 2, piece, local_width), lambda i: (i, 0, 0))],
+        + [pl.BlockSpec((block // piece // 2, piece, local_width), lambda i: (i, 0, 0)), whole],
         out_shape=[jax.ShapeDtypeStruct((side, piece, local_width), jnp.bfloat16)] * side
-        + [jax.ShapeDtypeStruct((side * side, piece, local_width), jnp.bfloat16)],
+        + [
+            jax.ShapeDtypeStruct((side * side, piece, local_width), jnp.bfloat16),
+            jax.ShapeDtypeStruct((clip_rows, local_width), jnp.bfloat16),
+        ],
+        scratch_shapes=[pltpu.VMEM((clip_rows, local_width), jnp.float32)],
         compiler_params=params(),
-        name="weight_grad",
-    )(place, attended, *own, *other)
+        name="project_and_weight_grad",
+    )(place, attended, w_all, *own, *other)
 
 
 def device_of(core, seq):
@@ -474,33 +488,21 @@
         own[r] = send(half_rows(after(out_grad, came), r), outward(r))
     packs = [packs[r] for r in range(SEQ)]
 
-    def project(part):
-        return jnp.dot(part, w_all, preferred_element_type=jnp.float32).astype(jnp.bfloat16)
-
     attended, probs = forward(place, tile_pairs, lens, packs)
-    one, two, three, last = ORDER
-    other = {one: swap_cores(own[one]), two: swap_cores(after(own[two], attended))}
-    own_grads = {one: project(own[one]), two: project(own[two])}
-    other_grads = {one: project(other[one]), two: project(other[two])}
-    other[three] = swap_cores(after(own[three], own_grads[one], other_grads[one]))
-    own_grads[three], other_grads[three] = project(own[three]), project(other[three])
-    done = ([own_grads[r] for r in ORDER[:-1]], [other_grads[r] for r in ORDER[:-2]])
-    other[last] = swap_cores(after(own[last], *done))
-    own_grads[last] = project(own[last])
-    other_grads[last] = project(other[last])
-    attended = after(attended, own_grads, other_grads)
-    own, other, own_grads, other_grads = [
-        [table[r] for r in range(SEQ)] for table in (own, other, own_grads, other_grads)
-    ]
-    *one, two = weight_grad(place, attended, own, other, 1.0 / (count_z * count_x * CORES), count_x)
+    other = {r: swap_cores(own[r] if r == ORDER[0] else after(own[r], attended)) for r in ORDER}
+    own, other = [[table[r] for r in range(SEQ)] for table in (own, other)]
+    *one, two, grads = project(
+        place, attended, w_all, own, other, 1.0 / (count_z * count_x * CORES), count_x
+    )
     two = lax.psum_scatter(two, "z", scatter_dimension=0, tiled=True)
     token = one[0]
     one = [one[0]] + [shift(one[by], "x", by) for by in (2, 1, 3)]
-    parts = backward(place, tile_pairs, packs, own_grads, other_grads, after(probs, token))
+    parts = backward(place, tile_pairs, packs, grads, after(probs, token))
     one = add(*after(one, parts[0]))
-    two = lax.optimization_barrier(add(*scatter(after(two, one), "x")))
-    one = lax.optimization_barrier(add(*scatter(one, "z")))
-    parts = {r: send(parts[r] if r in ORDER[:2] else after(parts[r], two), inward(r)) for r in ORDER}
+    sent = {r: send(parts[r], inward(r)) for r in ORDER}
+    two = lax.optimization_barrier(add(*scatter(after(two, [sent[r] for r in ORDER[:2]]), "x")))
+    one = lax.optimization_barrier(add(*scatter(after(one, [sent[r] for r in ORDER[:2]]), "z")))
+    parts = sent
     grad_w = to_owners((one, two), seq)
     grad_q, grad_k, grad_v = finish(
         place, queries, keys, gain_q, gain_k, [parts[r] for r in range(SEQ)]

time: 271 us -> 290 us (1.070)
  matrix products: 21.2 us -> 0 us
  waiting for transfers between devices: 99.2 us -> 120 us
  Pallas kernels: 56.7 us -> 75.5 us
    dot_general x8 -> x0, matrix products: 21.2 us -> none  [project(): jnp.dot(part, w_all, preferred_element_type=jnp.float32)]
    pallas_call x1, Pallas kernels: 14.3 us -> 32.9 us  [project(): pl.pallas_call(lambda place_ref, *refs: project_kernel(place_ref, mean, s...]
    ppermute x16, waiting for transfers between devices: 83.3 us -> 101 us  [send(): got = lax.ppermute(value, ('core', 'seq'), others)]
    ppermute x5, waiting for transfers between devices: 0.01 us -> 4.3 us  [swap_cores(): return lax.ppermute(value, 'core', [(0, 1), (1, 0)])]
    unnamed x57 -> x53, local copies, waits for them, and re-layouts: 8.16 us -> 7.83 us
  transfers between devices with their start and end apart: 32 -> 32, of which waited for: 17 -> 17; matrix products, arithmetic and copies ran while one was open for 14% -> 6% of each run, Pallas kernels for 14% -> 15%
where the time goes in v8:
time: 290 us; the launch traced here: 287 us
  waiting for transfers between devices  120 us (41%)
  Pallas kernels  75.5 us (26%)
  starting transfers between devices  50 us (17%)
  between operations  14.5 us (5%)
  other arithmetic  14.4 us (5%)
  local copies, waits for them, and re-layouts  12.1 us (4%)
    ppermute x16, waiting for transfers between devices, send(): got = lax.ppermute(value, ('core', 'seq'), others)  101 us
    pallas_call x1, Pallas kernels, project(): pl.pallas_call(lambda place_ref, *refs: project_kernel(place_ref, mean, s...  32.9 us
    ppermute x16, starting transfers between devices, send(): got = lax.ppermute(value, ('core', 'seq'), others)  30.5 us
    pallas_call x1, Pallas kernels, backward(): pl.pallas_call(backward_kernel, grid=(heads,), in_specs=[smem()] * 2 + [s...  19.3 us
    ppermute x9, starting transfers between devices, shift(): lax.ppermute(value, axis, [(i, (i + by) % count) for i in range(count)])  16.7 us
    ppermute x9, waiting for transfers between devices, shift(): lax.ppermute(value, axis, [(i, (i + by) % count) for i in range(count)])  15.3 us
    pallas_call x1, Pallas kernels, forward(): pl.pallas_call(forward_kernel, grid=(heads,), in_specs=[smem()] * 3 + [sp...  11.9 us
    unnamed x53, local copies, waits for them, and re-layouts  7.83 us
  transfers between devices with their start and end apart: 32, of which 17 were waited for; matrix products, arithmetic and copies ran while one was open for 6% of the time, Pallas kernels for 15%

profile of v8, /device:TPU:24, one launch (start us, length us, event | category | flops | bytes accessed | tf_op | source)
XLA Modules:
  0.0 286.7 jit_solution(17767122059539640541)
XLA Ops:
  7.2 2.6 collective-permute-start.5
  10.5 5.4 %norm_rows.1 = (bf16[3,256,640]{2,1,0:T(8,128)(2,1)}, bf16[3,256,640]{2,1,0:T(8,128)(2,1)}, bf16[3,256,640]{2,1,0:T(8,128)(2,1)}, bf16[3,256,640]{2,1,0:T(8,128)(2,1)}) custom-call(s32[5]{0:T(128)} %stack.23.place_ref, bf16[256,2560]{1,0:T(8,128)(2,1)} %q_ref.3, bf16[256,2560]{1,0:T(8,128)(2,1)} %k_ref.3, bf16[256,2560]{1,0:T(8,128)(2,1)} %v_ref.1, ...), custom_call_target="tpu_custom_call" | custom-call | tf_op jit(solution)/shard_map/norm_rows/pallas_call | solution.py:61
  17.6 4.8 %collective-permute-start = (bf16[3,256,640]{2,1,0:T(8,128)(2,1)}, bf16[3,256,640]{2,1,0:T(8,128)(2,1)}, u32[]{:S(2)}, u32[]{:S(2)}) collective-permute-start(bf16[3,256,640]{2,1,0:T(8,128)(2,1)} %get-tuple-element.36), channel_id=1, source_target_pairs={{1,4},{2,1},{3,5},{4,2},{5,6},{6,3},{9,12},{10,9},{11,13},{12,10},... | collective-permute-start | bytes 2949128 | tf_op jit(solution)/shard_map/ppermute | solution.py:399
  22.5 1.9 collective-permute-start.3
  24.4 3.1 %collective-permute-start.1 = (bf16[3,256,640]{2,1,0:T(8,128)(2,1)}, bf16[3,256,640]{2,1,0:T(8,128)(2,1)S(1)}, u32[]{:S(2)}, u32[]{:S(2)}) collective-permute-start(bf16[3,256,640]{2,1,0:T(8,128)(2,1)} %get-tuple-element.37), channel_id=1, source_target_pairs={{0,4},{1,0},{2,5},{3,1},{4,6},{5,2},{6,7},{7,3},{8,12},{9,8},{10,1... | collective-permute-start | bytes 2949128 | tf_op jit(solution)/shard_map/ppermute | solution.py:399
  27.7 13.6 %collective-permute-done = bf16[3,256,640]{2,1,0:T(8,128)(2,1)} collective-permute-done((bf16[3,256,640]{2,1,0:T(8,128)(2,1)}, bf16[3,256,640]{2,1,0:T(8,128)(2,1)}, u32[]{:S(2)}, u32[]{:S(2)}) %collective-permute-start) | collective-permute-done | bytes 983072 | tf_op jit(solution)/shard_map/ppermute | solution.py:399
  42.6 7.4 %collective-permute-done.3 = bf16[3,256,640]{2,1,0:T(8,128)(2,1)} collective-permute-done((bf16[3,256,640]{2,1,0:T(8,128)(2,1)S(1)}, bf16[3,256,640]{2,1,0:T(8,128)(2,1)}, u32[]{:S(2)}, u32[]{:S(2)}) %collective-permute-start.3) | collective-permute-done | bytes 983072 | tf_op jit(solution)/shard_map/ppermute | solution.py:399
  51.4 10.2 %collective-permute-done.1.refs_1_.refs_5_.refs_9_ = bf16[3,256,640]{2,1,0:T(8,128)(2,1)S(1)} collective-permute-done((bf16[3,256,640]{2,1,0:T(8,128)(2,1)}, bf16[3,256,640]{2,1,0:T(8,128)(2,1)S(1)}, u32[]{:S(2)}, u32[]{:S(2)}) %collective-permute-start.1) | collective-permute-done | bytes 983072 | tf_op jit(solution)/shard_map/ppermute | solution.py:399
  61.6 9.3 %collective-permute-done.2.refs_2_.refs_6_.refs_10_ = bf16[3,256,640]{2,1,0:T(8,128)(2,1)} collective-permute-done((bf16[3,256,640]{2,1,0:T(8,128)(2,1)}, bf16[3,256,640]{2,1,0:T(8,128)(2,1)}, u32[]{:S(2)}, u32[]{:S(2)}) %collective-permute-start.2) | collective-permute-done | bytes 983072 | tf_op jit(solution)/shard_map/ppermute | solution.py:399
  74.7 3.6 %collective-permute-start.8 = (bf16[128,5120]{1,0:T(8,128)(2,1)}, bf16[128,5120]{1,0:T(8,128)(2,1)S(1)}, u32[]{:S(2)}, u32[]{:S(2)}) collective-permute-start(bf16[128,5120]{1,0:T(8,128)(2,1)} %get-tuple-element.68), channel_id=1, source_target_pairs={{0,4},{1,0},{2,5},{3,1},{4,6},{5,2},{6,7},{7,3},{8,12},{9,8},{10,1... | collective-permute-start | bytes 3932168 | tf_op jit(solution)/shard_map/ppermute | solution.py:399
  80.2 11.9 %attention_forward.1 = (bf16[1024,640]{1,0:T(8,128)(2,1)S(1)}, bf16[5,4096,128]{2,1,0:T(8,128)(2,1)}) custom-call(s32[5]{0:T(128)S(1)} %copy-done.5, s32[16,8]{1,0:T(8,128)S(1)} %copy.14.pairs_ref, s32[1,16]{1,0:T(1,128)S(1)} %broadcast_select_fusion.9.lens_ref, bf16[3,256,640]{2,1,0:T(8,128)(2,1)S(1)} %broadcast_select_fusion.5.refs_0_.refs_4_.refs_8_, ...), custom_call_target="tpu_custom_call" | custom-call | tf_op jit(solution)/shard_map/attention_forward/pallas_call | solution.py:212
  92.1 14.4 %collective-permute-done.10 = bf16[128,5120]{1,0:T(8,128)(2,1)} collective-permute-done((bf16[128,5120]{1,0:T(8,128)(2,1)}, bf16[128,5120]{1,0:T(8,128)(2,1)}, u32[]{:S(2)}, u32[]{:S(2)}) %collective-permute-start.10) | collective-permute-done | bytes 1310752 | tf_op jit(solution)/shard_map/ppermute | solution.py:399
  108.1 24.3 %collective-permute-done.9.refs_4_ = bf16[128,5120]{1,0:T(8,128)(2,1)S(1)} collective-permute-done((bf16[128,5120]{1,0:T(8,128)(2,1)}, bf16[128,5120]{1,0:T(8,128)(2,1)S(1)}, u32[]{:S(2)}, u32[]{:S(2)}) %collective-permute-start.9) | collective-permute-done | bytes 1310752 | tf_op jit(solution)/shard_map/ppermute | solution.py:399
  132.3 2.0 collective-permute-start.13
  136.9 3.7 %collective-permute-done.12.refs_7_ = bf16[128,5120]{1,0:T(8,128)(2,1)S(1)} collective-permute-done((bf16[128,5120]{1,0:T(8,128)(2,1)S(1)}, bf16[128,5120]{1,0:T(8,128)(2,1)S(1)}, u32[]{:S(2)}, u32[]{:S(2)}) %collective-permute-start.12) | collective-permute-done | bytes 1310752 | tf_op jit(solution)/shard_map/ppermute | solution.py:409
  143.1 32.9 %project_and_weight_grad.1 = (bf16[4,160,640]{2,1,0:T(8,128)(2,1)S(1)}, bf16[4,160,640]{2,1,0:T(8,128)(2,1)}, bf16[4,160,640]{2,1,0:T(8,128)(2,1)}, bf16[4,160,6...) custom-call(s32[5]{0:T(128)S(1)} %copy-done.5, bf16[1024,640]{1,0:T(8,128)(2,1)S(1)} %copy-done.3, ...), custom_call_target="tpu_custom_call" | custom-call | tf_op jit(solution)/shard_map/project_and_weight_grad/pallas_call | solution.py:362
  178.0 3.1 %collective-permute-start.19 = (bf16[4,160,640]{2,1,0:T(8,128)(2,1)}, bf16[4,160,640]{2,1,0:T(8,128)(2,1)}, u32[]{:S(2)}, u32[]{:S(2)}) collective-permute-start(bf16[4,160,640]{2,1,0:T(8,128)(2,1)} %get-tuple-element.58), channel_id=1, source_target_pairs={{0,16},{8,24},{16,0},{24,8},{1,17},{9,25},{17,1},{25,9},{2,18},{10... | collective-permute-start | bytes 2457608 | tf_op jit(solution)/shard_map/ppermute | solution.py:414
  181.7 2.6 collective-permute-start.21
  184.3 19.3 %attention_backward.1 = (bf16[3,256,640]{2,1,0:T(8,128)(2,1)S(1)}, bf16[3,256,640]{2,1,0:T(8,128)(2,1)S(1)}, bf16[3,256,640]{2,1,0:T(8,128)(2,1)S(1)}, bf16[3,256,640]{2,1,0:T(8,128)(2,1)}) custom-call(s32[5]{0:T(128)S(1)} %copy-done.5, s32[16,8]{1,0:T(8,128)S(1)} %copy.14.pairs_ref, bf16[3,256,640]{2,1,0:T(8,128)(2,1)S(1)} %broadcast_select_fusion.5.refs_0_.refs_4_.refs_8_, ...), custom_call_target="tpu_custom_call" | custom-call | tf_op jit(solution)/shard_map/attention_backward/pallas_call | solution.py:299
  207.4 1.9 collective-permute-start.15
  209.4 8.5 %collective-permute-done.20 = bf16[4,160,640]{2,1,0:T(8,128)(2,1)} collective-permute-done((bf16[4,160,640]{2,1,0:T(8,128)(2,1)}, bf16[4,160,640]{2,1,0:T(8,128)(2,1)}, u32[]{:S(2)}, u32[]{:S(2)}) %collective-permute-start.20) | collective-permute-done | bytes 819232 | tf_op jit(solution)/shard_map/ppermute | solution.py:414
  218.1 2.3 add_convert_fusion
  220.4 13.0 %collective-permute-done.18 = bf16[3,256,640]{2,1,0:T(8,128)(2,1)S(1)} collective-permute-done((bf16[3,256,640]{2,1,0:T(8,128)(2,1)}, bf16[3,256,640]{2,1,0:T(8,128)(2,1)S(1)}, u32[]{:S(2)}, u32[]{:S(2)}) %collective-permute-start.18) | collective-permute-done | bytes 983072 | tf_op jit(solution)/shard_map/ppermute | solution.py:399
  236.5 3.9 %collective-permute-start.22 = (bf16[160,640]{1,0:T(8,128)(2,1)}, bf16[160,640]{1,0:T(8,128)(2,1)S(1)}, u32[]{:S(2)}, u32[]{:S(2)}) collective-permute-start(bf16[160,640]{1,0:T(8,128)(2,1)} %get-tuple-element.73), channel_id=1, source_target_pairs={{0,64},{32,96},{64,0},{96,32},{1,65},{33,97},{65,1},{97,33},{2,66}... | collective-permute-start | bytes 614408 | tf_op jit(solution)/shard_map/ppermute | solution.py:414
  241.4 2.2 collective-permute-start.24
  245.0 2.5 collective-permute-done.23
  247.6 3.2 %collective-permute-start.27 = (bf16[160,640]{1,0:T(8,128)(2,1)S(1)}, bf16[160,640]{1,0:T(8,128)(2,1)S(1)}, u32[]{:S(2)}, u32[]{:S(2)}) collective-permute-start(bf16[160,640]{1,0:T(8,128)(2,1)S(1)} %get-tuple-element.71), channel_id=1, source_target_pairs={{0,24},{8,0},{16,8},{24,16},{1,25},{9,1},{17,9},{25,17},{2,26},{10... | collective-permute-start | bytes 614408 | tf_op jit(solution)/shard_map/ppermute | solution.py:414
  251.9 2.2 collective-permute-done.25
  257.8 2.1 collective-permute-start.28
  259.9 4.4 %collective-permute-start.29 = (bf16[160,640]{1,0:T(8,128)(2,1)}, bf16[160,640]{1,0:T(8,128)(2,1)}, u32[]{:S(2)}, u32[]{:S(2)}) collective-permute-start(bf16[160,640]{1,0:T(8,128)(2,1)} %get-tuple-element.77), channel_id=1, source_target_pairs={{0,4},{1,6},{2,0},{3,2},{4,5},{5,7},{6,1},{7,3},{8,12},{9,14},{10,... | collective-permute-start | bytes 614408 | tf_op jit(solution)/shard_map/ppermute | solution.py:399
  264.3 7.7 %collective-permute-done.17.refs_2_ = bf16[3,256,640]{2,1,0:T(8,128)(2,1)} collective-permute-done((bf16[3,256,640]{2,1,0:T(8,128)(2,1)S(1)}, bf16[3,256,640]{2,1,0:T(8,128)(2,1)}, u32[]{:S(2)}, u32[]{:S(2)}) %collective-permute-start.17) | collective-permute-done | bytes 983072 | tf_op jit(solution)/shard_map/ppermute | solution.py:399
  272.0 6.1 %norm_back.1 = (bf16[256,2560]{1,0:T(8,128)(2,1)}, bf16[256,2560]{1,0:T(8,128)(2,1)}, bf16[256,2560]{1,0:T(8,128)(2,1)}) custom-call(s32[5]{0:T(128)} %stack.23.place_ref, bf16[256,2560]{1,0:T(8,128)(2,1)} %q_ref.3, bf16[256,2560]{1,0:T(8,128)(2,1)} %k_ref.3, f32[2560]{0:T(1024)} %gain_q_ref.3, f32[2560]{0:T(1024)} %gain_k_ref.3, ...), custom_call_target="tpu_custom_call" | custom-call | tf_op jit(solution)/shard_map/norm_back/pallas_call | solution.py:93
  (110 shorter events, 36.1 us)
Async XLA Ops:
  7.2 134.6 %all-gather.2.cloned.1.call-start = ((), (), s32[]{:S(2)}) async-start(), calls=%async_computation.1 | async-start | bytes 6963200 | tf_op jit(solution)/shard_map/all_gather | solution.py:483
  7.2 8.7 %collective-permute-start.5 = (bf16[160,640]{1,0:T(8,128)(2,1)}, bf16[160,640]{1,0:T(8,128)(2,1)S(1)}, u32[]{:S(2)}, u32[]{:S(2)}) collective-permute-start(bf16[160,640]{1,0:T(8,128)(2,1)} %param.17), channel_id=1, source_target_pairs={{1,4},{2,1},{3,5},{4,2},{5,6},{6,3},{9,12},{10,9},{11,13},{12,10},... | collective-permute-start | bytes 614408 | tf_op jit(solution)/shard_map/ppermute | solution.py:399
  9.8 6.9 %collective-permute-start.6 = (bf16[160,640]{1,0:T(8,128)(2,1)}, bf16[160,640]{1,0:T(8,128)(2,1)S(1)}, u32[]{:S(2)}, u32[]{:S(2)}) collective-permute-start(bf16[160,640]{1,0:T(8,128)(2,1)} %param.17), channel_id=1, source_target_pairs={{0,2},{1,6},{2,3},{3,7},{4,0},{5,4},{6,1},{7,5},{8,10},{9,14},{10,... | collective-permute-start | bytes 614408 | tf_op jit(solution)/shard_map/ppermute | solution.py:399
  17.6 226.2 %reduce-scatter.2.cloned.1.call-start = ((), (), s32[]{:S(2)}) async-start(), calls=%async_computation.2 | async-start | bytes 4096000 | tf_op jit(solution)/shard_map/reduce_scatter | solution.py:497
  17.6 23.7 %collective-permute-start = (bf16[3,256,640]{2,1,0:T(8,128)(2,1)}, bf16[3,256,640]{2,1,0:T(8,128)(2,1)}, u32[]{:S(2)}, u32[]{:S(2)}) collective-permute-start(bf16[3,256,640]{2,1,0:T(8,128)(2,1)} %get-tuple-element.36), channel_id=1, source_target_pairs={{1,4},{2,1},{3,5},{4,2},{5,6},{6,3},{9,12},{10,9},{11,13},{12,10},... | collective-permute-start | bytes 2949128 | tf_op jit(solution)/shard_map/ppermute | solution.py:399
  22.5 27.6 %collective-permute-start.3 = (bf16[3,256,640]{2,1,0:T(8,128)(2,1)S(1)}, bf16[3,256,640]{2,1,0:T(8,128)(2,1)}, u32[]{:S(2)}, u32[]{:S(2)}) collective-permute-start(bf16[3,256,640]{2,1,0:T(8,128)(2,1)S(1)} %copy-done.21), channel_id=1, source_target_pairs={{0,5},{2,4},{3,0},{4,7},{5,3},{7,2},{8,13},{10,12},{11,8},{12,15},... | collective-permute-start | bytes 2949128 | tf_op jit(solution)/shard_map/ppermute | solution.py:399
  24.4 37.2 %collective-permute-start.1 = (bf16[3,256,640]{2,1,0:T(8,128)(2,1)}, bf16[3,256,640]{2,1,0:T(8,128)(2,1)S(1)}, u32[]{:S(2)}, u32[]{:S(2)}) collective-permute-start(bf16[3,256,640]{2,1,0:T(8,128)(2,1)} %get-tuple-element.37), channel_id=1, source_target_pairs={{0,4},{1,0},{2,5},{3,1},{4,6},{5,2},{6,7},{7,3},{8,12},{9,8},{10,1... | collective-permute-start | bytes 2949128 | tf_op jit(solution)/shard_map/ppermute | solution.py:399
  27.5 43.4 %collective-permute-start.2 = (bf16[3,256,640]{2,1,0:T(8,128)(2,1)}, bf16[3,256,640]{2,1,0:T(8,128)(2,1)}, u32[]{:S(2)}, u32[]{:S(2)}) collective-permute-start(bf16[3,256,640]{2,1,0:T(8,128)(2,1)} %get-tuple-element.38), channel_id=1, source_target_pairs={{0,1},{1,5},{2,0},{3,4},{4,3},{5,7},{6,2},{7,6},{8,9},{9,13},{10,8... | collective-permute-start | bytes 2949128 | tf_op jit(solution)/shard_map/ppermute | solution.py:399
  72.6 33.9 %collective-permute-start.10 = (bf16[128,5120]{1,0:T(8,128)(2,1)}, bf16[128,5120]{1,0:T(8,128)(2,1)}, u32[]{:S(2)}, u32[]{:S(2)}) collective-permute-start(bf16[128,5120]{1,0:T(8,128)(2,1)} %get-tuple-element.68), channel_id=1, source_target_pairs={{0,5},{2,4},{3,0},{4,7},{5,3},{7,2},{8,13},{10,12},{11,8},{12,15},... | collective-permute-start | bytes 3932168 | tf_op jit(solution)/shard_map/ppermute | solution.py:399
  74.5 5.7 %collective-permute-start.4 = (s32[1,16]{1,0:T(1,128)S(1)}, s32[1,16]{1,0:T(1,128)S(1)}, u32[]{:S(2)}, u32[]{:S(2)}) collective-permute-start(s32[1,16]{1,0:T(1,128)S(1)} %copy-done.25), channel_id=1, source_target_pairs={{0,4},{4,0},{1,5},{5,1},{2,6},{6,2},{3,7},{7,3},{8,12},{12,8},{9,1... | collective-permute-start | bytes 200 | tf_op jit(solution)/shard_map/ppermute | solution.py:409
  74.7 59.6 %collective-permute-start.8 = (bf16[128,5120]{1,0:T(8,128)(2,1)}, bf16[128,5120]{1,0:T(8,128)(2,1)S(1)}, u32[]{:S(2)}, u32[]{:S(2)}) collective-permute-start(bf16[128,5120]{1,0:T(8,128)(2,1)} %get-tuple-element.68), channel_id=1, source_target_pairs={{0,4},{1,0},{2,5},{3,1},{4,6},{5,2},{6,7},{7,3},{8,12},{9,8},{10,1... | collective-permute-start | bytes 3932168 | tf_op jit(solution)/shard_map/ppermute | solution.py:399
  78.3 54.0 %collective-permute-start.9 = (bf16[128,5120]{1,0:T(8,128)(2,1)}, bf16[128,5120]{1,0:T(8,128)(2,1)S(1)}, u32[]{:S(2)}, u32[]{:S(2)}) collective-permute-start(bf16[128,5120]{1,0:T(8,128)(2,1)} %get-tuple-element.69), channel_id=1, source_target_pairs={{0,1},{1,5},{2,0},{3,4},{4,3},{5,7},{6,2},{7,6},{8,9},{9,13},{10,8... | collective-permute-start | bytes 3932168 | tf_op jit(solution)/shard_map/ppermute | solution.py:399
  78.3 56.1 %collective-permute-start.7 = (bf16[128,5120]{1,0:T(8,128)(2,1)}, bf16[128,5120]{1,0:T(8,128)(2,1)S(1)}, u32[]{:S(2)}, u32[]{:S(2)}) collective-permute-start(bf16[128,5120]{1,0:T(8,128)(2,1)} %get-tuple-element.69), channel_id=1, source_target_pairs={{1,4},{2,1},{3,5},{4,2},{5,6},{6,3},{9,12},{10,9},{11,13},{12,10},... | collective-permute-start | bytes 3932168 | tf_op jit(solution)/shard_map/ppermute | solution.py:399
  108.0 27.8 %collective-permute-start.14 = (bf16[128,5120]{1,0:T(8,128)(2,1)S(1)}, bf16[128,5120]{1,0:T(8,128)(2,1)S(1)}, u32[]{:S(2)}, u32[]{:S(2)}) collective-permute-start(bf16[128,5120]{1,0:T(8,128)(2,1)S(1)} %broadcast_select_fusion.refs_5_), channel_id=1, source_target_pairs={{0,4},{4,0},{1,5},{5,1},{2,6},{6,2},{3,7},{7,3},{8,12},{12,8},{9,1... | collective-permute-start | bytes 3932168 | tf_op jit(solution)/shard_map/ppermute | solution.py:409
  132.3 4.6 %collective-permute-start.13 = (bf16[128,5120]{1,0:T(8,128)(2,1)S(1)}, bf16[128,5120]{1,0:T(8,128)(2,1)S(1)}, u32[]{:S(2)}, u32[]{:S(2)}) collective-permute-start(bf16[128,5120]{1,0:T(8,128)(2,1)S(1)} %collective-permute-done.9.refs_4_), channel_id=1, source_target_pairs={{0,4},{4,0},{1,5},{5,1},{2,6},{6,2},{3,7},{7,3},{8,12},{12,8},{9,1... | collective-permute-start | bytes 3932168 | tf_op jit(solution)/shard_map/ppermute | solution.py:409
  134.3 6.4 %collective-permute-start.12 = (bf16[128,5120]{1,0:T(8,128)(2,1)S(1)}, bf16[128,5120]{1,0:T(8,128)(2,1)S(1)}, u32[]{:S(2)}, u32[]{:S(2)}) collective-permute-start(bf16[128,5120]{1,0:T(8,128)(2,1)S(1)} %collective-permute-done.8.refs_3_), channel_id=1, source_target_pairs={{0,4},{4,0},{1,5},{5,1},{2,6},{6,2},{3,7},{7,3},{8,12},{12,8},{9,1... | collective-permute-start | bytes 3932168 | tf_op jit(solution)/shard_map/ppermute | solution.py:409
  135.3 6.4 %collective-permute-start.11 = (bf16[128,5120]{1,0:T(8,128)(2,1)S(1)}, bf16[128,5120]{1,0:T(8,128)(2,1)}, u32[]{:S(2)}, u32[]{:S(2)}) collective-permute-start(bf16[128,5120]{1,0:T(8,128)(2,1)S(1)} %broadcast_select_fusion.1.refs_2_), channel_id=1, source_target_pairs={{0,4},{4,0},{1,5},{5,1},{2,6},{6,2},{3,7},{7,3},{8,12},{12,8},{9,1... | collective-permute-start | bytes 3932168 | tf_op jit(solution)/shard_map/ppermute | solution.py:409
  178.0 31.5 %collective-permute-start.19 = (bf16[4,160,640]{2,1,0:T(8,128)(2,1)}, bf16[4,160,640]{2,1,0:T(8,128)(2,1)}, u32[]{:S(2)}, u32[]{:S(2)}) collective-permute-start(bf16[4,160,640]{2,1,0:T(8,128)(2,1)} %get-tuple-element.58), channel_id=1, source_target_pairs={{0,16},{8,24},{16,0},{24,8},{1,17},{9,25},{17,1},{25,9},{2,18},{10... | collective-permute-start | bytes 2457608 | tf_op jit(solution)/shard_map/ppermute | solution.py:414
  181.1 36.9 %collective-permute-start.20 = (bf16[4,160,640]{2,1,0:T(8,128)(2,1)}, bf16[4,160,640]{2,1,0:T(8,128)(2,1)}, u32[]{:S(2)}, u32[]{:S(2)}) collective-permute-start(bf16[4,160,640]{2,1,0:T(8,128)(2,1)} %get-tuple-element.59), channel_id=1, source_target_pairs={{0,8},{8,16},{16,24},{24,0},{1,9},{9,17},{17,25},{25,1},{2,10},{10... | collective-permute-start | bytes 2457608 | tf_op jit(solution)/shard_map/ppermute | solution.py:414
  181.7 36.4 %collective-permute-start.21 = (bf16[4,160,640]{2,1,0:T(8,128)(2,1)}, bf16[4,160,640]{2,1,0:T(8,128)(2,1)}, u32[]{:S(2)}, u32[]{:S(2)}) collective-permute-start(bf16[4,160,640]{2,1,0:T(8,128)(2,1)} %get-tuple-element.60), channel_id=1, source_target_pairs={{0,24},{8,0},{16,8},{24,16},{1,25},{9,1},{17,9},{25,17},{2,26},{10... | collective-permute-start | bytes 2457608 | tf_op jit(solution)/shard_map/ppermute | solution.py:414
  205.5 27.9 %collective-permute-start.18 = (bf16[3,256,640]{2,1,0:T(8,128)(2,1)}, bf16[3,256,640]{2,1,0:T(8,128)(2,1)S(1)}, u32[]{:S(2)}, u32[]{:S(2)}) collective-permute-start(bf16[3,256,640]{2,1,0:T(8,128)(2,1)} %get-tuple-element.54), channel_id=1, source_target_pairs={{5,0},{4,2},{0,3},{7,4},{3,5},{2,7},{13,8},{12,10},{8,11},{15,12},... | collective-permute-start | bytes 2949128 | tf_op jit(solution)/shard_map/ppermute | solution.py:399
  207.4 27.1 %collective-permute-start.15 = (bf16[3,256,640]{2,1,0:T(8,128)(2,1)S(1)}, bf16[3,256,640]{2,1,0:T(8,128)(2,1)S(1)}, u32[]{:S(2)}, u32[]{:S(2)}) collective-permute-start(bf16[3,256,640]{2,1,0:T(8,128)(2,1)S(1)} %get-tuple-element.51), channel_id=1, source_target_pairs={{4,1},{1,2},{5,3},{2,4},{6,5},{3,6},{12,9},{9,10},{13,11},{10,12},... | collective-permute-start | bytes 2949128 | tf_op jit(solution)/shard_map/ppermute | solution.py:399
  236.5 8.4 %collective-permute-start.22 = (bf16[160,640]{1,0:T(8,128)(2,1)}, bf16[160,640]{1,0:T(8,128)(2,1)S(1)}, u32[]{:S(2)}, u32[]{:S(2)}) collective-permute-start(bf16[160,640]{1,0:T(8,128)(2,1)} %get-tuple-element.73), channel_id=1, source_target_pairs={{0,64},{32,96},{64,0},{96,32},{1,65},{33,97},{65,1},{97,33},{2,66}... | collective-permute-start | bytes 614408 | tf_op jit(solution)/shard_map/ppermute | solution.py:414
  240.4 7.2 %collective-permute-start.23 = (bf16[160,640]{1,0:T(8,128)(2,1)}, bf16[160,640]{1,0:T(8,128)(2,1)S(1)}, u32[]{:S(2)}, u32[]{:S(2)}) collective-permute-start(bf16[160,640]{1,0:T(8,128)(2,1)} %get-tuple-element.75), channel_id=1, source_target_pairs={{0,32},{32,64},{64,96},{96,0},{1,33},{33,65},{65,97},{97,1},{2,34}... | collective-permute-start | bytes 614408 | tf_op jit(solution)/shard_map/ppermute | solution.py:414
  241.4 6.2 %collective-permute-start.24 = (bf16[160,640]{1,0:T(8,128)(2,1)}, bf16[160,640]{1,0:T(8,128)(2,1)}, u32[]{:S(2)}, u32[]{:S(2)}) collective-permute-start(bf16[160,640]{1,0:T(8,128)(2,1)} %get-tuple-element.74), channel_id=1, source_target_pairs={{0,96},{32,0},{64,32},{96,64},{1,97},{33,1},{65,33},{97,65},{2,98}... | collective-permute-start | bytes 614408 | tf_op jit(solution)/shard_map/ppermute | solution.py:414
  243.6 20.7 %collective-permute-start.16 = (bf16[3,256,640]{2,1,0:T(8,128)(2,1)S(1)}, bf16[3,256,640]{2,1,0:T(8,128)(2,1)S(1)}, u32[]{:S(2)}, u32[]{:S(2)}) collective-permute-start(bf16[3,256,640]{2,1,0:T(8,128)(2,1)S(1)} %copy-done.9), channel_id=1, source_target_pairs={{4,0},{0,1},{5,2},{1,3},{6,4},{2,5},{7,6},{3,7},{12,8},{8,9},{13,1... | collective-permute-start | bytes 2949128 | tf_op jit(solution)/shard_map/ppermute | solution.py:399
  243.6 28.4 %collective-permute-start.17 = (bf16[3,256,640]{2,1,0:T(8,128)(2,1)S(1)}, bf16[3,256,640]{2,1,0:T(8,128)(2,1)}, u32[]{:S(2)}, u32[]{:S(2)}) collective-permute-start(bf16[3,256,640]{2,1,0:T(8,128)(2,1)S(1)} %copy-done.7), channel_id=1, source_target_pairs={{1,0},{5,1},{0,2},{4,3},{3,4},{7,5},{2,6},{6,7},{9,8},{13,9},{8,10... | collective-permute-start | bytes 2949128 | tf_op jit(solution)/shard_map/ppermute | solution.py:399
  244.9 9.2 %collective-permute-start.25 = (bf16[160,640]{1,0:T(8,128)(2,1)S(1)}, bf16[160,640]{1,0:T(8,128)(2,1)S(1)}, u32[]{:S(2)}, u32[]{:S(2)}) collective-permute-start(bf16[160,640]{1,0:T(8,128)(2,1)S(1)} %get-tuple-element.70), channel_id=1, source_target_pairs={{0,16},{8,24},{16,0},{24,8},{1,17},{9,25},{17,1},{25,9},{2,18},{10... | collective-permute-start | bytes 614408 | tf_op jit(solution)/shard_map/ppermute | solution.py:414
  247.6 8.5 %collective-permute-start.26 = (bf16[160,640]{1,0:T(8,128)(2,1)S(1)}, bf16[160,640]{1,0:T(8,128)(2,1)S(1)}, u32[]{:S(2)}, u32[]{:S(2)}) collective-permute-start(bf16[160,640]{1,0:T(8,128)(2,1)S(1)} %get-tuple-element.72), channel_id=1, source_target_pairs={{0,8},{8,16},{16,24},{24,0},{1,9},{9,17},{17,25},{25,1},{2,10},{10... | collective-permute-start | bytes 614408 | tf_op jit(solution)/shard_map/ppermute | solution.py:414
  247.6 8.4 %collective-permute-start.27 = (bf16[160,640]{1,0:T(8,128)(2,1)S(1)}, bf16[160,640]{1,0:T(8,128)(2,1)S(1)}, u32[]{:S(2)}, u32[]{:S(2)}) collective-permute-start(bf16[160,640]{1,0:T(8,128)(2,1)S(1)} %get-tuple-element.71), channel_id=1, source_target_pairs={{0,24},{8,0},{16,8},{24,16},{1,25},{9,1},{17,9},{25,17},{2,26},{10... | collective-permute-start | bytes 614408 | tf_op jit(solution)/shard_map/ppermute | solution.py:414
  257.8 20.2 %collective-permute-start.28 = (bf16[160,640]{1,0:T(8,128)(2,1)S(1)}, bf16[160,640]{1,0:T(8,128)(2,1)S(1)}, u32[]{:S(2)}, u32[]{:S(2)}) collective-permute-start(bf16[160,640]{1,0:T(8,128)(2,1)S(1)} %get-tuple-element.76), channel_id=1, source_target_pairs={{1,2},{2,4},{3,6},{4,1},{5,3},{6,5},{9,10},{10,12},{11,14},{12,9},... | collective-permute-start | bytes 614408 | tf_op jit(solution)/shard_map/ppermute | solution.py:399
  259.9 18.1 %collective-permute-start.29 = (bf16[160,640]{1,0:T(8,128)(2,1)}, bf16[160,640]{1,0:T(8,128)(2,1)}, u32[]{:S(2)}, u32[]{:S(2)}) collective-permute-start(bf16[160,640]{1,0:T(8,128)(2,1)} %get-tuple-element.77), channel_id=1, source_target_pairs={{0,4},{1,6},{2,0},{3,2},{4,5},{5,7},{6,1},{7,3},{8,12},{9,14},{10,... | collective-permute-start | bytes 614408 | tf_op jit(solution)/shard_map/ppermute | solution.py:399
  (26 other events, 251.4 us)
Sparse Core Ops, SparseCore 0:
  17.7 68.0 all-gather.1
  178.1 41.5 reduce-scatter.1

commit v9 on v7

--- a/solution.py
+++ b/solution.py
@@ -482,7 +482,7 @@
     other = {one: swap_cores(own[one]), two: swap_cores(after(own[two], attended))}
     own_grads = {one: project(own[one]), two: project(own[two])}
     other_grads = {one: project(other[one]), two: project(other[two])}
-    other[three] = swap_cores(after(own[three], own_grads[one], other_grads[one]))
+    other[three] = swap_cores(after(own[three], list(own_grads.values()), list(other_grads.values())))
     own_grads[three], other_grads[three] = project(own[three]), project(other[three])
     done = ([own_grads[r] for r in ORDER[:-1]], [other_grads[r] for r in ORDER[:-2]])
     other[last] = swap_cores(after(own[last], *done))
@@ -498,9 +498,9 @@
     one = [one[0]] + [shift(one[by], "x", by) for by in (2, 1, 3)]
     parts = backward(place, tile_pairs, packs, own_grads, other_grads, after(probs, token))
     one = add(*after(one, parts[0]))
+    parts = {r: send(parts[r] if r in ORDER[:2] else after(parts[r], one), inward(r)) for r in ORDER}
     two = lax.optimization_barrier(add(*scatter(after(two, one), "x")))
     one = lax.optimization_barrier(add(*scatter(one, "z")))
-    parts = {r: send(parts[r] if r in ORDER[:2] else after(parts[r], two), inward(r)) for r in ORDER}
     grad_w = to_owners((one, two), seq)
     grad_q, grad_k, grad_v = finish(
         place, queries, keys, gain_q, gain_k, [parts[r] for r in range(SEQ)]

time: 271 us -> 263 us (0.970)
  waiting for transfers between devices: 99.2 us -> 87.6 us
    ppermute x16, waiting for transfers between devices: 83.3 us -> 74.7 us  [send(): got = lax.ppermute(value, ('core', 'seq'), others)]
    ppermute x9, starting transfers between devices: 14.8 us -> 19.2 us  [shift(): lax.ppermute(value, axis, [(i, (i + by) % count) for i in range(count)])]
    ppermute x9, waiting for transfers between devices: 15.8 us -> 12.8 us  [shift(): lax.ppermute(value, axis, [(i, (i + by) % count) for i in range(count)])]
  transfers between devices with their start and end apart: 32 -> 32, of which waited for: 17 -> 16; matrix products, arithmetic and copies ran while one was open for 14% -> 14% of each run, Pallas kernels for 14% -> 16%
where the time goes in v9:
time: 263 us; the launch traced here: 262 us
  waiting for transfers between devices  87.6 us (33%)
  Pallas kernels  57 us (22%)
  starting transfers between devices  52.5 us (20%)
  matrix products  21.2 us (8%)
  other arithmetic  16.4 us (6%)
  between operations  14.6 us (6%)
  local copies, waits for them, and re-layouts  12.4 us (5%)
    ppermute x16, waiting for transfers between devices, send(): got = lax.ppermute(value, ('core', 'seq'), others)  74.7 us
    ppermute x16, starting transfers between devices, send(): got = lax.ppermute(value, ('core', 'seq'), others)  30.2 us
    dot_general x8, matrix products, project(): jnp.dot(part, w_all, preferred_element_type=jnp.float32)  21.2 us
    pallas_call x1, Pallas kernels, backward(): pl.pallas_call(backward_kernel, grid=(heads,), in_specs=[smem()] * 2 + [s...  19.4 us
    ppermute x9, starting transfers between devices, shift(): lax.ppermute(value, axis, [(i, (i + by) % count) for i in range(count)])  19.2 us
    pallas_call x1, Pallas kernels, weight_grad(): pl.pallas_call(lambda place_ref, *refs: weight_grad_kernel(place_ref, mea...  14.3 us
    ppermute x9, waiting for transfers between devices, shift(): lax.ppermute(value, axis, [(i, (i + by) % count) for i in range(count)])  12.8 us
    pallas_call x1, Pallas kernels, forward(): pl.pallas_call(forward_kernel, grid=(heads,), in_specs=[smem()] * 3 + [sp...  11.8 us
  transfers between devices with their start and end apart: 32, of which 16 were waited for; matrix products, arithmetic and copies ran while one was open for 14% of the time, Pallas kernels for 16%

profile of v9, /device:TPU:24, one launch (start us, length us, event | category | flops | bytes accessed | tf_op | source)
XLA Modules:
  0.0 261.7 jit_solution(14085919897336103502)
XLA Ops:
  10.6 5.4 %norm_rows.1 = (bf16[3,256,640]{2,1,0:T(8,128)(2,1)}, bf16[3,256,640]{2,1,0:T(8,128)(2,1)}, bf16[3,256,640]{2,1,0:T(8,128)(2,1)}, bf16[3,256,640]{2,1,0:T(8,128)(2,1)}) custom-call(s32[5]{0:T(128)} %stack.23.place_ref, bf16[256,2560]{1,0:T(8,128)(2,1)} %q_ref.3, bf16[256,2560]{1,0:T(8,128)(2,1)} %k_ref.3, bf16[256,2560]{1,0:T(8,128)(2,1)} %v_ref.1, ...), custom_call_target="tpu_custom_call" | custom-call | tf_op jit(solution)/shard_map/norm_rows/pallas_call | solution.py:61
  17.6 4.8 %collective-permute-start = (bf16[3,256,640]{2,1,0:T(8,128)(2,1)}, bf16[3,256,640]{2,1,0:T(8,128)(2,1)}, u32[]{:S(2)}, u32[]{:S(2)}) collective-permute-start(bf16[3,256,640]{2,1,0:T(8,128)(2,1)} %get-tuple-element.37), channel_id=1, source_target_pairs={{1,4},{2,1},{3,5},{4,2},{5,6},{6,3},{9,12},{10,9},{11,13},{12,10},... | collective-permute-start | bytes 2949128 | tf_op jit(solution)/shard_map/ppermute | solution.py:385
  24.4 3.0 %collective-permute-start.1 = (bf16[3,256,640]{2,1,0:T(8,128)(2,1)}, bf16[3,256,640]{2,1,0:T(8,128)(2,1)S(1)}, u32[]{:S(2)}, u32[]{:S(2)}) collective-permute-start(bf16[3,256,640]{2,1,0:T(8,128)(2,1)} %get-tuple-element.38), channel_id=1, source_target_pairs={{0,4},{1,0},{2,5},{3,1},{4,6},{5,2},{6,7},{7,3},{8,12},{9,8},{10,1... | collective-permute-start | bytes 2949128 | tf_op jit(solution)/shard_map/ppermute | solution.py:385
  27.6 13.7 %collective-permute-done = bf16[3,256,640]{2,1,0:T(8,128)(2,1)} collective-permute-done((bf16[3,256,640]{2,1,0:T(8,128)(2,1)}, bf16[3,256,640]{2,1,0:T(8,128)(2,1)}, u32[]{:S(2)}, u32[]{:S(2)}) %collective-permute-start) | collective-permute-done | bytes 983072 | tf_op jit(solution)/shard_map/ppermute | solution.py:385
  42.6 7.5 %collective-permute-done.3 = bf16[3,256,640]{2,1,0:T(8,128)(2,1)} collective-permute-done((bf16[3,256,640]{2,1,0:T(8,128)(2,1)S(1)}, bf16[3,256,640]{2,1,0:T(8,128)(2,1)}, u32[]{:S(2)}, u32[]{:S(2)}) %collective-permute-start.3) | collective-permute-done | bytes 983072 | tf_op jit(solution)/shard_map/ppermute | solution.py:385
  51.4 10.2 %collective-permute-done.1.refs_1_.refs_5_.refs_9_ = bf16[3,256,640]{2,1,0:T(8,128)(2,1)S(1)} collective-permute-done((bf16[3,256,640]{2,1,0:T(8,128)(2,1)}, bf16[3,256,640]{2,1,0:T(8,128)(2,1)S(1)}, u32[]{:S(2)}, u32[]{:S(2)}) %collective-permute-start.1) | collective-permute-done | bytes 983072 | tf_op jit(solution)/shard_map/ppermute | solution.py:385
  61.6 9.3 %collective-permute-done.2.refs_2_.refs_6_.refs_10_ = bf16[3,256,640]{2,1,0:T(8,128)(2,1)} collective-permute-done((bf16[3,256,640]{2,1,0:T(8,128)(2,1)}, bf16[3,256,640]{2,1,0:T(8,128)(2,1)}, u32[]{:S(2)}, u32[]{:S(2)}) %collective-permute-start.2) | collective-permute-done | bytes 983072 | tf_op jit(solution)/shard_map/ppermute | solution.py:385
  74.7 2.7 %collective-permute-start.9 = (bf16[128,5120]{1,0:T(8,128)(2,1)}, bf16[128,5120]{1,0:T(8,128)(2,1)S(1)}, u32[]{:S(2)}, u32[]{:S(2)}) collective-permute-start(bf16[128,5120]{1,0:T(8,128)(2,1)} %get-tuple-element.70), channel_id=1, source_target_pairs={{0,5},{2,4},{3,0},{4,7},{5,3},{7,2},{8,13},{10,12},{11,8},{12,15},... | collective-permute-start | bytes 3932168 | tf_op jit(solution)/shard_map/ppermute | solution.py:385
  79.8 11.8 %attention_forward.1 = (bf16[1024,640]{1,0:T(8,128)(2,1)S(1)}, bf16[5,4096,128]{2,1,0:T(8,128)(2,1)}) custom-call(s32[5]{0:T(128)S(1)} %copy-done.9, s32[16,8]{1,0:T(8,128)S(1)} %copy.14.pairs_ref, s32[1,16]{1,0:T(1,128)S(1)} %broadcast_select_fusion.9.lens_ref, bf16[3,256,640]{2,1,0:T(8,128)(2,1)S(1)} %broadcast_select_fusion.5.refs_0_.refs_4_.refs_8_, ...), custom_call_target="tpu_custom_call" | custom-call | tf_op jit(solution)/shard_map/attention_forward/pallas_call | solution.py:212
  91.7 11.3 %collective-permute-done.4 = bf16[128,5120]{1,0:T(8,128)(2,1)} collective-permute-done((bf16[128,5120]{1,0:T(8,128)(2,1)}, bf16[128,5120]{1,0:T(8,128)(2,1)}, u32[]{:S(2)}, u32[]{:S(2)}) %collective-permute-start.4) | collective-permute-done | bytes 1310752 | tf_op jit(solution)/shard_map/ppermute | solution.py:385
  104.6 4.9 %collective-permute-done.9 = bf16[128,5120]{1,0:T(8,128)(2,1)S(1)} collective-permute-done((bf16[128,5120]{1,0:T(8,128)(2,1)}, bf16[128,5120]{1,0:T(8,128)(2,1)S(1)}, u32[]{:S(2)}, u32[]{:S(2)}) %collective-permute-start.9) | collective-permute-done | bytes 1310752 | tf_op jit(solution)/shard_map/ppermute | solution.py:385
  109.7 4.4 %convolution_convert_fusion.7.refs_12_ = bf16[128,640]{1,0:T(8,128)(2,1)S(1)} fusion(bf16[128,5120]{1,0:T(8,128)(2,1)S(1)} %broadcast_select_fusion.1.refs_1_, bf16[5120,640]{1,0:T(8,128)(2,1)} %all-gather.2.cloned.1.call-done), kind=kOutput, calls=%fused_computation.12 | convolution fusion | flops 838942720 | bytes 8028160 | tf_op jit(solution)/shard_map/dot_general | solution.py:478
  118.7 2.6 convolution_convert_fusion.2.refs_19_
  121.3 7.2 %collective-permute-done.7.refs_2_ = bf16[128,5120]{1,0:T(8,128)(2,1)} collective-permute-done((bf16[128,5120]{1,0:T(8,128)(2,1)}, bf16[128,5120]{1,0:T(8,128)(2,1)}, u32[]{:S(2)}, u32[]{:S(2)}) %collective-permute-start.7) | collective-permute-done | bytes 1310752 | tf_op jit(solution)/shard_map/ppermute | solution.py:385
  128.4 2.8 %collective-permute-start.13 = (bf16[128,5120]{1,0:T(8,128)(2,1)}, bf16[128,5120]{1,0:T(8,128)(2,1)S(1)}, u32[]{:S(2)}, u32[]{:S(2)}) collective-permute-start(bf16[128,5120]{1,0:T(8,128)(2,1)} %collective-permute-done.7.refs_2_), channel_id=1, source_target_pairs={{0,4},{4,0},{1,5},{5,1},{2,6},{6,2},{3,7},{7,3},{8,12},{12,8},{9,1... | collective-permute-start | bytes 3932168 | tf_op jit(solution)/shard_map/ppermute | solution.py:395
  131.2 3.3 %convolution_convert_fusion.6.refs_13_ = bf16[128,640]{1,0:T(8,128)(2,1)} fusion(bf16[128,5120]{1,0:T(8,128)(2,1)} %collective-permute-done.7.refs_2_, bf16[5120,640]{1,0:T(8,128)(2,1)S(1)} %copy-done.14), kind=kOutput, calls=%fused_computation.11 | convolution fusion | flops 838942720 | bytes 8028160 | tf_op jit(solution)/shard_map/dot_general | solution.py:478
  134.5 2.9 %collective-permute-done.8.refs_3_ = bf16[128,5120]{1,0:T(8,128)(2,1)} collective-permute-done((bf16[128,5120]{1,0:T(8,128)(2,1)}, bf16[128,5120]{1,0:T(8,128)(2,1)}, u32[]{:S(2)}, u32[]{:S(2)}) %collective-permute-start.8) | collective-permute-done | bytes 1310752 | tf_op jit(solution)/shard_map/ppermute | solution.py:385
  137.3 3.3 %convolution_convert_fusion.5.refs_14_ = bf16[128,640]{1,0:T(8,128)(2,1)} fusion(bf16[128,5120]{1,0:T(8,128)(2,1)} %collective-permute-done.8.refs_3_, bf16[5120,640]{1,0:T(8,128)(2,1)S(1)} %copy-done.14), kind=kOutput, calls=%fused_computation.10 | convolution fusion | flops 838942720 | bytes 8028160 | tf_op jit(solution)/shard_map/dot_general | solution.py:478
  144.4 14.3 %weight_grad.1 = (bf16[4,160,640]{2,1,0:T(8,128)(2,1)S(1)}, bf16[4,160,640]{2,1,0:T(8,128)(2,1)}, bf16[4,160,640]{2,1,0:T(8,128)(2,1)}, bf16[4,160,640]{2,1,0:T(8,128)(2,1)}, bf16[16,160,640]{2,1,0:T(8,128)(2,1)}) custom-call(s32[5]{0:T(128)S(1)} %copy-done.9, bf16[1024,640]{1,0:T(8,128)(2,1)S(1)} %copy-done.4, ...), custom_call_target="tpu_custom_call" | custom-call | tf_op jit(solution)/shard_map/weight_grad/pallas_call | solution.py:352
  158.7 3.1 %collective-permute-start.16 = (bf16[4,160,640]{2,1,0:T(8,128)(2,1)}, bf16[4,160,640]{2,1,0:T(8,128)(2,1)}, u32[]{:S(2)}, u32[]{:S(2)}) collective-permute-start(bf16[4,160,640]{2,1,0:T(8,128)(2,1)} %get-tuple-element.54), channel_id=1, source_target_pairs={{0,16},{8,24},{16,0},{24,8},{1,17},{9,25},{17,1},{25,9},{2,18},{10... | collective-permute-start | bytes 2457608 | tf_op jit(solution)/shard_map/ppermute | solution.py:400
  162.4 2.7 %collective-permute-start.18 = (bf16[4,160,640]{2,1,0:T(8,128)(2,1)}, bf16[4,160,640]{2,1,0:T(8,128)(2,1)}, u32[]{:S(2)}, u32[]{:S(2)}) collective-permute-start(bf16[4,160,640]{2,1,0:T(8,128)(2,1)} %get-tuple-element.56), channel_id=1, source_target_pairs={{0,24},{8,0},{16,8},{24,16},{1,25},{9,1},{17,9},{25,17},{2,26},{10... | collective-permute-start | bytes 2457608 | tf_op jit(solution)/shard_map/ppermute | solution.py:400
  168.7 19.4 %attention_backward.1 = (bf16[3,256,640]{2,1,0:T(8,128)(2,1)S(1)}, bf16[3,256,640]{2,1,0:T(8,128)(2,1)S(1)}, bf16[3,256,640]{2,1,0:T(8,128)(2,1)S(1)}, bf16[3,256,640]{2,1,0:T(8,128)(2,1)S(1)}) custom-call(s32[5]{0:T(128)S(1)} %copy-done.9, s32[16,8]{1,0:T(8,128)S(1)} %copy.14.pairs_ref, bf16[3,256,640]{2,1,0:T(8,128)(2,1)} %copy-done, ...), custom_call_target="tpu_custom_call" | custom-call | tf_op jit(solution)/shard_map/attention_backward/pallas_call | solution.py:306
  192.1 5.1 %collective-permute-start.21 = (bf16[3,256,640]{2,1,0:T(8,128)(2,1)S(1)}, bf16[3,256,640]{2,1,0:T(8,128)(2,1)}, u32[]{:S(2)}, u32[]{:S(2)}) collective-permute-start(bf16[3,256,640]{2,1,0:T(8,128)(2,1)S(1)} %get-tuple-element.64), channel_id=1, source_target_pairs={{5,0},{4,2},{0,3},{7,4},{3,5},{2,7},{13,8},{12,10},{8,11},{15,12},... | collective-permute-start | bytes 2949128 | tf_op jit(solution)/shard_map/ppermute | solution.py:385
  202.6 4.0 %collective-permute-start.24 = (bf16[160,640]{1,0:T(8,128)(2,1)S(1)}, bf16[160,640]{1,0:T(8,128)(2,1)S(1)}, u32[]{:S(2)}, u32[]{:S(2)}) collective-permute-start(bf16[160,640]{1,0:T(8,128)(2,1)S(1)} %get-tuple-element.76), channel_id=1, source_target_pairs={{0,96},{32,0},{64,32},{96,64},{1,97},{33,1},{65,33},{97,65},{2,98}... | collective-permute-start | bytes 614408 | tf_op jit(solution)/shard_map/ppermute | solution.py:400
  209.8 2.7 %collective-permute-start.27 = (bf16[160,640]{1,0:T(8,128)(2,1)S(1)}, bf16[160,640]{1,0:T(8,128)(2,1)S(1)}, u32[]{:S(2)}, u32[]{:S(2)}) collective-permute-start(bf16[160,640]{1,0:T(8,128)(2,1)S(1)} %get-tuple-element.73), channel_id=1, source_target_pairs={{0,24},{8,0},{16,8},{24,16},{1,25},{9,1},{17,9},{25,17},{2,26},{10... | collective-permute-start | bytes 614408 | tf_op jit(solution)/shard_map/ppermute | solution.py:400
  215.5 3.4 %collective-permute-done.23 = bf16[160,640]{1,0:T(8,128)(2,1)S(1)} collective-permute-done((bf16[160,640]{1,0:T(8,128)(2,1)S(1)}, bf16[160,640]{1,0:T(8,128)(2,1)S(1)}, u32[]{:S(2)}, u32[]{:S(2)}) %collective-permute-start.23) | collective-permute-done | bytes 204832 | tf_op jit(solution)/shard_map/ppermute | solution.py:400
  220.5 2.7 %collective-permute-start.25 = (bf16[160,640]{1,0:T(8,128)(2,1)S(1)}, bf16[160,640]{1,0:T(8,128)(2,1)S(1)}, u32[]{:S(2)}, u32[]{:S(2)}) collective-permute-start(bf16[160,640]{1,0:T(8,128)(2,1)S(1)} %get-tuple-element.72), channel_id=1, source_target_pairs={{0,16},{8,24},{16,0},{24,8},{1,17},{9,25},{17,1},{25,9},{2,18},{10... | collective-permute-start | bytes 614408 | tf_op jit(solution)/shard_map/ppermute | solution.py:400
  224.3 2.9 %collective-permute-done.26 = bf16[160,640]{1,0:T(8,128)(2,1)S(1)} collective-permute-done((bf16[160,640]{1,0:T(8,128)(2,1)S(1)}, bf16[160,640]{1,0:T(8,128)(2,1)S(1)}, u32[]{:S(2)}, u32[]{:S(2)}) %collective-permute-start.26) | collective-permute-done | bytes 204832 | tf_op jit(solution)/shard_map/ppermute | solution.py:400
  227.2 4.1 %collective-permute-done.25 = bf16[160,640]{1,0:T(8,128)(2,1)S(1)} collective-permute-done((bf16[160,640]{1,0:T(8,128)(2,1)S(1)}, bf16[160,640]{1,0:T(8,128)(2,1)S(1)}, u32[]{:S(2)}, u32[]{:S(2)}) %collective-permute-start.25) | collective-permute-done | bytes 204832 | tf_op jit(solution)/shard_map/ppermute | solution.py:400
  233.1 3.5 %collective-permute-start.28 = (bf16[160,640]{1,0:T(8,128)(2,1)S(1)}, bf16[160,640]{1,0:T(8,128)(2,1)}, u32[]{:S(2)}, u32[]{:S(2)}) collective-permute-start(bf16[160,640]{1,0:T(8,128)(2,1)S(1)} %get-tuple-element.78), channel_id=1, source_target_pairs={{1,2},{2,4},{3,6},{4,1},{5,3},{6,5},{9,10},{10,12},{11,14},{12,9},... | collective-permute-start | bytes 614408 | tf_op jit(solution)/shard_map/ppermute | solution.py:385
  238.9 7.2 %collective-permute-done.20.refs_2_ = bf16[3,256,640]{2,1,0:T(8,128)(2,1)S(1)} collective-permute-done((bf16[3,256,640]{2,1,0:T(8,128)(2,1)S(1)}, bf16[3,256,640]{2,1,0:T(8,128)(2,1)S(1)}, u32[]{:S(2)}, u32[]{:S(2)}) %collective-permute-start.20) | collective-permute-done | bytes 983072 | tf_op jit(solution)/shard_map/ppermute | solution.py:385
  247.0 6.1 %norm_back.1 = (bf16[256,2560]{1,0:T(8,128)(2,1)}, bf16[256,2560]{1,0:T(8,128)(2,1)}, bf16[256,2560]{1,0:T(8,128)(2,1)}) custom-call(s32[5]{0:T(128)} %stack.23.place_ref, bf16[256,2560]{1,0:T(8,128)(2,1)} %q_ref.3, bf16[256,2560]{1,0:T(8,128)(2,1)} %k_ref.3, f32[2560]{0:T(1024)} %gain_q_ref.3, f32[2560]{0:T(1024)} %gain_k_ref.3, ...), custom_call_target="tpu_custom_call" | custom-call | tf_op jit(solution)/shard_map/norm_back/pallas_call | solution.py:93
  (122 shorter events, 55.1 us)
Async XLA Ops:
  7.2 102.5 %all-gather.2.cloned.1.call-start = ((), (), s32[]{:S(2)}) async-start(), calls=%async_computation.1 | async-start | bytes 6963200 | tf_op jit(solution)/shard_map/all_gather | solution.py:469
  7.2 8.7 %collective-permute-start.5 = (bf16[160,640]{1,0:T(8,128)(2,1)}, bf16[160,640]{1,0:T(8,128)(2,1)S(1)}, u32[]{:S(2)}, u32[]{:S(2)}) collective-permute-start(bf16[160,640]{1,0:T(8,128)(2,1)} %param.17), channel_id=1, source_target_pairs={{1,4},{2,1},{3,5},{4,2},{5,6},{6,3},{9,12},{10,9},{11,13},{12,10},... | collective-permute-start | bytes 614408 | tf_op jit(solution)/shard_map/ppermute | solution.py:385
  9.8 6.9 %collective-permute-start.6 = (bf16[160,640]{1,0:T(8,128)(2,1)}, bf16[160,640]{1,0:T(8,128)(2,1)S(1)}, u32[]{:S(2)}, u32[]{:S(2)}) collective-permute-start(bf16[160,640]{1,0:T(8,128)(2,1)} %param.17), channel_id=1, source_target_pairs={{0,2},{1,6},{2,3},{3,7},{4,0},{5,4},{6,1},{7,5},{8,10},{9,14},{10,... | collective-permute-start | bytes 614408 | tf_op jit(solution)/shard_map/ppermute | solution.py:385
  17.6 191.0 %reduce-scatter.2.cloned.1.call-start = ((), (), s32[]{:S(2)}) async-start(), calls=%async_computation.2 | async-start | bytes 4096000 | tf_op jit(solution)/shard_map/reduce_scatter | solution.py:496
  17.6 23.7 %collective-permute-start = (bf16[3,256,640]{2,1,0:T(8,128)(2,1)}, bf16[3,256,640]{2,1,0:T(8,128)(2,1)}, u32[]{:S(2)}, u32[]{:S(2)}) collective-permute-start(bf16[3,256,640]{2,1,0:T(8,128)(2,1)} %get-tuple-element.37), channel_id=1, source_target_pairs={{1,4},{2,1},{3,5},{4,2},{5,6},{6,3},{9,12},{10,9},{11,13},{12,10},... | collective-permute-start | bytes 2949128 | tf_op jit(solution)/shard_map/ppermute | solution.py:385
  22.5 27.6 %collective-permute-start.3 = (bf16[3,256,640]{2,1,0:T(8,128)(2,1)S(1)}, bf16[3,256,640]{2,1,0:T(8,128)(2,1)}, u32[]{:S(2)}, u32[]{:S(2)}) collective-permute-start(bf16[3,256,640]{2,1,0:T(8,128)(2,1)S(1)} %copy-done.23), channel_id=1, source_target_pairs={{0,5},{2,4},{3,0},{4,7},{5,3},{7,2},{8,13},{10,12},{11,8},{12,15},... | collective-permute-start | bytes 2949128 | tf_op jit(solution)/shard_map/ppermute | solution.py:385
  24.4 37.2 %collective-permute-start.1 = (bf16[3,256,640]{2,1,0:T(8,128)(2,1)}, bf16[3,256,640]{2,1,0:T(8,128)(2,1)S(1)}, u32[]{:S(2)}, u32[]{:S(2)}) collective-permute-start(bf16[3,256,640]{2,1,0:T(8,128)(2,1)} %get-tuple-element.38), channel_id=1, source_target_pairs={{0,4},{1,0},{2,5},{3,1},{4,6},{5,2},{6,7},{7,3},{8,12},{9,8},{10,1... | collective-permute-start | bytes 2949128 | tf_op jit(solution)/shard_map/ppermute | solution.py:385
  27.4 43.5 %collective-permute-start.2 = (bf16[3,256,640]{2,1,0:T(8,128)(2,1)}, bf16[3,256,640]{2,1,0:T(8,128)(2,1)}, u32[]{:S(2)}, u32[]{:S(2)}) collective-permute-start(bf16[3,256,640]{2,1,0:T(8,128)(2,1)} %get-tuple-element.39), channel_id=1, source_target_pairs={{0,1},{1,5},{2,0},{3,4},{4,3},{5,7},{6,2},{7,6},{8,9},{9,13},{10,8... | collective-permute-start | bytes 2949128 | tf_op jit(solution)/shard_map/ppermute | solution.py:385
  72.6 30.4 %collective-permute-start.4 = (bf16[128,5120]{1,0:T(8,128)(2,1)}, bf16[128,5120]{1,0:T(8,128)(2,1)}, u32[]{:S(2)}, u32[]{:S(2)}) collective-permute-start(bf16[128,5120]{1,0:T(8,128)(2,1)} %get-tuple-element.71), channel_id=1, source_target_pairs={{1,4},{2,1},{3,5},{4,2},{5,6},{6,3},{9,12},{10,9},{11,13},{12,10},... | collective-permute-start | bytes 3932168 | tf_op jit(solution)/shard_map/ppermute | solution.py:385
  74.5 2.9 %collective-permute-start.11 = (s32[1,16]{1,0:T(1,128)S(1)}, s32[1,16]{1,0:T(1,128)S(1)}, u32[]{:S(2)}, u32[]{:S(2)}) collective-permute-start(s32[1,16]{1,0:T(1,128)S(1)} %copy-done.27), channel_id=1, source_target_pairs={{0,4},{4,0},{1,5},{5,1},{2,6},{6,2},{3,7},{7,3},{8,12},{12,8},{9,1... | collective-permute-start | bytes 200 | tf_op jit(solution)/shard_map/ppermute | solution.py:395
  74.7 34.7 %collective-permute-start.9 = (bf16[128,5120]{1,0:T(8,128)(2,1)}, bf16[128,5120]{1,0:T(8,128)(2,1)S(1)}, u32[]{:S(2)}, u32[]{:S(2)}) collective-permute-start(bf16[128,5120]{1,0:T(8,128)(2,1)} %get-tuple-element.70), channel_id=1, source_target_pairs={{0,5},{2,4},{3,0},{4,7},{5,3},{7,2},{8,13},{10,12},{11,8},{12,15},... | collective-permute-start | bytes 3932168 | tf_op jit(solution)/shard_map/ppermute | solution.py:385
  77.4 51.0 %collective-permute-start.7 = (bf16[128,5120]{1,0:T(8,128)(2,1)}, bf16[128,5120]{1,0:T(8,128)(2,1)}, u32[]{:S(2)}, u32[]{:S(2)}) collective-permute-start(bf16[128,5120]{1,0:T(8,128)(2,1)} %get-tuple-element.70), channel_id=1, source_target_pairs={{0,4},{1,0},{2,5},{3,1},{4,6},{5,2},{6,7},{7,3},{8,12},{9,8},{10,1... | collective-permute-start | bytes 3932168 | tf_op jit(solution)/shard_map/ppermute | solution.py:385
  77.5 59.8 %collective-permute-start.8 = (bf16[128,5120]{1,0:T(8,128)(2,1)}, bf16[128,5120]{1,0:T(8,128)(2,1)}, u32[]{:S(2)}, u32[]{:S(2)}) collective-permute-start(bf16[128,5120]{1,0:T(8,128)(2,1)} %get-tuple-element.71), channel_id=1, source_target_pairs={{0,1},{1,5},{2,0},{3,4},{4,3},{5,7},{6,2},{7,6},{8,9},{9,13},{10,8... | collective-permute-start | bytes 3932168 | tf_op jit(solution)/shard_map/ppermute | solution.py:385
  104.5 11.6 %collective-permute-start.10 = (bf16[128,5120]{1,0:T(8,128)(2,1)S(1)}, bf16[128,5120]{1,0:T(8,128)(2,1)}, u32[]{:S(2)}, u32[]{:S(2)}) collective-permute-start(bf16[128,5120]{1,0:T(8,128)(2,1)S(1)} %broadcast_select_fusion.1.refs_1_), channel_id=1, source_target_pairs={{0,4},{4,0},{1,5},{5,1},{2,6},{6,2},{3,7},{7,3},{8,12},{12,8},{9,1... | collective-permute-start | bytes 3932168 | tf_op jit(solution)/shard_map/ppermute | solution.py:395
  109.6 9.1 %collective-permute-start.12 = (bf16[128,5120]{1,0:T(8,128)(2,1)S(1)}, bf16[128,5120]{1,0:T(8,128)(2,1)}, u32[]{:S(2)}, u32[]{:S(2)}) collective-permute-start(bf16[128,5120]{1,0:T(8,128)(2,1)S(1)} %broadcast_select_fusion.refs_4_), channel_id=1, source_target_pairs={{0,4},{4,0},{1,5},{5,1},{2,6},{6,2},{3,7},{7,3},{8,12},{12,8},{9,1... | collective-permute-start | bytes 3932168 | tf_op jit(solution)/shard_map/ppermute | solution.py:395
  128.4 12.2 %collective-permute-start.13 = (bf16[128,5120]{1,0:T(8,128)(2,1)}, bf16[128,5120]{1,0:T(8,128)(2,1)S(1)}, u32[]{:S(2)}, u32[]{:S(2)}) collective-permute-start(bf16[128,5120]{1,0:T(8,128)(2,1)} %collective-permute-done.7.refs_2_), channel_id=1, source_target_pairs={{0,4},{4,0},{1,5},{5,1},{2,6},{6,2},{3,7},{7,3},{8,12},{12,8},{9,1... | collective-permute-start | bytes 3932168 | tf_op jit(solution)/shard_map/ppermute | solution.py:395
  137.3 5.2 %collective-permute-start.14 = (bf16[128,5120]{1,0:T(8,128)(2,1)}, bf16[128,5120]{1,0:T(8,128)(2,1)S(1)}, u32[]{:S(2)}, u32[]{:S(2)}) collective-permute-start(bf16[128,5120]{1,0:T(8,128)(2,1)} %collective-permute-done.8.refs_3_), channel_id=1, source_target_pairs={{0,4},{4,0},{1,5},{5,1},{2,6},{6,2},{3,7},{7,3},{8,12},{12,8},{9,1... | collective-permute-start | bytes 3932168 | tf_op jit(solution)/shard_map/ppermute | solution.py:395
  158.7 38.5 %collective-permute-start.16 = (bf16[4,160,640]{2,1,0:T(8,128)(2,1)}, bf16[4,160,640]{2,1,0:T(8,128)(2,1)}, u32[]{:S(2)}, u32[]{:S(2)}) collective-permute-start(bf16[4,160,640]{2,1,0:T(8,128)(2,1)} %get-tuple-element.54), channel_id=1, source_target_pairs={{0,16},{8,24},{16,0},{24,8},{1,17},{9,25},{17,1},{25,9},{2,18},{10... | collective-permute-start | bytes 2457608 | tf_op jit(solution)/shard_map/ppermute | solution.py:400
  161.8 37.0 %collective-permute-start.17 = (bf16[4,160,640]{2,1,0:T(8,128)(2,1)}, bf16[4,160,640]{2,1,0:T(8,128)(2,1)}, u32[]{:S(2)}, u32[]{:S(2)}) collective-permute-start(bf16[4,160,640]{2,1,0:T(8,128)(2,1)} %get-tuple-element.55), channel_id=1, source_target_pairs={{0,8},{8,16},{16,24},{24,0},{1,9},{9,17},{17,25},{25,1},{2,10},{10... | collective-permute-start | bytes 2457608 | tf_op jit(solution)/shard_map/ppermute | solution.py:400
  162.4 36.5 %collective-permute-start.18 = (bf16[4,160,640]{2,1,0:T(8,128)(2,1)}, bf16[4,160,640]{2,1,0:T(8,128)(2,1)}, u32[]{:S(2)}, u32[]{:S(2)}) collective-permute-start(bf16[4,160,640]{2,1,0:T(8,128)(2,1)} %get-tuple-element.56), channel_id=1, source_target_pairs={{0,24},{8,0},{16,8},{24,16},{1,25},{9,1},{17,9},{25,17},{2,26},{10... | collective-permute-start | bytes 2457608 | tf_op jit(solution)/shard_map/ppermute | solution.py:400
  190.1 19.6 %collective-permute-start.15 = (bf16[3,256,640]{2,1,0:T(8,128)(2,1)S(1)}, bf16[3,256,640]{2,1,0:T(8,128)(2,1)}, u32[]{:S(2)}, u32[]{:S(2)}) collective-permute-start(bf16[3,256,640]{2,1,0:T(8,128)(2,1)S(1)} %get-tuple-element.52), channel_id=1, source_target_pairs={{4,1},{1,2},{5,3},{2,4},{6,5},{3,6},{12,9},{9,10},{13,11},{10,12},... | collective-permute-start | bytes 2949128 | tf_op jit(solution)/shard_map/ppermute | solution.py:385
  192.1 44.5 %collective-permute-start.21 = (bf16[3,256,640]{2,1,0:T(8,128)(2,1)S(1)}, bf16[3,256,640]{2,1,0:T(8,128)(2,1)}, u32[]{:S(2)}, u32[]{:S(2)}) collective-permute-start(bf16[3,256,640]{2,1,0:T(8,128)(2,1)S(1)} %get-tuple-element.64), channel_id=1, source_target_pairs={{5,0},{4,2},{0,3},{7,4},{3,5},{2,7},{13,8},{12,10},{8,11},{15,12},... | collective-permute-start | bytes 2949128 | tf_op jit(solution)/shard_map/ppermute | solution.py:385
  202.6 12.9 %collective-permute-start.24 = (bf16[160,640]{1,0:T(8,128)(2,1)S(1)}, bf16[160,640]{1,0:T(8,128)(2,1)S(1)}, u32[]{:S(2)}, u32[]{:S(2)}) collective-permute-start(bf16[160,640]{1,0:T(8,128)(2,1)S(1)} %get-tuple-element.76), channel_id=1, source_target_pairs={{0,96},{32,0},{64,32},{96,64},{1,97},{33,1},{65,33},{97,65},{2,98}... | collective-permute-start | bytes 614408 | tf_op jit(solution)/shard_map/ppermute | solution.py:400
  206.7 12.2 %collective-permute-start.23 = (bf16[160,640]{1,0:T(8,128)(2,1)S(1)}, bf16[160,640]{1,0:T(8,128)(2,1)S(1)}, u32[]{:S(2)}, u32[]{:S(2)}) collective-permute-start(bf16[160,640]{1,0:T(8,128)(2,1)S(1)} %get-tuple-element.77), channel_id=1, source_target_pairs={{0,32},{32,64},{64,96},{96,0},{1,33},{33,65},{65,97},{97,1},{2,34}... | collective-permute-start | bytes 614408 | tf_op jit(solution)/shard_map/ppermute | solution.py:400
  206.7 12.2 %collective-permute-start.22 = (bf16[160,640]{1,0:T(8,128)(2,1)}, bf16[160,640]{1,0:T(8,128)(2,1)}, u32[]{:S(2)}, u32[]{:S(2)}) collective-permute-start(bf16[160,640]{1,0:T(8,128)(2,1)} %get-tuple-element.75), channel_id=1, source_target_pairs={{0,64},{32,96},{64,0},{96,32},{1,65},{33,97},{65,1},{97,33},{2,66}... | collective-permute-start | bytes 614408 | tf_op jit(solution)/shard_map/ppermute | solution.py:400
  209.8 10.7 %collective-permute-start.27 = (bf16[160,640]{1,0:T(8,128)(2,1)S(1)}, bf16[160,640]{1,0:T(8,128)(2,1)S(1)}, u32[]{:S(2)}, u32[]{:S(2)}) collective-permute-start(bf16[160,640]{1,0:T(8,128)(2,1)S(1)} %get-tuple-element.73), channel_id=1, source_target_pairs={{0,24},{8,0},{16,8},{24,16},{1,25},{9,1},{17,9},{25,17},{2,26},{10... | collective-permute-start | bytes 614408 | tf_op jit(solution)/shard_map/ppermute | solution.py:400
  215.5 23.4 %collective-permute-start.19 = (bf16[3,256,640]{2,1,0:T(8,128)(2,1)S(1)}, bf16[3,256,640]{2,1,0:T(8,128)(2,1)S(1)}, u32[]{:S(2)}, u32[]{:S(2)}) collective-permute-start(bf16[3,256,640]{2,1,0:T(8,128)(2,1)S(1)} %copy-done.13), channel_id=1, source_target_pairs={{4,0},{0,1},{5,2},{1,3},{6,4},{2,5},{7,6},{3,7},{12,8},{8,9},{13,1... | collective-permute-start | bytes 2949128 | tf_op jit(solution)/shard_map/ppermute | solution.py:385
  218.9 27.1 %collective-permute-start.20 = (bf16[3,256,640]{2,1,0:T(8,128)(2,1)S(1)}, bf16[3,256,640]{2,1,0:T(8,128)(2,1)S(1)}, u32[]{:S(2)}, u32[]{:S(2)}) collective-permute-start(bf16[3,256,640]{2,1,0:T(8,128)(2,1)S(1)} %copy-done.11), channel_id=1, source_target_pairs={{1,0},{5,1},{0,2},{4,3},{3,4},{7,5},{2,6},{6,7},{9,8},{13,9},{8,10... | collective-permute-start | bytes 2949128 | tf_op jit(solution)/shard_map/ppermute | solution.py:385
  218.9 8.3 %collective-permute-start.26 = (bf16[160,640]{1,0:T(8,128)(2,1)S(1)}, bf16[160,640]{1,0:T(8,128)(2,1)S(1)}, u32[]{:S(2)}, u32[]{:S(2)}) collective-permute-start(bf16[160,640]{1,0:T(8,128)(2,1)S(1)} %get-tuple-element.74), channel_id=1, source_target_pairs={{0,8},{8,16},{16,24},{24,0},{1,9},{9,17},{17,25},{25,1},{2,10},{10... | collective-permute-start | bytes 614408 | tf_op jit(solution)/shard_map/ppermute | solution.py:400
  220.5 10.8 %collective-permute-start.25 = (bf16[160,640]{1,0:T(8,128)(2,1)S(1)}, bf16[160,640]{1,0:T(8,128)(2,1)S(1)}, u32[]{:S(2)}, u32[]{:S(2)}) collective-permute-start(bf16[160,640]{1,0:T(8,128)(2,1)S(1)} %get-tuple-element.72), channel_id=1, source_target_pairs={{0,16},{8,24},{16,0},{24,8},{1,17},{9,25},{17,1},{25,9},{2,18},{10... | collective-permute-start | bytes 614408 | tf_op jit(solution)/shard_map/ppermute | solution.py:400
  233.1 20.0 %collective-permute-start.29 = (bf16[160,640]{1,0:T(8,128)(2,1)}, bf16[160,640]{1,0:T(8,128)(2,1)S(1)}, u32[]{:S(2)}, u32[]{:S(2)}) collective-permute-start(bf16[160,640]{1,0:T(8,128)(2,1)} %get-tuple-element.79), channel_id=1, source_target_pairs={{0,4},{1,6},{2,0},{3,2},{4,5},{5,7},{6,1},{7,3},{8,12},{9,14},{10,... | collective-permute-start | bytes 614408 | tf_op jit(solution)/shard_map/ppermute | solution.py:385
  233.1 20.0 %collective-permute-start.28 = (bf16[160,640]{1,0:T(8,128)(2,1)S(1)}, bf16[160,640]{1,0:T(8,128)(2,1)}, u32[]{:S(2)}, u32[]{:S(2)}) collective-permute-start(bf16[160,640]{1,0:T(8,128)(2,1)S(1)} %get-tuple-element.78), channel_id=1, source_target_pairs={{1,2},{2,4},{3,6},{4,1},{5,3},{6,5},{9,10},{10,12},{11,14},{12,9},... | collective-permute-start | bytes 614408 | tf_op jit(solution)/shard_map/ppermute | solution.py:385
  (28 other events, 238.3 us)
Sparse Core Ops, SparseCore 0:
  17.7 68.0 all-gather.1
  158.8 41.6 reduce-scatter.1

commit v10 on v9

--- a/solution.py
+++ b/solution.py
@@ -411,11 +411,15 @@
     return lax.dynamic_index_in_dim(value, index, axis, keepdims=False)
 
 
-def scatter(value, axis, dim=0):
+def pair_sum(value, axis):
     here = lax.axis_index(axis)
-    count = lax.axis_size(axis)
-    got = [shift(take(value, (here + by) % count, dim), axis, by) for by in (2, 1, 3)]
-    return [take(value, here, dim)] + got
+
+    def swap(part, mask):
+        return lax.ppermute(part, axis, [(i, i ^ mask) for i in range(lax.axis_size(axis))])
+
+    got = swap(jnp.stack([take(value, here ^ 1), take(value, here ^ 2)]), 1)
+    mine, theirs = add(take(value, here), got[0]), add(take(value, here ^ 3), got[1])
+    return add(mine, swap(theirs, 3))
 
 
 def to_shard_holders(w_out, seq, token):
@@ -499,8 +503,8 @@
     parts = backward(place, tile_pairs, packs, own_grads, other_grads, after(probs, token))
     one = add(*after(one, parts[0]))
     parts = {r: send(parts[r] if r in ORDER[:2] else after(parts[r], one), inward(r)) for r in ORDER}
-    two = lax.optimization_barrier(add(*scatter(after(two, one), "x")))
-    one = lax.optimization_barrier(add(*scatter(one, "z")))
+    two = lax.optimization_barrier(pair_sum(after(two, one), "x"))
+    one = lax.optimization_barrier(pair_sum(one, "z"))
     grad_w = to_owners((one, two), seq)
     grad_q, grad_k, grad_v = finish(
         place, queries, keys, gain_q, gain_k, [parts[r] for r in range(SEQ)]

time: 263 us -> 260 us (0.989)
  local copies, waits for them, and re-layouts: 12.4 us -> 8.83 us
    ppermute x9 -> x3, starting transfers between devices: 19.2 us -> 6.36 us  [shift(): lax.ppermute(value, axis, [(i, (i + by) % count) for i in range(count)])]
    ppermute x0 -> x4, starting transfers between devices: none -> 9.72 us  [swap(): lax.ppermute(part, axis, [(i, i ^ mask) for i in range(lax.axis_size(axis...]
    ppermute x9 -> x3, waiting for transfers between devices: 12.8 us -> 3.26 us  [shift(): lax.ppermute(value, axis, [(i, (i + by) % count) for i in range(count)])]
    ppermute x0 -> x4, waiting for transfers between devices: none -> 7.92 us  [swap(): lax.ppermute(part, axis, [(i, i ^ mask) for i in range(lax.axis_size(axis...]
    ppermute x16, waiting for transfers between devices: 74.7 us -> 77.8 us  [send(): got = lax.ppermute(value, ('core', 'seq'), others)]
    ppermute x16, starting transfers between devices: 30.2 us -> 33.2 us  [send(): got = lax.ppermute(value, ('core', 'seq'), others)]
    unnamed x57 -> x51, local copies, waits for them, and re-layouts: 8.19 us -> 5.41 us
  transfers between devices with their start and end apart: 32 -> 30, of which waited for: 16 -> 16; matrix products, arithmetic and copies ran while one was open for 14% -> 14% of each run, Pallas kernels for 16% -> 17%
where the time goes in v10:
time: 260 us; the launch traced here: 258 us
  waiting for transfers between devices  89.1 us (34%)
  Pallas kernels  57.4 us (22%)
  starting transfers between devices  52.4 us (20%)
  matrix products  21.2 us (8%)
  other arithmetic  15 us (6%)
  between operations  14.6 us (6%)
  local copies, waits for them, and re-layouts  8.83 us (3%)
    ppermute x16, waiting for transfers between devices, send(): got = lax.ppermute(value, ('core', 'seq'), others)  77.8 us
    ppermute x16, starting transfers between devices, send(): got = lax.ppermute(value, ('core', 'seq'), others)  33.2 us
    dot_general x8, matrix products, project(): jnp.dot(part, w_all, preferred_element_type=jnp.float32)  21.2 us
    pallas_call x1, Pallas kernels, backward(): pl.pallas_call(backward_kernel, grid=(heads,), in_specs=[smem()] * 2 + [s...  19.8 us
    pallas_call x1, Pallas kernels, weight_grad(): pl.pallas_call(lambda place_ref, *refs: weight_grad_kernel(place_ref, mea...  14.2 us
    pallas_call x1, Pallas kernels, forward(): pl.pallas_call(forward_kernel, grid=(heads,), in_specs=[smem()] * 3 + [sp...  11.9 us
    ppermute x4, starting transfers between devices, swap(): lax.ppermute(part, axis, [(i, i ^ mask) for i in range(lax.axis_size(axis...  9.72 us
    select_n x7, other arithmetic, send(): return jnp.where(keep, value, got)  8.89 us
  transfers between devices with their start and end apart: 30, of which 16 were waited for; matrix products, arithmetic and copies ran while one was open for 14% of the time, Pallas kernels for 17%

profile of v10, /device:TPU:24, one launch (start us, length us, event | category | flops | bytes accessed | tf_op | source)
XLA Modules:
  0.0 258.4 jit_solution(2636122873277960060)
XLA Ops:
  7.2 2.6 %collective-permute-start.5 = (bf16[160,640]{1,0:T(8,128)(2,1)}, bf16[160,640]{1,0:T(8,128)(2,1)S(1)}, u32[]{:S(2)}, u32[]{:S(2)}) collective-permute-start(bf16[160,640]{1,0:T(8,128)(2,1)} %param.17), channel_id=1, source_target_pairs={{1,4},{2,1},{3,5},{4,2},{5,6},{6,3},{9,12},{10,9},{11,13},{12,10},... | collective-permute-start | bytes 614408 | tf_op jit(solution)/shard_map/ppermute | solution.py:385
  10.6 5.4 %norm_rows.1 = (bf16[3,256,640]{2,1,0:T(8,128)(2,1)}, bf16[3,256,640]{2,1,0:T(8,128)(2,1)}, bf16[3,256,640]{2,1,0:T(8,128)(2,1)}, bf16[3,256,640]{2,1,0:T(8,128)(2,1)}) custom-call(s32[5]{0:T(128)} %stack.33.place_ref, bf16[256,2560]{1,0:T(8,128)(2,1)} %q_ref.3, bf16[256,2560]{1,0:T(8,128)(2,1)} %k_ref.3, bf16[256,2560]{1,0:T(8,128)(2,1)} %v_ref.1, ...), custom_call_target="tpu_custom_call" | custom-call | tf_op jit(solution)/shard_map/norm_rows/pallas_call | solution.py:61
  17.6 4.8 %collective-permute-start = (bf16[3,256,640]{2,1,0:T(8,128)(2,1)}, bf16[3,256,640]{2,1,0:T(8,128)(2,1)}, u32[]{:S(2)}, u32[]{:S(2)}) collective-permute-start(bf16[3,256,640]{2,1,0:T(8,128)(2,1)} %get-tuple-element.37), channel_id=1, source_target_pairs={{1,4},{2,1},{3,5},{4,2},{5,6},{6,3},{9,12},{10,9},{11,13},{12,10},... | collective-permute-start | bytes 2949128 | tf_op jit(solution)/shard_map/ppermute | solution.py:385
  24.4 3.1 %collective-permute-start.1 = (bf16[3,256,640]{2,1,0:T(8,128)(2,1)}, bf16[3,256,640]{2,1,0:T(8,128)(2,1)S(1)}, u32[]{:S(2)}, u32[]{:S(2)}) collective-permute-start(bf16[3,256,640]{2,1,0:T(8,128)(2,1)} %get-tuple-element.38), channel_id=1, source_target_pairs={{0,4},{1,0},{2,5},{3,1},{4,6},{5,2},{6,7},{7,3},{8,12},{9,8},{10,1... | collective-permute-start | bytes 2949128 | tf_op jit(solution)/shard_map/ppermute | solution.py:385
  27.7 13.6 %collective-permute-done = bf16[3,256,640]{2,1,0:T(8,128)(2,1)} collective-permute-done((bf16[3,256,640]{2,1,0:T(8,128)(2,1)}, bf16[3,256,640]{2,1,0:T(8,128)(2,1)}, u32[]{:S(2)}, u32[]{:S(2)}) %collective-permute-start) | collective-permute-done | bytes 983072 | tf_op jit(solution)/shard_map/ppermute | solution.py:385
  42.6 7.4 %collective-permute-done.3 = bf16[3,256,640]{2,1,0:T(8,128)(2,1)} collective-permute-done((bf16[3,256,640]{2,1,0:T(8,128)(2,1)S(1)}, bf16[3,256,640]{2,1,0:T(8,128)(2,1)}, u32[]{:S(2)}, u32[]{:S(2)}) %collective-permute-start.3) | collective-permute-done | bytes 983072 | tf_op jit(solution)/shard_map/ppermute | solution.py:385
  51.4 10.2 %collective-permute-done.1.refs_1_.refs_5_.refs_9_ = bf16[3,256,640]{2,1,0:T(8,128)(2,1)S(1)} collective-permute-done((bf16[3,256,640]{2,1,0:T(8,128)(2,1)}, bf16[3,256,640]{2,1,0:T(8,128)(2,1)S(1)}, u32[]{:S(2)}, u32[]{:S(2)}) %collective-permute-start.1) | collective-permute-done | bytes 983072 | tf_op jit(solution)/shard_map/ppermute | solution.py:385
  61.6 9.3 %collective-permute-done.2.refs_2_.refs_6_.refs_10_ = bf16[3,256,640]{2,1,0:T(8,128)(2,1)} collective-permute-done((bf16[3,256,640]{2,1,0:T(8,128)(2,1)}, bf16[3,256,640]{2,1,0:T(8,128)(2,1)}, u32[]{:S(2)}, u32[]{:S(2)}) %collective-permute-start.2) | collective-permute-done | bytes 983072 | tf_op jit(solution)/shard_map/ppermute | solution.py:385
  74.7 2.7 %collective-permute-start.9 = (bf16[128,5120]{1,0:T(8,128)(2,1)}, bf16[128,5120]{1,0:T(8,128)(2,1)S(1)}, u32[]{:S(2)}, u32[]{:S(2)}) collective-permute-start(bf16[128,5120]{1,0:T(8,128)(2,1)} %get-tuple-element.70), channel_id=1, source_target_pairs={{0,5},{2,4},{3,0},{4,7},{5,3},{7,2},{8,13},{10,12},{11,8},{12,15},... | collective-permute-start | bytes 3932168 | tf_op jit(solution)/shard_map/ppermute | solution.py:385
  79.8 11.9 %attention_forward.1 = (bf16[1024,640]{1,0:T(8,128)(2,1)S(1)}, bf16[5,4096,128]{2,1,0:T(8,128)(2,1)}) custom-call(s32[5]{0:T(128)S(1)} %copy-done.9, s32[16,8]{1,0:T(8,128)S(1)} %copy.14.pairs_ref, s32[1,16]{1,0:T(1,128)S(1)} %broadcast_select_fusion.9.lens_ref, bf16[3,256,640]{2,1,0:T(8,128)(2,1)S(1)} %broadcast_select_fusion.5.refs_0_.refs_4_.refs_8_, ...), custom_call_target="tpu_custom_call" | custom-call | tf_op jit(solution)/shard_map/attention_forward/pallas_call | solution.py:212
  91.7 11.3 %collective-permute-done.4 = bf16[128,5120]{1,0:T(8,128)(2,1)} collective-permute-done((bf16[128,5120]{1,0:T(8,128)(2,1)}, bf16[128,5120]{1,0:T(8,128)(2,1)}, u32[]{:S(2)}, u32[]{:S(2)}) %collective-permute-start.4) | collective-permute-done | bytes 1310752 | tf_op jit(solution)/shard_map/ppermute | solution.py:385
  104.6 4.8 %collective-permute-done.9 = bf16[128,5120]{1,0:T(8,128)(2,1)S(1)} collective-permute-done((bf16[128,5120]{1,0:T(8,128)(2,1)}, bf16[128,5120]{1,0:T(8,128)(2,1)S(1)}, u32[]{:S(2)}, u32[]{:S(2)}) %collective-permute-start.9) | collective-permute-done | bytes 1310752 | tf_op jit(solution)/shard_map/ppermute | solution.py:385
  109.7 4.4 %convolution_convert_fusion.7.refs_12_ = bf16[128,640]{1,0:T(8,128)(2,1)S(1)} fusion(bf16[128,5120]{1,0:T(8,128)(2,1)S(1)} %broadcast_select_fusion.1.refs_1_, bf16[5120,640]{1,0:T(8,128)(2,1)} %all-gather.2.cloned.1.call-done), kind=kOutput, calls=%fused_computation.12 | convolution fusion | flops 838942720 | bytes 8028160 | tf_op jit(solution)/shard_map/dot_general | solution.py:482
  116.0 2.6 %convolution_convert_fusion.3.refs_16_ = bf16[128,640]{1,0:T(8,128)(2,1)S(1)} fusion(bf16[128,5120]{1,0:T(8,128)(2,1)} %collective-permute-done.10.refs_5_, bf16[5120,640]{1,0:T(8,128)(2,1)S(1)} %copy-done.10), kind=kOutput, calls=%fused_computation.8 | convolution fusion | flops 838942720 | bytes 8028160 | tf_op jit(solution)/shard_map/dot_general | solution.py:482
  118.7 2.6 %convolution_convert_fusion.2.refs_19_ = bf16[128,640]{1,0:T(8,128)(2,1)S(1)} fusion(bf16[128,5120]{1,0:T(8,128)(2,1)} %collective-permute-done.12.refs_8_, bf16[5120,640]{1,0:T(8,128)(2,1)S(1)} %copy-done.10), kind=kOutput, calls=%fused_computation.7 | convolution fusion | flops 838942720 | bytes 8028160 | tf_op jit(solution)/shard_map/dot_general | solution.py:482
  121.3 7.2 %collective-permute-done.7.refs_2_ = bf16[128,5120]{1,0:T(8,128)(2,1)} collective-permute-done((bf16[128,5120]{1,0:T(8,128)(2,1)}, bf16[128,5120]{1,0:T(8,128)(2,1)}, u32[]{:S(2)}, u32[]{:S(2)}) %collective-permute-start.7) | collective-permute-done | bytes 1310752 | tf_op jit(solution)/shard_map/ppermute | solution.py:385
  128.4 2.8 %collective-permute-start.13 = (bf16[128,5120]{1,0:T(8,128)(2,1)}, bf16[128,5120]{1,0:T(8,128)(2,1)S(1)}, u32[]{:S(2)}, u32[]{:S(2)}) collective-permute-start(bf16[128,5120]{1,0:T(8,128)(2,1)} %collective-permute-done.7.refs_2_), channel_id=1, source_target_pairs={{0,4},{4,0},{1,5},{5,1},{2,6},{6,2},{3,7},{7,3},{8,12},{12,8},{9,1... | collective-permute-start | bytes 3932168 | tf_op jit(solution)/shard_map/ppermute | solution.py:395
  131.2 3.3 %convolution_convert_fusion.6.refs_13_ = bf16[128,640]{1,0:T(8,128)(2,1)} fusion(bf16[128,5120]{1,0:T(8,128)(2,1)} %collective-permute-done.7.refs_2_, bf16[5120,640]{1,0:T(8,128)(2,1)S(1)} %copy-done.10), kind=kOutput, calls=%fused_computation.11 | convolution fusion | flops 838942720 | bytes 8028160 | tf_op jit(solution)/shard_map/dot_general | solution.py:482
  134.5 2.9 %collective-permute-done.8.refs_3_ = bf16[128,5120]{1,0:T(8,128)(2,1)} collective-permute-done((bf16[128,5120]{1,0:T(8,128)(2,1)}, bf16[128,5120]{1,0:T(8,128)(2,1)}, u32[]{:S(2)}, u32[]{:S(2)}) %collective-permute-start.8) | collective-permute-done | bytes 1310752 | tf_op jit(solution)/shard_map/ppermute | solution.py:385
  137.3 3.3 %convolution_convert_fusion.5.refs_14_ = bf16[128,640]{1,0:T(8,128)(2,1)} fusion(bf16[128,5120]{1,0:T(8,128)(2,1)} %collective-permute-done.8.refs_3_, bf16[5120,640]{1,0:T(8,128)(2,1)S(1)} %copy-done.10), kind=kOutput, calls=%fused_computation.10 | convolution fusion | flops 838942720 | bytes 8028160 | tf_op jit(solution)/shard_map/dot_general | solution.py:482
  144.4 14.2 %weight_grad.1 = (bf16[4,160,640]{2,1,0:T(8,128)(2,1)S(1)}, bf16[4,160,640]{2,1,0:T(8,128)(2,1)}, bf16[4,160,640]{2,1,0:T(8,128)(2,1)}, bf16[4,160,640]{2,1,0:T(8,128)(2,1)}, bf16[16,160,640]{2,1,0:T(8,128)(2,1)}) custom-call(s32[5]{0:T(128)S(1)} %copy-done.9, bf16[1024,640]{1,0:T(8,128)(2,1)S(1)} %copy-done.4, ...), custom_call_target="tpu_custom_call" | custom-call | tf_op jit(solution)/shard_map/weight_grad/pallas_call | solution.py:352
  158.7 3.1 %collective-permute-start.16 = (bf16[4,160,640]{2,1,0:T(8,128)(2,1)}, bf16[4,160,640]{2,1,0:T(8,128)(2,1)}, u32[]{:S(2)}, u32[]{:S(2)}) collective-permute-start(bf16[4,160,640]{2,1,0:T(8,128)(2,1)} %get-tuple-element.54), channel_id=1, source_target_pairs={{0,16},{8,24},{16,0},{24,8},{1,17},{9,25},{17,1},{25,9},{2,18},{10... | collective-permute-start | bytes 2457608 | tf_op jit(solution)/shard_map/ppermute | solution.py:400
  162.4 2.7 %collective-permute-start.18 = (bf16[4,160,640]{2,1,0:T(8,128)(2,1)}, bf16[4,160,640]{2,1,0:T(8,128)(2,1)}, u32[]{:S(2)}, u32[]{:S(2)}) collective-permute-start(bf16[4,160,640]{2,1,0:T(8,128)(2,1)} %get-tuple-element.56), channel_id=1, source_target_pairs={{0,24},{8,0},{16,8},{24,16},{1,25},{9,1},{17,9},{25,17},{2,26},{10... | collective-permute-start | bytes 2457608 | tf_op jit(solution)/shard_map/ppermute | solution.py:400
  168.7 19.8 %attention_backward.1 = (bf16[3,256,640]{2,1,0:T(8,128)(2,1)S(1)}, bf16[3,256,640]{2,1,0:T(8,128)(2,1)}, bf16[3,256,640]{2,1,0:T(8,128)(2,1)}, bf16[3,256,640]{2,1,0:T(8,128)(2,1)S(1)}) custom-call(s32[5]{0:T(128)S(1)} %copy-done.9, s32[16,8]{1,0:T(8,128)S(1)} %copy.14.pairs_ref, bf16[3,256,640]{2,1,0:T(8,128)(2,1)} %copy-done, ...), custom_call_target="tpu_custom_call" | custom-call | tf_op jit(solution)/shard_map/attention_backward/pallas_call | solution.py:306
  190.5 5.1 %collective-permute-start.21 = (bf16[3,256,640]{2,1,0:T(8,128)(2,1)S(1)}, bf16[3,256,640]{2,1,0:T(8,128)(2,1)}, u32[]{:S(2)}, u32[]{:S(2)}) collective-permute-start(bf16[3,256,640]{2,1,0:T(8,128)(2,1)S(1)} %get-tuple-element.64), channel_id=1, source_target_pairs={{5,0},{4,2},{0,3},{7,4},{3,5},{2,7},{13,8},{12,10},{8,11},{15,12},... | collective-permute-start | bytes 2949128 | tf_op jit(solution)/shard_map/ppermute | solution.py:385
  195.6 3.1 %collective-permute-done.17 = bf16[4,160,640]{2,1,0:T(8,128)(2,1)} collective-permute-done((bf16[4,160,640]{2,1,0:T(8,128)(2,1)}, bf16[4,160,640]{2,1,0:T(8,128)(2,1)}, u32[]{:S(2)}, u32[]{:S(2)}) %collective-permute-start.17) | collective-permute-done | bytes 819232 | tf_op jit(solution)/shard_map/ppermute | solution.py:400
  208.9 4.7 %collective-permute-done.22 = bf16[2,160,640]{2,1,0:T(8,128)(2,1)} collective-permute-done((bf16[2,160,640]{2,1,0:T(8,128)(2,1)S(1)}, bf16[2,160,640]{2,1,0:T(8,128)(2,1)}, u32[]{:S(2)}, u32[]{:S(2)}) %collective-permute-start.22) | collective-permute-done | bytes 409632 | tf_op jit(solution)/shard_map/ppermute | solution.py:418
  214.6 3.9 %collective-permute-start.23 = (bf16[160,640]{1,0:T(8,128)(2,1)S(1)}, bf16[160,640]{1,0:T(8,128)(2,1)S(1)}, u32[]{:S(2)}, u32[]{:S(2)}) collective-permute-start(bf16[160,640]{1,0:T(8,128)(2,1)S(1)} %fusion.3), channel_id=1, source_target_pairs={{0,96},{32,64},{64,32},{96,0},{1,97},{33,65},{65,33},{97,1},{2,98}... | collective-permute-start | bytes 614408 | tf_op jit(solution)/shard_map/ppermute | solution.py:418
  218.6 2.8 %collective-permute-start.25 = (bf16[160,640]{1,0:T(8,128)(2,1)S(1)}, bf16[160,640]{1,0:T(8,128)(2,1)S(1)}, u32[]{:S(2)}, u32[]{:S(2)}) collective-permute-start(bf16[160,640]{1,0:T(8,128)(2,1)S(1)} %fusion.5), channel_id=1, source_target_pairs={{0,24},{8,16},{16,8},{24,0},{1,25},{9,17},{17,9},{25,1},{2,26},{10... | collective-permute-start | bytes 614408 | tf_op jit(solution)/shard_map/ppermute | solution.py:418
  227.6 3.8 %collective-permute-start.26 = (bf16[160,640]{1,0:T(8,128)(2,1)S(1)}, bf16[160,640]{1,0:T(8,128)(2,1)S(1)}, u32[]{:S(2)}, u32[]{:S(2)}) collective-permute-start(bf16[160,640]{1,0:T(8,128)(2,1)S(1)} %get-tuple-element.76), channel_id=1, source_target_pairs={{1,2},{2,4},{3,6},{4,1},{5,3},{6,5},{9,10},{10,12},{11,14},{12,9},... | collective-permute-start | bytes 614408 | tf_op jit(solution)/shard_map/ppermute | solution.py:385
  231.5 9.9 %collective-permute-done.21 = bf16[3,256,640]{2,1,0:T(8,128)(2,1)} collective-permute-done((bf16[3,256,640]{2,1,0:T(8,128)(2,1)S(1)}, bf16[3,256,640]{2,1,0:T(8,128)(2,1)}, u32[]{:S(2)}, u32[]{:S(2)}) %collective-permute-start.21) | collective-permute-done | bytes 983072 | tf_op jit(solution)/shard_map/ppermute | solution.py:385
  244.7 6.1 %norm_back.1 = (bf16[256,2560]{1,0:T(8,128)(2,1)}, bf16[256,2560]{1,0:T(8,128)(2,1)}, bf16[256,2560]{1,0:T(8,128)(2,1)}) custom-call(s32[5]{0:T(128)} %stack.33.place_ref, bf16[256,2560]{1,0:T(8,128)(2,1)} %q_ref.3, bf16[256,2560]{1,0:T(8,128)(2,1)} %k_ref.3, f32[2560]{0:T(1024)} %gain_q_ref.3, f32[2560]{0:T(1024)} %gain_k_ref.3, ...), custom_call_target="tpu_custom_call" | custom-call | tf_op jit(solution)/shard_map/norm_back/pallas_call | solution.py:93
  (116 shorter events, 48.4 us)
Async XLA Ops:
  7.2 102.5 %all-gather.2.cloned.1.call-start = ((), (), s32[]{:S(2)}) async-start(), calls=%async_computation.1 | async-start | bytes 6963200 | tf_op jit(solution)/shard_map/all_gather | solution.py:473
  7.2 8.7 %collective-permute-start.5 = (bf16[160,640]{1,0:T(8,128)(2,1)}, bf16[160,640]{1,0:T(8,128)(2,1)S(1)}, u32[]{:S(2)}, u32[]{:S(2)}) collective-permute-start(bf16[160,640]{1,0:T(8,128)(2,1)} %param.17), channel_id=1, source_target_pairs={{1,4},{2,1},{3,5},{4,2},{5,6},{6,3},{9,12},{10,9},{11,13},{12,10},... | collective-permute-start | bytes 614408 | tf_op jit(solution)/shard_map/ppermute | solution.py:385
  9.8 6.9 %collective-permute-start.6 = (bf16[160,640]{1,0:T(8,128)(2,1)}, bf16[160,640]{1,0:T(8,128)(2,1)S(1)}, u32[]{:S(2)}, u32[]{:S(2)}) collective-permute-start(bf16[160,640]{1,0:T(8,128)(2,1)} %param.17), channel_id=1, source_target_pairs={{0,2},{1,6},{2,3},{3,7},{4,0},{5,4},{6,1},{7,5},{8,10},{9,14},{10,... | collective-permute-start | bytes 614408 | tf_op jit(solution)/shard_map/ppermute | solution.py:385
  17.6 186.4 %reduce-scatter.2.cloned.1.call-start = ((), (), s32[]{:S(2)}) async-start(), calls=%async_computation.2 | async-start | bytes 4096000 | tf_op jit(solution)/shard_map/reduce_scatter | solution.py:500
  17.6 23.7 %collective-permute-start = (bf16[3,256,640]{2,1,0:T(8,128)(2,1)}, bf16[3,256,640]{2,1,0:T(8,128)(2,1)}, u32[]{:S(2)}, u32[]{:S(2)}) collective-permute-start(bf16[3,256,640]{2,1,0:T(8,128)(2,1)} %get-tuple-element.37), channel_id=1, source_target_pairs={{1,4},{2,1},{3,5},{4,2},{5,6},{6,3},{9,12},{10,9},{11,13},{12,10},... | collective-permute-start | bytes 2949128 | tf_op jit(solution)/shard_map/ppermute | solution.py:385
  22.5 27.6 %collective-permute-start.3 = (bf16[3,256,640]{2,1,0:T(8,128)(2,1)S(1)}, bf16[3,256,640]{2,1,0:T(8,128)(2,1)}, u32[]{:S(2)}, u32[]{:S(2)}) collective-permute-start(bf16[3,256,640]{2,1,0:T(8,128)(2,1)S(1)} %copy-done.19), channel_id=1, source_target_pairs={{0,5},{2,4},{3,0},{4,7},{5,3},{7,2},{8,13},{10,12},{11,8},{12,15},... | collective-permute-start | bytes 2949128 | tf_op jit(solution)/shard_map/ppermute | solution.py:385
  24.4 37.2 %collective-permute-start.1 = (bf16[3,256,640]{2,1,0:T(8,128)(2,1)}, bf16[3,256,640]{2,1,0:T(8,128)(2,1)S(1)}, u32[]{:S(2)}, u32[]{:S(2)}) collective-permute-start(bf16[3,256,640]{2,1,0:T(8,128)(2,1)} %get-tuple-element.38), channel_id=1, source_target_pairs={{0,4},{1,0},{2,5},{3,1},{4,6},{5,2},{6,7},{7,3},{8,12},{9,8},{10,1... | collective-permute-start | bytes 2949128 | tf_op jit(solution)/shard_map/ppermute | solution.py:385
  27.5 43.4 %collective-permute-start.2 = (bf16[3,256,640]{2,1,0:T(8,128)(2,1)}, bf16[3,256,640]{2,1,0:T(8,128)(2,1)}, u32[]{:S(2)}, u32[]{:S(2)}) collective-permute-start(bf16[3,256,640]{2,1,0:T(8,128)(2,1)} %get-tuple-element.39), channel_id=1, source_target_pairs={{0,1},{1,5},{2,0},{3,4},{4,3},{5,7},{6,2},{7,6},{8,9},{9,13},{10,8... | collective-permute-start | bytes 2949128 | tf_op jit(solution)/shard_map/ppermute | solution.py:385
  42.6 37.2 %copy-start = (bf16[3,256,640]{2,1,0:T(8,128)(2,1)}, bf16[3,256,640]{2,1,0:T(8,128)(2,1)S(1)}, u32[]{:S(2)}) copy-start(bf16[3,256,640]{2,1,0:T(8,128)(2,1)S(1)} %broadcast_select_fusion.5.refs_0_.refs_4_.refs_8_) | copy-start | bytes 2949124
  51.4 28.4 %copy-start.1 = (bf16[3,256,640]{2,1,0:T(8,128)(2,1)}, bf16[3,256,640]{2,1,0:T(8,128)(2,1)S(1)}, u32[]{:S(2)}) copy-start(bf16[3,256,640]{2,1,0:T(8,128)(2,1)S(1)} %broadcast_select_fusion.3.refs_3_.refs_7_.refs_11_) | copy-start | bytes 2949124
  72.6 30.4 %collective-permute-start.4 = (bf16[128,5120]{1,0:T(8,128)(2,1)}, bf16[128,5120]{1,0:T(8,128)(2,1)}, u32[]{:S(2)}, u32[]{:S(2)}) collective-permute-start(bf16[128,5120]{1,0:T(8,128)(2,1)} %get-tuple-element.71), channel_id=1, source_target_pairs={{1,4},{2,1},{3,5},{4,2},{5,6},{6,3},{9,12},{10,9},{11,13},{12,10},... | collective-permute-start | bytes 3932168 | tf_op jit(solution)/shard_map/ppermute | solution.py:385
  74.5 2.9 %collective-permute-start.11 = (s32[1,16]{1,0:T(1,128)S(1)}, s32[1,16]{1,0:T(1,128)S(1)}, u32[]{:S(2)}, u32[]{:S(2)}) collective-permute-start(s32[1,16]{1,0:T(1,128)S(1)} %copy-done.24), channel_id=1, source_target_pairs={{0,4},{4,0},{1,5},{5,1},{2,6},{6,2},{3,7},{7,3},{8,12},{12,8},{9,1... | collective-permute-start | bytes 200 | tf_op jit(solution)/shard_map/ppermute | solution.py:395
  74.7 34.7 %collective-permute-start.9 = (bf16[128,5120]{1,0:T(8,128)(2,1)}, bf16[128,5120]{1,0:T(8,128)(2,1)S(1)}, u32[]{:S(2)}, u32[]{:S(2)}) collective-permute-start(bf16[128,5120]{1,0:T(8,128)(2,1)} %get-tuple-element.70), channel_id=1, source_target_pairs={{0,5},{2,4},{3,0},{4,7},{5,3},{7,2},{8,13},{10,12},{11,8},{12,15},... | collective-permute-start | bytes 3932168 | tf_op jit(solution)/shard_map/ppermute | solution.py:385
  77.4 51.0 %collective-permute-start.7 = (bf16[128,5120]{1,0:T(8,128)(2,1)}, bf16[128,5120]{1,0:T(8,128)(2,1)}, u32[]{:S(2)}, u32[]{:S(2)}) collective-permute-start(bf16[128,5120]{1,0:T(8,128)(2,1)} %get-tuple-element.70), channel_id=1, source_target_pairs={{0,4},{1,0},{2,5},{3,1},{4,6},{5,2},{6,7},{7,3},{8,12},{9,8},{10,1... | collective-permute-start | bytes 3932168 | tf_op jit(solution)/shard_map/ppermute | solution.py:385
  77.5 59.8 %collective-permute-start.8 = (bf16[128,5120]{1,0:T(8,128)(2,1)}, bf16[128,5120]{1,0:T(8,128)(2,1)}, u32[]{:S(2)}, u32[]{:S(2)}) collective-permute-start(bf16[128,5120]{1,0:T(8,128)(2,1)} %get-tuple-element.71), channel_id=1, source_target_pairs={{0,1},{1,5},{2,0},{3,4},{4,3},{5,7},{6,2},{7,6},{8,9},{9,13},{10,8... | collective-permute-start | bytes 3932168 | tf_op jit(solution)/shard_map/ppermute | solution.py:385
  104.5 11.6 %collective-permute-start.10 = (bf16[128,5120]{1,0:T(8,128)(2,1)S(1)}, bf16[128,5120]{1,0:T(8,128)(2,1)}, u32[]{:S(2)}, u32[]{:S(2)}) collective-permute-start(bf16[128,5120]{1,0:T(8,128)(2,1)S(1)} %broadcast_select_fusion.1.refs_1_), channel_id=1, source_target_pairs={{0,4},{4,0},{1,5},{5,1},{2,6},{6,2},{3,7},{7,3},{8,12},{12,8},{9,1... | collective-permute-start | bytes 3932168 | tf_op jit(solution)/shard_map/ppermute | solution.py:395
  109.6 9.1 %collective-permute-start.12 = (bf16[128,5120]{1,0:T(8,128)(2,1)S(1)}, bf16[128,5120]{1,0:T(8,128)(2,1)}, u32[]{:S(2)}, u32[]{:S(2)}) collective-permute-start(bf16[128,5120]{1,0:T(8,128)(2,1)S(1)} %broadcast_select_fusion.refs_4_), channel_id=1, source_target_pairs={{0,4},{4,0},{1,5},{5,1},{2,6},{6,2},{3,7},{7,3},{8,12},{12,8},{9,1... | collective-permute-start | bytes 3932168 | tf_op jit(solution)/shard_map/ppermute | solution.py:395
  128.4 12.2 %collective-permute-start.13 = (bf16[128,5120]{1,0:T(8,128)(2,1)}, bf16[128,5120]{1,0:T(8,128)(2,1)S(1)}, u32[]{:S(2)}, u32[]{:S(2)}) collective-permute-start(bf16[128,5120]{1,0:T(8,128)(2,1)} %collective-permute-done.7.refs_2_), channel_id=1, source_target_pairs={{0,4},{4,0},{1,5},{5,1},{2,6},{6,2},{3,7},{7,3},{8,12},{12,8},{9,1... | collective-permute-start | bytes 3932168 | tf_op jit(solution)/shard_map/ppermute | solution.py:395
  137.3 5.2 %collective-permute-start.14 = (bf16[128,5120]{1,0:T(8,128)(2,1)}, bf16[128,5120]{1,0:T(8,128)(2,1)S(1)}, u32[]{:S(2)}, u32[]{:S(2)}) collective-permute-start(bf16[128,5120]{1,0:T(8,128)(2,1)} %collective-permute-done.8.refs_3_), channel_id=1, source_target_pairs={{0,4},{4,0},{1,5},{5,1},{2,6},{6,2},{3,7},{7,3},{8,12},{12,8},{9,1... | collective-permute-start | bytes 3932168 | tf_op jit(solution)/shard_map/ppermute | solution.py:395
  158.7 37.0 %collective-permute-start.16 = (bf16[4,160,640]{2,1,0:T(8,128)(2,1)}, bf16[4,160,640]{2,1,0:T(8,128)(2,1)}, u32[]{:S(2)}, u32[]{:S(2)}) collective-permute-start(bf16[4,160,640]{2,1,0:T(8,128)(2,1)} %get-tuple-element.54), channel_id=1, source_target_pairs={{0,16},{8,24},{16,0},{24,8},{1,17},{9,25},{17,1},{25,9},{2,18},{10... | collective-permute-start | bytes 2457608 | tf_op jit(solution)/shard_map/ppermute | solution.py:400
  161.8 37.0 %collective-permute-start.17 = (bf16[4,160,640]{2,1,0:T(8,128)(2,1)}, bf16[4,160,640]{2,1,0:T(8,128)(2,1)}, u32[]{:S(2)}, u32[]{:S(2)}) collective-permute-start(bf16[4,160,640]{2,1,0:T(8,128)(2,1)} %get-tuple-element.55), channel_id=1, source_target_pairs={{0,8},{8,16},{16,24},{24,0},{1,9},{9,17},{17,25},{25,1},{2,10},{10... | collective-permute-start | bytes 2457608 | tf_op jit(solution)/shard_map/ppermute | solution.py:400
  162.4 36.5 %collective-permute-start.18 = (bf16[4,160,640]{2,1,0:T(8,128)(2,1)}, bf16[4,160,640]{2,1,0:T(8,128)(2,1)}, u32[]{:S(2)}, u32[]{:S(2)}) collective-permute-start(bf16[4,160,640]{2,1,0:T(8,128)(2,1)} %get-tuple-element.56), channel_id=1, source_target_pairs={{0,24},{8,0},{16,8},{24,16},{1,25},{9,1},{17,9},{25,17},{2,26},{10... | collective-permute-start | bytes 2457608 | tf_op jit(solution)/shard_map/ppermute | solution.py:400
  188.5 17.1 %collective-permute-start.15 = (bf16[3,256,640]{2,1,0:T(8,128)(2,1)S(1)}, bf16[3,256,640]{2,1,0:T(8,128)(2,1)}, u32[]{:S(2)}, u32[]{:S(2)}) collective-permute-start(bf16[3,256,640]{2,1,0:T(8,128)(2,1)S(1)} %get-tuple-element.52), channel_id=1, source_target_pairs={{4,1},{1,2},{5,3},{2,4},{6,5},{3,6},{12,9},{9,10},{13,11},{10,12},... | collective-permute-start | bytes 2949128 | tf_op jit(solution)/shard_map/ppermute | solution.py:385
  190.5 50.9 %collective-permute-start.21 = (bf16[3,256,640]{2,1,0:T(8,128)(2,1)S(1)}, bf16[3,256,640]{2,1,0:T(8,128)(2,1)}, u32[]{:S(2)}, u32[]{:S(2)}) collective-permute-start(bf16[3,256,640]{2,1,0:T(8,128)(2,1)S(1)} %get-tuple-element.64), channel_id=1, source_target_pairs={{5,0},{4,2},{0,3},{7,4},{3,5},{2,7},{13,8},{12,10},{8,11},{15,12},... | collective-permute-start | bytes 2949128 | tf_op jit(solution)/shard_map/ppermute | solution.py:385
  201.0 42.7 %collective-permute-start.19 = (bf16[3,256,640]{2,1,0:T(8,128)(2,1)}, bf16[3,256,640]{2,1,0:T(8,128)(2,1)S(1)}, u32[]{:S(2)}, u32[]{:S(2)}) collective-permute-start(bf16[3,256,640]{2,1,0:T(8,128)(2,1)} %get-tuple-element.61), channel_id=1, source_target_pairs={{4,0},{0,1},{5,2},{1,3},{6,4},{2,5},{7,6},{3,7},{12,8},{8,9},{13,1... | collective-permute-start | bytes 2949128 | tf_op jit(solution)/shard_map/ppermute | solution.py:385
  201.1 42.6 %collective-permute-start.20 = (bf16[3,256,640]{2,1,0:T(8,128)(2,1)}, bf16[3,256,640]{2,1,0:T(8,128)(2,1)}, u32[]{:S(2)}, u32[]{:S(2)}) collective-permute-start(bf16[3,256,640]{2,1,0:T(8,128)(2,1)} %get-tuple-element.63), channel_id=1, source_target_pairs={{1,0},{5,1},{0,2},{4,3},{3,4},{7,5},{2,6},{6,7},{9,8},{13,9},{8,10... | collective-permute-start | bytes 2949128 | tf_op jit(solution)/shard_map/ppermute | solution.py:385
  202.0 11.6 %collective-permute-start.22 = (bf16[2,160,640]{2,1,0:T(8,128)(2,1)S(1)}, bf16[2,160,640]{2,1,0:T(8,128)(2,1)}, u32[]{:S(2)}, u32[]{:S(2)}) collective-permute-start(bf16[2,160,640]{2,1,0:T(8,128)(2,1)S(1)} %pad_maximum_fusion), channel_id=1, source_target_pairs={{0,32},{32,0},{64,96},{96,64},{1,33},{33,1},{65,97},{97,65},{2,34}... | collective-permute-start | bytes 1228808 | tf_op jit(solution)/shard_map/ppermute | solution.py:418
  205.6 12.9 %collective-permute-start.24 = (bf16[2,160,640]{2,1,0:T(8,128)(2,1)S(1)}, bf16[2,160,640]{2,1,0:T(8,128)(2,1)S(1)}, u32[]{:S(2)}, u32[]{:S(2)}) collective-permute-start(bf16[2,160,640]{2,1,0:T(8,128)(2,1)S(1)} %pad_maximum_fusion.1), channel_id=1, source_target_pairs={{0,8},{8,0},{16,24},{24,16},{1,9},{9,1},{17,25},{25,17},{2,10},{10... | collective-permute-start | bytes 1228808 | tf_op jit(solution)/shard_map/ppermute | solution.py:418
  214.6 8.2 %collective-permute-start.23 = (bf16[160,640]{1,0:T(8,128)(2,1)S(1)}, bf16[160,640]{1,0:T(8,128)(2,1)S(1)}, u32[]{:S(2)}, u32[]{:S(2)}) collective-permute-start(bf16[160,640]{1,0:T(8,128)(2,1)S(1)} %fusion.3), channel_id=1, source_target_pairs={{0,96},{32,64},{64,32},{96,0},{1,97},{33,65},{65,33},{97,1},{2,98}... | collective-permute-start | bytes 614408 | tf_op jit(solution)/shard_map/ppermute | solution.py:418
  218.6 7.1 %collective-permute-start.25 = (bf16[160,640]{1,0:T(8,128)(2,1)S(1)}, bf16[160,640]{1,0:T(8,128)(2,1)S(1)}, u32[]{:S(2)}, u32[]{:S(2)}) collective-permute-start(bf16[160,640]{1,0:T(8,128)(2,1)S(1)} %fusion.5), channel_id=1, source_target_pairs={{0,24},{8,16},{16,8},{24,0},{1,25},{9,17},{17,9},{25,1},{2,26},{10... | collective-permute-start | bytes 614408 | tf_op jit(solution)/shard_map/ppermute | solution.py:418
  225.8 24.9 %collective-permute-start.27 = (bf16[160,640]{1,0:T(8,128)(2,1)S(1)}, bf16[160,640]{1,0:T(8,128)(2,1)S(1)}, u32[]{:S(2)}, u32[]{:S(2)}) collective-permute-start(bf16[160,640]{1,0:T(8,128)(2,1)S(1)} %get-tuple-element.77), channel_id=1, source_target_pairs={{0,4},{1,6},{2,0},{3,2},{4,5},{5,7},{6,1},{7,3},{8,12},{9,14},{10,... | collective-permute-start | bytes 614408 | tf_op jit(solution)/shard_map/ppermute | solution.py:385
  227.6 23.1 %collective-permute-start.26 = (bf16[160,640]{1,0:T(8,128)(2,1)S(1)}, bf16[160,640]{1,0:T(8,128)(2,1)S(1)}, u32[]{:S(2)}, u32[]{:S(2)}) collective-permute-start(bf16[160,640]{1,0:T(8,128)(2,1)S(1)} %get-tuple-element.76), channel_id=1, source_target_pairs={{1,2},{2,4},{3,6},{4,1},{5,3},{6,5},{9,10},{10,12},{11,14},{12,9},... | collective-permute-start | bytes 614408 | tf_op jit(solution)/shard_map/ppermute | solution.py:385
  (23 other events, 170.4 us)
Sparse Core Ops, SparseCore 0:
  17.7 68.0 all-gather.1
  158.8 41.6 reduce-scatter.1

commit v11 on v10

--- a/solution.py
+++ b/solution.py
@@ -502,7 +502,7 @@
     one = [one[0]] + [shift(one[by], "x", by) for by in (2, 1, 3)]
     parts = backward(place, tile_pairs, packs, own_grads, other_grads, after(probs, token))
     one = add(*after(one, parts[0]))
-    parts = {r: send(parts[r] if r in ORDER[:2] else after(parts[r], one), inward(r)) for r in ORDER}
+    parts = {r: send(parts[r] if r in ORDER[:3] else after(parts[r], one), inward(r)) for r in ORDER}
     two = lax.optimization_barrier(pair_sum(after(two, one), "x"))
     one = lax.optimization_barrier(pair_sum(one, "z"))
     grad_w = to_owners((one, two), seq)

time: 260 us -> 258 us (level)
  starting transfers between devices: 52.4 us -> 47.8 us
    ppermute x4, starting transfers between devices: 9.72 us -> 5.83 us  [swap(): lax.ppermute(part, axis, [(i, i ^ mask) for i in range(lax.axis_size(axis...]
    ppermute x16, waiting for transfers between devices: 77.8 us -> 80.6 us  [send(): got = lax.ppermute(value, ('core', 'seq'), others)]
    unnamed x51 -> x53, local copies, waits for them, and re-layouts: 5.41 us -> 6.85 us
where the time goes in v11:
time: 258 us; the launch traced here: 256 us
  waiting for transfers between devices  89.6 us (35%)
  Pallas kernels  57.5 us (22%)
  starting transfers between devices  47.8 us (19%)
  matrix products  21.2 us (8%)
  other arithmetic  15 us (6%)
  between operations  14.6 us (6%)
  local copies, waits for them, and re-layouts  10.3 us (4%)
    ppermute x16, waiting for transfers between devices, send(): got = lax.ppermute(value, ('core', 'seq'), others)  80.6 us
    ppermute x16, starting transfers between devices, send(): got = lax.ppermute(value, ('core', 'seq'), others)  32.5 us
    dot_general x8, matrix products, project(): jnp.dot(part, w_all, preferred_element_type=jnp.float32)  21.2 us
    pallas_call x1, Pallas kernels, backward(): pl.pallas_call(backward_kernel, grid=(heads,), in_specs=[smem()] * 2 + [s...  19.9 us
    pallas_call x1, Pallas kernels, weight_grad(): pl.pallas_call(lambda place_ref, *refs: weight_grad_kernel(place_ref, mea...  14.2 us
    pallas_call x1, Pallas kernels, forward(): pl.pallas_call(forward_kernel, grid=(heads,), in_specs=[smem()] * 3 + [sp...  11.9 us
    select_n x7, other arithmetic, send(): return jnp.where(keep, value, got)  8.9 us
    unnamed x53, local copies, waits for them, and re-layouts  6.85 us
  transfers between devices with their start and end apart: 30, of which 16 were waited for; matrix products, arithmetic and copies ran while one was open for 14% of the time, Pallas kernels for 17%

profile of v11, /device:TPU:24, one launch (start us, length us, event | category | flops | bytes accessed | tf_op | source)
XLA Modules:
  0.0 255.9 jit_solution(3733016722709142546)
XLA Ops:
  7.2 2.6 %collective-permute-start.5 = (bf16[160,640]{1,0:T(8,128)(2,1)}, bf16[160,640]{1,0:T(8,128)(2,1)S(1)}, u32[]{:S(2)}, u32[]{:S(2)}) collective-permute-start(bf16[160,640]{1,0:T(8,128)(2,1)} %param.17), channel_id=1, source_target_pairs={{1,4},{2,1},{3,5},{4,2},{5,6},{6,3},{9,12},{10,9},{11,13},{12,10},... | collective-permute-start | bytes 614408 | tf_op jit(solution)/shard_map/ppermute | solution.py:385
  10.6 5.4 %norm_rows.1 = (bf16[3,256,640]{2,1,0:T(8,128)(2,1)}, bf16[3,256,640]{2,1,0:T(8,128)(2,1)}, bf16[3,256,640]{2,1,0:T(8,128)(2,1)}, bf16[3,256,640]{2,1,0:T(8,128)(2,1)}) custom-call(s32[5]{0:T(128)} %stack.33.place_ref, bf16[256,2560]{1,0:T(8,128)(2,1)} %q_ref.3, bf16[256,2560]{1,0:T(8,128)(2,1)} %k_ref.3, bf16[256,2560]{1,0:T(8,128)(2,1)} %v_ref.1, ...), custom_call_target="tpu_custom_call" | custom-call | tf_op jit(solution)/shard_map/norm_rows/pallas_call | solution.py:61
  17.6 4.9 %collective-permute-start = (bf16[3,256,640]{2,1,0:T(8,128)(2,1)}, bf16[3,256,640]{2,1,0:T(8,128)(2,1)}, u32[]{:S(2)}, u32[]{:S(2)}) collective-permute-start(bf16[3,256,640]{2,1,0:T(8,128)(2,1)} %get-tuple-element.36), channel_id=1, source_target_pairs={{1,4},{2,1},{3,5},{4,2},{5,6},{6,3},{9,12},{10,9},{11,13},{12,10},... | collective-permute-start | bytes 2949128 | tf_op jit(solution)/shard_map/ppermute | solution.py:385
  24.4 3.1 %collective-permute-start.1 = (bf16[3,256,640]{2,1,0:T(8,128)(2,1)}, bf16[3,256,640]{2,1,0:T(8,128)(2,1)S(1)}, u32[]{:S(2)}, u32[]{:S(2)}) collective-permute-start(bf16[3,256,640]{2,1,0:T(8,128)(2,1)} %get-tuple-element.37), channel_id=1, source_target_pairs={{0,4},{1,0},{2,5},{3,1},{4,6},{5,2},{6,7},{7,3},{8,12},{9,8},{10,1... | collective-permute-start | bytes 2949128 | tf_op jit(solution)/shard_map/ppermute | solution.py:385
  27.7 13.6 %collective-permute-done = bf16[3,256,640]{2,1,0:T(8,128)(2,1)} collective-permute-done((bf16[3,256,640]{2,1,0:T(8,128)(2,1)}, bf16[3,256,640]{2,1,0:T(8,128)(2,1)}, u32[]{:S(2)}, u32[]{:S(2)}) %collective-permute-start) | collective-permute-done | bytes 983072 | tf_op jit(solution)/shard_map/ppermute | solution.py:385
  42.6 7.5 %collective-permute-done.3 = bf16[3,256,640]{2,1,0:T(8,128)(2,1)} collective-permute-done((bf16[3,256,640]{2,1,0:T(8,128)(2,1)S(1)}, bf16[3,256,640]{2,1,0:T(8,128)(2,1)}, u32[]{:S(2)}, u32[]{:S(2)}) %collective-permute-start.3) | collective-permute-done | bytes 983072 | tf_op jit(solution)/shard_map/ppermute | solution.py:385
  51.5 10.2 %collective-permute-done.1.refs_1_.refs_5_.refs_9_ = bf16[3,256,640]{2,1,0:T(8,128)(2,1)S(1)} collective-permute-done((bf16[3,256,640]{2,1,0:T(8,128)(2,1)}, bf16[3,256,640]{2,1,0:T(8,128)(2,1)S(1)}, u32[]{:S(2)}, u32[]{:S(2)}) %collective-permute-start.1) | collective-permute-done | bytes 983072 | tf_op jit(solution)/shard_map/ppermute | solution.py:385
  61.7 9.2 %collective-permute-done.2.refs_2_.refs_6_.refs_10_ = bf16[3,256,640]{2,1,0:T(8,128)(2,1)} collective-permute-done((bf16[3,256,640]{2,1,0:T(8,128)(2,1)}, bf16[3,256,640]{2,1,0:T(8,128)(2,1)}, u32[]{:S(2)}, u32[]{:S(2)}) %collective-permute-start.2) | collective-permute-done | bytes 983072 | tf_op jit(solution)/shard_map/ppermute | solution.py:385
  74.7 2.7 %collective-permute-start.9 = (bf16[128,5120]{1,0:T(8,128)(2,1)}, bf16[128,5120]{1,0:T(8,128)(2,1)S(1)}, u32[]{:S(2)}, u32[]{:S(2)}) collective-permute-start(bf16[128,5120]{1,0:T(8,128)(2,1)} %get-tuple-element.68), channel_id=1, source_target_pairs={{0,5},{2,4},{3,0},{4,7},{5,3},{7,2},{8,13},{10,12},{11,8},{12,15},... | collective-permute-start | bytes 3932168 | tf_op jit(solution)/shard_map/ppermute | solution.py:385
  79.8 11.9 %attention_forward.1 = (bf16[1024,640]{1,0:T(8,128)(2,1)S(1)}, bf16[5,4096,128]{2,1,0:T(8,128)(2,1)}) custom-call(s32[5]{0:T(128)S(1)} %copy-done.9, s32[16,8]{1,0:T(8,128)S(1)} %copy.14.pairs_ref, s32[1,16]{1,0:T(1,128)S(1)} %broadcast_select_fusion.9.lens_ref, bf16[3,256,640]{2,1,0:T(8,128)(2,1)S(1)} %broadcast_select_fusion.5.refs_0_.refs_4_.refs_8_, ...), custom_call_target="tpu_custom_call" | custom-call | tf_op jit(solution)/shard_map/attention_forward/pallas_call | solution.py:212
  91.7 11.3 %collective-permute-done.4 = bf16[128,5120]{1,0:T(8,128)(2,1)} collective-permute-done((bf16[128,5120]{1,0:T(8,128)(2,1)}, bf16[128,5120]{1,0:T(8,128)(2,1)}, u32[]{:S(2)}, u32[]{:S(2)}) %collective-permute-start.4) | collective-permute-done | bytes 1310752 | tf_op jit(solution)/shard_map/ppermute | solution.py:385
  104.6 4.8 %collective-permute-done.9 = bf16[128,5120]{1,0:T(8,128)(2,1)S(1)} collective-permute-done((bf16[128,5120]{1,0:T(8,128)(2,1)}, bf16[128,5120]{1,0:T(8,128)(2,1)S(1)}, u32[]{:S(2)}, u32[]{:S(2)}) %collective-permute-start.9) | collective-permute-done | bytes 1310752 | tf_op jit(solution)/shard_map/ppermute | solution.py:385
  109.7 4.4 %convolution_convert_fusion.7.refs_12_ = bf16[128,640]{1,0:T(8,128)(2,1)S(1)} fusion(bf16[128,5120]{1,0:T(8,128)(2,1)S(1)} %broadcast_select_fusion.1.refs_1_, bf16[5120,640]{1,0:T(8,128)(2,1)} %all-gather.2.cloned.1.call-done), kind=kOutput, calls=%fused_computation.12 | convolution fusion | flops 838942720 | bytes 8028160 | tf_op jit(solution)/shard_map/dot_general | solution.py:482
  116.0 2.6 %convolution_convert_fusion.3.refs_16_ = bf16[128,640]{1,0:T(8,128)(2,1)S(1)} fusion(bf16[128,5120]{1,0:T(8,128)(2,1)} %collective-permute-done.10.refs_5_, bf16[5120,640]{1,0:T(8,128)(2,1)S(1)} %copy-done.11), kind=kOutput, calls=%fused_computation.8 | convolution fusion | flops 838942720 | bytes 8028160 | tf_op jit(solution)/shard_map/dot_general | solution.py:482
  118.7 2.6 %convolution_convert_fusion.2.refs_19_ = bf16[128,640]{1,0:T(8,128)(2,1)S(1)} fusion(bf16[128,5120]{1,0:T(8,128)(2,1)} %collective-permute-done.12.refs_8_, bf16[5120,640]{1,0:T(8,128)(2,1)S(1)} %copy-done.11), kind=kOutput, calls=%fused_computation.7 | convolution fusion | flops 838942720 | bytes 8028160 | tf_op jit(solution)/shard_map/dot_general | solution.py:482
  121.3 7.2 %collective-permute-done.7.refs_2_ = bf16[128,5120]{1,0:T(8,128)(2,1)} collective-permute-done((bf16[128,5120]{1,0:T(8,128)(2,1)}, bf16[128,5120]{1,0:T(8,128)(2,1)}, u32[]{:S(2)}, u32[]{:S(2)}) %collective-permute-start.7) | collective-permute-done | bytes 1310752 | tf_op jit(solution)/shard_map/ppermute | solution.py:385
  128.4 2.8 %collective-permute-start.13 = (bf16[128,5120]{1,0:T(8,128)(2,1)}, bf16[128,5120]{1,0:T(8,128)(2,1)S(1)}, u32[]{:S(2)}, u32[]{:S(2)}) collective-permute-start(bf16[128,5120]{1,0:T(8,128)(2,1)} %collective-permute-done.7.refs_2_), channel_id=1, source_target_pairs={{0,4},{4,0},{1,5},{5,1},{2,6},{6,2},{3,7},{7,3},{8,12},{12,8},{9,1... | collective-permute-start | bytes 3932168 | tf_op jit(solution)/shard_map/ppermute | solution.py:395
  131.2 3.3 %convolution_convert_fusion.6.refs_13_ = bf16[128,640]{1,0:T(8,128)(2,1)} fusion(bf16[128,5120]{1,0:T(8,128)(2,1)} %collective-permute-done.7.refs_2_, bf16[5120,640]{1,0:T(8,128)(2,1)S(1)} %copy-done.11), kind=kOutput, calls=%fused_computation.11 | convolution fusion | flops 838942720 | bytes 8028160 | tf_op jit(solution)/shard_map/dot_general | solution.py:482
  134.5 2.9 %collective-permute-done.8.refs_3_ = bf16[128,5120]{1,0:T(8,128)(2,1)} collective-permute-done((bf16[128,5120]{1,0:T(8,128)(2,1)}, bf16[128,5120]{1,0:T(8,128)(2,1)}, u32[]{:S(2)}, u32[]{:S(2)}) %collective-permute-start.8) | collective-permute-done | bytes 1310752 | tf_op jit(solution)/shard_map/ppermute | solution.py:385
  137.3 3.3 %convolution_convert_fusion.5.refs_14_ = bf16[128,640]{1,0:T(8,128)(2,1)} fusion(bf16[128,5120]{1,0:T(8,128)(2,1)} %collective-permute-done.8.refs_3_, bf16[5120,640]{1,0:T(8,128)(2,1)S(1)} %copy-done.11), kind=kOutput, calls=%fused_computation.10 | convolution fusion | flops 838942720 | bytes 8028160 | tf_op jit(solution)/shard_map/dot_general | solution.py:482
  144.4 14.2 %weight_grad.1 = (bf16[4,160,640]{2,1,0:T(8,128)(2,1)S(1)}, bf16[4,160,640]{2,1,0:T(8,128)(2,1)}, bf16[4,160,640]{2,1,0:T(8,128)(2,1)}, bf16[4,160,640]{2,1,0:T(8,128)(2,1)}, bf16[16,160,640]{2,1,0:T(8,128)(2,1)}) custom-call(s32[5]{0:T(128)S(1)} %copy-done.9, bf16[1024,640]{1,0:T(8,128)(2,1)S(1)} %copy-done.4, ...), custom_call_target="tpu_custom_call" | custom-call | tf_op jit(solution)/shard_map/weight_grad/pallas_call | solution.py:352
  158.7 3.1 %collective-permute-start.17 = (bf16[4,160,640]{2,1,0:T(8,128)(2,1)}, bf16[4,160,640]{2,1,0:T(8,128)(2,1)}, u32[]{:S(2)}, u32[]{:S(2)}) collective-permute-start(bf16[4,160,640]{2,1,0:T(8,128)(2,1)} %get-tuple-element.54), channel_id=1, source_target_pairs={{0,16},{8,24},{16,0},{24,8},{1,17},{9,25},{17,1},{25,9},{2,18},{10... | collective-permute-start | bytes 2457608 | tf_op jit(solution)/shard_map/ppermute | solution.py:400
  162.4 2.7 %collective-permute-start.19 = (bf16[4,160,640]{2,1,0:T(8,128)(2,1)}, bf16[4,160,640]{2,1,0:T(8,128)(2,1)}, u32[]{:S(2)}, u32[]{:S(2)}) collective-permute-start(bf16[4,160,640]{2,1,0:T(8,128)(2,1)} %get-tuple-element.56), channel_id=1, source_target_pairs={{0,24},{8,0},{16,8},{24,16},{1,25},{9,1},{17,9},{25,17},{2,26},{10... | collective-permute-start | bytes 2457608 | tf_op jit(solution)/shard_map/ppermute | solution.py:400
  168.7 19.9 %attention_backward.1 = (bf16[3,256,640]{2,1,0:T(8,128)(2,1)S(1)}, bf16[3,256,640]{2,1,0:T(8,128)(2,1)S(1)}, bf16[3,256,640]{2,1,0:T(8,128)(2,1)}, bf16[3,256,640]{2,1,0:T(8,128)(2,1)S(1)}) custom-call(s32[5]{0:T(128)S(1)} %copy-done.9, s32[16,8]{1,0:T(8,128)S(1)} %copy.14.pairs_ref, bf16[3,256,640]{2,1,0:T(8,128)(2,1)} %copy-done, ...), custom_call_target="tpu_custom_call" | custom-call | tf_op jit(solution)/shard_map/attention_backward/pallas_call | solution.py:306
  191.7 5.1 %collective-permute-start.21 = (bf16[3,256,640]{2,1,0:T(8,128)(2,1)S(1)}, bf16[3,256,640]{2,1,0:T(8,128)(2,1)}, u32[]{:S(2)}, u32[]{:S(2)}) collective-permute-start(bf16[3,256,640]{2,1,0:T(8,128)(2,1)S(1)} %get-tuple-element.62), channel_id=1, source_target_pairs={{5,0},{4,2},{0,3},{7,4},{3,5},{2,7},{13,8},{12,10},{8,11},{15,12},... | collective-permute-start | bytes 2949128 | tf_op jit(solution)/shard_map/ppermute | solution.py:385
  205.1 11.2 %collective-permute-done.15 = bf16[3,256,640]{2,1,0:T(8,128)(2,1)} collective-permute-done((bf16[3,256,640]{2,1,0:T(8,128)(2,1)S(1)}, bf16[3,256,640]{2,1,0:T(8,128)(2,1)}, u32[]{:S(2)}, u32[]{:S(2)}) %collective-permute-start.15) | collective-permute-done | bytes 983072 | tf_op jit(solution)/shard_map/ppermute | solution.py:385
  216.3 2.3 broadcast_select_fusion.4.refs_0_
  219.7 3.7 %collective-permute-start.23 = (bf16[160,640]{1,0:T(8,128)(2,1)S(1)}, bf16[160,640]{1,0:T(8,128)(2,1)S(1)}, u32[]{:S(2)}, u32[]{:S(2)}) collective-permute-start(bf16[160,640]{1,0:T(8,128)(2,1)S(1)} %fusion.3), channel_id=1, source_target_pairs={{0,96},{32,64},{64,32},{96,0},{1,97},{33,65},{65,33},{97,1},{2,98}... | collective-permute-start | bytes 614408 | tf_op jit(solution)/shard_map/ppermute | solution.py:418
  224.4 2.7 %collective-permute-done.23 = bf16[160,640]{1,0:T(8,128)(2,1)S(1)} collective-permute-done((bf16[160,640]{1,0:T(8,128)(2,1)S(1)}, bf16[160,640]{1,0:T(8,128)(2,1)S(1)}, u32[]{:S(2)}, u32[]{:S(2)}) %collective-permute-start.23) | collective-permute-done | bytes 204832 | tf_op jit(solution)/shard_map/ppermute | solution.py:418
  228.2 3.2 %collective-permute-done.25 = bf16[160,640]{1,0:T(8,128)(2,1)S(1)} collective-permute-done((bf16[160,640]{1,0:T(8,128)(2,1)S(1)}, bf16[160,640]{1,0:T(8,128)(2,1)S(1)}, u32[]{:S(2)}, u32[]{:S(2)}) %collective-permute-start.25) | collective-permute-done | bytes 204832 | tf_op jit(solution)/shard_map/ppermute | solution.py:418
  231.6 3.3 %collective-permute-start.27 = (bf16[160,640]{1,0:T(8,128)(2,1)S(1)}, bf16[160,640]{1,0:T(8,128)(2,1)S(1)}, u32[]{:S(2)}, u32[]{:S(2)}) collective-permute-start(bf16[160,640]{1,0:T(8,128)(2,1)S(1)} %get-tuple-element.75), channel_id=1, source_target_pairs={{0,4},{1,6},{2,0},{3,2},{4,5},{5,7},{6,1},{7,3},{8,12},{9,14},{10,... | collective-permute-start | bytes 614408 | tf_op jit(solution)/shard_map/ppermute | solution.py:385
  242.2 6.1 %norm_back.1 = (bf16[256,2560]{1,0:T(8,128)(2,1)}, bf16[256,2560]{1,0:T(8,128)(2,1)}, bf16[256,2560]{1,0:T(8,128)(2,1)}) custom-call(s32[5]{0:T(128)} %stack.33.place_ref, bf16[256,2560]{1,0:T(8,128)(2,1)} %q_ref.3, bf16[256,2560]{1,0:T(8,128)(2,1)} %k_ref.3, f32[2560]{0:T(1024)} %gain_q_ref.3, f32[2560]{0:T(1024)} %gain_k_ref.3, ...), custom_call_target="tpu_custom_call" | custom-call | tf_op jit(solution)/shard_map/norm_back/pallas_call | solution.py:93
  (118 shorter events, 47.5 us)
Async XLA Ops:
  7.2 102.5 %all-gather.2.cloned.1.call-start = ((), (), s32[]{:S(2)}) async-start(), calls=%async_computation.1 | async-start | bytes 6963200 | tf_op jit(solution)/shard_map/all_gather | solution.py:473
  7.2 8.8 %collective-permute-start.5 = (bf16[160,640]{1,0:T(8,128)(2,1)}, bf16[160,640]{1,0:T(8,128)(2,1)S(1)}, u32[]{:S(2)}, u32[]{:S(2)}) collective-permute-start(bf16[160,640]{1,0:T(8,128)(2,1)} %param.17), channel_id=1, source_target_pairs={{1,4},{2,1},{3,5},{4,2},{5,6},{6,3},{9,12},{10,9},{11,13},{12,10},... | collective-permute-start | bytes 614408 | tf_op jit(solution)/shard_map/ppermute | solution.py:385
  9.8 6.9 %collective-permute-start.6 = (bf16[160,640]{1,0:T(8,128)(2,1)}, bf16[160,640]{1,0:T(8,128)(2,1)S(1)}, u32[]{:S(2)}, u32[]{:S(2)}) collective-permute-start(bf16[160,640]{1,0:T(8,128)(2,1)} %param.17), channel_id=1, source_target_pairs={{0,2},{1,6},{2,3},{3,7},{4,0},{5,4},{6,1},{7,5},{8,10},{9,14},{10,... | collective-permute-start | bytes 614408 | tf_op jit(solution)/shard_map/ppermute | solution.py:385
  17.6 186.4 %reduce-scatter.2.cloned.1.call-start = ((), (), s32[]{:S(2)}) async-start(), calls=%async_computation.2 | async-start | bytes 4096000 | tf_op jit(solution)/shard_map/reduce_scatter | solution.py:500
  17.6 23.7 %collective-permute-start = (bf16[3,256,640]{2,1,0:T(8,128)(2,1)}, bf16[3,256,640]{2,1,0:T(8,128)(2,1)}, u32[]{:S(2)}, u32[]{:S(2)}) collective-permute-start(bf16[3,256,640]{2,1,0:T(8,128)(2,1)} %get-tuple-element.36), channel_id=1, source_target_pairs={{1,4},{2,1},{3,5},{4,2},{5,6},{6,3},{9,12},{10,9},{11,13},{12,10},... | collective-permute-start | bytes 2949128 | tf_op jit(solution)/shard_map/ppermute | solution.py:385
  22.5 27.6 %collective-permute-start.3 = (bf16[3,256,640]{2,1,0:T(8,128)(2,1)S(1)}, bf16[3,256,640]{2,1,0:T(8,128)(2,1)}, u32[]{:S(2)}, u32[]{:S(2)}) collective-permute-start(bf16[3,256,640]{2,1,0:T(8,128)(2,1)S(1)} %copy-done.20), channel_id=1, source_target_pairs={{0,5},{2,4},{3,0},{4,7},{5,3},{7,2},{8,13},{10,12},{11,8},{12,15},... | collective-permute-start | bytes 2949128 | tf_op jit(solution)/shard_map/ppermute | solution.py:385
  24.4 37.2 %collective-permute-start.1 = (bf16[3,256,640]{2,1,0:T(8,128)(2,1)}, bf16[3,256,640]{2,1,0:T(8,128)(2,1)S(1)}, u32[]{:S(2)}, u32[]{:S(2)}) collective-permute-start(bf16[3,256,640]{2,1,0:T(8,128)(2,1)} %get-tuple-element.37), channel_id=1, source_target_pairs={{0,4},{1,0},{2,5},{3,1},{4,6},{5,2},{6,7},{7,3},{8,12},{9,8},{10,1... | collective-permute-start | bytes 2949128 | tf_op jit(solution)/shard_map/ppermute | solution.py:385
  27.5 43.4 %collective-permute-start.2 = (bf16[3,256,640]{2,1,0:T(8,128)(2,1)}, bf16[3,256,640]{2,1,0:T(8,128)(2,1)}, u32[]{:S(2)}, u32[]{:S(2)}) collective-permute-start(bf16[3,256,640]{2,1,0:T(8,128)(2,1)} %get-tuple-element.38), channel_id=1, source_target_pairs={{0,1},{1,5},{2,0},{3,4},{4,3},{5,7},{6,2},{7,6},{8,9},{9,13},{10,8... | collective-permute-start | bytes 2949128 | tf_op jit(solution)/shard_map/ppermute | solution.py:385
  42.6 37.2 %copy-start = (bf16[3,256,640]{2,1,0:T(8,128)(2,1)}, bf16[3,256,640]{2,1,0:T(8,128)(2,1)S(1)}, u32[]{:S(2)}) copy-start(bf16[3,256,640]{2,1,0:T(8,128)(2,1)S(1)} %broadcast_select_fusion.5.refs_0_.refs_4_.refs_8_) | copy-start | bytes 2949124
  51.5 28.4 %copy-start.1 = (bf16[3,256,640]{2,1,0:T(8,128)(2,1)}, bf16[3,256,640]{2,1,0:T(8,128)(2,1)S(1)}, u32[]{:S(2)}) copy-start(bf16[3,256,640]{2,1,0:T(8,128)(2,1)S(1)} %broadcast_select_fusion.3.refs_3_.refs_7_.refs_11_) | copy-start | bytes 2949124
  72.6 30.4 %collective-permute-start.4 = (bf16[128,5120]{1,0:T(8,128)(2,1)}, bf16[128,5120]{1,0:T(8,128)(2,1)}, u32[]{:S(2)}, u32[]{:S(2)}) collective-permute-start(bf16[128,5120]{1,0:T(8,128)(2,1)} %get-tuple-element.69), channel_id=1, source_target_pairs={{1,4},{2,1},{3,5},{4,2},{5,6},{6,3},{9,12},{10,9},{11,13},{12,10},... | collective-permute-start | bytes 3932168 | tf_op jit(solution)/shard_map/ppermute | solution.py:385
  74.5 2.9 %collective-permute-start.11 = (s32[1,16]{1,0:T(1,128)S(1)}, s32[1,16]{1,0:T(1,128)S(1)}, u32[]{:S(2)}, u32[]{:S(2)}) collective-permute-start(s32[1,16]{1,0:T(1,128)S(1)} %copy-done.25), channel_id=1, source_target_pairs={{0,4},{4,0},{1,5},{5,1},{2,6},{6,2},{3,7},{7,3},{8,12},{12,8},{9,1... | collective-permute-start | bytes 200 | tf_op jit(solution)/shard_map/ppermute | solution.py:395
  74.7 34.7 %collective-permute-start.9 = (bf16[128,5120]{1,0:T(8,128)(2,1)}, bf16[128,5120]{1,0:T(8,128)(2,1)S(1)}, u32[]{:S(2)}, u32[]{:S(2)}) collective-permute-start(bf16[128,5120]{1,0:T(8,128)(2,1)} %get-tuple-element.68), channel_id=1, source_target_pairs={{0,5},{2,4},{3,0},{4,7},{5,3},{7,2},{8,13},{10,12},{11,8},{12,15},... | collective-permute-start | bytes 3932168 | tf_op jit(solution)/shard_map/ppermute | solution.py:385
  77.4 51.0 %collective-permute-start.7 = (bf16[128,5120]{1,0:T(8,128)(2,1)}, bf16[128,5120]{1,0:T(8,128)(2,1)}, u32[]{:S(2)}, u32[]{:S(2)}) collective-permute-start(bf16[128,5120]{1,0:T(8,128)(2,1)} %get-tuple-element.68), channel_id=1, source_target_pairs={{0,4},{1,0},{2,5},{3,1},{4,6},{5,2},{6,7},{7,3},{8,12},{9,8},{10,1... | collective-permute-start | bytes 3932168 | tf_op jit(solution)/shard_map/ppermute | solution.py:385
  77.5 59.8 %collective-permute-start.8 = (bf16[128,5120]{1,0:T(8,128)(2,1)}, bf16[128,5120]{1,0:T(8,128)(2,1)}, u32[]{:S(2)}, u32[]{:S(2)}) collective-permute-start(bf16[128,5120]{1,0:T(8,128)(2,1)} %get-tuple-element.69), channel_id=1, source_target_pairs={{0,1},{1,5},{2,0},{3,4},{4,3},{5,7},{6,2},{7,6},{8,9},{9,13},{10,8... | collective-permute-start | bytes 3932168 | tf_op jit(solution)/shard_map/ppermute | solution.py:385
  104.5 11.6 %collective-permute-start.10 = (bf16[128,5120]{1,0:T(8,128)(2,1)S(1)}, bf16[128,5120]{1,0:T(8,128)(2,1)}, u32[]{:S(2)}, u32[]{:S(2)}) collective-permute-start(bf16[128,5120]{1,0:T(8,128)(2,1)S(1)} %broadcast_select_fusion.1.refs_1_), channel_id=1, source_target_pairs={{0,4},{4,0},{1,5},{5,1},{2,6},{6,2},{3,7},{7,3},{8,12},{12,8},{9,1... | collective-permute-start | bytes 3932168 | tf_op jit(solution)/shard_map/ppermute | solution.py:395
  109.6 9.1 %collective-permute-start.12 = (bf16[128,5120]{1,0:T(8,128)(2,1)S(1)}, bf16[128,5120]{1,0:T(8,128)(2,1)}, u32[]{:S(2)}, u32[]{:S(2)}) collective-permute-start(bf16[128,5120]{1,0:T(8,128)(2,1)S(1)} %broadcast_select_fusion.refs_4_), channel_id=1, source_target_pairs={{0,4},{4,0},{1,5},{5,1},{2,6},{6,2},{3,7},{7,3},{8,12},{12,8},{9,1... | collective-permute-start | bytes 3932168 | tf_op jit(solution)/shard_map/ppermute | solution.py:395
  128.4 12.2 %collective-permute-start.13 = (bf16[128,5120]{1,0:T(8,128)(2,1)}, bf16[128,5120]{1,0:T(8,128)(2,1)S(1)}, u32[]{:S(2)}, u32[]{:S(2)}) collective-permute-start(bf16[128,5120]{1,0:T(8,128)(2,1)} %collective-permute-done.7.refs_2_), channel_id=1, source_target_pairs={{0,4},{4,0},{1,5},{5,1},{2,6},{6,2},{3,7},{7,3},{8,12},{12,8},{9,1... | collective-permute-start | bytes 3932168 | tf_op jit(solution)/shard_map/ppermute | solution.py:395
  137.3 5.2 %collective-permute-start.14 = (bf16[128,5120]{1,0:T(8,128)(2,1)}, bf16[128,5120]{1,0:T(8,128)(2,1)S(1)}, u32[]{:S(2)}, u32[]{:S(2)}) collective-permute-start(bf16[128,5120]{1,0:T(8,128)(2,1)} %collective-permute-done.8.refs_3_), channel_id=1, source_target_pairs={{0,4},{4,0},{1,5},{5,1},{2,6},{6,2},{3,7},{7,3},{8,12},{12,8},{9,1... | collective-permute-start | bytes 3932168 | tf_op jit(solution)/shard_map/ppermute | solution.py:395
  158.7 33.0 %collective-permute-start.17 = (bf16[4,160,640]{2,1,0:T(8,128)(2,1)}, bf16[4,160,640]{2,1,0:T(8,128)(2,1)}, u32[]{:S(2)}, u32[]{:S(2)}) collective-permute-start(bf16[4,160,640]{2,1,0:T(8,128)(2,1)} %get-tuple-element.54), channel_id=1, source_target_pairs={{0,16},{8,24},{16,0},{24,8},{1,17},{9,25},{17,1},{25,9},{2,18},{10... | collective-permute-start | bytes 2457608 | tf_op jit(solution)/shard_map/ppermute | solution.py:400
  161.8 37.0 %collective-permute-start.18 = (bf16[4,160,640]{2,1,0:T(8,128)(2,1)}, bf16[4,160,640]{2,1,0:T(8,128)(2,1)}, u32[]{:S(2)}, u32[]{:S(2)}) collective-permute-start(bf16[4,160,640]{2,1,0:T(8,128)(2,1)} %get-tuple-element.55), channel_id=1, source_target_pairs={{0,8},{8,16},{16,24},{24,0},{1,9},{9,17},{17,25},{25,1},{2,10},{10... | collective-permute-start | bytes 2457608 | tf_op jit(solution)/shard_map/ppermute | solution.py:400
  162.4 36.5 %collective-permute-start.19 = (bf16[4,160,640]{2,1,0:T(8,128)(2,1)}, bf16[4,160,640]{2,1,0:T(8,128)(2,1)}, u32[]{:S(2)}, u32[]{:S(2)}) collective-permute-start(bf16[4,160,640]{2,1,0:T(8,128)(2,1)} %get-tuple-element.56), channel_id=1, source_target_pairs={{0,24},{8,0},{16,8},{24,16},{1,25},{9,1},{17,9},{25,17},{2,26},{10... | collective-permute-start | bytes 2457608 | tf_op jit(solution)/shard_map/ppermute | solution.py:400
  189.6 26.7 %collective-permute-start.15 = (bf16[3,256,640]{2,1,0:T(8,128)(2,1)S(1)}, bf16[3,256,640]{2,1,0:T(8,128)(2,1)}, u32[]{:S(2)}, u32[]{:S(2)}) collective-permute-start(bf16[3,256,640]{2,1,0:T(8,128)(2,1)S(1)} %get-tuple-element.51), channel_id=1, source_target_pairs={{4,1},{1,2},{5,3},{2,4},{6,5},{3,6},{12,9},{9,10},{13,11},{10,12},... | collective-permute-start | bytes 2949128 | tf_op jit(solution)/shard_map/ppermute | solution.py:385
  191.6 49.6 %collective-permute-start.16 = (bf16[3,256,640]{2,1,0:T(8,128)(2,1)}, bf16[3,256,640]{2,1,0:T(8,128)(2,1)}, u32[]{:S(2)}, u32[]{:S(2)}) collective-permute-start(bf16[3,256,640]{2,1,0:T(8,128)(2,1)} %copy-done.10), channel_id=1, source_target_pairs={{4,0},{0,1},{5,2},{1,3},{6,4},{2,5},{7,6},{3,7},{12,8},{8,9},{13,1... | collective-permute-start | bytes 2949128 | tf_op jit(solution)/shard_map/ppermute | solution.py:385
  191.7 47.2 %collective-permute-start.21 = (bf16[3,256,640]{2,1,0:T(8,128)(2,1)S(1)}, bf16[3,256,640]{2,1,0:T(8,128)(2,1)}, u32[]{:S(2)}, u32[]{:S(2)}) collective-permute-start(bf16[3,256,640]{2,1,0:T(8,128)(2,1)S(1)} %get-tuple-element.62), channel_id=1, source_target_pairs={{5,0},{4,2},{0,3},{7,4},{3,5},{2,7},{13,8},{12,10},{8,11},{15,12},... | collective-permute-start | bytes 2949128 | tf_op jit(solution)/shard_map/ppermute | solution.py:385
  201.0 40.2 %collective-permute-start.20 = (bf16[3,256,640]{2,1,0:T(8,128)(2,1)}, bf16[3,256,640]{2,1,0:T(8,128)(2,1)S(1)}, u32[]{:S(2)}, u32[]{:S(2)}) collective-permute-start(bf16[3,256,640]{2,1,0:T(8,128)(2,1)} %get-tuple-element.61), channel_id=1, source_target_pairs={{1,0},{5,1},{0,2},{4,3},{3,4},{7,5},{2,6},{6,7},{9,8},{13,9},{8,10... | collective-permute-start | bytes 2949128 | tf_op jit(solution)/shard_map/ppermute | solution.py:385
  202.0 16.7 %collective-permute-start.22 = (bf16[2,160,640]{2,1,0:T(8,128)(2,1)S(1)}, bf16[2,160,640]{2,1,0:T(8,128)(2,1)}, u32[]{:S(2)}, u32[]{:S(2)}) collective-permute-start(bf16[2,160,640]{2,1,0:T(8,128)(2,1)S(1)} %pad_maximum_fusion), channel_id=1, source_target_pairs={{0,32},{32,0},{64,96},{96,64},{1,33},{33,1},{65,97},{97,65},{2,34}... | collective-permute-start | bytes 1228808 | tf_op jit(solution)/shard_map/ppermute | solution.py:418
  216.3 8.0 %collective-permute-start.24 = (bf16[2,160,640]{2,1,0:T(8,128)(2,1)S(1)}, bf16[2,160,640]{2,1,0:T(8,128)(2,1)S(1)}, u32[]{:S(2)}, u32[]{:S(2)}) collective-permute-start(bf16[2,160,640]{2,1,0:T(8,128)(2,1)S(1)} %pad_maximum_fusion.1), channel_id=1, source_target_pairs={{0,8},{8,0},{16,24},{24,16},{1,9},{9,1},{17,25},{25,17},{2,10},{10... | collective-permute-start | bytes 1228808 | tf_op jit(solution)/shard_map/ppermute | solution.py:418
  219.7 7.5 %collective-permute-start.23 = (bf16[160,640]{1,0:T(8,128)(2,1)S(1)}, bf16[160,640]{1,0:T(8,128)(2,1)S(1)}, u32[]{:S(2)}, u32[]{:S(2)}) collective-permute-start(bf16[160,640]{1,0:T(8,128)(2,1)S(1)} %fusion.3), channel_id=1, source_target_pairs={{0,96},{32,64},{64,32},{96,0},{1,97},{33,65},{65,33},{97,1},{2,98}... | collective-permute-start | bytes 614408 | tf_op jit(solution)/shard_map/ppermute | solution.py:418
  224.3 7.0 %collective-permute-start.25 = (bf16[160,640]{1,0:T(8,128)(2,1)S(1)}, bf16[160,640]{1,0:T(8,128)(2,1)S(1)}, u32[]{:S(2)}, u32[]{:S(2)}) collective-permute-start(bf16[160,640]{1,0:T(8,128)(2,1)S(1)} %fusion.5), channel_id=1, source_target_pairs={{0,24},{8,16},{16,8},{24,0},{1,25},{9,17},{17,9},{25,1},{2,26},{10... | collective-permute-start | bytes 614408 | tf_op jit(solution)/shard_map/ppermute | solution.py:418
  231.6 16.7 %collective-permute-start.27 = (bf16[160,640]{1,0:T(8,128)(2,1)S(1)}, bf16[160,640]{1,0:T(8,128)(2,1)S(1)}, u32[]{:S(2)}, u32[]{:S(2)}) collective-permute-start(bf16[160,640]{1,0:T(8,128)(2,1)S(1)} %get-tuple-element.75), channel_id=1, source_target_pairs={{0,4},{1,6},{2,0},{3,2},{4,5},{5,7},{6,1},{7,3},{8,12},{9,14},{10,... | collective-permute-start | bytes 614408 | tf_op jit(solution)/shard_map/ppermute | solution.py:385
  234.9 13.4 %collective-permute-start.26 = (bf16[160,640]{1,0:T(8,128)(2,1)S(1)}, bf16[160,640]{1,0:T(8,128)(2,1)S(1)}, u32[]{:S(2)}, u32[]{:S(2)}) collective-permute-start(bf16[160,640]{1,0:T(8,128)(2,1)S(1)} %get-tuple-element.74), channel_id=1, source_target_pairs={{1,2},{2,4},{3,6},{4,1},{5,3},{6,5},{9,10},{10,12},{11,14},{12,9},... | collective-permute-start | bytes 614408 | tf_op jit(solution)/shard_map/ppermute | solution.py:385
  (24 other events, 182.1 us)
Sparse Core Ops, SparseCore 0:
  17.7 68.0 all-gather.1
  158.8 41.6 reduce-scatter.1
